TPU v7x, 256 devices: a whole 4x4x8 slice. The times are simulated.
256 devices in a mesh: aa: 16 (over x_lo, y, core), ba: 16 (over z, x_hi).
Axes of the slice: x: 4 (x_hi: 2, x_lo: 2; x = x_hi * 2 + x_lo), y: 4, z: 8, core: 2. Of those that a mesh axis runs over, the one named last changes fastest.
Arguments:
- query: bfloat16 [6144, 4096], P('aa', 'ba'), may hold values from -28 to 28
- keys: bfloat16 [6144, 2048], P('aa', 'ba'), may hold values from -6 to 6
- values: bfloat16 [6144, 2048], P('aa', 'ba'), may hold values from -6 to 6
- grad_out: bfloat16 [6144, 5376], P('aa', 'ba'), may hold values from -6 to 6
- segment_ids: int32 [6144], P('aa'), may hold values from 0 to 5, never falling along the last dimension, each value on 1 to 3456 neighbouring positions
- w_query: bfloat16 [5376, 4096], P(None, 'ba'), may hold values from -0.125 to 0.125
- w_key: bfloat16 [5376, 2048], P(None, 'ba'), may hold values from -0.1875 to 0.1875
- w_value: bfloat16 [5376, 2048], P(None, 'ba'), may hold values from -0.1875 to 0.1875
- w_out: bfloat16 [4096, 5376], P('ba'), may hold values from -0.078125 to 0.078125
Outputs:
- grad_input: bfloat16 [6144, 5376], P('aa', 'ba')
Inputs may be any that keep to these rules, and one draw needn't show every extreme that they name: `segment_ids`: never falls along the sequence; each document has at most 3456 positions.
All inputs are finite; a program needn't handle non-finite values.
Results may differ from a plain program's by a relative error of at most 0.019.
Values may be sent and summed in bfloat16 or wider, within the bound.
No kernel may reach another device: no remote copies, remote signals or barrier semaphores. Data moves between devices by JAX's collectives and lax.ppermute only.
A program may use at most 128 MiB of HBM per device.

v0:
```python
import math

import jax
import jax.numpy as jnp
from jax import lax
from jax.experimental import pallas as pl
from jax.experimental.pallas import tpu as pltpu
from jax.sharding import Mesh
from jax.sharding import PartitionSpec as P


D = 5376
HQ = 32
HD = 128
DOCS = 6
ROWS = 384
HALF = 5
BLOCKS = 2 * HALF
SEG_ROWS = 16
PACKED = ROWS + SEG_ROWS
FEATS = 336
CHUNK = 384
WINDOW = 512
NEAR = 6
RING = 8
AA = ("xl", "y", "core")
BA = ("z", "xh")
NEG_FILL = -1e30
SCALE = (D / HQ) ** (-0.5)
SCALE2 = SCALE * math.log2(math.e)
F32 = jnp.float32
BF16 = jnp.bfloat16
VMEM = pl.BlockSpec(memory_space=pltpu.VMEM)
SMEM = pl.BlockSpec(memory_space=pltpu.SMEM)
ANY = pl.BlockSpec(memory_space=pl.ANY)


def dot(a, b):
    return lax.dot_general(a, b, (((1,), (0,)), ((), ())), preferred_element_type=F32)


def sources(low, high):
    odd = [d for d in range(HALF) if low <= BLOCKS - 1 - 2 * d < high]
    even = [k for k in range(HALF) if low <= BLOCKS - 2 - 2 * k < high]
    return odd, even, sorted({k for e in even for k in (e, e + 1)})


def load_window(low, high, core, kv_refs, buf, sem):
    odd, even, extra = sources(low, high)
    twin = dict(zip(odd, kv_refs))
    other = dict(zip(extra, kv_refs[len(odd) :]))
    copies = []
    for d in odd:
        at = BLOCKS - 1 - 2 * d - low
        copies.append(pltpu.make_async_copy(twin[d], buf.at[at], sem.at[at]))
        copies[-1].start()
    for k in even:
        at = BLOCKS - 2 - 2 * k - low
        from_low = pltpu.make_async_copy(other[k], buf.at[at], sem.at[at])
        from_high = pltpu.make_async_copy(other[k + 1], buf.at[at], sem.at[at])

        @pl.when(core == 1)
        def _(copy=from_low):
            copy.start()

        @pl.when(core == 0)
        def _(copy=from_high):
            copy.start()

        copies.append(from_low)
    return copies


def window_refs(low, high, twins, others):
    odd, _, extra = sources(low, high)
    return [twins[d] for d in odd] + [others[k] for k in extra]


def stats_kernel(low, high, own_ref, qseg_ref, q_ref, *refs):
    near = high == BLOCKS
    odd, _, extra = sources(low, high)
    count = len(odd) + len(extra)
    if near:
        kv_refs = refs[:count]
        m_ref, l_ref, out_ref, start_ref, buf, qt_ref, sem = refs[count:]
    else:
        m_in, l_in, out_in, start_in = refs[:4]
        kv_refs = refs[4 : 4 + count]
        lse_ref, out_ref, start_ref, low_ref, buf, qt_ref, m_ref, l_ref, sem = refs[4 + count :]
    own = own_ref[0]
    copies = load_window(low, high, lax.rem(own, 2), kv_refs, buf, sem)
    qt_ref[...] = q_ref[...].T
    if near:
        m_ref[...] = jnp.full(m_ref.shape, NEG_FILL, F32)
        l_ref[...] = jnp.zeros(l_ref.shape, F32)
        out_ref[...] = jnp.zeros(out_ref.shape, F32)
    else:
        m_ref[...] = m_in[...]
        l_ref[...] = l_in[...]
        out_ref[...] = out_in[...]
    seg = qseg_ref[...]
    seg0 = jnp.min(seg, axis=1, keepdims=True)
    for c in copies:
        c.wait()
    before = jnp.zeros((SEG_ROWS, HD), jnp.int32)
    line = lax.broadcasted_iota(jnp.int32, (SEG_ROWS, HD), 0)
    for b in range(low, min(high, BLOCKS - 1)):
        ids = buf[b - low, ROWS:, :HD].astype(F32).astype(jnp.int32)
        hit = (line < ROWS // HD) & (ids < seg0) & (own + b >= BLOCKS - 1)
        before = before + hit.astype(jnp.int32)
    start0 = jnp.sum(before) + jnp.maximum(own + low - (BLOCKS - 1), 0) * ROWS
    first_next = (own + high - (BLOCKS - 1)) * ROWS
    start = jnp.zeros((1, ROWS), jnp.int32) + start0
    if near:
        for s in range(1, DOCS):
            here = own * ROWS + jnp.sum((seg < s).astype(jnp.int32), axis=1, keepdims=True)
            start = jnp.where((seg == s) & (seg > seg0), here, start)
        start_ref[...] = start
    else:
        start = jnp.where((seg == seg0) & (start0 < first_next), start, start_in[...])
        start_ref[...] = start
        start0 = jnp.min(start)
    lowest = lax.div(start0, ROWS) - own + (BLOCKS - 1)
    pos = own * ROWS + lax.broadcasted_iota(jnp.int32, (1, ROWS), 1)
    key_at = lax.broadcasted_iota(jnp.int32, (ROWS, ROWS), 0)

    def one_block(back_to, carry):
        b = high - 1 - back_to
        first = (own + b - (BLOCKS - 1)) * ROWS
        allowed = (key_at >= start - first) & (key_at <= pos - first)
        kb = buf[b - low, :ROWS, :HD]
        vt = buf[b - low, :ROWS, HD:].T
        for h in range(2):
            part = slice(h * HD, (h + 1) * HD)
            s = jnp.where(allowed, dot(kb, qt_ref[part, :]) * SCALE2, NEG_FILL)
            m_old = m_ref[h : h + 1, :]
            m_new = jnp.maximum(m_old, jnp.max(s, axis=0, keepdims=True))
            p = jnp.exp2(s - m_new)
            back = jnp.exp2(m_old - m_new)
            l_ref[h : h + 1, :] = l_ref[h : h + 1, :] * back + jnp.sum(p, axis=0, keepdims=True)
            m_ref[h : h + 1, :] = m_new
            out_ref[part, :] = out_ref[part, :] * back + dot(vt, p.astype(BF16))
        return carry

    lax.fori_loop(0, high - jnp.clip(lowest, low, high), one_block, 0)
    if not near:
        low_ref[0] = lowest
        lse_ref[...] = m_ref[...] + jnp.log2(l_ref[...])
        for h in range(2):
            part = slice(h * HD, (h + 1) * HD)
            out_ref[part, :] = out_ref[part, :] / l_ref[h : h + 1, :]


def grads_kernel(own_ref, low_ref, start_ref, q_ref, near_ref, far_ref, lse_ref, out_ref, *refs):
    kv_refs, refs = refs[: BLOCKS + 1], refs[BLOCKS + 1 :]
    gqt_ref, mine_ref, theirs_ref = refs[:3]
    buf, qt_ref, dout_ref, doutt_ref, delta_ref, acc_ref, sem = refs[3:]
    own = own_ref[0]
    copies = load_window(0, BLOCKS, lax.rem(own, 2), kv_refs, buf, sem)
    lowest = low_ref[0]
    qt_ref[...] = q_ref[...].T
    doutt_ref[...] = (near_ref[...] + far_ref[...].astype(F32)).astype(BF16)
    dout_ref[...] = doutt_ref[...].T
    for h in range(2):
        part = slice(h * HD, (h + 1) * HD)
        delta_ref[h : h + 1, :] = jnp.sum(
            doutt_ref[part, :].astype(F32) * out_ref[part, :], axis=0, keepdims=True
        )
    acc_ref[...] = jnp.zeros(acc_ref.shape, F32)
    start = start_ref[...]
    pos = own * ROWS + lax.broadcasted_iota(jnp.int32, (1, ROWS), 1)
    key_at = lax.broadcasted_iota(jnp.int32, (ROWS, ROWS), 0)
    for c in copies:
        c.wait()

    def one_block(b, target, d):
        @pl.when(b >= lowest)
        def _():
            first = (own + b - (BLOCKS - 1)) * ROWS
            allowed = (key_at >= start - first) & (key_at <= pos - first)
            kb = buf[b, :ROWS, :HD]
            vb = buf[b, :ROWS, HD:]
            kt = kb.T
            gk = gv = None
            for h in range(2):
                part = slice(h * HD, (h + 1) * HD)
                s = dot(kb, qt_ref[part, :]) * SCALE2
                dp = dot(vb, doutt_ref[part, :])
                p = jnp.where(allowed, jnp.exp2(s - lse_ref[h : h + 1, :]), 0.0)
                ds = (p * (dp - delta_ref[h : h + 1, :])).astype(BF16)
                add_v = dot(p.astype(BF16), dout_ref[:, part])
                add_k = dot(ds, q_ref[:, part])
                gv = add_v if h == 0 else gv + add_v
                gk = add_k if h == 0 else gk + add_k
                acc_ref[part, :] += dot(kt, ds)
            target[d, :, :HD] = (gk * SCALE).astype(BF16)
            target[d, :, HD:] = gv.astype(BF16)

        @pl.when(b < lowest)
        def _():
            target[d] = jnp.zeros((ROWS, 2 * HD), BF16)

    def two_blocks(d, carry):
        one_block(BLOCKS - 1 - 2 * d, mine_ref, d)
        one_block(BLOCKS - 2 - 2 * d, theirs_ref, d)
        return carry

    lax.fori_loop(0, HALF, two_blocks, 0)
    gqt_ref[...] = (acc_ref[...] * SCALE).astype(BF16)


def attention_stats(own, qseg, query, twins, others, low, high, state=()):
    count = high - low
    window = window_refs(low, high, twins, others)
    row = jax.ShapeDtypeStruct((2, ROWS), F32)
    wide = jax.ShapeDtypeStruct((2 * HD, ROWS), F32)
    start = jax.ShapeDtypeStruct((1, ROWS), jnp.int32)
    lowest = jax.ShapeDtypeStruct((1,), jnp.int32)
    scratch = [
        pltpu.VMEM((count, PACKED, 2 * HD), BF16),
        pltpu.VMEM((2 * HD, ROWS), BF16),
    ]
    if state:
        scratch += [pltpu.VMEM((2, ROWS), F32), pltpu.VMEM((2, ROWS), F32)]
    return pl.pallas_call(
        lambda *refs: stats_kernel(low, high, *refs),
        name="stats_far" if state else "stats_near",
        out_shape=(row, wide, start, lowest) if state else (row, row, wide, start),
        in_specs=[SMEM, VMEM, VMEM] + [VMEM] * len(state) + [ANY] * len(window),
        out_specs=(VMEM, VMEM, VMEM, SMEM if state else VMEM),
        scratch_shapes=scratch + [pltpu.SemaphoreType.DMA((count,))],
    )(own, qseg, query, *state, *window)


def attention_grads(own, stats, query, near, far, twins, others):
    lse, out, start, lowest = stats
    window = window_refs(0, BLOCKS, twins, others)
    return pl.pallas_call(
        grads_kernel,
        name="attention_grads",
        out_shape=(
            jax.ShapeDtypeStruct((2 * HD, ROWS), BF16),
            jax.ShapeDtypeStruct((HALF, ROWS, 2 * HD), BF16),
            jax.ShapeDtypeStruct((HALF, ROWS, 2 * HD), BF16),
        ),
        in_specs=[SMEM, SMEM] + [VMEM] * 6 + [ANY] * len(window),
        out_specs=(VMEM, VMEM, VMEM),
        scratch_shapes=[
            pltpu.VMEM((BLOCKS, PACKED, 2 * HD), BF16),
            pltpu.VMEM((2 * HD, ROWS), BF16),
            pltpu.VMEM((ROWS, 2 * HD), BF16),
            pltpu.VMEM((2 * HD, ROWS), BF16),
            pltpu.VMEM((2, ROWS), F32),
            pltpu.VMEM((2 * HD, ROWS), F32),
            pltpu.SemaphoreType.DMA((BLOCKS,)),
        ],
    )(own, lowest, start, query, near, far, lse, out, *window)


def column_window(chunk):
    base = jnp.minimum(lax.div(chunk * FEATS, HD) * HD, D - WINDOW)
    return pl.ds(pl.multiple_of(base, HD), WINDOW), chunk * FEATS - base


def split_kernel(at_ref, w_ref, send_ref, buf, sem):
    first = at_ref[2] * (RING // 2)
    other = 1 - at_ref[1]
    copies = []
    for i in range(RING // 2):
        lanes, skip = column_window(2 * (first + i) + other)
        copy = pltpu.make_async_copy(w_ref.at[:, lanes], buf.at[i], sem.at[i])
        copy.start()
        copies.append((copy, skip))
    lane = lax.broadcasted_iota(jnp.int32, (2 * HD, CHUNK), 1)
    for i, (copy, skip) in enumerate(copies):
        copy.wait()
        moved = pltpu.roll(buf[i].astype(F32), lax.rem(WINDOW - skip, WINDOW), 1)[:, :CHUNK]
        send_ref[i] = jnp.where(lane < FEATS, moved, 0.0).astype(BF16)


def split_w_out(at, w_out):
    n = RING // 2
    return pl.pallas_call(
        split_kernel,
        name="split_w_out",
        out_shape=jax.ShapeDtypeStruct((n, 2 * HD, CHUNK), BF16),
        in_specs=[SMEM, ANY],
        out_specs=VMEM,
        scratch_shapes=[
            pltpu.VMEM((n, 2 * HD, WINDOW), BF16),
            pltpu.SemaphoreType.DMA((n,)),
        ],
    )(at, w_out)


def dout_kernel(deltas, at_ref, w_ref, pa, pb, *refs):
    shards = refs[:RING]
    near_ref, send_ref, wbuf, fbuf, gbuf, hbuf, sem = refs[RING:]
    z, xh, core = at_ref[0], at_ref[1], at_ref[2]
    copies = []
    for i in range(RING):
        chunk = lax.rem(z + deltas[i] + RING, RING)
        half = lax.div(chunk, RING // 2)
        inner = lax.rem(chunk, RING // 2)
        lanes, skip = column_window(2 * chunk + xh)
        place = pl.ds(pl.multiple_of(skip, 16), FEATS)
        far = pltpu.make_async_copy(pa.at[inner], fbuf.at[i], sem.at[i, 1])
        far_too = pltpu.make_async_copy(pb.at[inner], fbuf.at[i], sem.at[i, 1])
        pltpu.make_async_copy(w_ref.at[:, lanes], wbuf.at[i], sem.at[i, 0]).start()

        @pl.when(half == core)
        def _(copy=far):
            copy.start()

        @pl.when(half != core)
        def _(copy=far_too):
            copy.start()

        gbuf[i] = jnp.zeros((WINDOW, ROWS), BF16)
        hbuf[i, FEATS:] = jnp.zeros((CHUNK - FEATS, ROWS), BF16)
        to_far = pltpu.make_async_copy(shards[i], hbuf.at[i, :FEATS], sem.at[i, 2])
        to_far.start()
        to_own = pltpu.make_async_copy(shards[i], gbuf.at[i, place], sem.at[i, 3])
        to_own.start()
        copies.append(
            (pltpu.make_async_copy(w_ref.at[:, lanes], wbuf.at[i], sem.at[i, 0]), far, to_far, to_own)
        )
    near = far = None
    for i in range(RING):
        for c in copies[i]:
            c.wait()
        add_far = dot(fbuf[i], hbuf[i])
        add_near = dot(wbuf[i], gbuf[i])
        far = add_far if i == 0 else far + add_far
        near = add_near if i == 0 else near + add_near
    near_ref[...] = near
    send_ref[...] = far.astype(BF16)


def dout_parts(at, w_out, far_w, shards):
    deltas = tuple(shards)
    half = (2 * HD, ROWS)
    return pl.pallas_call(
        lambda *refs: dout_kernel(deltas, *refs),
        name="dout_parts",
        out_shape=(jax.ShapeDtypeStruct(half, F32), jax.ShapeDtypeStruct(half, BF16)),
        in_specs=[SMEM] + [ANY] * (3 + RING),
        out_specs=(VMEM, VMEM),
        scratch_shapes=[
            pltpu.VMEM((RING, 2 * HD, WINDOW), BF16),
            pltpu.VMEM((RING, 2 * HD, CHUNK), BF16),
            pltpu.VMEM((RING, WINDOW, ROWS), BF16),
            pltpu.VMEM((RING, CHUNK, ROWS), BF16),
            pltpu.SemaphoreType.DMA((RING, 4)),
        ],
    )(at, w_out, *far_w, *shards.values())


def join_kernel(core_ref, mine_ref, got_ref, own_ref, *send_refs):
    core = core_ref[0]
    for d in range(HALF + 1):
        at = d - core
        inside = (at >= 0) & (at < HALF)
        other = got_ref[jnp.clip(at, 0, HALF - 1)].astype(F32)
        total = jnp.where(inside, other, 0.0)
        if d < HALF:
            total = total + mine_ref[d].astype(F32)
        if d == 0:
            own_ref[...] = total
        else:
            send_refs[d - 1][...] = total.astype(BF16)


def join_partials(core, mine, got):
    shape = (ROWS, 2 * HD)
    result = pl.pallas_call(
        join_kernel,
        name="join_partials",
        out_shape=(jax.ShapeDtypeStruct(shape, F32),) + (jax.ShapeDtypeStruct(shape, BF16),) * HALF,
        in_specs=[SMEM, VMEM, VMEM],
        out_specs=(VMEM,) * (HALF + 1),
    )(core, mine, got)
    return result[0], result[1:]


def total_kernel(own_ref, *refs):
    total = own_ref[...]
    for ref in refs[:HALF]:
        total = total + ref[...].astype(F32)
    refs[HALF][...] = total.astype(BF16).T


def total_partials(own, parts):
    return pl.pallas_call(
        total_kernel,
        name="total_partials",
        out_shape=jax.ShapeDtypeStruct((2 * HD, ROWS), BF16),
        in_specs=[VMEM] * (HALF + 1),
        out_specs=VMEM,
    )(own, *parts)


def project_kernel(deltas, at_ref, *refs):
    wq, wk, wv, pa, pb, gq, gkv, gq2, gkv2 = refs[:9]
    outs = refs[9 : 9 + len(deltas)]
    bq, bk, bv, bp, sem = refs[9 + len(deltas) :]
    z, xh, core = at_ref[0], at_ref[1], at_ref[2]
    copies = []
    for n, delta in enumerate(deltas):
        chunk = lax.rem(z + delta + RING, RING)
        rows = pl.ds(pl.multiple_of((2 * chunk + xh) * FEATS, 16), FEATS)
        mine = [
            pltpu.make_async_copy(w.at[rows, :], b.at[n], sem.at[n, i])
            for i, (w, b) in enumerate(((wq, bq), (wk, bk), (wv, bv)))
        ]
        for c in mine:
            c.start()
        half = lax.div(chunk, RING // 2)
        inner = lax.rem(chunk, RING // 2)

        @pl.when(half == core)
        def _(n=n, inner=inner):
            pltpu.make_async_copy(pa.at[inner], bp.at[n], sem.at[n, 3]).start()

        @pl.when(half != core)
        def _(n=n, inner=inner):
            pltpu.make_async_copy(pb.at[inner], bp.at[n], sem.at[n, 3]).start()

        copies.append(mine + [pltpu.make_async_copy(pa.at[0], bp.at[n], sem.at[n, 3])])
    for n in range(len(deltas)):
        for c in copies[n]:
            c.wait()
        total = dot(bq[n], gq[...]) + dot(bk[n], gkv[:HD, :]) + dot(bv[n], gkv[HD:, :])
        total = total + dot(bp[n, :, : 2 * HD], gq2[...]) + dot(bp[n, :, 2 * HD :], gkv2[...])
        outs[n][...] = total.astype(outs[n].dtype)


def project(deltas, at, weights, far, grads, kind):
    n = len(deltas)
    return pl.pallas_call(
        lambda *refs: project_kernel(deltas, *refs),
        name="project",
        out_shape=(jax.ShapeDtypeStruct((FEATS, ROWS), kind),) * n,
        in_specs=[SMEM] + [ANY] * 5 + [VMEM] * 4,
        out_specs=(VMEM,) * n,
        scratch_shapes=[
            pltpu.VMEM((n, FEATS, 2 * HD), BF16),
            pltpu.VMEM((n, FEATS, HD), BF16),
            pltpu.VMEM((n, FEATS, HD), BF16),
            pltpu.VMEM((n, FEATS, 4 * HD), BF16),
            pltpu.SemaphoreType.DMA((n, 4)),
        ],
    )(at, *weights, *far, *grads)


def swapped(x, axis):
    return lax.ppermute(x, axis, [(0, 1), (1, 0)])


def chip_pairs(d):
    return [(i, i + 2 * d) for i in range(lax.axis_size(AA) - 2 * d) if d < HALF or i % 2]


def chips_on(x, d):
    return lax.ppermute(x, AA, chip_pairs(d))


def chips_back(x, d):
    return lax.ppermute(x, AA, [(j, i) for i, j in chip_pairs(d)])


def round_z(x, step):
    return lax.ppermute(x, "z", [(i, (i + step) % RING) for i in range(RING)])


def body(query, keys, values, grad_out, segment_ids, w_query, w_key, w_value, w_out):
    core = lax.axis_index("core")
    z = lax.axis_index("z")
    xh = lax.axis_index("xh")
    own = lax.axis_index(AA)[None]
    at = jnp.stack((z, xh, core))
    shards = {0: grad_out.T}
    for k in range(1, RING // 2 + 1):
        shards[-k] = round_z(shards[1 - k], 1)
        if k < RING // 2:
            shards[k] = round_z(shards[k - 1], -1)
    send_w = split_w_out(at, w_out)
    far_w = swapped(send_w, "xh")
    far_w = (far_w, swapped(far_w, "core"))
    ids = jnp.pad(
        segment_ids.astype(BF16).reshape(ROWS // HD, HD),
        ((0, SEG_ROWS - ROWS // HD), (0, HD)),
    )
    block = jnp.concatenate((jnp.concatenate((keys, values), axis=1), ids), axis=0)
    twins = [block] + [chips_on(block, d) for d in range(1, HALF + 1)]
    others = [swapped(twins[d], "core") for d in range(HALF + 1)]
    wanted = [
        lax.dynamic_index_in_dim(w.reshape(2, RING // 2, 2, FEATS, -1), core, 0, keepdims=False)
        for w in (w_query, w_key, w_value)
    ]
    wanted = [lax.dynamic_index_in_dim(w, 1 - xh, 1, keepdims=False) for w in wanted]
    far_mine = swapped(jnp.concatenate(wanted, axis=2), "xh")
    far_other = swapped(far_mine, "core")

    qseg = segment_ids[None, :]
    state = attention_stats(own, qseg, query, twins, others, NEAR, BLOCKS)
    near, send = dout_parts(at, w_out, far_w, shards)
    far = swapped(send, "xh")
    stats = attention_stats(own, qseg, query, twins, others, 0, NEAR, state)
    gqt, mine, theirs = attention_grads(own, stats, query, near, far, twins, others)
    got = swapped(theirs, "core")
    gqt_far = swapped(gqt, "xh")
    own_total, sends = join_partials(core[None], mine, got)
    parts = [chips_back(sends[d - 1], d) for d in range(HALF, 0, -1)]
    gkvt = total_partials(own_total, parts)
    gkvt_far = swapped(gkvt, "xh")

    weights = (w_query, w_key, w_value)
    far_rows = (far_mine, far_other)
    grads = (gqt, gkvt, gqt_far, gkvt_far)
    ahead, behind = project((4, -3), at, weights, far_rows, grads, BF16)
    rest = project((3, -2, 2, -1, 1, 0), at, weights, far_rows, grads, F32)
    ahead = round_z(ahead, 1)
    behind = round_z(behind, -1)
    for k in (2, 3):
        add_ahead, add_behind = rest[2 * k - 4], rest[2 * k - 3]
        ahead = round_z((ahead.astype(F32) + add_ahead).astype(BF16), 1)
        behind = round_z((behind.astype(F32) + add_behind).astype(BF16), -1)
    ahead = round_z((ahead.astype(F32) + rest[4]).astype(BF16), 1)
    result = (ahead.astype(F32) + behind.astype(F32) + rest[5]).astype(BF16)
    return result.T


def solution(mesh):
    finer = Mesh(mesh.devices.reshape(2, 4, 2, RING, 2), AA + BA)
    return jax.shard_map(
        body,
        mesh=finer,
        in_specs=(
            P(AA, BA),
            P(AA, BA),
            P(AA, BA),
            P(AA, BA),
            P(AA),
            P(None, BA),
            P(None, BA),
            P(None, BA),
            P(BA, None),
        ),
        out_specs=P(AA, BA),
        check_vma=False,
    )
```

profile of v0, /device:TPU:24, one launch (start us, length us, event | category | flops | bytes accessed | tf_op | source)
XLA Modules:
  0.0 211.0 jit_solution(1634296274170025760)
XLA Ops:
  0.0 0.6 pad_add_fusion.at_ref.refs_0_
  0.6 3.5 %split_w_out.1 = bf16[4,256,384]{2,1,0:T(8,128)(2,1)} custom-call(s32[3]{0:T(128)} %pad_add_fusion.at_ref.refs_0_, bf16[256,5376]{1,0:T(8,128)(2,1)} %refs_1_.3), custom_call_target="tpu_custom_call" | custom-call | tf_op jit(solution)/shard_map/split_w_out/pallas_call | solution.py:283
  4.0 3.1 %collective-permute-start.13 = (bf16[4,256,384]{2,1,0:T(8,128)(2,1)}, bf16[4,256,384]{2,1,0:T(8,128)(2,1)}, u32[]{:S(2)}, u32[]{:S(2)}) collective-permute-start(bf16[4,256,384]{2,1,0:T(8,128)(2,1)} %split_w_out.1), channel_id=1, source_target_pairs={{0,1},{1,0},{2,3},{3,2},{4,5},{5,4},{6,7},{7,6},{8,9},{9,8},{10,11... | collective-permute-start | bytes 2359304 | tf_op jit(solution)/shard_map/ppermute | solution.py:457
  7.2 3.2 %collective-permute-start.5 = (bf16[400,256]{1,0:T(8,128)(2,1)S(1)}, bf16[400,256]{1,0:T(8,128)(2,1)S(1)}, u32[]{:S(2)}, u32[]{:S(2)}) collective-permute-start(bf16[400,256]{1,0:T(8,128)(2,1)S(1)} %fusion.2.refs_3_.refs_0_), channel_id=1, source_target_pairs={{0,64},{16,80},{32,96},{48,112},{64,128},{80,144},{96,160},{112,17... | collective-permute-start | bytes 614408 | tf_op jit(solution)/shard_map/ppermute | solution.py:465
  10.4 4.1 %collective-permute-start.2 = (bf16[400,256]{1,0:T(8,128)(2,1)S(1)}, bf16[400,256]{1,0:T(8,128)(2,1)S(1)}, u32[]{:S(2)}, u32[]{:S(2)}) collective-permute-start(bf16[400,256]{1,0:T(8,128)(2,1)S(1)} %fusion.2.refs_3_.refs_0_), channel_id=1, source_target_pairs={{0,32},{16,48},{32,64},{48,80},{64,96},{80,112},{96,128},{112,144}... | collective-permute-start | bytes 614408 | tf_op jit(solution)/shard_map/ppermute | solution.py:465
  14.5 0.1 collective-permute-start.3
  14.6 2.0 collective-permute-start.8
  16.6 1.2 dynamic-slice_bitcast_fusion
  17.8 1.1 dynamic-slice_bitcast_fusion.1
  18.9 10.8 %collective-permute-done.5.refs_7_.refs_2_ = bf16[400,256]{1,0:T(8,128)(2,1)S(1)} collective-permute-done((bf16[400,256]{1,0:T(8,128)(2,1)S(1)}, bf16[400,256]{1,0:T(8,128)(2,1)S(1)}, u32[]{:S(2)}, u32[]{:S(2)}) %collective-permute-start.5) | collective-permute-done | bytes 204832 | tf_op jit(solution)/shard_map/ppermute | solution.py:465
  29.7 1.9 collective-permute-start.15
  31.6 0.1 pad_maximum_fusion
  31.7 2.5 %collective-permute-done.2.refs_4_.refs_1_ = bf16[400,256]{1,0:T(8,128)(2,1)S(1)} collective-permute-done((bf16[400,256]{1,0:T(8,128)(2,1)S(1)}, bf16[400,256]{1,0:T(8,128)(2,1)S(1)}, u32[]{:S(2)}, u32[]{:S(2)}) %collective-permute-start.2) | collective-permute-done | bytes 204832 | tf_op jit(solution)/shard_map/ppermute | solution.py:465
  34.2 0.5 collective-permute-start
  34.7 1.9 collective-permute-start.7
  36.6 0.1 collective-permute-start.14
  36.7 1.8 collective-permute-done.8.refs_9_.refs_4_
  38.6 5.9 %collective-permute-start.16 = (bf16[336,384]{1,0:T(8,128)(2,1)S(1)}, bf16[336,384]{1,0:T(8,128)(2,1)S(1)}, u32[]{:S(2)}, u32[]{:S(2)}) collective-permute-start(bf16[336,384]{1,0:T(8,128)(2,1)S(1)} %bitcast.29), channel_id=1, source_target_pairs={{0,14},{2,0},{4,2},{6,4},{8,6},{10,8},{12,10},{14,12},{1,15},{3,1}... | collective-permute-start | bytes 774152 | tf_op jit(solution)/shard_map/ppermute | solution.py:473
  44.5 26.9 %collective-permute-done.7.refs_8_.refs_3_ = bf16[400,256]{1,0:T(8,128)(2,1)} collective-permute-done((bf16[400,256]{1,0:T(8,128)(2,1)S(1)}, bf16[400,256]{1,0:T(8,128)(2,1)}, u32[]{:S(2)}, u32[]{:S(2)}) %collective-permute-start.7) | collective-permute-done | bytes 204832 | tf_op jit(solution)/shard_map/ppermute | solution.py:465
  71.3 1.4 collective-permute-start.11
  72.7 5.9 %collective-permute-start.18 = (bf16[336,384]{1,0:T(8,128)(2,1)S(1)}, bf16[336,384]{1,0:T(8,128)(2,1)S(1)}, u32[]{:S(2)}, u32[]{:S(2)}) collective-permute-start(bf16[336,384]{1,0:T(8,128)(2,1)S(1)} %collective-permute-done.16.refs_6_), channel_id=1, source_target_pairs={{0,14},{2,0},{4,2},{6,4},{8,6},{10,8},{12,10},{14,12},{1,15},{3,1}... | collective-permute-start | bytes 774152 | tf_op jit(solution)/shard_map/ppermute | solution.py:473
  78.6 0.1 collective-permute-start.6
  78.7 4.5 %collective-permute-done.18.refs_8_ = bf16[336,384]{1,0:T(8,128)(2,1)S(1)} collective-permute-done((bf16[336,384]{1,0:T(8,128)(2,1)S(1)}, bf16[336,384]{1,0:T(8,128)(2,1)S(1)}, u32[]{:S(2)}, u32[]{:S(2)}) %collective-permute-start.18) | collective-permute-done | bytes 258080 | tf_op jit(solution)/shard_map/ppermute | solution.py:473
  83.2 3.7 %collective-permute-start.20 = (bf16[336,384]{1,0:T(8,128)(2,1)S(1)}, bf16[336,384]{1,0:T(8,128)(2,1)S(1)}, u32[]{:S(2)}, u32[]{:S(2)}) collective-permute-start(bf16[336,384]{1,0:T(8,128)(2,1)S(1)} %collective-permute-done.18.refs_8_), channel_id=1, source_target_pairs={{0,14},{2,0},{4,2},{6,4},{8,6},{10,8},{12,10},{14,12},{1,15},{3,1}... | collective-permute-start | bytes 774152 | tf_op jit(solution)/shard_map/ppermute | solution.py:473
  86.9 0.1 collective-permute-start.4
  87.0 3.7 %collective-permute-done.20.refs_10_ = bf16[336,384]{1,0:T(8,128)(2,1)S(1)} collective-permute-done((bf16[336,384]{1,0:T(8,128)(2,1)S(1)}, bf16[336,384]{1,0:T(8,128)(2,1)S(1)}, u32[]{:S(2)}, u32[]{:S(2)}) %collective-permute-start.20) | collective-permute-done | bytes 258080 | tf_op jit(solution)/shard_map/ppermute | solution.py:473
  90.7 3.7 %collective-permute-done.21.refs_11_ = bf16[336,384]{1,0:T(8,128)(2,1)S(1)} collective-permute-done((bf16[336,384]{1,0:T(8,128)(2,1)S(1)}, bf16[336,384]{1,0:T(8,128)(2,1)S(1)}, u32[]{:S(2)}, u32[]{:S(2)}) %collective-permute-start.21) | collective-permute-done | bytes 258080 | tf_op jit(solution)/shard_map/ppermute | solution.py:473
  94.5 0.7 copy-done.22
  95.1 0.1 collective-permute-start.12
  95.2 7.0 %dout_parts.1 = (f32[256,384]{1,0:T(8,128)}, bf16[256,384]{1,0:T(8,128)(2,1)}) custom-call(s32[3]{0:T(128)} %pad_add_fusion.at_ref.refs_0_, bf16[256,5376]{1,0:T(8,128)(2,1)} %refs_1_.3, bf16[4,256,384]{2,1,0:T(8,128)(2,1)} %collective-permute-done.13.refs_2_, bf16[4,256,384]{2,1,0:T(8,128)(2,1)} %collective-permute-done.14.refs_3_, ...), custom_call_target="tpu_custom_call" | custom-call | tf_op jit(solution)/shard_map/dout_parts/pallas_call | solution.py:343
  102.3 0.5 collective-permute-start.22
  102.8 0.6 broadcast_in_dim.8.refs_1_
  103.4 7.5 %stats_near.1 = (f32[2,384]{1,0:T(2,128)}, f32[2,384]{1,0:T(2,128)}, f32[256,384]{1,0:T(8,128)}, s32[1,384]{1,0:T(1,128)}) custom-call(s32[1]{0:T(128)} %bitcast.9.refs_0_.own_ref, s32[1,384]{1,0:T(1,128)} %broadcast_in_dim.8.refs_1_, bf16[384,256]{1,0:T(8,128)(2,1)} %q_ref.1, bf16[400,256]{1,0:T(8,128)(2,1)} %copy-done.3, bf16[400,256]{1,0:T(8,128)(2,1)} %copy-done.5, ...), custom_call_target="tpu_custom_call" | custom-call | tf_op jit(solution)/shard_map/stats_near/pallas_call | solution.py:225
  110.9 7.0 %stats_far.1 = (f32[2,384]{1,0:T(2,128)}, f32[256,384]{1,0:T(8,128)}, s32[1,384]{1,0:T(1,128)}, s32[1]{0:T(128)}) custom-call(s32[1]{0:T(128)} %bitcast.9.refs_0_.own_ref, s32[1,384]{1,0:T(1,128)} %broadcast_in_dim.8.refs_1_, bf16[384,256]{1,0:T(8,128)(2,1)} %q_ref.1, f32[2,384]{1,0:T(2,128)} %get-tuple-element.32.refs_3_, ...), custom_call_target="tpu_custom_call" | custom-call | tf_op jit(solution)/shard_map/stats_far/pallas_call | solution.py:225
  117.9 0.7 copy-done.25
  118.6 12.9 %attention_grads.1 = (bf16[256,384]{1,0:T(8,128)(2,1)}, bf16[5,384,256]{2,1,0:T(8,128)(2,1)}, bf16[5,384,256]{2,1,0:T(8,128)(2,1)}) custom-call(s32[1]{0:T(128)} %bitcast.9.refs_0_.own_ref, s32[1]{0:T(128)} %get-tuple-element.36.low_ref, s32[1,384]{1,0:T(1,128)} %get-tuple-element.37.start_ref, bf16[384,256]{1,0:T(8,128)(2,1)} %q_ref.1, ...), custom_call_target="tpu_custom_call" | custom-call | tf_op jit(solution)/shard_map/attention_grads/pallas_call | solution.py:238
  131.5 2.4 %collective-permute-start.23 = (bf16[5,384,256]{2,1,0:T(8,128)(2,1)}, bf16[5,384,256]{2,1,0:T(8,128)(2,1)}, u32[]{:S(2)}, u32[]{:S(2)}) collective-permute-start(bf16[5,384,256]{2,1,0:T(8,128)(2,1)} %get-tuple-element.44), channel_id=1, source_target_pairs={{0,16},{16,0},{1,17},{17,1},{2,18},{18,2},{3,19},{19,3},{4,20},{20... | collective-permute-start | bytes 2949128 | tf_op jit(solution)/shard_map/ppermute | solution.py:457
  133.9 0.1 collective-permute-start.1
  134.1 2.4 %collective-permute-done.23.got_ref = bf16[5,384,256]{2,1,0:T(8,128)(2,1)} collective-permute-done((bf16[5,384,256]{2,1,0:T(8,128)(2,1)}, bf16[5,384,256]{2,1,0:T(8,128)(2,1)}, u32[]{:S(2)}, u32[]{:S(2)}) %collective-permute-start.23) | collective-permute-done | bytes 983072 | tf_op jit(solution)/shard_map/ppermute | solution.py:457
  136.5 2.7 %join_partials.1 = (f32[384,256]{1,0:T(8,128)}, bf16[384,256]{1,0:T(8,128)(2,1)}, bf16[384,256]{1,0:T(8,128)(2,1)}, bf16[384,256]{1,0:T(8,128)(2,1)}, bf16[384,2...) custom-call(s32[1]{0:T(128)} %bitcast.2.core_ref, bf16[5,384,256]{2,1,0:T(8,128)(2,1)} %get-tuple-element.43.mine_ref, ...), custom_call_target="tpu_custom_call" | custom-call | tf_op jit(solution)/shard_map/join_partials/pallas_call | solution.py:376
  139.1 0.7 collective-permute-start.24
  139.8 1.3 collective-permute-start.25
  141.1 1.9 collective-permute-start.26
  143.0 1.9 collective-permute-start.27
  145.0 1.9 collective-permute-start.28
  146.9 2.2 %collective-permute-done.25.refs_1_ = bf16[384,256]{1,0:T(8,128)(2,1)S(1)} collective-permute-done((bf16[384,256]{1,0:T(8,128)(2,1)}, bf16[384,256]{1,0:T(8,128)(2,1)S(1)}, u32[]{:S(2)}, u32[]{:S(2)}) %collective-permute-start.25) | collective-permute-done | bytes 196640 | tf_op jit(solution)/shard_map/ppermute | solution.py:469
  149.1 3.0 %collective-permute-start.29 = (bf16[256,384]{1,0:T(8,128)(2,1)S(1)}, bf16[256,384]{1,0:T(8,128)(2,1)S(1)}, u32[]{:S(2)}, u32[]{:S(2)}) collective-permute-start(bf16[256,384]{1,0:T(8,128)(2,1)S(1)} %copy-done.7), channel_id=1, source_target_pairs={{0,1},{1,0},{2,3},{3,2},{4,5},{5,4},{6,7},{7,6},{8,9},{9,8},{10,11... | collective-permute-start | bytes 589832 | tf_op jit(solution)/shard_map/ppermute | solution.py:457
  152.1 5.0 %collective-permute-done.27.refs_3_ = bf16[384,256]{1,0:T(8,128)(2,1)} collective-permute-done((bf16[384,256]{1,0:T(8,128)(2,1)}, bf16[384,256]{1,0:T(8,128)(2,1)}, u32[]{:S(2)}, u32[]{:S(2)}) %collective-permute-start.27) | collective-permute-done | bytes 196640 | tf_op jit(solution)/shard_map/ppermute | solution.py:469
  157.0 2.5 %collective-permute-done.28.refs_4_ = bf16[384,256]{1,0:T(8,128)(2,1)} collective-permute-done((bf16[384,256]{1,0:T(8,128)(2,1)}, bf16[384,256]{1,0:T(8,128)(2,1)}, u32[]{:S(2)}, u32[]{:S(2)}) %collective-permute-start.28) | collective-permute-done | bytes 196640 | tf_op jit(solution)/shard_map/ppermute | solution.py:469
  159.6 2.2 %total_partials.1.refs_7_ = bf16[256,384]{1,0:T(8,128)(2,1)} custom-call(f32[384,256]{1,0:T(8,128)} %get-tuple-element.45.own_ref, bf16[384,256]{1,0:T(8,128)(2,1)} %copy-done.23, bf16[384,256]{1,0:T(8,128)(2,1)} %copy-done.24, bf16[384,256]{1,0:T(8,128)(2,1)} %collective-permute-done.26.refs_2_, bf16[384,256]{1,0:T(8,128)(2,1)} %collective-permute-done.27.refs_3_, ...), custom_call_target="tpu_custom_call" | custom-call | tf_op jit(solution)/shard_map/total_partials/pallas_call | solution.py:394
  161.8 2.7 %collective-permute-start.30 = (bf16[256,384]{1,0:T(8,128)(2,1)}, bf16[256,384]{1,0:T(8,128)(2,1)S(1)}, u32[]{:S(2)}, u32[]{:S(2)}) collective-permute-start(bf16[256,384]{1,0:T(8,128)(2,1)} %total_partials.1.refs_7_), channel_id=1, source_target_pairs={{0,1},{1,0},{2,3},{3,2},{4,5},{5,4},{6,7},{7,6},{8,9},{9,8},{10,11... | collective-permute-start | bytes 589832 | tf_op jit(solution)/shard_map/ppermute | solution.py:457
  164.6 4.7 %collective-permute-done.30.refs_9_ = bf16[256,384]{1,0:T(8,128)(2,1)S(1)} collective-permute-done((bf16[256,384]{1,0:T(8,128)(2,1)}, bf16[256,384]{1,0:T(8,128)(2,1)S(1)}, u32[]{:S(2)}, u32[]{:S(2)}) %collective-permute-start.30) | collective-permute-done | bytes 196640 | tf_op jit(solution)/shard_map/ppermute | solution.py:457
  169.3 0.7 copy-done.9
  169.9 4.4 %project.2 = (bf16[336,384]{1,0:T(8,128)(2,1)}, bf16[336,384]{1,0:T(8,128)(2,1)}) custom-call(s32[3]{0:T(128)} %pad_add_fusion.at_ref.refs_0_, bf16[5376,256]{1,0:T(8,128)(2,1)} %refs_1_.5, bf16[5376,128]{1,0:T(8,128)(2,1)} %refs_2_.7, bf16[5376,128]{1,0:T(8,128)(2,1)} %refs_3_.3, bf16[4,336,512]{2,1,0:T(8,128)(2,1)} %copy-done, ...), custom_call_target="tpu_custom_call" | custom-call | tf_op jit(solution)/shard_map/project/pallas_call | solution.py:440
  174.3 0.3 collective-permute-start.31
  174.6 3.2 %collective-permute-start.35 = (bf16[336,384]{1,0:T(8,128)(2,1)}, bf16[336,384]{1,0:T(8,128)(2,1)S(1)}, u32[]{:S(2)}, u32[]{:S(2)}) collective-permute-start(bf16[336,384]{1,0:T(8,128)(2,1)} %get-tuple-element.55), channel_id=1, source_target_pairs={{0,14},{2,0},{4,2},{6,4},{8,6},{10,8},{12,10},{14,12},{1,15},{3,1}... | collective-permute-start | bytes 774152 | tf_op jit(solution)/shard_map/ppermute | solution.py:473
  177.9 7.3 %project.3 = (f32[336,384]{1,0:T(8,128)}, f32[336,384]{1,0:T(8,128)}, f32[336,384]{1,0:T(8,128)}, f32[336,384]{1,0:T(8,128)}, f32[336,384]{1,0:T(8,128)}, /*index=5*/f32[336,384]{1,0:T(8,128)}) custom-call(s32[3]{0:T(128)} %pad_add_fusion.at_ref.refs_0_, bf16[5376,256]{1,0:T(8,128)(2,1)} %refs_1_.5, bf16[5376,128]{1,0:T(8,128)(2,1)} %refs_2_.7, ...), custom_call_target="tpu_custom_call" | custom-call | tf_op jit(solution)/shard_map/project/pallas_call | solution.py:440
  185.2 1.2 add_convert_fusion.5
  186.6 3.3 %collective-permute-start.36 = (bf16[336,384]{1,0:T(8,128)(2,1)S(1)}, bf16[336,384]{1,0:T(8,128)(2,1)S(1)}, u32[]{:S(2)}, u32[]{:S(2)}) collective-permute-start(bf16[336,384]{1,0:T(8,128)(2,1)S(1)} %add_convert_fusion.2), channel_id=1, source_target_pairs={{0,14},{2,0},{4,2},{6,4},{8,6},{10,8},{12,10},{14,12},{1,15},{3,1}... | collective-permute-start | bytes 774152 | tf_op jit(solution)/shard_map/ppermute | solution.py:473
  189.9 4.1 %collective-permute-done.32 = bf16[336,384]{1,0:T(8,128)(2,1)S(1)} collective-permute-done((bf16[336,384]{1,0:T(8,128)(2,1)S(1)}, bf16[336,384]{1,0:T(8,128)(2,1)S(1)}, u32[]{:S(2)}, u32[]{:S(2)}) %collective-permute-start.32) | collective-permute-done | bytes 258080 | tf_op jit(solution)/shard_map/ppermute | solution.py:473
  194.3 3.3 %collective-permute-start.37 = (bf16[336,384]{1,0:T(8,128)(2,1)S(1)}, bf16[336,384]{1,0:T(8,128)(2,1)S(1)}, u32[]{:S(2)}, u32[]{:S(2)}) collective-permute-start(bf16[336,384]{1,0:T(8,128)(2,1)S(1)} %add_convert_fusion.1), channel_id=1, source_target_pairs={{0,14},{2,0},{4,2},{6,4},{8,6},{10,8},{12,10},{14,12},{1,15},{3,1}... | collective-permute-start | bytes 774152 | tf_op jit(solution)/shard_map/ppermute | solution.py:473
  197.6 5.0 %collective-permute-done.33 = bf16[336,384]{1,0:T(8,128)(2,1)S(1)} collective-permute-done((bf16[336,384]{1,0:T(8,128)(2,1)S(1)}, bf16[336,384]{1,0:T(8,128)(2,1)S(1)}, u32[]{:S(2)}, u32[]{:S(2)}) %collective-permute-start.33) | collective-permute-done | bytes 258080 | tf_op jit(solution)/shard_map/ppermute | solution.py:473
  202.7 7.5 %collective-permute-done.34 = bf16[336,384]{1,0:T(8,128)(2,1)S(1)} collective-permute-done((bf16[336,384]{1,0:T(8,128)(2,1)S(1)}, bf16[336,384]{1,0:T(8,128)(2,1)S(1)}, u32[]{:S(2)}, u32[]{:S(2)}) %collective-permute-start.34) | collective-permute-done | bytes 258080 | tf_op jit(solution)/shard_map/ppermute | solution.py:473
  210.2 0.8 fusion.1
  (92 shorter events, 0.7 us)
Async XLA Ops:
  0.6 6.6 %copy-start.28 = (s32[384]{0:T(512)S(1)}, s32[384]{0:T(512)}, u32[]{:S(2)}) copy-start(s32[384]{0:T(512)} %param.13) | copy-start | bytes 4612
  0.6 6.6 %copy-start.26 = (bf16[384,128]{1,0:T(8,128)(2,1)S(1)}, bf16[384,128]{1,0:T(8,128)(2,1)}, u32[]{:S(2)}) copy-start(bf16[384,128]{1,0:T(8,128)(2,1)} %param.11) | copy-start | bytes 294916
  0.6 6.6 %copy-start.27 = (bf16[384,128]{1,0:T(8,128)(2,1)S(1)}, bf16[384,128]{1,0:T(8,128)(2,1)}, u32[]{:S(2)}) copy-start(bf16[384,128]{1,0:T(8,128)(2,1)} %param.10) | copy-start | bytes 294916
  4.0 32.6 %collective-permute-start.13 = (bf16[4,256,384]{2,1,0:T(8,128)(2,1)}, bf16[4,256,384]{2,1,0:T(8,128)(2,1)}, u32[]{:S(2)}, u32[]{:S(2)}) collective-permute-start(bf16[4,256,384]{2,1,0:T(8,128)(2,1)} %split_w_out.1), channel_id=1, source_target_pairs={{0,1},{1,0},{2,3},{3,2},{4,5},{5,4},{6,7},{7,6},{8,9},{9,8},{10,11... | collective-permute-start | bytes 2359304 | tf_op jit(solution)/shard_map/ppermute | solution.py:457
  7.2 64.1 %copy-start.3 = (bf16[400,256]{1,0:T(8,128)(2,1)}, bf16[400,256]{1,0:T(8,128)(2,1)S(1)}, u32[]{:S(2)}) copy-start(bf16[400,256]{1,0:T(8,128)(2,1)S(1)} %fusion.2.refs_3_.refs_0_) | copy-start | bytes 614404
  7.2 22.5 %collective-permute-start.5 = (bf16[400,256]{1,0:T(8,128)(2,1)S(1)}, bf16[400,256]{1,0:T(8,128)(2,1)S(1)}, u32[]{:S(2)}, u32[]{:S(2)}) collective-permute-start(bf16[400,256]{1,0:T(8,128)(2,1)S(1)} %fusion.2.refs_3_.refs_0_), channel_id=1, source_target_pairs={{0,64},{16,80},{32,96},{48,112},{64,128},{80,144},{96,160},{112,17... | collective-permute-start | bytes 614408 | tf_op jit(solution)/shard_map/ppermute | solution.py:465
  10.4 23.8 %collective-permute-start.2 = (bf16[400,256]{1,0:T(8,128)(2,1)S(1)}, bf16[400,256]{1,0:T(8,128)(2,1)S(1)}, u32[]{:S(2)}, u32[]{:S(2)}) collective-permute-start(bf16[400,256]{1,0:T(8,128)(2,1)S(1)} %fusion.2.refs_3_.refs_0_), channel_id=1, source_target_pairs={{0,32},{16,48},{32,64},{48,80},{64,96},{80,112},{96,128},{112,144}... | collective-permute-start | bytes 614408 | tf_op jit(solution)/shard_map/ppermute | solution.py:465
  14.5 20.2 %collective-permute-start.3 = (bf16[400,256]{1,0:T(8,128)(2,1)S(1)}, bf16[400,256]{1,0:T(8,128)(2,1)}, u32[]{:S(2)}, u32[]{:S(2)}) collective-permute-start(bf16[400,256]{1,0:T(8,128)(2,1)S(1)} %fusion.2.refs_3_.refs_0_), channel_id=1, source_target_pairs={{0,16},{16,0},{1,17},{17,1},{2,18},{18,2},{3,19},{19,3},{4,20},{20... | collective-permute-start | bytes 614408 | tf_op jit(solution)/shard_map/ppermute | solution.py:457
  14.6 24.0 %collective-permute-start.8 = (bf16[400,256]{1,0:T(8,128)(2,1)S(1)}, bf16[400,256]{1,0:T(8,128)(2,1)}, u32[]{:S(2)}, u32[]{:S(2)}) collective-permute-start(bf16[400,256]{1,0:T(8,128)(2,1)S(1)} %fusion.2.refs_3_.refs_0_), channel_id=1, source_target_pairs={{0,128},{16,144},{32,160},{48,176},{64,192},{80,208},{96,224},{112... | collective-permute-start | bytes 614408 | tf_op jit(solution)/shard_map/ppermute | solution.py:465
  16.6 13.1 %copy-start.15 = (bf16[384,336]{0,1:T(8,128)(2,1)S(1)}, bf16[384,336]{0,1:T(8,128)(2,1)}, u32[]{:S(2)}) copy-start(bf16[384,336]{0,1:T(8,128)(2,1)} %param.12) | copy-start | bytes 774148
  29.7 48.9 %copy-start.4 = (bf16[400,256]{1,0:T(8,128)(2,1)}, bf16[400,256]{1,0:T(8,128)(2,1)S(1)}, u32[]{:S(2)}) copy-start(bf16[400,256]{1,0:T(8,128)(2,1)S(1)} %collective-permute-done.5.refs_7_.refs_2_) | copy-start | bytes 614404
  29.7 14.8 %collective-permute-start.15 = (bf16[336,384]{1,0:T(8,128)(2,1)S(1)}, bf16[336,384]{1,0:T(8,128)(2,1)S(1)}, u32[]{:S(2)}, u32[]{:S(2)}) collective-permute-start(bf16[336,384]{1,0:T(8,128)(2,1)S(1)} %bitcast.28), channel_id=1, source_target_pairs={{0,2},{2,4},{4,6},{6,8},{8,10},{10,12},{12,14},{14,0},{1,3},{3,5},... | collective-permute-start | bytes 774152 | tf_op jit(solution)/shard_map/ppermute | solution.py:473
  34.2 68.1 %copy-start.5 = (bf16[400,256]{1,0:T(8,128)(2,1)}, bf16[400,256]{1,0:T(8,128)(2,1)S(1)}, u32[]{:S(2)}) copy-start(bf16[400,256]{1,0:T(8,128)(2,1)S(1)} %collective-permute-done.2.refs_4_.refs_1_) | copy-start | bytes 614404
  34.2 99.7 %collective-permute-start = (bf16[4,336,512]{2,1,0:T(8,128)(2,1)S(1)}, bf16[4,336,512]{2,1,0:T(8,128)(2,1)S(1)}, u32[]{:S(2)}, u32[]{:S(2)}) collective-permute-start(bf16[4,336,512]{2,1,0:T(8,128)(2,1)S(1)} %pad_maximum_fusion), channel_id=1, source_target_pairs={{0,1},{1,0},{2,3},{3,2},{4,5},{5,4},{6,7},{7,6},{8,9},{9,8},{10,11... | collective-permute-start | bytes 4128776 | tf_op jit(solution)/shard_map/ppermute | solution.py:457
  34.7 36.6 %collective-permute-start.7 = (bf16[400,256]{1,0:T(8,128)(2,1)S(1)}, bf16[400,256]{1,0:T(8,128)(2,1)}, u32[]{:S(2)}, u32[]{:S(2)}) collective-permute-start(bf16[400,256]{1,0:T(8,128)(2,1)S(1)} %fusion.2.refs_3_.refs_0_), channel_id=1, source_target_pairs={{0,96},{16,112},{32,128},{48,144},{64,160},{80,176},{96,192},{112,... | collective-permute-start | bytes 614408 | tf_op jit(solution)/shard_map/ppermute | solution.py:465
  36.6 57.8 %collective-permute-start.14 = (bf16[4,256,384]{2,1,0:T(8,128)(2,1)}, bf16[4,256,384]{2,1,0:T(8,128)(2,1)}, u32[]{:S(2)}, u32[]{:S(2)}) collective-permute-start(bf16[4,256,384]{2,1,0:T(8,128)(2,1)} %collective-permute-done.13.refs_2_), channel_id=1, source_target_pairs={{0,16},{16,0},{1,17},{17,1},{2,18},{18,2},{3,19},{19,3},{4,20},{20... | collective-permute-start | bytes 2359304 | tf_op jit(solution)/shard_map/ppermute | solution.py:457
  38.6 34.1 %collective-permute-start.16 = (bf16[336,384]{1,0:T(8,128)(2,1)S(1)}, bf16[336,384]{1,0:T(8,128)(2,1)S(1)}, u32[]{:S(2)}, u32[]{:S(2)}) collective-permute-start(bf16[336,384]{1,0:T(8,128)(2,1)S(1)} %bitcast.29), channel_id=1, source_target_pairs={{0,14},{2,0},{4,2},{6,4},{8,6},{10,8},{12,10},{14,12},{1,15},{3,1}... | collective-permute-start | bytes 774152 | tf_op jit(solution)/shard_map/ppermute | solution.py:473
  44.4 42.5 %copy-start.16 = (bf16[336,384]{1,0:T(8,128)(2,1)}, bf16[336,384]{1,0:T(8,128)(2,1)S(1)}, u32[]{:S(2)}) copy-start(bf16[336,384]{1,0:T(8,128)(2,1)S(1)} %collective-permute-done.15.refs_5_) | copy-start | bytes 774148
  44.4 34.1 %collective-permute-start.17 = (bf16[336,384]{1,0:T(8,128)(2,1)S(1)}, bf16[336,384]{1,0:T(8,128)(2,1)S(1)}, u32[]{:S(2)}, u32[]{:S(2)}) collective-permute-start(bf16[336,384]{1,0:T(8,128)(2,1)S(1)} %collective-permute-done.15.refs_5_), channel_id=1, source_target_pairs={{0,2},{2,4},{4,6},{6,8},{8,10},{10,12},{12,14},{14,0},{1,3},{3,5},... | collective-permute-start | bytes 774152 | tf_op jit(solution)/shard_map/ppermute | solution.py:473
  71.3 7.2 %collective-permute-start.11 = (bf16[400,256]{1,0:T(8,128)(2,1)S(1)}, bf16[400,256]{1,0:T(8,128)(2,1)}, u32[]{:S(2)}, u32[]{:S(2)}) collective-permute-start(bf16[400,256]{1,0:T(8,128)(2,1)S(1)} %fusion.2.refs_3_.refs_0_), channel_id=1, source_target_pairs={{16,176},{48,208},{80,240},{17,177},{49,209},{81,241},{18,178},{50... | collective-permute-start | bytes 614408 | tf_op jit(solution)/shard_map/ppermute | solution.py:465
  72.7 14.3 %copy-start.17 = (bf16[336,384]{1,0:T(8,128)(2,1)}, bf16[336,384]{1,0:T(8,128)(2,1)S(1)}, u32[]{:S(2)}) copy-start(bf16[336,384]{1,0:T(8,128)(2,1)S(1)} %collective-permute-done.16.refs_6_) | copy-start | bytes 774148
  72.7 10.5 %collective-permute-start.18 = (bf16[336,384]{1,0:T(8,128)(2,1)S(1)}, bf16[336,384]{1,0:T(8,128)(2,1)S(1)}, u32[]{:S(2)}, u32[]{:S(2)}) collective-permute-start(bf16[336,384]{1,0:T(8,128)(2,1)S(1)} %collective-permute-done.16.refs_6_), channel_id=1, source_target_pairs={{0,14},{2,0},{4,2},{6,4},{8,6},{10,8},{12,10},{14,12},{1,15},{3,1}... | collective-permute-start | bytes 774152 | tf_op jit(solution)/shard_map/ppermute | solution.py:473
  78.6 12.2 %copy-start.18 = (bf16[336,384]{1,0:T(8,128)(2,1)}, bf16[336,384]{1,0:T(8,128)(2,1)S(1)}, u32[]{:S(2)}) copy-start(bf16[336,384]{1,0:T(8,128)(2,1)S(1)} %collective-permute-done.17.refs_7_) | copy-start | bytes 774148
  78.6 8.3 %collective-permute-start.19 = (bf16[336,384]{1,0:T(8,128)(2,1)S(1)}, bf16[336,384]{1,0:T(8,128)(2,1)S(1)}, u32[]{:S(2)}, u32[]{:S(2)}) collective-permute-start(bf16[336,384]{1,0:T(8,128)(2,1)S(1)} %collective-permute-done.17.refs_7_), channel_id=1, source_target_pairs={{0,2},{2,4},{4,6},{6,8},{8,10},{10,12},{12,14},{14,0},{1,3},{3,5},... | collective-permute-start | bytes 774152 | tf_op jit(solution)/shard_map/ppermute | solution.py:473
  78.6 8.3 %collective-permute-start.6 = (bf16[400,256]{1,0:T(8,128)(2,1)S(1)}, bf16[400,256]{1,0:T(8,128)(2,1)S(1)}, u32[]{:S(2)}, u32[]{:S(2)}) collective-permute-start(bf16[400,256]{1,0:T(8,128)(2,1)S(1)} %collective-permute-done.5.refs_7_.refs_2_), channel_id=1, source_target_pairs={{0,16},{16,0},{1,17},{17,1},{2,18},{18,2},{3,19},{19,3},{4,20},{20... | collective-permute-start | bytes 614408 | tf_op jit(solution)/shard_map/ppermute | solution.py:457
  83.2 7.6 %copy-start.19 = (bf16[336,384]{1,0:T(8,128)(2,1)}, bf16[336,384]{1,0:T(8,128)(2,1)S(1)}, u32[]{:S(2)}) copy-start(bf16[336,384]{1,0:T(8,128)(2,1)S(1)} %collective-permute-done.18.refs_8_) | copy-start | bytes 774148
  83.2 7.5 %collective-permute-start.20 = (bf16[336,384]{1,0:T(8,128)(2,1)S(1)}, bf16[336,384]{1,0:T(8,128)(2,1)S(1)}, u32[]{:S(2)}, u32[]{:S(2)}) collective-permute-start(bf16[336,384]{1,0:T(8,128)(2,1)S(1)} %collective-permute-done.18.refs_8_), channel_id=1, source_target_pairs={{0,14},{2,0},{4,2},{6,4},{8,6},{10,8},{12,10},{14,12},{1,15},{3,1}... | collective-permute-start | bytes 774152 | tf_op jit(solution)/shard_map/ppermute | solution.py:473
  86.9 7.5 %copy-start.20 = (bf16[336,384]{1,0:T(8,128)(2,1)}, bf16[336,384]{1,0:T(8,128)(2,1)S(1)}, u32[]{:S(2)}) copy-start(bf16[336,384]{1,0:T(8,128)(2,1)S(1)} %collective-permute-done.19.refs_9_) | copy-start | bytes 774148
  86.9 7.5 %collective-permute-start.21 = (bf16[336,384]{1,0:T(8,128)(2,1)S(1)}, bf16[336,384]{1,0:T(8,128)(2,1)S(1)}, u32[]{:S(2)}, u32[]{:S(2)}) collective-permute-start(bf16[336,384]{1,0:T(8,128)(2,1)S(1)} %collective-permute-done.19.refs_9_), channel_id=1, source_target_pairs={{0,2},{2,4},{4,6},{6,8},{8,10},{10,12},{12,14},{14,0},{1,3},{3,5},... | collective-permute-start | bytes 774152 | tf_op jit(solution)/shard_map/ppermute | solution.py:473
  86.9 15.4 %copy-start.2 = (bf16[400,256]{1,0:T(8,128)(2,1)}, bf16[400,256]{1,0:T(8,128)(2,1)S(1)}, u32[]{:S(2)}) copy-start(bf16[400,256]{1,0:T(8,128)(2,1)S(1)} %collective-permute-done.6.refs_7_.refs_10_) | copy-start | bytes 614404
  86.9 15.4 %collective-permute-start.4 = (bf16[400,256]{1,0:T(8,128)(2,1)S(1)}, bf16[400,256]{1,0:T(8,128)(2,1)S(1)}, u32[]{:S(2)}, u32[]{:S(2)}) collective-permute-start(bf16[400,256]{1,0:T(8,128)(2,1)S(1)} %collective-permute-done.2.refs_4_.refs_1_), channel_id=1, source_target_pairs={{0,16},{16,0},{1,17},{17,1},{2,18},{18,2},{3,19},{19,3},{4,20},{20... | collective-permute-start | bytes 614408 | tf_op jit(solution)/shard_map/ppermute | solution.py:457
  90.7 3.7 %copy-start.21 = (bf16[336,384]{1,0:T(8,128)(2,1)}, bf16[336,384]{1,0:T(8,128)(2,1)S(1)}, u32[]{:S(2)}) copy-start(bf16[336,384]{1,0:T(8,128)(2,1)S(1)} %collective-permute-done.20.refs_10_) | copy-start | bytes 774148
  90.7 20.2 %collective-permute-start.10 = (bf16[400,256]{1,0:T(8,128)(2,1)}, bf16[400,256]{1,0:T(8,128)(2,1)}, u32[]{:S(2)}, u32[]{:S(2)}) collective-permute-start(bf16[400,256]{1,0:T(8,128)(2,1)} %collective-permute-done.8.refs_9_.refs_4_), channel_id=1, source_target_pairs={{0,16},{16,0},{1,17},{17,1},{2,18},{18,2},{3,19},{19,3},{4,20},{20... | collective-permute-start | bytes 614408 | tf_op jit(solution)/shard_map/ppermute | solution.py:457
  94.4 16.5 %collective-permute-start.9 = (bf16[400,256]{1,0:T(8,128)(2,1)}, bf16[400,256]{1,0:T(8,128)(2,1)}, u32[]{:S(2)}, u32[]{:S(2)}) collective-permute-start(bf16[400,256]{1,0:T(8,128)(2,1)} %collective-permute-done.7.refs_8_.refs_3_), channel_id=1, source_target_pairs={{0,16},{16,0},{1,17},{17,1},{2,18},{18,2},{3,19},{19,3},{4,20},{20... | collective-permute-start | bytes 614408 | tf_op jit(solution)/shard_map/ppermute | solution.py:457
  95.1 15.8 %collective-permute-start.12 = (bf16[400,256]{1,0:T(8,128)(2,1)}, bf16[400,256]{1,0:T(8,128)(2,1)}, u32[]{:S(2)}, u32[]{:S(2)}) collective-permute-start(bf16[400,256]{1,0:T(8,128)(2,1)} %collective-permute-done.11), channel_id=1, source_target_pairs={{0,16},{16,0},{1,17},{17,1},{2,18},{18,2},{3,19},{19,3},{4,20},{20... | collective-permute-start | bytes 614408 | tf_op jit(solution)/shard_map/ppermute | solution.py:457
  102.3 1.1 copy-start.6
  102.3 15.6 %collective-permute-start.22 = (bf16[256,384]{1,0:T(8,128)(2,1)}, bf16[256,384]{1,0:T(8,128)(2,1)S(1)}, u32[]{:S(2)}, u32[]{:S(2)}) collective-permute-start(bf16[256,384]{1,0:T(8,128)(2,1)} %get-tuple-element.39), channel_id=1, source_target_pairs={{0,1},{1,0},{2,3},{3,2},{4,5},{5,4},{6,7},{7,6},{8,9},{9,8},{10,11... | collective-permute-start | bytes 589832 | tf_op jit(solution)/shard_map/ppermute | solution.py:457
  131.5 17.6 %copy-start.7 = (bf16[256,384]{1,0:T(8,128)(2,1)S(1)}, bf16[256,384]{1,0:T(8,128)(2,1)}, u32[]{:S(2)}) copy-start(bf16[256,384]{1,0:T(8,128)(2,1)} %get-tuple-element.42.refs_6_) | copy-start | bytes 589828
  131.5 4.9 %collective-permute-start.23 = (bf16[5,384,256]{2,1,0:T(8,128)(2,1)}, bf16[5,384,256]{2,1,0:T(8,128)(2,1)}, u32[]{:S(2)}, u32[]{:S(2)}) collective-permute-start(bf16[5,384,256]{2,1,0:T(8,128)(2,1)} %get-tuple-element.44), channel_id=1, source_target_pairs={{0,16},{16,0},{1,17},{17,1},{2,18},{18,2},{3,19},{19,3},{4,20},{20... | collective-permute-start | bytes 2949128 | tf_op jit(solution)/shard_map/ppermute | solution.py:457
  133.9 27.9 %copy-start = (bf16[4,336,512]{2,1,0:T(8,128)(2,1)}, bf16[4,336,512]{2,1,0:T(8,128)(2,1)S(1)}, u32[]{:S(2)}) copy-start(bf16[4,336,512]{2,1,0:T(8,128)(2,1)S(1)} %collective-permute-done.refs_4_) | copy-start | bytes 4128772
  133.9 30.6 %collective-permute-start.1 = (bf16[4,336,512]{2,1,0:T(8,128)(2,1)S(1)}, bf16[4,336,512]{2,1,0:T(8,128)(2,1)S(1)}, u32[]{:S(2)}, u32[]{:S(2)}) collective-permute-start(bf16[4,336,512]{2,1,0:T(8,128)(2,1)S(1)} %collective-permute-done.refs_4_), channel_id=1, source_target_pairs={{0,16},{16,0},{1,17},{17,1},{2,18},{18,2},{3,19},{19,3},{4,20},{20... | collective-permute-start | bytes 4128776 | tf_op jit(solution)/shard_map/ppermute | solution.py:457
  139.1 5.8 %collective-permute-start.24 = (bf16[384,256]{1,0:T(8,128)(2,1)}, bf16[384,256]{1,0:T(8,128)(2,1)S(1)}, u32[]{:S(2)}, u32[]{:S(2)}) collective-permute-start(bf16[384,256]{1,0:T(8,128)(2,1)} %get-tuple-element.46), channel_id=1, source_target_pairs={{176,16},{208,48},{240,80},{177,17},{209,49},{241,81},{178,18},{21... | collective-permute-start | bytes 589832 | tf_op jit(solution)/shard_map/ppermute | solution.py:469
  139.8 9.3 %collective-permute-start.25 = (bf16[384,256]{1,0:T(8,128)(2,1)}, bf16[384,256]{1,0:T(8,128)(2,1)S(1)}, u32[]{:S(2)}, u32[]{:S(2)}) collective-permute-start(bf16[384,256]{1,0:T(8,128)(2,1)} %get-tuple-element.47), channel_id=1, source_target_pairs={{128,0},{144,16},{160,32},{176,48},{192,64},{208,80},{224,96},{240... | collective-permute-start | bytes 589832 | tf_op jit(solution)/shard_map/ppermute | solution.py:469
  141.1 11.0 %collective-permute-start.26 = (bf16[384,256]{1,0:T(8,128)(2,1)}, bf16[384,256]{1,0:T(8,128)(2,1)}, u32[]{:S(2)}, u32[]{:S(2)}) collective-permute-start(bf16[384,256]{1,0:T(8,128)(2,1)} %get-tuple-element.48), channel_id=1, source_target_pairs={{96,0},{112,16},{128,32},{144,48},{160,64},{176,80},{192,96},{208,... | collective-permute-start | bytes 589832 | tf_op jit(solution)/shard_map/ppermute | solution.py:469
  143.0 14.0 %collective-permute-start.27 = (bf16[384,256]{1,0:T(8,128)(2,1)}, bf16[384,256]{1,0:T(8,128)(2,1)}, u32[]{:S(2)}, u32[]{:S(2)}) collective-permute-start(bf16[384,256]{1,0:T(8,128)(2,1)} %get-tuple-element.49), channel_id=1, source_target_pairs={{64,0},{80,16},{96,32},{112,48},{128,64},{144,80},{160,96},{176,11... | collective-permute-start | bytes 589832 | tf_op jit(solution)/shard_map/ppermute | solution.py:469
  145.0 14.6 %copy-start.23 = (bf16[384,256]{1,0:T(8,128)(2,1)}, bf16[384,256]{1,0:T(8,128)(2,1)S(1)}, u32[]{:S(2)}) copy-start(bf16[384,256]{1,0:T(8,128)(2,1)S(1)} %collective-permute-done.24.refs_0_) | copy-start | bytes 589828
  145.0 14.6 %collective-permute-start.28 = (bf16[384,256]{1,0:T(8,128)(2,1)}, bf16[384,256]{1,0:T(8,128)(2,1)}, u32[]{:S(2)}, u32[]{:S(2)}) collective-permute-start(bf16[384,256]{1,0:T(8,128)(2,1)} %get-tuple-element.50), channel_id=1, source_target_pairs={{32,0},{48,16},{64,32},{80,48},{96,64},{112,80},{128,96},{144,112}... | collective-permute-start | bytes 589832 | tf_op jit(solution)/shard_map/ppermute | solution.py:469
  149.1 10.5 %copy-start.24 = (bf16[384,256]{1,0:T(8,128)(2,1)}, bf16[384,256]{1,0:T(8,128)(2,1)S(1)}, u32[]{:S(2)}) copy-start(bf16[384,256]{1,0:T(8,128)(2,1)S(1)} %collective-permute-done.25.refs_1_) | copy-start | bytes 589828
  149.1 15.5 %collective-permute-start.29 = (bf16[256,384]{1,0:T(8,128)(2,1)S(1)}, bf16[256,384]{1,0:T(8,128)(2,1)S(1)}, u32[]{:S(2)}, u32[]{:S(2)}) collective-permute-start(bf16[256,384]{1,0:T(8,128)(2,1)S(1)} %copy-done.7), channel_id=1, source_target_pairs={{0,1},{1,0},{2,3},{3,2},{4,5},{5,4},{6,7},{7,6},{8,9},{9,8},{10,11... | collective-permute-start | bytes 589832 | tf_op jit(solution)/shard_map/ppermute | solution.py:457
  161.8 7.4 %collective-permute-start.30 = (bf16[256,384]{1,0:T(8,128)(2,1)}, bf16[256,384]{1,0:T(8,128)(2,1)S(1)}, u32[]{:S(2)}, u32[]{:S(2)}) collective-permute-start(bf16[256,384]{1,0:T(8,128)(2,1)} %total_partials.1.refs_7_), channel_id=1, source_target_pairs={{0,1},{1,0},{2,3},{3,2},{4,5},{5,4},{6,7},{7,6},{8,9},{9,8},{10,11... | collective-permute-start | bytes 589832 | tf_op jit(solution)/shard_map/ppermute | solution.py:457
  164.5 4.7 %copy-start.8 = (bf16[256,384]{1,0:T(8,128)(2,1)}, bf16[256,384]{1,0:T(8,128)(2,1)S(1)}, u32[]{:S(2)}) copy-start(bf16[256,384]{1,0:T(8,128)(2,1)S(1)} %collective-permute-done.29.refs_8_) | copy-start | bytes 589828
  164.5 4.7 %copy-start.1 = (bf16[4,336,512]{2,1,0:T(8,128)(2,1)}, bf16[4,336,512]{2,1,0:T(8,128)(2,1)S(1)}, u32[]{:S(2)}) copy-start(bf16[4,336,512]{2,1,0:T(8,128)(2,1)S(1)} %collective-permute-done.1.refs_5_) | copy-start | bytes 4128772
  174.3 10.8 %collective-permute-start.31 = (bf16[336,384]{1,0:T(8,128)(2,1)}, bf16[336,384]{1,0:T(8,128)(2,1)S(1)}, u32[]{:S(2)}, u32[]{:S(2)}) collective-permute-start(bf16[336,384]{1,0:T(8,128)(2,1)} %get-tuple-element.51), channel_id=1, source_target_pairs={{0,2},{2,4},{4,6},{6,8},{8,10},{10,12},{12,14},{14,0},{1,3},{3,5},... | collective-permute-start | bytes 774152 | tf_op jit(solution)/shard_map/ppermute | solution.py:473
  174.6 11.9 %collective-permute-start.35 = (bf16[336,384]{1,0:T(8,128)(2,1)}, bf16[336,384]{1,0:T(8,128)(2,1)S(1)}, u32[]{:S(2)}, u32[]{:S(2)}) collective-permute-start(bf16[336,384]{1,0:T(8,128)(2,1)} %get-tuple-element.55), channel_id=1, source_target_pairs={{0,14},{2,0},{4,2},{6,4},{8,6},{10,8},{12,10},{14,12},{1,15},{3,1}... | collective-permute-start | bytes 774152 | tf_op jit(solution)/shard_map/ppermute | solution.py:473
  185.2 1.4 copy-start.14
  185.2 8.9 %copy-start.13 = (f32[336,384]{1,0:T(8,128)S(1)}, f32[336,384]{1,0:T(8,128)}, u32[]{:S(2)}) copy-start(f32[336,384]{1,0:T(8,128)} %get-tuple-element.53) | copy-start | bytes 1548292
  185.2 9.0 %copy-start.12 = (f32[336,384]{1,0:T(8,128)S(1)}, f32[336,384]{1,0:T(8,128)}, u32[]{:S(2)}) copy-start(f32[336,384]{1,0:T(8,128)} %get-tuple-element.57) | copy-start | bytes 1548292
  186.4 7.6 %collective-permute-start.32 = (bf16[336,384]{1,0:T(8,128)(2,1)S(1)}, bf16[336,384]{1,0:T(8,128)(2,1)S(1)}, u32[]{:S(2)}, u32[]{:S(2)}) collective-permute-start(bf16[336,384]{1,0:T(8,128)(2,1)S(1)} %add_convert_fusion.5), channel_id=1, source_target_pairs={{0,2},{2,4},{4,6},{6,8},{8,10},{10,12},{12,14},{14,0},{1,3},{3,5},... | collective-permute-start | bytes 774152 | tf_op jit(solution)/shard_map/ppermute | solution.py:473
  186.5 16.0 %copy-start.11 = (f32[336,384]{1,0:T(8,128)S(1)}, f32[336,384]{1,0:T(8,128)}, u32[]{:S(2)}) copy-start(f32[336,384]{1,0:T(8,128)} %get-tuple-element.54) | copy-start | bytes 1548292
  186.6 7.6 %collective-permute-start.36 = (bf16[336,384]{1,0:T(8,128)(2,1)S(1)}, bf16[336,384]{1,0:T(8,128)(2,1)S(1)}, u32[]{:S(2)}, u32[]{:S(2)}) collective-permute-start(bf16[336,384]{1,0:T(8,128)(2,1)S(1)} %add_convert_fusion.2), channel_id=1, source_target_pairs={{0,14},{2,0},{4,2},{6,4},{8,6},{10,8},{12,10},{14,12},{1,15},{3,1}... | collective-permute-start | bytes 774152 | tf_op jit(solution)/shard_map/ppermute | solution.py:473
  194.0 16.2 %copy-start.10 = (f32[336,384]{1,0:T(8,128)S(1)}, f32[336,384]{1,0:T(8,128)}, u32[]{:S(2)}) copy-start(f32[336,384]{1,0:T(8,128)} %get-tuple-element.58) | copy-start | bytes 1548292
  194.1 8.5 %collective-permute-start.33 = (bf16[336,384]{1,0:T(8,128)(2,1)S(1)}, bf16[336,384]{1,0:T(8,128)(2,1)S(1)}, u32[]{:S(2)}, u32[]{:S(2)}) collective-permute-start(bf16[336,384]{1,0:T(8,128)(2,1)S(1)} %add_convert_fusion.4), channel_id=1, source_target_pairs={{0,2},{2,4},{4,6},{6,8},{8,10},{10,12},{12,14},{14,0},{1,3},{3,5},... | collective-permute-start | bytes 774152 | tf_op jit(solution)/shard_map/ppermute | solution.py:473
  194.3 8.4 %collective-permute-start.37 = (bf16[336,384]{1,0:T(8,128)(2,1)S(1)}, bf16[336,384]{1,0:T(8,128)(2,1)S(1)}, u32[]{:S(2)}, u32[]{:S(2)}) collective-permute-start(bf16[336,384]{1,0:T(8,128)(2,1)S(1)} %add_convert_fusion.1), channel_id=1, source_target_pairs={{0,14},{2,0},{4,2},{6,4},{8,6},{10,8},{12,10},{14,12},{1,15},{3,1}... | collective-permute-start | bytes 774152 | tf_op jit(solution)/shard_map/ppermute | solution.py:473
  202.6 7.6 %collective-permute-start.34 = (bf16[336,384]{1,0:T(8,128)(2,1)S(1)}, bf16[336,384]{1,0:T(8,128)(2,1)S(1)}, u32[]{:S(2)}, u32[]{:S(2)}) collective-permute-start(bf16[336,384]{1,0:T(8,128)(2,1)S(1)} %add_convert_fusion.3), channel_id=1, source_target_pairs={{0,2},{2,4},{4,6},{6,8},{8,10},{10,12},{12,14},{14,0},{1,3},{3,5},... | collective-permute-start | bytes 774152 | tf_op jit(solution)/shard_map/ppermute | solution.py:473
  (3 other events, 2.1 us)
where the time goes:
time: 212 us; the launch traced here: 211 us
  waiting for transfers between devices  87.3 us (41%)
  starting transfers between devices  60.7 us (29%)
  Pallas kernels  54.4 us (26%)
  local copies, waits for them, and re-layouts  5.05 us (2%)
  other arithmetic  2.99 us (1%)
    ppermute x5, waiting for transfers between devices, chips_on(): return lax.ppermute(x, AA, chip_pairs(d))  41.9 us
    ppermute x14, waiting for transfers between devices, round_z(): return lax.ppermute(x, 'z', [(i, (i + step) % RING) for i in range(RING)])  28.5 us
    ppermute x14, starting transfers between devices, round_z(): return lax.ppermute(x, 'z', [(i, (i + step) % RING) for i in range(RING)])  27.7 us
    pallas_call x2, Pallas kernels, attention_stats(): pl.pallas_call(lambda *refs: stats_kernel(low, high, *refs), name='stats_...  14.4 us
    pallas_call x1, Pallas kernels, attention_grads(): pl.pallas_call(grads_kernel, name='attention_grads', out_shape=(jax.Shape...  12.9 us
    ppermute x14, starting transfers between devices, swapped(): return lax.ppermute(x, axis, [(0, 1), (1, 0)])  12.8 us
    ppermute x5, starting transfers between devices, chips_on(): return lax.ppermute(x, AA, chip_pairs(d))  12.5 us
    pallas_call x2, Pallas kernels, project(): pl.pallas_call(lambda *refs: project_kernel(deltas, *refs), name='project...  11.7 us
  transfers between devices with their start and end apart: 38, of which 15 were waited for; matrix products, arithmetic and copies ran while one was open for 2% of the time, Pallas kernels for 22%

commit v1 on v0

--- a/solution.py
+++ b/solution.py
@@ -21,6 +21,9 @@
 FEATS = 336
 CHUNK = 384
 WINDOW = 512
+BOTH = 2 * ROWS
+TILE = 256
+STATS_TILE = 128
 NEAR = 6
 RING = 8
 AA = ("xl", "y", "core")
@@ -76,6 +79,18 @@
     return [twins[d] for d in odd] + [others[k] for k in extra]
 
 
+def side_by_side(x):
+    return jnp.concatenate((x[:HD, :], x[HD:, :]), axis=1)
+
+
+def one_above_other(x):
+    return jnp.concatenate((x[:, :HD], x[:, HD:]), axis=0)
+
+
+def tiles(width):
+    return [slice(t, t + width) for t in range(0, BOTH, width)]
+
+
 def stats_kernel(low, high, own_ref, qseg_ref, q_ref, *refs):
     near = high == BLOCKS
     odd, _, extra = sources(low, high)
@@ -89,7 +104,7 @@
         lse_ref, out_ref, start_ref, low_ref, buf, qt_ref, m_ref, l_ref, sem = refs[4 + count :]
     own = own_ref[0]
     copies = load_window(low, high, lax.rem(own, 2), kv_refs, buf, sem)
-    qt_ref[...] = q_ref[...].T
+    qt_ref[...] = one_above_other(q_ref[...]).T
     if near:
         m_ref[...] = jnp.full(m_ref.shape, NEG_FILL, F32)
         l_ref[...] = jnp.zeros(l_ref.shape, F32)
@@ -121,107 +136,151 @@
         start_ref[...] = start
         start0 = jnp.min(start)
     lowest = lax.div(start0, ROWS) - own + (BLOCKS - 1)
+    latest = jnp.max(start)
     pos = own * ROWS + lax.broadcasted_iota(jnp.int32, (1, ROWS), 1)
-    key_at = lax.broadcasted_iota(jnp.int32, (ROWS, ROWS), 0)
+    start = jnp.concatenate((start, start), axis=1)
+    pos = jnp.concatenate((pos, pos), axis=1)
+    key_at = lax.broadcasted_iota(jnp.int32, (ROWS, STATS_TILE), 0)
+
+    def add_block(b, first, whole):
+        kb = buf[b - low, :ROWS, :HD]
+        vt = buf[b - low, :ROWS, HD:].T
+        for t in tiles(STATS_TILE):
+            s = dot(kb, qt_ref[:, t]) * SCALE2
+            if not whole:
+                allowed = (key_at >= start[:, t] - first) & (key_at <= pos[:, t] - first)
+                s = jnp.where(allowed, s, NEG_FILL)
+            m_old = m_ref[:, t]
+            m_new = jnp.maximum(m_old, jnp.max(s, axis=0, keepdims=True))
+            p = jnp.exp2(s - m_new)
+            back = jnp.exp2(m_old - m_new)
+            l_ref[:, t] = l_ref[:, t] * back + jnp.sum(p, axis=0, keepdims=True)
+            m_ref[:, t] = m_new
+            out_ref[:, t] = out_ref[:, t] * back + dot(vt, p.astype(BF16))
 
     def one_block(back_to, carry):
         b = high - 1 - back_to
         first = (own + b - (BLOCKS - 1)) * ROWS
-        allowed = (key_at >= start - first) & (key_at <= pos - first)
-        kb = buf[b - low, :ROWS, :HD]
-        vt = buf[b - low, :ROWS, HD:].T
-        for h in range(2):
-            part = slice(h * HD, (h + 1) * HD)
-            s = jnp.where(allowed, dot(kb, qt_ref[part, :]) * SCALE2, NEG_FILL)
-            m_old = m_ref[h : h + 1, :]
-            m_new = jnp.maximum(m_old, jnp.max(s, axis=0, keepdims=True))
-            p = jnp.exp2(s - m_new)
-            back = jnp.exp2(m_old - m_new)
-            l_ref[h : h + 1, :] = l_ref[h : h + 1, :] * back + jnp.sum(p, axis=0, keepdims=True)
-            m_ref[h : h + 1, :] = m_new
-            out_ref[part, :] = out_ref[part, :] * back + dot(vt, p.astype(BF16))
+        whole = (first >= latest) & (b < BLOCKS - 1)
+
+        @pl.when(whole)
+        def _():
+            add_block(b, first, True)
+
+        @pl.when(jnp.logical_not(whole))
+        def _():
+            add_block(b, first, False)
+
         return carry
 
     lax.fori_loop(0, high - jnp.clip(lowest, low, high), one_block, 0)
     if not near:
         low_ref[0] = lowest
         lse_ref[...] = m_ref[...] + jnp.log2(l_ref[...])
-        for h in range(2):
-            part = slice(h * HD, (h + 1) * HD)
-            out_ref[part, :] = out_ref[part, :] / l_ref[h : h + 1, :]
-
-
-def grads_kernel(own_ref, low_ref, start_ref, q_ref, near_ref, far_ref, lse_ref, out_ref, *refs):
+        out_ref[...] = out_ref[...] / l_ref[...]
+
+
+def grads_kernel(own_ref, low_ref, *refs):
+    given, refs = refs[:6], refs[6:]
     kv_refs, refs = refs[: BLOCKS + 1], refs[BLOCKS + 1 :]
     gqt_ref, mine_ref, theirs_ref = refs[:3]
-    buf, qt_ref, dout_ref, doutt_ref, delta_ref, acc_ref, sem = refs[3:]
+    start_ref, q_ref, near_ref, far_ref, lse_ref, out_ref = held = refs[3:9]
+    buf, qt_ref, qn_ref, dout_ref, doutt_ref, delta_ref, acc_ref, made, sem, in_sem, out_sem = refs[9:]
     own = own_ref[0]
-    copies = load_window(0, BLOCKS, lax.rem(own, 2), kv_refs, buf, sem)
+    arrivals = [pltpu.make_async_copy(x, y, in_sem.at[i]) for i, (x, y) in enumerate(zip(given, held))]
+    for c in arrivals:
+        c.start()
+    load_window(0, BLOCKS, lax.rem(own, 2), kv_refs, buf, sem)
     lowest = low_ref[0]
-    qt_ref[...] = q_ref[...].T
-    doutt_ref[...] = (near_ref[...] + far_ref[...].astype(F32)).astype(BF16)
+    acc_ref[...] = jnp.zeros(acc_ref.shape, F32)
+    key_at = lax.broadcasted_iota(jnp.int32, (ROWS, TILE), 0)
+    for c in arrivals:
+        c.wait()
+    qn_ref[...] = one_above_other(q_ref[...])
+    qt_ref[...] = qn_ref[...].T
+    doutt_ref[...] = side_by_side((near_ref[...] + far_ref[...].astype(F32)).astype(BF16))
     dout_ref[...] = doutt_ref[...].T
-    for h in range(2):
-        part = slice(h * HD, (h + 1) * HD)
-        delta_ref[h : h + 1, :] = jnp.sum(
-            doutt_ref[part, :].astype(F32) * out_ref[part, :], axis=0, keepdims=True
-        )
-    acc_ref[...] = jnp.zeros(acc_ref.shape, F32)
+    delta_ref[...] = jnp.sum(doutt_ref[...].astype(F32) * out_ref[...], axis=0, keepdims=True)
     start = start_ref[...]
+    latest = jnp.max(start)
     pos = own * ROWS + lax.broadcasted_iota(jnp.int32, (1, ROWS), 1)
-    key_at = lax.broadcasted_iota(jnp.int32, (ROWS, ROWS), 0)
-    for c in copies:
-        c.wait()
-
-    def one_block(b, target, d):
-        @pl.when(b >= lowest)
+    start = jnp.concatenate((start, start), axis=1)
+    pos = jnp.concatenate((pos, pos), axis=1)
+
+    def add_block(b, first, whole):
+        kb = buf[b, :ROWS, :HD]
+        vb = buf[b, :ROWS, HD:]
+        kt = kb.T
+        gk = gv = None
+        for t in tiles(TILE):
+            s = dot(kb, qt_ref[:, t]) * SCALE2
+            dp = dot(vb, doutt_ref[:, t])
+            p = jnp.exp2(s - lse_ref[:, t])
+            if not whole:
+                allowed = (key_at >= start[:, t] - first) & (key_at <= pos[:, t] - first)
+                p = jnp.where(allowed, p, 0.0)
+            ds = (p * (dp - delta_ref[:, t])).astype(BF16)
+            add_v = dot(p.astype(BF16), dout_ref[t, :])
+            add_k = dot(ds, qn_ref[t, :])
+            gv = add_v if gv is None else gv + add_v
+            gk = add_k if gk is None else gk + add_k
+            acc_ref[:, t] += dot(kt, ds)
+        made[b, :, :HD] = (gk * SCALE).astype(BF16)
+        made[b, :, HD:] = gv.astype(BF16)
+
+    def departure(b, target):
+        d = (BLOCKS - 1 - b) // 2 if isinstance(b, int) else lax.div(BLOCKS - 1 - b, 2)
+        return pltpu.make_async_copy(made.at[b], target.at[d], out_sem.at[b])
+
+    def one_block(b, carry):
+        pltpu.make_async_copy(kv_refs[0], buf.at[b], sem.at[b]).wait()
+        first = (own + b - (BLOCKS - 1)) * ROWS
+        whole = (first >= latest) & (b < BLOCKS - 1)
+
+        @pl.when((b >= lowest) & whole)
         def _():
-            first = (own + b - (BLOCKS - 1)) * ROWS
-            allowed = (key_at >= start - first) & (key_at <= pos - first)
-            kb = buf[b, :ROWS, :HD]
-            vb = buf[b, :ROWS, HD:]
-            kt = kb.T
-            gk = gv = None
-            for h in range(2):
-                part = slice(h * HD, (h + 1) * HD)
-                s = dot(kb, qt_ref[part, :]) * SCALE2
-                dp = dot(vb, doutt_ref[part, :])
-                p = jnp.where(allowed, jnp.exp2(s - lse_ref[h : h + 1, :]), 0.0)
-                ds = (p * (dp - delta_ref[h : h + 1, :])).astype(BF16)
-                add_v = dot(p.astype(BF16), dout_ref[:, part])
-                add_k = dot(ds, q_ref[:, part])
-                gv = add_v if h == 0 else gv + add_v
-                gk = add_k if h == 0 else gk + add_k
-                acc_ref[part, :] += dot(kt, ds)
-            target[d, :, :HD] = (gk * SCALE).astype(BF16)
-            target[d, :, HD:] = gv.astype(BF16)
+            add_block(b, first, True)
+
+        @pl.when((b >= lowest) & jnp.logical_not(whole))
+        def _():
+            add_block(b, first, False)
 
         @pl.when(b < lowest)
         def _():
-            target[d] = jnp.zeros((ROWS, 2 * HD), BF16)
-
-    def two_blocks(d, carry):
-        one_block(BLOCKS - 1 - 2 * d, mine_ref, d)
-        one_block(BLOCKS - 2 - 2 * d, theirs_ref, d)
+            made[b] = jnp.zeros((ROWS, 2 * HD), BF16)
+
+        odd = lax.rem(b, 2) == 1
+
+        @pl.when(odd)
+        def _():
+            departure(b, mine_ref).start()
+
+        @pl.when(jnp.logical_not(odd))
+        def _():
+            departure(b, theirs_ref).start()
+
         return carry
 
-    lax.fori_loop(0, HALF, two_blocks, 0)
-    gqt_ref[...] = (acc_ref[...] * SCALE).astype(BF16)
+    lax.fori_loop(0, BLOCKS, one_block, 0)
+    gqt_ref[:HD, :] = (acc_ref[:, :ROWS] * SCALE).astype(BF16)
+    gqt_ref[HD:, :] = (acc_ref[:, ROWS:] * SCALE).astype(BF16)
+    for b in range(BLOCKS):
+        departure(b, mine_ref if b % 2 else theirs_ref).wait()
 
 
 def attention_stats(own, qseg, query, twins, others, low, high, state=()):
     count = high - low
     window = window_refs(low, high, twins, others)
-    row = jax.ShapeDtypeStruct((2, ROWS), F32)
-    wide = jax.ShapeDtypeStruct((2 * HD, ROWS), F32)
+    row = jax.ShapeDtypeStruct((1, BOTH), F32)
+    wide = jax.ShapeDtypeStruct((HD, BOTH), F32)
     start = jax.ShapeDtypeStruct((1, ROWS), jnp.int32)
     lowest = jax.ShapeDtypeStruct((1,), jnp.int32)
     scratch = [
         pltpu.VMEM((count, PACKED, 2 * HD), BF16),
-        pltpu.VMEM((2 * HD, ROWS), BF16),
+        pltpu.VMEM((HD, BOTH), BF16),
     ]
     if state:
-        scratch += [pltpu.VMEM((2, ROWS), F32), pltpu.VMEM((2, ROWS), F32)]
+        scratch += [pltpu.VMEM((1, BOTH), F32), pltpu.VMEM((1, BOTH), F32)]
     return pl.pallas_call(
         lambda *refs: stats_kernel(low, high, *refs),
         name="stats_far" if state else "stats_near",
@@ -235,6 +294,7 @@
 def attention_grads(own, stats, query, near, far, twins, others):
     lse, out, start, lowest = stats
     window = window_refs(0, BLOCKS, twins, others)
+    given = (start, query, near, far, lse, out)
     return pl.pallas_call(
         grads_kernel,
         name="attention_grads",
@@ -243,18 +303,23 @@
             jax.ShapeDtypeStruct((HALF, ROWS, 2 * HD), BF16),
             jax.ShapeDtypeStruct((HALF, ROWS, 2 * HD), BF16),
         ),
-        in_specs=[SMEM, SMEM] + [VMEM] * 6 + [ANY] * len(window),
-        out_specs=(VMEM, VMEM, VMEM),
-        scratch_shapes=[
+        in_specs=[SMEM, SMEM] + [ANY] * (len(given) + len(window)),
+        out_specs=(VMEM, ANY, ANY),
+        scratch_shapes=[pltpu.VMEM(x.shape, x.dtype) for x in given]
+        + [
             pltpu.VMEM((BLOCKS, PACKED, 2 * HD), BF16),
-            pltpu.VMEM((2 * HD, ROWS), BF16),
-            pltpu.VMEM((ROWS, 2 * HD), BF16),
-            pltpu.VMEM((2 * HD, ROWS), BF16),
-            pltpu.VMEM((2, ROWS), F32),
-            pltpu.VMEM((2 * HD, ROWS), F32),
+            pltpu.VMEM((HD, BOTH), BF16),
+            pltpu.VMEM((BOTH, HD), BF16),
+            pltpu.VMEM((BOTH, HD), BF16),
+            pltpu.VMEM((HD, BOTH), BF16),
+            pltpu.VMEM((1, BOTH), F32),
+            pltpu.VMEM((HD, BOTH), F32),
+            pltpu.VMEM((BLOCKS, ROWS, 2 * HD), BF16),
+            pltpu.SemaphoreType.DMA((BLOCKS,)),
+            pltpu.SemaphoreType.DMA((len(given),)),
             pltpu.SemaphoreType.DMA((BLOCKS,)),
         ],
-    )(own, lowest, start, query, near, far, lse, out, *window)
+    )(own, lowest, *given, *window)
 
 
 def column_window(chunk):
@@ -320,15 +385,13 @@
         hbuf[i, FEATS:] = jnp.zeros((CHUNK - FEATS, ROWS), BF16)
         to_far = pltpu.make_async_copy(shards[i], hbuf.at[i, :FEATS], sem.at[i, 2])
         to_far.start()
-        to_own = pltpu.make_async_copy(shards[i], gbuf.at[i, place], sem.at[i, 3])
-        to_own.start()
-        copies.append(
-            (pltpu.make_async_copy(w_ref.at[:, lanes], wbuf.at[i], sem.at[i, 0]), far, to_far, to_own)
-        )
+        own_rows = pltpu.make_async_copy(w_ref.at[:, lanes], wbuf.at[i], sem.at[i, 0])
+        copies.append((own_rows, far, to_far, place))
     near = far = None
     for i in range(RING):
-        for c in copies[i]:
+        for c in copies[i][:3]:
             c.wait()
+        gbuf[i, copies[i][3], :] = hbuf[i, :FEATS]
         add_far = dot(fbuf[i], hbuf[i])
         add_near = dot(wbuf[i], gbuf[i])
         far = add_far if i == 0 else far + add_far
@@ -351,7 +414,7 @@
             pltpu.VMEM((RING, 2 * HD, CHUNK), BF16),
             pltpu.VMEM((RING, WINDOW, ROWS), BF16),
             pltpu.VMEM((RING, CHUNK, ROWS), BF16),
-            pltpu.SemaphoreType.DMA((RING, 4)),
+            pltpu.SemaphoreType.DMA((RING, 3)),
         ],
     )(at, w_out, *far_w, *shards.values())
 
@@ -400,57 +463,139 @@
     )(own, *parts)
 
 
-def project_kernel(deltas, at_ref, *refs):
-    wq, wk, wv, pa, pb, gq, gkv, gq2, gkv2 = refs[:9]
-    outs = refs[9 : 9 + len(deltas)]
-    bq, bk, bv, bp, sem = refs[9 + len(deltas) :]
+def own_project_kernel(deltas, at_ref, *refs):
+    n = len(deltas)
+    wq, wk, wv, pa, pb, gq, gkv, gq2 = refs[:8]
+    outs = refs[8 : 8 + n]
+    wbuf, gbuf, obuf, sem, g_sem, out_sem = refs[8 + n :]
     z, xh, core = at_ref[0], at_ref[1], at_ref[2]
+    g_copies = [
+        pltpu.make_async_copy(g, gbuf.at[2 * HD * i : 2 * HD * (i + 1)], g_sem.at[i])
+        for i, g in enumerate((gq, gkv, gq2))
+    ]
+    for c in g_copies:
+        c.start()
     copies = []
-    for n, delta in enumerate(deltas):
+    for i, delta in enumerate(deltas):
         chunk = lax.rem(z + delta + RING, RING)
         rows = pl.ds(pl.multiple_of((2 * chunk + xh) * FEATS, 16), FEATS)
+        place = ((wq, 0, 2 * HD), (wk, 2 * HD, HD), (wv, 3 * HD, HD))
         mine = [
-            pltpu.make_async_copy(w.at[rows, :], b.at[n], sem.at[n, i])
-            for i, (w, b) in enumerate(((wq, bq), (wk, bk), (wv, bv)))
+            pltpu.make_async_copy(w.at[rows, :], wbuf.at[i, :, lane : lane + size], sem.at[i, j])
+            for j, (w, lane, size) in enumerate(place)
         ]
         for c in mine:
             c.start()
-        half = lax.div(chunk, RING // 2)
         inner = lax.rem(chunk, RING // 2)
-
-        @pl.when(half == core)
-        def _(n=n, inner=inner):
-            pltpu.make_async_copy(pa.at[inner], bp.at[n], sem.at[n, 3]).start()
-
-        @pl.when(half != core)
-        def _(n=n, inner=inner):
-            pltpu.make_async_copy(pb.at[inner], bp.at[n], sem.at[n, 3]).start()
-
-        copies.append(mine + [pltpu.make_async_copy(pa.at[0], bp.at[n], sem.at[n, 3])])
-    for n in range(len(deltas)):
-        for c in copies[n]:
+        near, far = [
+            pltpu.make_async_copy(
+                p.at[inner, :, : 2 * HD], wbuf.at[i, :, 4 * HD :], sem.at[i, 3]
+            )
+            for p in (pa, pb)
+        ]
+        same = lax.div(chunk, RING // 2) == core
+
+        @pl.when(same)
+        def _(copy=near):
+            copy.start()
+
+        @pl.when(jnp.logical_not(same))
+        def _(copy=far):
+            copy.start()
+
+        copies.append(mine + [near])
+    for c in g_copies:
+        c.wait()
+    results = []
+    for i in range(n):
+        for c in copies[i]:
             c.wait()
-        total = dot(bq[n], gq[...]) + dot(bk[n], gkv[:HD, :]) + dot(bv[n], gkv[HD:, :])
-        total = total + dot(bp[n, :, : 2 * HD], gq2[...]) + dot(bp[n, :, 2 * HD :], gkv2[...])
-        outs[n][...] = total.astype(outs[n].dtype)
-
-
-def project(deltas, at, weights, far, grads, kind):
+        obuf[i] = dot(wbuf[i], gbuf[...])
+        results.append(pltpu.make_async_copy(obuf.at[i], outs[i], out_sem.at[i]))
+        results[-1].start()
+    for c in results:
+        c.wait()
+
+
+def own_project(deltas, at, weights, far, grads):
     n = len(deltas)
     return pl.pallas_call(
-        lambda *refs: project_kernel(deltas, *refs),
-        name="project",
+        lambda *refs: own_project_kernel(deltas, *refs),
+        name="own_project",
+        out_shape=(jax.ShapeDtypeStruct((FEATS, ROWS), F32),) * n,
+        in_specs=[SMEM] + [ANY] * 8,
+        out_specs=(ANY,) * n,
+        scratch_shapes=[
+            pltpu.VMEM((n, FEATS, 6 * HD), BF16),
+            pltpu.VMEM((6 * HD, ROWS), BF16),
+            pltpu.VMEM((n, FEATS, ROWS), F32),
+            pltpu.SemaphoreType.DMA((n, 4)),
+            pltpu.SemaphoreType.DMA((3,)),
+            pltpu.SemaphoreType.DMA((n,)),
+        ],
+    )(at, *weights, *far, *grads)
+
+
+def far_project_kernel(deltas, at_ref, *refs):
+    n = len(deltas)
+    pa, pb, gkv2 = refs[:3]
+    sums = refs[3 : 3 + n]
+    outs = refs[3 + n : 3 + 2 * n]
+    wbuf, gbuf, abuf, obuf, sem, g_sem, out_sem = refs[3 + 2 * n :]
+    z, core = at_ref[0], at_ref[2]
+    g_copy = pltpu.make_async_copy(gkv2, gbuf, g_sem.at[0])
+    g_copy.start()
+    copies = []
+    for i, delta in enumerate(deltas):
+        chunk = lax.rem(z + delta + RING, RING)
+        inner = lax.rem(chunk, RING // 2)
+        near, far = [
+            pltpu.make_async_copy(p.at[inner, :, 2 * HD :], wbuf.at[i], sem.at[i, 0])
+            for p in (pa, pb)
+        ]
+        same = lax.div(chunk, RING // 2) == core
+
+        @pl.when(same)
+        def _(copy=near):
+            copy.start()
+
+        @pl.when(jnp.logical_not(same))
+        def _(copy=far):
+            copy.start()
+
+        before = pltpu.make_async_copy(sums[i], abuf.at[i], sem.at[i, 1])
+        before.start()
+        copies.append((near, before))
+    g_copy.wait()
+    results = []
+    for i in range(n):
+        for c in copies[i]:
+            c.wait()
+        obuf[i] = (abuf[i] + dot(wbuf[i], gbuf[...])).astype(obuf.dtype)
+        results.append(pltpu.make_async_copy(obuf.at[i], outs[i], out_sem.at[i]))
+        results[-1].start()
+    for c in results:
+        c.wait()
+
+
+def far_project(deltas, at, far, gkvt_far, sums, kind):
+    n = len(deltas)
+    return pl.pallas_call(
+        lambda *refs: far_project_kernel(deltas, *refs),
+        name="far_project",
         out_shape=(jax.ShapeDtypeStruct((FEATS, ROWS), kind),) * n,
-        in_specs=[SMEM] + [ANY] * 5 + [VMEM] * 4,
-        out_specs=(VMEM,) * n,
+        in_specs=[SMEM] + [ANY] * (3 + n),
+        out_specs=(ANY,) * n,
         scratch_shapes=[
             pltpu.VMEM((n, FEATS, 2 * HD), BF16),
-            pltpu.VMEM((n, FEATS, HD), BF16),
-            pltpu.VMEM((n, FEATS, HD), BF16),
-            pltpu.VMEM((n, FEATS, 4 * HD), BF16),
-            pltpu.SemaphoreType.DMA((n, 4)),
+            pltpu.VMEM((2 * HD, ROWS), BF16),
+            pltpu.VMEM((n, FEATS, ROWS), F32),
+            pltpu.VMEM((n, FEATS, ROWS), kind),
+            pltpu.SemaphoreType.DMA((n, 2)),
+            pltpu.SemaphoreType.DMA((1,)),
+            pltpu.SemaphoreType.DMA((n,)),
         ],
-    )(at, *weights, *far, *grads)
+    )(at, *far, gkvt_far, *sums)
 
 
 def swapped(x, axis):
@@ -495,11 +640,14 @@
     twins = [block] + [chips_on(block, d) for d in range(1, HALF + 1)]
     others = [swapped(twins[d], "core") for d in range(HALF + 1)]
     wanted = [
-        lax.dynamic_index_in_dim(w.reshape(2, RING // 2, 2, FEATS, -1), core, 0, keepdims=False)
+        lax.dynamic_index_in_dim(
+            w.reshape(2, RING // 2, 2, FEATS, -1), core, 0, keepdims=False
+        )
         for w in (w_query, w_key, w_value)
     ]
     wanted = [lax.dynamic_index_in_dim(w, 1 - xh, 1, keepdims=False) for w in wanted]
-    far_mine = swapped(jnp.concatenate(wanted, axis=2), "xh")
+    wanted = jnp.concatenate(wanted, axis=2)
+    far_mine = swapped(wanted, "xh")
     far_other = swapped(far_mine, "core")
 
     qseg = segment_ids[None, :]
@@ -517,9 +665,10 @@
 
     weights = (w_query, w_key, w_value)
     far_rows = (far_mine, far_other)
-    grads = (gqt, gkvt, gqt_far, gkvt_far)
-    ahead, behind = project((4, -3), at, weights, far_rows, grads, BF16)
-    rest = project((3, -2, 2, -1, 1, 0), at, weights, far_rows, grads, F32)
+    deltas = (4, -3, 3, -2, 2, -1, 1, 0)
+    sums = own_project(deltas, at, weights, far_rows, (gqt, gkvt, gqt_far))
+    ahead, behind = far_project(deltas[:2], at, far_rows, gkvt_far, sums[:2], BF16)
+    rest = far_project(deltas[2:], at, far_rows, gkvt_far, sums[2:], F32)
     ahead = round_z(ahead, 1)
     behind = round_z(behind, -1)
     for k in (2, 3):

time: 212 us -> 210 us (level)
  waiting for transfers between devices: 87.3 us -> 80 us
    ppermute x5, waiting for transfers between devices: 9.67 us -> 15.9 us  [chips_back(): return lax.ppermute(x, AA, [(j, i) for i, j in chip_pairs(d)])]
    ppermute x5, waiting for transfers between devices: 41.9 us -> 36.4 us  [chips_on(): return lax.ppermute(x, AA, chip_pairs(d))]
    ppermute x14, waiting for transfers between devices: 7.14 us -> 2.45 us  [swapped(): return lax.ppermute(x, axis, [(0, 1), (1, 0)])]
    pallas_call x2 -> x3, Pallas kernels: 11.7 us -> 16.2 us  [the longest x2 8.38 us: far_project(): pl.pallas_call(lambda *refs: far_project_kernel(deltas, *refs), name='far...]
    ppermute x14, waiting for transfers between devices: 28.5 us -> 25.2 us  [round_z(): return lax.ppermute(x, 'z', [(i, (i + step) % RING) for i in range(RING)])]
    pallas_call x2, Pallas kernels: 14.4 us -> 12.1 us  [attention_stats(): pl.pallas_call(lambda *refs: stats_kernel(low, high, *refs), name='stats_...]
  transfers between devices with their start and end apart: 38 -> 38, of which waited for: 15 -> 13; matrix products, arithmetic and copies ran while one was open for 2% -> 2% of each run, Pallas kernels for 22% -> 23%
where the time goes in v1:
time: 210 us; the launch traced here: 209 us
  waiting for transfers between devices  80 us (38%)
  starting transfers between devices  62.7 us (30%)
  Pallas kernels  55.4 us (26%)
  local copies, waits for them, and re-layouts  6.94 us (3%)
  other arithmetic  3.02 us (1%)
    ppermute x5, waiting for transfers between devices, chips_on(): return lax.ppermute(x, AA, chip_pairs(d))  36.4 us
    ppermute x14, starting transfers between devices, round_z(): return lax.ppermute(x, 'z', [(i, (i + step) % RING) for i in range(RING)])  27.2 us
    ppermute x14, waiting for transfers between devices, round_z(): return lax.ppermute(x, 'z', [(i, (i + step) % RING) for i in range(RING)])  25.2 us
    ppermute x5, waiting for transfers between devices, chips_back(): return lax.ppermute(x, AA, [(j, i) for i, j in chip_pairs(d)])  15.9 us
    ppermute x14, starting transfers between devices, swapped(): return lax.ppermute(x, axis, [(0, 1), (1, 0)])  14.4 us
    ppermute x5, starting transfers between devices, chips_on(): return lax.ppermute(x, AA, chip_pairs(d))  13.4 us
    pallas_call x1, Pallas kernels, attention_grads(): pl.pallas_call(grads_kernel, name='attention_grads', out_shape=(jax.Shape...  12.3 us
    pallas_call x2, Pallas kernels, attention_stats(): pl.pallas_call(lambda *refs: stats_kernel(low, high, *refs), name='stats_...  12.1 us
  transfers between devices with their start and end apart: 38, of which 13 were waited for; matrix products, arithmetic and copies ran while one was open for 2% of the time, Pallas kernels for 23%

profile of v1, /device:TPU:24, one launch (start us, length us, event | category | flops | bytes accessed | tf_op | source)
XLA Modules:
  0.0 208.7 jit_solution(4351688033087430256)
XLA Ops:
  0.0 0.6 pad_add_fusion.at_ref.refs_0_
  0.6 3.5 %split_w_out.1 = bf16[4,256,384]{2,1,0:T(8,128)(2,1)} custom-call(s32[3]{0:T(128)} %pad_add_fusion.at_ref.refs_0_, bf16[256,5376]{1,0:T(8,128)(2,1)} %refs_1_.3), custom_call_target="tpu_custom_call" | custom-call | tf_op jit(solution)/shard_map/split_w_out/pallas_call | solution.py:348
  4.1 3.1 %collective-permute-start.13 = (bf16[4,256,384]{2,1,0:T(8,128)(2,1)}, bf16[4,256,384]{2,1,0:T(8,128)(2,1)}, u32[]{:S(2)}, u32[]{:S(2)}) collective-permute-start(bf16[4,256,384]{2,1,0:T(8,128)(2,1)} %split_w_out.1), channel_id=1, source_target_pairs={{0,1},{1,0},{2,3},{3,2},{4,5},{5,4},{6,7},{7,6},{8,9},{9,8},{10,11... | collective-permute-start | bytes 2359304 | tf_op jit(solution)/shard_map/ppermute | solution.py:602
  7.3 0.7 collective-permute-start.11
  8.0 2.5 %collective-permute-start.8 = (bf16[400,256]{1,0:T(8,128)(2,1)S(1)}, bf16[400,256]{1,0:T(8,128)(2,1)S(1)}, u32[]{:S(2)}, u32[]{:S(2)}) collective-permute-start(bf16[400,256]{1,0:T(8,128)(2,1)S(1)} %fusion.2.refs_3_.refs_6_), channel_id=1, source_target_pairs={{0,128},{16,144},{32,160},{48,176},{64,192},{80,208},{96,224},{112... | collective-permute-start | bytes 614408 | tf_op jit(solution)/shard_map/ppermute | solution.py:610
  10.5 1.9 collective-permute-start.7
  12.4 1.9 collective-permute-start.5
  14.4 1.2 dynamic-slice_bitcast_fusion
  15.6 1.1 dynamic-slice_bitcast_fusion.1
  16.7 2.0 collective-permute-start.15
  18.7 0.1 pad_maximum_fusion
  18.9 10.9 %collective-permute-done.8.refs_9_.refs_10_ = bf16[400,256]{1,0:T(8,128)(2,1)S(1)} collective-permute-done((bf16[400,256]{1,0:T(8,128)(2,1)S(1)}, bf16[400,256]{1,0:T(8,128)(2,1)S(1)}, u32[]{:S(2)}, u32[]{:S(2)}) %collective-permute-start.8) | collective-permute-done | bytes 204832 | tf_op jit(solution)/shard_map/ppermute | solution.py:610
  29.7 0.5 collective-permute-start
  30.2 3.9 %collective-permute-done.7.refs_8_.refs_9_ = bf16[400,256]{1,0:T(8,128)(2,1)S(1)} collective-permute-done((bf16[400,256]{1,0:T(8,128)(2,1)S(1)}, bf16[400,256]{1,0:T(8,128)(2,1)S(1)}, u32[]{:S(2)}, u32[]{:S(2)}) %collective-permute-start.7) | collective-permute-done | bytes 204832 | tf_op jit(solution)/shard_map/ppermute | solution.py:610
  34.1 0.5 collective-permute-start.14
  34.6 4.5 %collective-permute-done.5.refs_7_.refs_8_ = bf16[400,256]{1,0:T(8,128)(2,1)} collective-permute-done((bf16[400,256]{1,0:T(8,128)(2,1)S(1)}, bf16[400,256]{1,0:T(8,128)(2,1)}, u32[]{:S(2)}, u32[]{:S(2)}) %collective-permute-start.5) | collective-permute-done | bytes 204832 | tf_op jit(solution)/shard_map/ppermute | solution.py:610
  39.2 5.9 %collective-permute-start.16 = (bf16[336,384]{1,0:T(8,128)(2,1)S(1)}, bf16[336,384]{1,0:T(8,128)(2,1)S(1)}, u32[]{:S(2)}, u32[]{:S(2)}) collective-permute-start(bf16[336,384]{1,0:T(8,128)(2,1)S(1)} %bitcast.29), channel_id=1, source_target_pairs={{0,14},{2,0},{4,2},{6,4},{8,6},{10,8},{12,10},{14,12},{1,15},{3,1}... | collective-permute-start | bytes 774152 | tf_op jit(solution)/shard_map/ppermute | solution.py:618
  45.1 6.4 %collective-permute-start.2 = (bf16[400,256]{1,0:T(8,128)(2,1)S(1)}, bf16[400,256]{1,0:T(8,128)(2,1)}, u32[]{:S(2)}, u32[]{:S(2)}) collective-permute-start(bf16[400,256]{1,0:T(8,128)(2,1)S(1)} %fusion.2.refs_3_.refs_6_), channel_id=1, source_target_pairs={{0,32},{16,48},{32,64},{48,80},{64,96},{80,112},{96,128},{112,144}... | collective-permute-start | bytes 614408 | tf_op jit(solution)/shard_map/ppermute | solution.py:610
  51.5 3.3 %collective-permute-start.18 = (bf16[336,384]{1,0:T(8,128)(2,1)S(1)}, bf16[336,384]{1,0:T(8,128)(2,1)S(1)}, u32[]{:S(2)}, u32[]{:S(2)}) collective-permute-start(bf16[336,384]{1,0:T(8,128)(2,1)S(1)} %collective-permute-done.16.refs_6_), channel_id=1, source_target_pairs={{0,14},{2,0},{4,2},{6,4},{8,6},{10,8},{12,10},{14,12},{1,15},{3,1}... | collective-permute-start | bytes 774152 | tf_op jit(solution)/shard_map/ppermute | solution.py:618
  54.8 17.2 %collective-permute-done.2.refs_4_.refs_7_ = bf16[400,256]{1,0:T(8,128)(2,1)} collective-permute-done((bf16[400,256]{1,0:T(8,128)(2,1)S(1)}, bf16[400,256]{1,0:T(8,128)(2,1)}, u32[]{:S(2)}, u32[]{:S(2)}) %collective-permute-start.2) | collective-permute-done | bytes 204832 | tf_op jit(solution)/shard_map/ppermute | solution.py:610
  71.9 5.9 %collective-permute-start.20 = (bf16[336,384]{1,0:T(8,128)(2,1)S(1)}, bf16[336,384]{1,0:T(8,128)(2,1)S(1)}, u32[]{:S(2)}, u32[]{:S(2)}) collective-permute-start(bf16[336,384]{1,0:T(8,128)(2,1)S(1)} %collective-permute-done.18.refs_8_), channel_id=1, source_target_pairs={{0,14},{2,0},{4,2},{6,4},{8,6},{10,8},{12,10},{14,12},{1,15},{3,1}... | collective-permute-start | bytes 774152 | tf_op jit(solution)/shard_map/ppermute | solution.py:618
  77.9 0.2 collective-permute-start.4
  78.1 5.8 %collective-permute-done.20.refs_10_ = bf16[336,384]{1,0:T(8,128)(2,1)S(1)} collective-permute-done((bf16[336,384]{1,0:T(8,128)(2,1)S(1)}, bf16[336,384]{1,0:T(8,128)(2,1)S(1)}, u32[]{:S(2)}, u32[]{:S(2)}) %collective-permute-start.20) | collective-permute-done | bytes 258080 | tf_op jit(solution)/shard_map/ppermute | solution.py:618
  83.9 3.4 %collective-permute-done.21.refs_11_ = bf16[336,384]{1,0:T(8,128)(2,1)S(1)} collective-permute-done((bf16[336,384]{1,0:T(8,128)(2,1)S(1)}, bf16[336,384]{1,0:T(8,128)(2,1)S(1)}, u32[]{:S(2)}, u32[]{:S(2)}) %collective-permute-start.21) | collective-permute-done | bytes 258080 | tf_op jit(solution)/shard_map/ppermute | solution.py:618
  87.4 0.6 copy-done.21
  88.0 0.9 copy-done.8
  88.9 6.4 %dout_parts.1 = (f32[256,384]{1,0:T(8,128)}, bf16[256,384]{1,0:T(8,128)(2,1)}) custom-call(s32[3]{0:T(128)} %pad_add_fusion.at_ref.refs_0_, bf16[256,5376]{1,0:T(8,128)(2,1)} %refs_1_.3, bf16[4,256,384]{2,1,0:T(8,128)(2,1)} %collective-permute-done.13.refs_2_, bf16[4,256,384]{2,1,0:T(8,128)(2,1)} %copy-done.8, bf16[336,384]{1,0:T(8,128)(2,1)} %bitcast.27, ...), custom_call_target="tpu_custom_call" | custom-call | tf_op jit(solution)/shard_map/dout_parts/pallas_call | solution.py:406
  95.4 0.6 collective-permute-start.22
  96.0 0.6 broadcast_in_dim.8.refs_1_
  96.6 6.3 %stats_near.1 = (f32[1,768]{1,0:T(1,128)}, f32[1,768]{1,0:T(1,128)}, f32[128,768]{1,0:T(8,128)}, s32[1,384]{1,0:T(1,128)}) custom-call(s32[1]{0:T(128)} %bitcast.9.refs_0_.own_ref, s32[1,384]{1,0:T(1,128)} %broadcast_in_dim.8.refs_1_, bf16[384,256]{1,0:T(8,128)(2,1)} %refs_1_.4, bf16[400,256]{1,0:T(8,128)(2,1)} %copy-done.3, ...), custom_call_target="tpu_custom_call" | custom-call | tf_op jit(solution)/shard_map/stats_near/pallas_call | solution.py:284
  102.9 5.8 %stats_far.1 = (f32[1,768]{1,0:T(1,128)}, f32[128,768]{1,0:T(8,128)}, s32[1,384]{1,0:T(1,128)}, s32[1]{0:T(128)}) custom-call(s32[1]{0:T(128)} %bitcast.9.refs_0_.own_ref, s32[1,384]{1,0:T(1,128)} %broadcast_in_dim.8.refs_1_, bf16[384,256]{1,0:T(8,128)(2,1)} %refs_1_.4, f32[1,768]{1,0:T(1,128)} %get-tuple-element.40.refs_3_, ...), custom_call_target="tpu_custom_call" | custom-call | tf_op jit(solution)/shard_map/stats_far/pallas_call | solution.py:284
  108.8 0.7 copy-done.26
  109.4 12.3 %attention_grads.1 = (bf16[256,384]{1,0:T(8,128)(2,1)}, bf16[5,384,256]{2,1,0:T(8,128)(2,1)}, bf16[5,384,256]{2,1,0:T(8,128)(2,1)}) custom-call(s32[1]{0:T(128)} %bitcast.9.refs_0_.own_ref, s32[1]{0:T(128)} %get-tuple-element.44.low_ref, s32[1,384]{1,0:T(1,128)} %get-tuple-element.45.refs_0_, bf16[384,256]{1,0:T(8,128)(2,1)} %refs_1_.4, ...), custom_call_target="tpu_custom_call" | custom-call | tf_op jit(solution)/shard_map/attention_grads/pallas_call | solution.py:298
  121.7 2.1 %collective-permute-start.23 = (bf16[5,384,256]{2,1,0:T(8,128)(2,1)}, bf16[5,384,256]{2,1,0:T(8,128)(2,1)}, u32[]{:S(2)}, u32[]{:S(2)}) collective-permute-start(bf16[5,384,256]{2,1,0:T(8,128)(2,1)} %get-tuple-element.51), channel_id=1, source_target_pairs={{0,16},{16,0},{1,17},{17,1},{2,18},{18,2},{3,19},{19,3},{4,20},{20... | collective-permute-start | bytes 2949128 | tf_op jit(solution)/shard_map/ppermute | solution.py:602
  123.9 0.1 collective-permute-start.1
  124.0 2.4 %collective-permute-done.23.got_ref = bf16[5,384,256]{2,1,0:T(8,128)(2,1)} collective-permute-done((bf16[5,384,256]{2,1,0:T(8,128)(2,1)}, bf16[5,384,256]{2,1,0:T(8,128)(2,1)}, u32[]{:S(2)}, u32[]{:S(2)}) %collective-permute-start.23) | collective-permute-done | bytes 983072 | tf_op jit(solution)/shard_map/ppermute | solution.py:602
  126.4 2.6 %join_partials.1 = (f32[384,256]{1,0:T(8,128)}, bf16[384,256]{1,0:T(8,128)(2,1)}, bf16[384,256]{1,0:T(8,128)(2,1)}, bf16[384,256]{1,0:T(8,128)(2,1)}, bf16[384,2...) custom-call(s32[1]{0:T(128)} %bitcast.2.core_ref, bf16[5,384,256]{2,1,0:T(8,128)(2,1)} %get-tuple-element.50.mine_ref, ...), custom_call_target="tpu_custom_call" | custom-call | tf_op jit(solution)/shard_map/join_partials/pallas_call | solution.py:439
  129.1 0.7 collective-permute-start.24
  129.7 1.3 collective-permute-start.25
  131.0 1.9 collective-permute-start.26
  132.9 1.9 collective-permute-start.27
  134.9 1.9 collective-permute-start.28
  136.8 2.2 %collective-permute-done.25.refs_1_ = bf16[384,256]{1,0:T(8,128)(2,1)S(1)} collective-permute-done((bf16[384,256]{1,0:T(8,128)(2,1)}, bf16[384,256]{1,0:T(8,128)(2,1)S(1)}, u32[]{:S(2)}, u32[]{:S(2)}) %collective-permute-start.25) | collective-permute-done | bytes 196640 | tf_op jit(solution)/shard_map/ppermute | solution.py:614
  139.0 3.0 %collective-permute-start.30 = (bf16[256,384]{1,0:T(8,128)(2,1)}, bf16[256,384]{1,0:T(8,128)(2,1)}, u32[]{:S(2)}, u32[]{:S(2)}) collective-permute-start(bf16[256,384]{1,0:T(8,128)(2,1)} %get-tuple-element.58.refs_6_), channel_id=1, source_target_pairs={{0,1},{1,0},{2,3},{3,2},{4,5},{5,4},{6,7},{7,6},{8,9},{9,8},{10,11... | collective-permute-start | bytes 589832 | tf_op jit(solution)/shard_map/ppermute | solution.py:602
  142.0 2.6 %collective-permute-done.27.refs_3_ = bf16[384,256]{1,0:T(8,128)(2,1)S(1)} collective-permute-done((bf16[384,256]{1,0:T(8,128)(2,1)}, bf16[384,256]{1,0:T(8,128)(2,1)S(1)}, u32[]{:S(2)}, u32[]{:S(2)}) %collective-permute-start.27) | collective-permute-done | bytes 196640 | tf_op jit(solution)/shard_map/ppermute | solution.py:614
  144.6 11.2 %collective-permute-done.28.refs_4_ = bf16[384,256]{1,0:T(8,128)(2,1)} collective-permute-done((bf16[384,256]{1,0:T(8,128)(2,1)}, bf16[384,256]{1,0:T(8,128)(2,1)}, u32[]{:S(2)}, u32[]{:S(2)}) %collective-permute-start.28) | collective-permute-done | bytes 196640 | tf_op jit(solution)/shard_map/ppermute | solution.py:614
  155.8 2.2 %total_partials.1.refs_7_ = bf16[256,384]{1,0:T(8,128)(2,1)} custom-call(f32[384,256]{1,0:T(8,128)} %get-tuple-element.52.own_ref, bf16[384,256]{1,0:T(8,128)(2,1)} %copy-done.22, bf16[384,256]{1,0:T(8,128)(2,1)} %copy-done.23, bf16[384,256]{1,0:T(8,128)(2,1)} %copy-done.24, bf16[384,256]{1,0:T(8,128)(2,1)} %copy-done.25, ...), custom_call_target="tpu_custom_call" | custom-call | tf_op jit(solution)/shard_map/total_partials/pallas_call | solution.py:457
  158.0 4.1 %collective-permute-start.29 = (bf16[256,384]{1,0:T(8,128)(2,1)}, bf16[256,384]{1,0:T(8,128)(2,1)S(1)}, u32[]{:S(2)}, u32[]{:S(2)}) collective-permute-start(bf16[256,384]{1,0:T(8,128)(2,1)} %total_partials.1.refs_7_), channel_id=1, source_target_pairs={{0,1},{1,0},{2,3},{3,2},{4,5},{5,4},{6,7},{7,6},{8,9},{9,8},{10,11... | collective-permute-start | bytes 589832 | tf_op jit(solution)/shard_map/ppermute | solution.py:602
  162.2 1.1 copy-done.1
  163.3 7.8 %own_project.1 = (f32[336,384]{1,0:T(8,128)}, f32[336,384]{1,0:T(8,128)}, f32[336,384]{1,0:T(8,128)}, f32[336,384]{1,0:T(8,128)}, f32[336,384]{1,0:T(8,128)}, /*...) custom-call(s32[3]{0:T(128)} %pad_add_fusion.at_ref.refs_0_, bf16[5376,256]{1,0:T(8,128)(2,1)} %refs_1_.5, ...), custom_call_target="tpu_custom_call" | custom-call | tf_op jit(solution)/shard_map/own_project/pallas_call | solution.py:522
  171.1 0.7 copy-done.7
  171.7 3.2 %far_project.2 = (bf16[336,384]{1,0:T(8,128)(2,1)}, bf16[336,384]{1,0:T(8,128)(2,1)}) custom-call(s32[3]{0:T(128)} %pad_add_fusion.at_ref.refs_0_, bf16[4,336,512]{2,1,0:T(8,128)(2,1)} %copy-done, bf16[4,336,512]{2,1,0:T(8,128)(2,1)} %copy-done.1, bf16[256,384]{1,0:T(8,128)(2,1)} %copy-done.7, f32[336,384]{1,0:T(8,128)} %get-tuple-element.59.refs_4_, ...), custom_call_target="tpu_custom_call" | custom-call | tf_op jit(solution)/shard_map/far_project/pallas_call | solution.py:583
  175.0 3.2 %collective-permute-start.35 = (bf16[336,384]{1,0:T(8,128)(2,1)}, bf16[336,384]{1,0:T(8,128)(2,1)S(1)}, u32[]{:S(2)}, u32[]{:S(2)}) collective-permute-start(bf16[336,384]{1,0:T(8,128)(2,1)} %get-tuple-element.71), channel_id=1, source_target_pairs={{0,14},{2,0},{4,2},{6,4},{8,6},{10,8},{12,10},{14,12},{1,15},{3,1}... | collective-permute-start | bytes 774152 | tf_op jit(solution)/shard_map/ppermute | solution.py:618
  178.2 5.2 %far_project.3 = (f32[336,384]{1,0:T(8,128)}, f32[336,384]{1,0:T(8,128)}, f32[336,384]{1,0:T(8,128)}, f32[336,384]{1,0:T(8,128)}, f32[336,384]{1,0:T(8,128)}, /*index=5*/f32[336,384]{1,0:T(8,128)}) custom-call(s32[3]{0:T(128)} %pad_add_fusion.at_ref.refs_0_, bf16[4,336,512]{2,1,0:T(8,128)(2,1)} %copy-done, bf16[4,336,512]{2,1,0:T(8,128)(2,1)} %copy-done.1, ...), custom_call_target="tpu_custom_call" | custom-call | tf_op jit(solution)/shard_map/far_project/pallas_call | solution.py:583
  183.5 1.2 add_convert_fusion.5
  184.7 0.1 collective-permute-start.32
  184.9 3.3 %collective-permute-start.36 = (bf16[336,384]{1,0:T(8,128)(2,1)S(1)}, bf16[336,384]{1,0:T(8,128)(2,1)S(1)}, u32[]{:S(2)}, u32[]{:S(2)}) collective-permute-start(bf16[336,384]{1,0:T(8,128)(2,1)S(1)} %add_convert_fusion.2), channel_id=1, source_target_pairs={{0,14},{2,0},{4,2},{6,4},{8,6},{10,8},{12,10},{14,12},{1,15},{3,1}... | collective-permute-start | bytes 774152 | tf_op jit(solution)/shard_map/ppermute | solution.py:618
  188.2 4.1 %collective-permute-done.32 = bf16[336,384]{1,0:T(8,128)(2,1)S(1)} collective-permute-done((bf16[336,384]{1,0:T(8,128)(2,1)S(1)}, bf16[336,384]{1,0:T(8,128)(2,1)S(1)}, u32[]{:S(2)}, u32[]{:S(2)}) %collective-permute-start.32) | collective-permute-done | bytes 258080 | tf_op jit(solution)/shard_map/ppermute | solution.py:618
  192.4 0.1 collective-permute-start.33
  192.6 3.3 %collective-permute-start.37 = (bf16[336,384]{1,0:T(8,128)(2,1)S(1)}, bf16[336,384]{1,0:T(8,128)(2,1)S(1)}, u32[]{:S(2)}, u32[]{:S(2)}) collective-permute-start(bf16[336,384]{1,0:T(8,128)(2,1)S(1)} %add_convert_fusion.1), channel_id=1, source_target_pairs={{0,14},{2,0},{4,2},{6,4},{8,6},{10,8},{12,10},{14,12},{1,15},{3,1}... | collective-permute-start | bytes 774152 | tf_op jit(solution)/shard_map/ppermute | solution.py:618
  195.9 4.3 %collective-permute-done.33 = bf16[336,384]{1,0:T(8,128)(2,1)S(1)} collective-permute-done((bf16[336,384]{1,0:T(8,128)(2,1)S(1)}, bf16[336,384]{1,0:T(8,128)(2,1)S(1)}, u32[]{:S(2)}, u32[]{:S(2)}) %collective-permute-start.33) | collective-permute-done | bytes 258080 | tf_op jit(solution)/shard_map/ppermute | solution.py:618
  200.3 0.1 collective-permute-start.34
  200.4 7.5 %collective-permute-done.34 = bf16[336,384]{1,0:T(8,128)(2,1)S(1)} collective-permute-done((bf16[336,384]{1,0:T(8,128)(2,1)S(1)}, bf16[336,384]{1,0:T(8,128)(2,1)S(1)}, u32[]{:S(2)}, u32[]{:S(2)}) %collective-permute-start.34) | collective-permute-done | bytes 258080 | tf_op jit(solution)/shard_map/ppermute | solution.py:618
  207.9 0.8 fusion.1
  (97 shorter events, 0.6 us)
Async XLA Ops:
  0.6 6.6 %copy-start.29 = (s32[384]{0:T(512)S(1)}, s32[384]{0:T(512)}, u32[]{:S(2)}) copy-start(s32[384]{0:T(512)} %param.13) | copy-start | bytes 4612
  0.6 6.6 %copy-start.27 = (bf16[384,128]{1,0:T(8,128)(2,1)S(1)}, bf16[384,128]{1,0:T(8,128)(2,1)}, u32[]{:S(2)}) copy-start(bf16[384,128]{1,0:T(8,128)(2,1)} %param.11) | copy-start | bytes 294916
  0.6 6.6 %copy-start.28 = (bf16[384,128]{1,0:T(8,128)(2,1)S(1)}, bf16[384,128]{1,0:T(8,128)(2,1)}, u32[]{:S(2)}) copy-start(bf16[384,128]{1,0:T(8,128)(2,1)} %param.10) | copy-start | bytes 294916
  4.1 30.0 %collective-permute-start.13 = (bf16[4,256,384]{2,1,0:T(8,128)(2,1)}, bf16[4,256,384]{2,1,0:T(8,128)(2,1)}, u32[]{:S(2)}, u32[]{:S(2)}) collective-permute-start(bf16[4,256,384]{2,1,0:T(8,128)(2,1)} %split_w_out.1), channel_id=1, source_target_pairs={{0,1},{1,0},{2,3},{3,2},{4,5},{5,4},{6,7},{7,6},{8,9},{9,8},{10,11... | collective-permute-start | bytes 2359304 | tf_op jit(solution)/shard_map/ppermute | solution.py:602
  7.3 37.8 %copy-start.3 = (bf16[400,256]{1,0:T(8,128)(2,1)}, bf16[400,256]{1,0:T(8,128)(2,1)S(1)}, u32[]{:S(2)}) copy-start(bf16[400,256]{1,0:T(8,128)(2,1)S(1)} %fusion.2.refs_3_.refs_6_) | copy-start | bytes 614404
  7.3 9.4 %collective-permute-start.11 = (bf16[400,256]{1,0:T(8,128)(2,1)S(1)}, bf16[400,256]{1,0:T(8,128)(2,1)S(1)}, u32[]{:S(2)}, u32[]{:S(2)}) collective-permute-start(bf16[400,256]{1,0:T(8,128)(2,1)S(1)} %fusion.2.refs_3_.refs_6_), channel_id=1, source_target_pairs={{16,176},{48,208},{80,240},{17,177},{49,209},{81,241},{18,178},{50... | collective-permute-start | bytes 614408 | tf_op jit(solution)/shard_map/ppermute | solution.py:610
  8.0 21.8 %collective-permute-start.8 = (bf16[400,256]{1,0:T(8,128)(2,1)S(1)}, bf16[400,256]{1,0:T(8,128)(2,1)S(1)}, u32[]{:S(2)}, u32[]{:S(2)}) collective-permute-start(bf16[400,256]{1,0:T(8,128)(2,1)S(1)} %fusion.2.refs_3_.refs_6_), channel_id=1, source_target_pairs={{0,128},{16,144},{32,160},{48,176},{64,192},{80,208},{96,224},{112... | collective-permute-start | bytes 614408 | tf_op jit(solution)/shard_map/ppermute | solution.py:610
  10.5 23.7 %collective-permute-start.7 = (bf16[400,256]{1,0:T(8,128)(2,1)S(1)}, bf16[400,256]{1,0:T(8,128)(2,1)S(1)}, u32[]{:S(2)}, u32[]{:S(2)}) collective-permute-start(bf16[400,256]{1,0:T(8,128)(2,1)S(1)} %fusion.2.refs_3_.refs_6_), channel_id=1, source_target_pairs={{0,96},{16,112},{32,128},{48,144},{64,160},{80,176},{96,192},{112,... | collective-permute-start | bytes 614408 | tf_op jit(solution)/shard_map/ppermute | solution.py:610
  12.4 26.8 %collective-permute-start.5 = (bf16[400,256]{1,0:T(8,128)(2,1)S(1)}, bf16[400,256]{1,0:T(8,128)(2,1)}, u32[]{:S(2)}, u32[]{:S(2)}) collective-permute-start(bf16[400,256]{1,0:T(8,128)(2,1)S(1)} %fusion.2.refs_3_.refs_6_), channel_id=1, source_target_pairs={{0,64},{16,80},{32,96},{48,112},{64,128},{80,144},{96,160},{112,17... | collective-permute-start | bytes 614408 | tf_op jit(solution)/shard_map/ppermute | solution.py:610
  14.3 2.4 %copy-start.14 = (bf16[384,336]{0,1:T(8,128)(2,1)S(1)}, bf16[384,336]{0,1:T(8,128)(2,1)}, u32[]{:S(2)}) copy-start(bf16[384,336]{0,1:T(8,128)(2,1)} %param.12) | copy-start | bytes 774148
  16.7 2.2 %copy-start.30 = (bf16[400,256]{1,0:T(8,128)(2,1)}, bf16[400,256]{1,0:T(8,128)(2,1)S(1)}, u32[]{:S(2)}) copy-start(bf16[400,256]{1,0:T(8,128)(2,1)S(1)} %collective-permute-done.11) | copy-start | bytes 614404
  16.7 28.3 %collective-permute-start.15 = (bf16[336,384]{1,0:T(8,128)(2,1)S(1)}, bf16[336,384]{1,0:T(8,128)(2,1)S(1)}, u32[]{:S(2)}, u32[]{:S(2)}) collective-permute-start(bf16[336,384]{1,0:T(8,128)(2,1)S(1)} %bitcast.28), channel_id=1, source_target_pairs={{0,2},{2,4},{4,6},{6,8},{8,10},{10,12},{12,14},{14,0},{1,3},{3,5},... | collective-permute-start | bytes 774152 | tf_op jit(solution)/shard_map/ppermute | solution.py:618
  29.7 65.6 %copy-start.4 = (bf16[400,256]{1,0:T(8,128)(2,1)}, bf16[400,256]{1,0:T(8,128)(2,1)S(1)}, u32[]{:S(2)}) copy-start(bf16[400,256]{1,0:T(8,128)(2,1)S(1)} %collective-permute-done.8.refs_9_.refs_10_) | copy-start | bytes 614404
  29.7 94.1 %collective-permute-start = (bf16[4,336,512]{2,1,0:T(8,128)(2,1)S(1)}, bf16[4,336,512]{2,1,0:T(8,128)(2,1)S(1)}, u32[]{:S(2)}, u32[]{:S(2)}) collective-permute-start(bf16[4,336,512]{2,1,0:T(8,128)(2,1)S(1)} %pad_maximum_fusion), channel_id=1, source_target_pairs={{0,1},{1,0},{2,3},{3,2},{4,5},{5,4},{6,7},{7,6},{8,9},{9,8},{10,11... | collective-permute-start | bytes 4128776 | tf_op jit(solution)/shard_map/ppermute | solution.py:602
  34.1 68.8 %copy-start.5 = (bf16[400,256]{1,0:T(8,128)(2,1)}, bf16[400,256]{1,0:T(8,128)(2,1)S(1)}, u32[]{:S(2)}) copy-start(bf16[400,256]{1,0:T(8,128)(2,1)S(1)} %collective-permute-done.7.refs_8_.refs_9_) | copy-start | bytes 614404
  34.1 10.9 %collective-permute-start.3 = (bf16[400,256]{1,0:T(8,128)(2,1)S(1)}, bf16[400,256]{1,0:T(8,128)(2,1)S(1)}, u32[]{:S(2)}, u32[]{:S(2)}) collective-permute-start(bf16[400,256]{1,0:T(8,128)(2,1)S(1)} %fusion.2.refs_3_.refs_6_), channel_id=1, source_target_pairs={{0,16},{16,0},{1,17},{17,1},{2,18},{18,2},{3,19},{19,3},{4,20},{20... | collective-permute-start | bytes 614408 | tf_op jit(solution)/shard_map/ppermute | solution.py:602
  34.1 53.2 %collective-permute-start.14 = (bf16[4,256,384]{2,1,0:T(8,128)(2,1)}, bf16[4,256,384]{2,1,0:T(8,128)(2,1)S(1)}, u32[]{:S(2)}, u32[]{:S(2)}) collective-permute-start(bf16[4,256,384]{2,1,0:T(8,128)(2,1)} %collective-permute-done.13.refs_2_), channel_id=1, source_target_pairs={{0,16},{16,0},{1,17},{17,1},{2,18},{18,2},{3,19},{19,3},{4,20},{20... | collective-permute-start | bytes 2359304 | tf_op jit(solution)/shard_map/ppermute | solution.py:602
  39.2 12.3 %collective-permute-start.16 = (bf16[336,384]{1,0:T(8,128)(2,1)S(1)}, bf16[336,384]{1,0:T(8,128)(2,1)S(1)}, u32[]{:S(2)}, u32[]{:S(2)}) collective-permute-start(bf16[336,384]{1,0:T(8,128)(2,1)S(1)} %bitcast.29), channel_id=1, source_target_pairs={{0,14},{2,0},{4,2},{6,4},{8,6},{10,8},{12,10},{14,12},{1,15},{3,1}... | collective-permute-start | bytes 774152 | tf_op jit(solution)/shard_map/ppermute | solution.py:618
  45.0 42.3 %copy-start.15 = (bf16[336,384]{1,0:T(8,128)(2,1)}, bf16[336,384]{1,0:T(8,128)(2,1)S(1)}, u32[]{:S(2)}) copy-start(bf16[336,384]{1,0:T(8,128)(2,1)S(1)} %collective-permute-done.15.refs_5_) | copy-start | bytes 774148
  45.0 9.7 %collective-permute-start.17 = (bf16[336,384]{1,0:T(8,128)(2,1)S(1)}, bf16[336,384]{1,0:T(8,128)(2,1)S(1)}, u32[]{:S(2)}, u32[]{:S(2)}) collective-permute-start(bf16[336,384]{1,0:T(8,128)(2,1)S(1)} %collective-permute-done.15.refs_5_), channel_id=1, source_target_pairs={{0,2},{2,4},{4,6},{6,8},{8,10},{10,12},{12,14},{14,0},{1,3},{3,5},... | collective-permute-start | bytes 774152 | tf_op jit(solution)/shard_map/ppermute | solution.py:618
  45.1 42.3 %copy-start.6 = (bf16[400,256]{1,0:T(8,128)(2,1)}, bf16[400,256]{1,0:T(8,128)(2,1)S(1)}, u32[]{:S(2)}) copy-start(bf16[400,256]{1,0:T(8,128)(2,1)S(1)} %collective-permute-done.3.refs_5_.refs_11_) | copy-start | bytes 614404
  45.1 26.9 %collective-permute-start.2 = (bf16[400,256]{1,0:T(8,128)(2,1)S(1)}, bf16[400,256]{1,0:T(8,128)(2,1)}, u32[]{:S(2)}, u32[]{:S(2)}) collective-permute-start(bf16[400,256]{1,0:T(8,128)(2,1)S(1)} %fusion.2.refs_3_.refs_6_), channel_id=1, source_target_pairs={{0,32},{16,48},{32,64},{48,80},{64,96},{80,112},{96,128},{112,144}... | collective-permute-start | bytes 614408 | tf_op jit(solution)/shard_map/ppermute | solution.py:610
  51.5 35.9 %copy-start.16 = (bf16[336,384]{1,0:T(8,128)(2,1)}, bf16[336,384]{1,0:T(8,128)(2,1)S(1)}, u32[]{:S(2)}) copy-start(bf16[336,384]{1,0:T(8,128)(2,1)S(1)} %collective-permute-done.16.refs_6_) | copy-start | bytes 774148
  51.5 20.5 %collective-permute-start.18 = (bf16[336,384]{1,0:T(8,128)(2,1)S(1)}, bf16[336,384]{1,0:T(8,128)(2,1)S(1)}, u32[]{:S(2)}, u32[]{:S(2)}) collective-permute-start(bf16[336,384]{1,0:T(8,128)(2,1)S(1)} %collective-permute-done.16.refs_6_), channel_id=1, source_target_pairs={{0,14},{2,0},{4,2},{6,4},{8,6},{10,8},{12,10},{14,12},{1,15},{3,1}... | collective-permute-start | bytes 774152 | tf_op jit(solution)/shard_map/ppermute | solution.py:618
  54.7 32.6 %copy-start.17 = (bf16[336,384]{1,0:T(8,128)(2,1)}, bf16[336,384]{1,0:T(8,128)(2,1)S(1)}, u32[]{:S(2)}) copy-start(bf16[336,384]{1,0:T(8,128)(2,1)S(1)} %collective-permute-done.17.refs_7_) | copy-start | bytes 774148
  54.8 23.1 %collective-permute-start.19 = (bf16[336,384]{1,0:T(8,128)(2,1)S(1)}, bf16[336,384]{1,0:T(8,128)(2,1)S(1)}, u32[]{:S(2)}, u32[]{:S(2)}) collective-permute-start(bf16[336,384]{1,0:T(8,128)(2,1)S(1)} %collective-permute-done.17.refs_7_), channel_id=1, source_target_pairs={{0,2},{2,4},{4,6},{6,8},{8,10},{10,12},{12,14},{14,0},{1,3},{3,5},... | collective-permute-start | bytes 774152 | tf_op jit(solution)/shard_map/ppermute | solution.py:618
  71.9 6.0 %collective-permute-start.6 = (bf16[400,256]{1,0:T(8,128)(2,1)}, bf16[400,256]{1,0:T(8,128)(2,1)S(1)}, u32[]{:S(2)}, u32[]{:S(2)}) collective-permute-start(bf16[400,256]{1,0:T(8,128)(2,1)} %collective-permute-done.5.refs_7_.refs_8_), channel_id=1, source_target_pairs={{0,16},{16,0},{1,17},{17,1},{2,18},{18,2},{3,19},{19,3},{4,20},{20... | collective-permute-start | bytes 614408 | tf_op jit(solution)/shard_map/ppermute | solution.py:602
  71.9 15.5 %copy-start.18 = (bf16[336,384]{1,0:T(8,128)(2,1)}, bf16[336,384]{1,0:T(8,128)(2,1)S(1)}, u32[]{:S(2)}) copy-start(bf16[336,384]{1,0:T(8,128)(2,1)S(1)} %collective-permute-done.18.refs_8_) | copy-start | bytes 774148
  71.9 12.0 %collective-permute-start.20 = (bf16[336,384]{1,0:T(8,128)(2,1)S(1)}, bf16[336,384]{1,0:T(8,128)(2,1)S(1)}, u32[]{:S(2)}, u32[]{:S(2)}) collective-permute-start(bf16[336,384]{1,0:T(8,128)(2,1)S(1)} %collective-permute-done.18.refs_8_), channel_id=1, source_target_pairs={{0,14},{2,0},{4,2},{6,4},{8,6},{10,8},{12,10},{14,12},{1,15},{3,1}... | collective-permute-start | bytes 774152 | tf_op jit(solution)/shard_map/ppermute | solution.py:618
  77.9 9.6 %copy-start.19 = (bf16[336,384]{1,0:T(8,128)(2,1)}, bf16[336,384]{1,0:T(8,128)(2,1)S(1)}, u32[]{:S(2)}) copy-start(bf16[336,384]{1,0:T(8,128)(2,1)S(1)} %collective-permute-done.19.refs_9_) | copy-start | bytes 774148
  77.9 9.5 %collective-permute-start.21 = (bf16[336,384]{1,0:T(8,128)(2,1)S(1)}, bf16[336,384]{1,0:T(8,128)(2,1)S(1)}, u32[]{:S(2)}, u32[]{:S(2)}) collective-permute-start(bf16[336,384]{1,0:T(8,128)(2,1)S(1)} %collective-permute-done.19.refs_9_), channel_id=1, source_target_pairs={{0,2},{2,4},{4,6},{6,8},{8,10},{10,12},{12,14},{14,0},{1,3},{3,5},... | collective-permute-start | bytes 774152 | tf_op jit(solution)/shard_map/ppermute | solution.py:618
  77.9 17.5 %copy-start.2 = (bf16[400,256]{1,0:T(8,128)(2,1)}, bf16[400,256]{1,0:T(8,128)(2,1)S(1)}, u32[]{:S(2)}) copy-start(bf16[400,256]{1,0:T(8,128)(2,1)S(1)} %collective-permute-done.6.refs_7_.refs_10_.refs_13_) | copy-start | bytes 614404
  77.9 17.5 %collective-permute-start.4 = (bf16[400,256]{1,0:T(8,128)(2,1)}, bf16[400,256]{1,0:T(8,128)(2,1)}, u32[]{:S(2)}, u32[]{:S(2)}) collective-permute-start(bf16[400,256]{1,0:T(8,128)(2,1)} %collective-permute-done.2.refs_4_.refs_7_), channel_id=1, source_target_pairs={{0,16},{16,0},{1,17},{17,1},{2,18},{18,2},{3,19},{19,3},{4,20},{20... | collective-permute-start | bytes 614408 | tf_op jit(solution)/shard_map/ppermute | solution.py:602
  83.9 3.5 %copy-start.20 = (bf16[336,384]{1,0:T(8,128)(2,1)}, bf16[336,384]{1,0:T(8,128)(2,1)S(1)}, u32[]{:S(2)}) copy-start(bf16[336,384]{1,0:T(8,128)(2,1)S(1)} %collective-permute-done.20.refs_10_) | copy-start | bytes 774148
  83.9 18.9 %collective-permute-start.12 = (bf16[400,256]{1,0:T(8,128)(2,1)}, bf16[400,256]{1,0:T(8,128)(2,1)}, u32[]{:S(2)}, u32[]{:S(2)}) collective-permute-start(bf16[400,256]{1,0:T(8,128)(2,1)} %copy-done.30), channel_id=1, source_target_pairs={{0,16},{16,0},{1,17},{17,1},{2,18},{18,2},{3,19},{19,3},{4,20},{20... | collective-permute-start | bytes 614408 | tf_op jit(solution)/shard_map/ppermute | solution.py:602
  87.3 15.5 %collective-permute-start.10 = (bf16[400,256]{1,0:T(8,128)(2,1)S(1)}, bf16[400,256]{1,0:T(8,128)(2,1)}, u32[]{:S(2)}, u32[]{:S(2)}) collective-permute-start(bf16[400,256]{1,0:T(8,128)(2,1)S(1)} %collective-permute-done.8.refs_9_.refs_10_), channel_id=1, source_target_pairs={{0,16},{16,0},{1,17},{17,1},{2,18},{18,2},{3,19},{19,3},{4,20},{20... | collective-permute-start | bytes 614408 | tf_op jit(solution)/shard_map/ppermute | solution.py:602
  88.9 13.9 %collective-permute-start.9 = (bf16[400,256]{1,0:T(8,128)(2,1)S(1)}, bf16[400,256]{1,0:T(8,128)(2,1)}, u32[]{:S(2)}, u32[]{:S(2)}) collective-permute-start(bf16[400,256]{1,0:T(8,128)(2,1)S(1)} %collective-permute-done.7.refs_8_.refs_9_), channel_id=1, source_target_pairs={{0,16},{16,0},{1,17},{17,1},{2,18},{18,2},{3,19},{19,3},{4,20},{20... | collective-permute-start | bytes 614408 | tf_op jit(solution)/shard_map/ppermute | solution.py:602
  95.4 13.3 %collective-permute-start.22 = (bf16[256,384]{1,0:T(8,128)(2,1)}, bf16[256,384]{1,0:T(8,128)(2,1)S(1)}, u32[]{:S(2)}, u32[]{:S(2)}) collective-permute-start(bf16[256,384]{1,0:T(8,128)(2,1)} %get-tuple-element.47), channel_id=1, source_target_pairs={{0,1},{1,0},{2,3},{3,2},{4,5},{5,4},{6,7},{7,6},{8,9},{9,8},{10,11... | collective-permute-start | bytes 589832 | tf_op jit(solution)/shard_map/ppermute | solution.py:602
  121.7 4.7 %collective-permute-start.23 = (bf16[5,384,256]{2,1,0:T(8,128)(2,1)}, bf16[5,384,256]{2,1,0:T(8,128)(2,1)}, u32[]{:S(2)}, u32[]{:S(2)}) collective-permute-start(bf16[5,384,256]{2,1,0:T(8,128)(2,1)} %get-tuple-element.51), channel_id=1, source_target_pairs={{0,16},{16,0},{1,17},{17,1},{2,18},{18,2},{3,19},{19,3},{4,20},{20... | collective-permute-start | bytes 2949128 | tf_op jit(solution)/shard_map/ppermute | solution.py:602
  123.9 34.2 %copy-start = (bf16[4,336,512]{2,1,0:T(8,128)(2,1)}, bf16[4,336,512]{2,1,0:T(8,128)(2,1)S(1)}, u32[]{:S(2)}) copy-start(bf16[4,336,512]{2,1,0:T(8,128)(2,1)S(1)} %collective-permute-done.refs_4_.refs_1_) | copy-start | bytes 4128772
  123.9 38.3 %collective-permute-start.1 = (bf16[4,336,512]{2,1,0:T(8,128)(2,1)S(1)}, bf16[4,336,512]{2,1,0:T(8,128)(2,1)S(1)}, u32[]{:S(2)}, u32[]{:S(2)}) collective-permute-start(bf16[4,336,512]{2,1,0:T(8,128)(2,1)S(1)} %collective-permute-done.refs_4_.refs_1_), channel_id=1, source_target_pairs={{0,16},{16,0},{1,17},{17,1},{2,18},{18,2},{3,19},{19,3},{4,20},{20... | collective-permute-start | bytes 4128776 | tf_op jit(solution)/shard_map/ppermute | solution.py:602
  129.1 5.8 %collective-permute-start.24 = (bf16[384,256]{1,0:T(8,128)(2,1)}, bf16[384,256]{1,0:T(8,128)(2,1)S(1)}, u32[]{:S(2)}, u32[]{:S(2)}) collective-permute-start(bf16[384,256]{1,0:T(8,128)(2,1)} %get-tuple-element.53), channel_id=1, source_target_pairs={{176,16},{208,48},{240,80},{177,17},{209,49},{241,81},{178,18},{21... | collective-permute-start | bytes 589832 | tf_op jit(solution)/shard_map/ppermute | solution.py:614
  129.7 9.3 %collective-permute-start.25 = (bf16[384,256]{1,0:T(8,128)(2,1)}, bf16[384,256]{1,0:T(8,128)(2,1)S(1)}, u32[]{:S(2)}, u32[]{:S(2)}) collective-permute-start(bf16[384,256]{1,0:T(8,128)(2,1)} %get-tuple-element.54), channel_id=1, source_target_pairs={{128,0},{144,16},{160,32},{176,48},{192,64},{208,80},{224,96},{240... | collective-permute-start | bytes 589832 | tf_op jit(solution)/shard_map/ppermute | solution.py:614
  131.0 11.0 %collective-permute-start.26 = (bf16[384,256]{1,0:T(8,128)(2,1)}, bf16[384,256]{1,0:T(8,128)(2,1)S(1)}, u32[]{:S(2)}, u32[]{:S(2)}) collective-permute-start(bf16[384,256]{1,0:T(8,128)(2,1)} %get-tuple-element.55), channel_id=1, source_target_pairs={{96,0},{112,16},{128,32},{144,48},{160,64},{176,80},{192,96},{208,... | collective-permute-start | bytes 589832 | tf_op jit(solution)/shard_map/ppermute | solution.py:614
  132.9 11.7 %collective-permute-start.27 = (bf16[384,256]{1,0:T(8,128)(2,1)}, bf16[384,256]{1,0:T(8,128)(2,1)S(1)}, u32[]{:S(2)}, u32[]{:S(2)}) collective-permute-start(bf16[384,256]{1,0:T(8,128)(2,1)} %get-tuple-element.56), channel_id=1, source_target_pairs={{64,0},{80,16},{96,32},{112,48},{128,64},{144,80},{160,96},{176,11... | collective-permute-start | bytes 589832 | tf_op jit(solution)/shard_map/ppermute | solution.py:614
  134.9 20.9 %copy-start.22 = (bf16[384,256]{1,0:T(8,128)(2,1)}, bf16[384,256]{1,0:T(8,128)(2,1)S(1)}, u32[]{:S(2)}) copy-start(bf16[384,256]{1,0:T(8,128)(2,1)S(1)} %collective-permute-done.24.refs_0_) | copy-start | bytes 589828
  134.9 20.9 %collective-permute-start.28 = (bf16[384,256]{1,0:T(8,128)(2,1)}, bf16[384,256]{1,0:T(8,128)(2,1)}, u32[]{:S(2)}, u32[]{:S(2)}) collective-permute-start(bf16[384,256]{1,0:T(8,128)(2,1)} %get-tuple-element.57), channel_id=1, source_target_pairs={{32,0},{48,16},{64,32},{80,48},{96,64},{112,80},{128,96},{144,112}... | collective-permute-start | bytes 589832 | tf_op jit(solution)/shard_map/ppermute | solution.py:614
  139.0 16.8 %copy-start.23 = (bf16[384,256]{1,0:T(8,128)(2,1)}, bf16[384,256]{1,0:T(8,128)(2,1)S(1)}, u32[]{:S(2)}) copy-start(bf16[384,256]{1,0:T(8,128)(2,1)S(1)} %collective-permute-done.25.refs_1_) | copy-start | bytes 589828
  139.0 23.2 %collective-permute-start.30 = (bf16[256,384]{1,0:T(8,128)(2,1)}, bf16[256,384]{1,0:T(8,128)(2,1)}, u32[]{:S(2)}, u32[]{:S(2)}) collective-permute-start(bf16[256,384]{1,0:T(8,128)(2,1)} %get-tuple-element.58.refs_6_), channel_id=1, source_target_pairs={{0,1},{1,0},{2,3},{3,2},{4,5},{5,4},{6,7},{7,6},{8,9},{9,8},{10,11... | collective-permute-start | bytes 589832 | tf_op jit(solution)/shard_map/ppermute | solution.py:602
  142.0 13.8 %copy-start.24 = (bf16[384,256]{1,0:T(8,128)(2,1)}, bf16[384,256]{1,0:T(8,128)(2,1)S(1)}, u32[]{:S(2)}) copy-start(bf16[384,256]{1,0:T(8,128)(2,1)S(1)} %collective-permute-done.26.refs_2_) | copy-start | bytes 589828
  144.6 11.2 %copy-start.25 = (bf16[384,256]{1,0:T(8,128)(2,1)}, bf16[384,256]{1,0:T(8,128)(2,1)S(1)}, u32[]{:S(2)}) copy-start(bf16[384,256]{1,0:T(8,128)(2,1)S(1)} %collective-permute-done.27.refs_3_) | copy-start | bytes 589828
  158.0 13.0 %collective-permute-start.29 = (bf16[256,384]{1,0:T(8,128)(2,1)}, bf16[256,384]{1,0:T(8,128)(2,1)S(1)}, u32[]{:S(2)}, u32[]{:S(2)}) collective-permute-start(bf16[256,384]{1,0:T(8,128)(2,1)} %total_partials.1.refs_7_), channel_id=1, source_target_pairs={{0,1},{1,0},{2,3},{3,2},{4,5},{5,4},{6,7},{7,6},{8,9},{9,8},{10,11... | collective-permute-start | bytes 589832 | tf_op jit(solution)/shard_map/ppermute | solution.py:602
  174.9 8.6 %collective-permute-start.31 = (bf16[336,384]{1,0:T(8,128)(2,1)}, bf16[336,384]{1,0:T(8,128)(2,1)S(1)}, u32[]{:S(2)}, u32[]{:S(2)}) collective-permute-start(bf16[336,384]{1,0:T(8,128)(2,1)} %get-tuple-element.61), channel_id=1, source_target_pairs={{0,2},{2,4},{4,6},{6,8},{8,10},{10,12},{12,14},{14,0},{1,3},{3,5},... | collective-permute-start | bytes 774152 | tf_op jit(solution)/shard_map/ppermute | solution.py:618
  175.0 9.8 %collective-permute-start.35 = (bf16[336,384]{1,0:T(8,128)(2,1)}, bf16[336,384]{1,0:T(8,128)(2,1)S(1)}, u32[]{:S(2)}, u32[]{:S(2)}) collective-permute-start(bf16[336,384]{1,0:T(8,128)(2,1)} %get-tuple-element.71), channel_id=1, source_target_pairs={{0,14},{2,0},{4,2},{6,4},{8,6},{10,8},{12,10},{14,12},{1,15},{3,1}... | collective-permute-start | bytes 774152 | tf_op jit(solution)/shard_map/ppermute | solution.py:618
  183.5 1.4 copy-start.13
  183.5 8.9 %copy-start.12 = (f32[336,384]{1,0:T(8,128)S(1)}, f32[336,384]{1,0:T(8,128)}, u32[]{:S(2)}) copy-start(f32[336,384]{1,0:T(8,128)} %get-tuple-element.69) | copy-start | bytes 1548292
  183.5 9.0 %copy-start.11 = (f32[336,384]{1,0:T(8,128)S(1)}, f32[336,384]{1,0:T(8,128)}, u32[]{:S(2)}) copy-start(f32[336,384]{1,0:T(8,128)} %get-tuple-element.73) | copy-start | bytes 1548292
  184.7 7.6 %collective-permute-start.32 = (bf16[336,384]{1,0:T(8,128)(2,1)S(1)}, bf16[336,384]{1,0:T(8,128)(2,1)S(1)}, u32[]{:S(2)}, u32[]{:S(2)}) collective-permute-start(bf16[336,384]{1,0:T(8,128)(2,1)S(1)} %add_convert_fusion.5), channel_id=1, source_target_pairs={{0,2},{2,4},{4,6},{6,8},{8,10},{10,12},{12,14},{14,0},{1,3},{3,5},... | collective-permute-start | bytes 774152 | tf_op jit(solution)/shard_map/ppermute | solution.py:618
  184.8 15.4 %copy-start.10 = (f32[336,384]{1,0:T(8,128)S(1)}, f32[336,384]{1,0:T(8,128)}, u32[]{:S(2)}) copy-start(f32[336,384]{1,0:T(8,128)} %get-tuple-element.70) | copy-start | bytes 1548292
  184.9 7.6 %collective-permute-start.36 = (bf16[336,384]{1,0:T(8,128)(2,1)S(1)}, bf16[336,384]{1,0:T(8,128)(2,1)S(1)}, u32[]{:S(2)}, u32[]{:S(2)}) collective-permute-start(bf16[336,384]{1,0:T(8,128)(2,1)S(1)} %add_convert_fusion.2), channel_id=1, source_target_pairs={{0,14},{2,0},{4,2},{6,4},{8,6},{10,8},{12,10},{14,12},{1,15},{3,1}... | collective-permute-start | bytes 774152 | tf_op jit(solution)/shard_map/ppermute | solution.py:618
  192.3 15.6 %copy-start.9 = (f32[336,384]{1,0:T(8,128)S(1)}, f32[336,384]{1,0:T(8,128)}, u32[]{:S(2)}) copy-start(f32[336,384]{1,0:T(8,128)} %get-tuple-element.74) | copy-start | bytes 1548292
  192.4 7.8 %collective-permute-start.33 = (bf16[336,384]{1,0:T(8,128)(2,1)S(1)}, bf16[336,384]{1,0:T(8,128)(2,1)S(1)}, u32[]{:S(2)}, u32[]{:S(2)}) collective-permute-start(bf16[336,384]{1,0:T(8,128)(2,1)S(1)} %add_convert_fusion.4), channel_id=1, source_target_pairs={{0,2},{2,4},{4,6},{6,8},{8,10},{10,12},{12,14},{14,0},{1,3},{3,5},... | collective-permute-start | bytes 774152 | tf_op jit(solution)/shard_map/ppermute | solution.py:618
  192.6 7.8 %collective-permute-start.37 = (bf16[336,384]{1,0:T(8,128)(2,1)S(1)}, bf16[336,384]{1,0:T(8,128)(2,1)S(1)}, u32[]{:S(2)}, u32[]{:S(2)}) collective-permute-start(bf16[336,384]{1,0:T(8,128)(2,1)S(1)} %add_convert_fusion.1), channel_id=1, source_target_pairs={{0,14},{2,0},{4,2},{6,4},{8,6},{10,8},{12,10},{14,12},{1,15},{3,1}... | collective-permute-start | bytes 774152 | tf_op jit(solution)/shard_map/ppermute | solution.py:618
  200.3 7.6 %collective-permute-start.34 = (bf16[336,384]{1,0:T(8,128)(2,1)S(1)}, bf16[336,384]{1,0:T(8,128)(2,1)S(1)}, u32[]{:S(2)}, u32[]{:S(2)}) collective-permute-start(bf16[336,384]{1,0:T(8,128)(2,1)S(1)} %add_convert_fusion.3), channel_id=1, source_target_pairs={{0,2},{2,4},{4,6},{6,8},{8,10},{10,12},{12,14},{14,0},{1,3},{3,5},... | collective-permute-start | bytes 774152 | tf_op jit(solution)/shard_map/ppermute | solution.py:618
  (5 other events, 4.0 us)

commit v2 on v1

--- a/solution.py
+++ b/solution.py
@@ -19,6 +19,7 @@
 SEG_ROWS = 16
 PACKED = ROWS + SEG_ROWS
 FEATS = 336
+UP_ROWS = 176
 CHUNK = 384
 WINDOW = 512
 BOTH = 2 * ROWS
@@ -419,19 +420,41 @@
     )(at, w_out, *far_w, *shards.values())
 
 
-def join_kernel(core_ref, mine_ref, got_ref, own_ref, *send_refs):
+def join_kernel(core_ref, mine_ref, got_ref, own_ref, *refs):
+    send_refs = refs[:HALF]
+    mine, got, own, made, in_sem, out_sem = refs[HALF:]
     core = core_ref[0]
-    for d in range(HALF + 1):
+    arrivals = []
+    for d in reversed(range(HALF)):
+        pair = [
+            pltpu.make_async_copy(x.at[d], y.at[d], in_sem.at[i, d])
+            for i, (x, y) in enumerate(((got_ref, got), (mine_ref, mine)))
+        ]
+        for c in pair:
+            c.start()
+        arrivals.append(pair)
+    arrivals.reverse()
+    departures = []
+    for d in reversed(range(HALF + 1)):
+        if d > 0:
+            for c in arrivals[d - 1]:
+                c.wait()
         at = d - core
         inside = (at >= 0) & (at < HALF)
-        other = got_ref[jnp.clip(at, 0, HALF - 1)].astype(F32)
-        total = jnp.where(inside, other, 0.0)
+        total = jnp.where(inside, got[jnp.clip(at, 0, HALF - 1)].astype(F32), 0.0)
         if d < HALF:
-            total = total + mine_ref[d].astype(F32)
+            total = total + mine[d].astype(F32)
         if d == 0:
-            own_ref[...] = total
+            own[...] = total
+            departures.append(pltpu.make_async_copy(own, own_ref, out_sem.at[d]))
         else:
-            send_refs[d - 1][...] = total.astype(BF16)
+            made[d - 1] = total.astype(BF16)
+            departures.append(
+                pltpu.make_async_copy(made.at[d - 1], send_refs[d - 1], out_sem.at[d])
+            )
+        departures[-1].start()
+    for c in departures:
+        c.wait()
 
 
 def join_partials(core, mine, got):
@@ -440,38 +463,63 @@
         join_kernel,
         name="join_partials",
         out_shape=(jax.ShapeDtypeStruct(shape, F32),) + (jax.ShapeDtypeStruct(shape, BF16),) * HALF,
-        in_specs=[SMEM, VMEM, VMEM],
-        out_specs=(VMEM,) * (HALF + 1),
+        in_specs=[SMEM, ANY, ANY],
+        out_specs=(ANY,) * (HALF + 1),
+        scratch_shapes=[
+            pltpu.VMEM((HALF, *shape), BF16),
+            pltpu.VMEM((HALF, *shape), BF16),
+            pltpu.VMEM(shape, F32),
+            pltpu.VMEM((HALF, *shape), BF16),
+            pltpu.SemaphoreType.DMA((2, HALF)),
+            pltpu.SemaphoreType.DMA((HALF + 1,)),
+        ],
     )(core, mine, got)
     return result[0], result[1:]
 
 
 def total_kernel(own_ref, *refs):
-    total = own_ref[...]
-    for ref in refs[:HALF]:
-        total = total + ref[...].astype(F32)
-    refs[HALF][...] = total.astype(BF16).T
+    part_refs, (out_ref, own, parts, sem) = refs[:HALF], refs[HALF:]
+    copies = [pltpu.make_async_copy(own_ref, own, sem.at[HALF])]
+    copies += [pltpu.make_async_copy(x, parts.at[i], sem.at[i]) for i, x in enumerate(part_refs)]
+    for c in copies:
+        c.start()
+    for c in copies:
+        c.wait()
+    total = own[...]
+    for i in range(HALF):
+        total = total + parts[i].astype(F32)
+    out_ref[...] = total.astype(BF16).T
 
 
 def total_partials(own, parts):
+    shape = (ROWS, 2 * HD)
     return pl.pallas_call(
         total_kernel,
         name="total_partials",
         out_shape=jax.ShapeDtypeStruct((2 * HD, ROWS), BF16),
-        in_specs=[VMEM] * (HALF + 1),
+        in_specs=[ANY] * (HALF + 1),
         out_specs=VMEM,
+        scratch_shapes=[
+            pltpu.VMEM(shape, F32),
+            pltpu.VMEM((HALF, *shape), BF16),
+            pltpu.SemaphoreType.DMA((HALF + 1,)),
+        ],
     )(own, *parts)
 
 
-def own_project_kernel(deltas, at_ref, *refs):
-    n = len(deltas)
-    wq, wk, wv, pa, pb, gq, gkv, gq2 = refs[:8]
-    outs = refs[8 : 8 + n]
-    wbuf, gbuf, obuf, sem, g_sem, out_sem = refs[8 + n :]
+def project_kernel(deltas, own_lanes, far_lane, more, at_ref, *refs):
+    n, k = len(deltas), len(own_lanes)
+    weights = refs[:k]
+    pa, pb, g_own, g_far = refs[k : k + 4]
+    refs = refs[k + 4 :]
+    sums, refs = (refs[:n], refs[n:]) if more else ((), refs)
+    outs, refs = refs[:n], refs[n:]
+    wbuf, gbuf, obuf, sem, g_sem, out_sem, *held = refs
     z, xh, core = at_ref[0], at_ref[1], at_ref[2]
+    width = 2 * HD
     g_copies = [
-        pltpu.make_async_copy(g, gbuf.at[2 * HD * i : 2 * HD * (i + 1)], g_sem.at[i])
-        for i, g in enumerate((gq, gkv, gq2))
+        pltpu.make_async_copy(g, gbuf.at[width * i : width * (i + 1)], g_sem.at[i])
+        for i, g in enumerate((g_own, g_far))
     ]
     for c in g_copies:
         c.start()
@@ -479,17 +527,18 @@
     for i, delta in enumerate(deltas):
         chunk = lax.rem(z + delta + RING, RING)
         rows = pl.ds(pl.multiple_of((2 * chunk + xh) * FEATS, 16), FEATS)
-        place = ((wq, 0, 2 * HD), (wk, 2 * HD, HD), (wv, 3 * HD, HD))
         mine = [
             pltpu.make_async_copy(w.at[rows, :], wbuf.at[i, :, lane : lane + size], sem.at[i, j])
-            for j, (w, lane, size) in enumerate(place)
+            for j, (w, (lane, size)) in enumerate(zip(weights, own_lanes))
         ]
+        if more:
+            mine.append(pltpu.make_async_copy(sums[i], held[0].at[i], sem.at[i, k + 1]))
         for c in mine:
             c.start()
         inner = lax.rem(chunk, RING // 2)
         near, far = [
             pltpu.make_async_copy(
-                p.at[inner, :, : 2 * HD], wbuf.at[i, :, 4 * HD :], sem.at[i, 3]
+                p.at[inner, :, far_lane : far_lane + width], wbuf.at[i, :, width:], sem.at[i, k]
             )
             for p in (pa, pb)
         ]
@@ -510,92 +559,39 @@
     for i in range(n):
         for c in copies[i]:
             c.wait()
-        obuf[i] = dot(wbuf[i], gbuf[...])
+        total = dot(wbuf[i], gbuf[...])
+        if more:
+            total = total + held[0][i]
+        obuf[i] = total.astype(obuf.dtype)
         results.append(pltpu.make_async_copy(obuf.at[i], outs[i], out_sem.at[i]))
         results[-1].start()
     for c in results:
         c.wait()
 
 
-def own_project(deltas, at, weights, far, grads):
-    n = len(deltas)
+def project(deltas, at, weights, own_lanes, far, far_lane, g_own, g_far, sums, kind):
+    n, k = len(deltas), len(weights)
+    more = len(sums) > 0
     return pl.pallas_call(
-        lambda *refs: own_project_kernel(deltas, *refs),
-        name="own_project",
-        out_shape=(jax.ShapeDtypeStruct((FEATS, ROWS), F32),) * n,
-        in_specs=[SMEM] + [ANY] * 8,
+        lambda *refs: project_kernel(deltas, own_lanes, far_lane, more, *refs),
+        name="project",
+        out_shape=(jax.ShapeDtypeStruct((FEATS, ROWS), kind),) * n,
+        in_specs=[SMEM] + [ANY] * (k + 4 + len(sums)),
         out_specs=(ANY,) * n,
         scratch_shapes=[
-            pltpu.VMEM((n, FEATS, 6 * HD), BF16),
-            pltpu.VMEM((6 * HD, ROWS), BF16),
-            pltpu.VMEM((n, FEATS, ROWS), F32),
-            pltpu.SemaphoreType.DMA((n, 4)),
-            pltpu.SemaphoreType.DMA((3,)),
+            pltpu.VMEM((n, FEATS, 4 * HD), BF16),
+            pltpu.VMEM((4 * HD, ROWS), BF16),
+            pltpu.VMEM((n, FEATS, ROWS), kind),
+            pltpu.SemaphoreType.DMA((n, k + 2)),
+            pltpu.SemaphoreType.DMA((2,)),
             pltpu.SemaphoreType.DMA((n,)),
-        ],
-    )(at, *weights, *far, *grads)
-
-
-def far_project_kernel(deltas, at_ref, *refs):
-    n = len(deltas)
-    pa, pb, gkv2 = refs[:3]
-    sums = refs[3 : 3 + n]
-    outs = refs[3 + n : 3 + 2 * n]
-    wbuf, gbuf, abuf, obuf, sem, g_sem, out_sem = refs[3 + 2 * n :]
-    z, core = at_ref[0], at_ref[2]
-    g_copy = pltpu.make_async_copy(gkv2, gbuf, g_sem.at[0])
-    g_copy.start()
-    copies = []
-    for i, delta in enumerate(deltas):
-        chunk = lax.rem(z + delta + RING, RING)
-        inner = lax.rem(chunk, RING // 2)
-        near, far = [
-            pltpu.make_async_copy(p.at[inner, :, 2 * HD :], wbuf.at[i], sem.at[i, 0])
-            for p in (pa, pb)
         ]
-        same = lax.div(chunk, RING // 2) == core
-
-        @pl.when(same)
-        def _(copy=near):
-            copy.start()
-
-        @pl.when(jnp.logical_not(same))
-        def _(copy=far):
-            copy.start()
-
-        before = pltpu.make_async_copy(sums[i], abuf.at[i], sem.at[i, 1])
-        before.start()
-        copies.append((near, before))
-    g_copy.wait()
-    results = []
-    for i in range(n):
-        for c in copies[i]:
-            c.wait()
-        obuf[i] = (abuf[i] + dot(wbuf[i], gbuf[...])).astype(obuf.dtype)
-        results.append(pltpu.make_async_copy(obuf.at[i], outs[i], out_sem.at[i]))
-        results[-1].start()
-    for c in results:
-        c.wait()
-
-
-def far_project(deltas, at, far, gkvt_far, sums, kind):
-    n = len(deltas)
-    return pl.pallas_call(
-        lambda *refs: far_project_kernel(deltas, *refs),
-        name="far_project",
-        out_shape=(jax.ShapeDtypeStruct((FEATS, ROWS), kind),) * n,
-        in_specs=[SMEM] + [ANY] * (3 + n),
-        out_specs=(ANY,) * n,
-        scratch_shapes=[
-            pltpu.VMEM((n, FEATS, 2 * HD), BF16),
-            pltpu.VMEM((2 * HD, ROWS), BF16),
-            pltpu.VMEM((n, FEATS, ROWS), F32),
-            pltpu.VMEM((n, FEATS, ROWS), kind),
-            pltpu.SemaphoreType.DMA((n, 2)),
-            pltpu.SemaphoreType.DMA((1,)),
-            pltpu.SemaphoreType.DMA((n,)),
-        ],
-    )(at, *far, gkvt_far, *sums)
+        + [pltpu.VMEM((n, FEATS, ROWS), F32)] * more,
+    )(at, *weights, *far, g_own, g_far, *sums)
+
+
+def arrive(x):
+    return pltpu.with_memory_space_constraint(x, pltpu.VMEM)
 
 
 def swapped(x, axis):
@@ -611,7 +607,7 @@
 
 
 def chips_back(x, d):
-    return lax.ppermute(x, AA, [(j, i) for i, j in chip_pairs(d)])
+    return arrive(lax.ppermute(x, AA, [(j, i) for i, j in chip_pairs(d)]))
 
 
 def round_z(x, step):
@@ -653,30 +649,35 @@
     qseg = segment_ids[None, :]
     state = attention_stats(own, qseg, query, twins, others, NEAR, BLOCKS)
     near, send = dout_parts(at, w_out, far_w, shards)
-    far = swapped(send, "xh")
+    far = arrive(swapped(send, "xh"))
     stats = attention_stats(own, qseg, query, twins, others, 0, NEAR, state)
     gqt, mine, theirs = attention_grads(own, stats, query, near, far, twins, others)
     got = swapped(theirs, "core")
-    gqt_far = swapped(gqt, "xh")
+    gqt_far = arrive(swapped(gqt, "xh"))
     own_total, sends = join_partials(core[None], mine, got)
     parts = [chips_back(sends[d - 1], d) for d in range(HALF, 0, -1)]
     gkvt = total_partials(own_total, parts)
-    gkvt_far = swapped(gkvt, "xh")
-
-    weights = (w_query, w_key, w_value)
+    gkvt_far = arrive(swapped(gkvt, "xh"))
+
+    deltas = (4, 3, -3, 2, -2, 1, -1, 0)
     far_rows = (far_mine, far_other)
-    deltas = (4, -3, 3, -2, 2, -1, 1, 0)
-    sums = own_project(deltas, at, weights, far_rows, (gqt, gkvt, gqt_far))
-    ahead, behind = far_project(deltas[:2], at, far_rows, gkvt_far, sums[:2], BF16)
-    rest = far_project(deltas[2:], at, far_rows, gkvt_far, sums[2:], F32)
-    ahead = round_z(ahead, 1)
-    behind = round_z(behind, -1)
-    for k in (2, 3):
-        add_ahead, add_behind = rest[2 * k - 4], rest[2 * k - 3]
-        ahead = round_z((ahead.astype(F32) + add_ahead).astype(BF16), 1)
-        behind = round_z((behind.astype(F32) + add_behind).astype(BF16), -1)
-    ahead = round_z((ahead.astype(F32) + rest[4]).astype(BF16), 1)
-    result = (ahead.astype(F32) + behind.astype(F32) + rest[5]).astype(BF16)
+    q_lanes = ((0, 2 * HD),)
+    sums = project(deltas, at, (w_query,), q_lanes, far_rows, 0, gqt, gqt_far, (), F32)
+    kv = (w_key, w_value)
+    kv_lanes = ((0, HD), (HD, HD))
+    args = (at, kv, kv_lanes, far_rows, 2 * HD, gkvt, gkvt_far)
+    (across,) = project(deltas[:1], *args, sums[:1], BF16)
+    rest = project(deltas[1:], *args, sums[1:], F32)
+    ahead = round_z(across[:UP_ROWS], 1).astype(F32)
+    behind = round_z(across[UP_ROWS:], -1).astype(F32)
+    ahead = rest[0] + jnp.pad(ahead, ((0, FEATS - UP_ROWS), (0, 0)))
+    behind = rest[1] + jnp.pad(behind, ((UP_ROWS, 0), (0, 0)))
+    for k in (2, 3, 4):
+        ahead = round_z(ahead.astype(BF16), 1).astype(F32)
+        behind = round_z(behind.astype(BF16), -1).astype(F32)
+        if k < 4:
+            ahead, behind = ahead + rest[2 * k - 2], behind + rest[2 * k - 1]
+    result = (ahead + behind + rest[6]).astype(BF16)
     return result.T
 
 

time: 210 us -> 208 us (level)
  waiting for transfers between devices: 80 us -> 83.2 us
  starting transfers between devices: 62.7 us -> 60.2 us
    ppermute x5, waiting for transfers between devices: 15.9 us -> 9.54 us  [chips_back(): return arrive(lax.ppermute(x, AA, [(j, i) for i, j in chip_pairs(d)]))]
    ppermute x5, waiting for transfers between devices: 36.4 us -> 42 us  [chips_on(): return lax.ppermute(x, AA, chip_pairs(d))]
    ppermute x14 -> x15, waiting for transfers between devices: 25.2 us -> 29.2 us  [round_z(): return lax.ppermute(x, 'z', [(i, (i + step) % RING) for i in range(RING)])]
    unnamed x62 -> x46, local copies, waits for them, and re-layouts: 4.02 us -> 0.76 us
    ppermute x14 -> x15, starting transfers between devices: 27.2 us -> 26.8 us  [round_z(): return lax.ppermute(x, 'z', [(i, (i + step) % RING) for i in range(RING)])]
  transfers between devices with their start and end apart: 38 -> 39, of which waited for: 13 -> 17; matrix products, arithmetic and copies ran while one was open for 2% -> 3% of each run, Pallas kernels for 23% -> 23%
where the time goes in v2:
time: 208 us; the launch traced here: 207 us
  waiting for transfers between devices  83.2 us (40%)
  starting transfers between devices  60.2 us (29%)
  Pallas kernels  53.8 us (26%)
  local copies, waits for them, and re-layouts  5.5 us (3%)
  other arithmetic  4.14 us (2%)
    ppermute x5, waiting for transfers between devices, chips_on(): return lax.ppermute(x, AA, chip_pairs(d))  42 us
    ppermute x15, waiting for transfers between devices, round_z(): return lax.ppermute(x, 'z', [(i, (i + step) % RING) for i in range(RING)])  29.2 us
    ppermute x15, starting transfers between devices, round_z(): return lax.ppermute(x, 'z', [(i, (i + step) % RING) for i in range(RING)])  26.8 us
    pallas_call x3, Pallas kernels, project(): pl.pallas_call(lambda *refs: project_kernel(deltas, own_lanes, far_lane,...  14.7 us
    ppermute x14, starting transfers between devices, swapped(): return lax.ppermute(x, axis, [(0, 1), (1, 0)])  13.2 us
    ppermute x5, starting transfers between devices, chips_on(): return lax.ppermute(x, AA, chip_pairs(d))  12.5 us
    pallas_call x1, Pallas kernels, attention_grads(): pl.pallas_call(grads_kernel, name='attention_grads', out_shape=(jax.Shape...  12.4 us
    pallas_call x2, Pallas kernels, attention_stats(): pl.pallas_call(lambda *refs: stats_kernel(low, high, *refs), name='stats_...  12.1 us
  transfers between devices with their start and end apart: 39, of which 17 were waited for; matrix products, arithmetic and copies ran while one was open for 3% of the time, Pallas kernels for 23%

profile of v2, /device:TPU:24, one launch (start us, length us, event | category | flops | bytes accessed | tf_op | source)
XLA Modules:
  0.0 207.4 jit_solution(1568623027123097457)
XLA Ops:
  0.0 0.7 pad_add_fusion.at_ref.refs_0_
  0.7 3.4 %split_w_out.1 = bf16[4,256,384]{2,1,0:T(8,128)(2,1)} custom-call(s32[3]{0:T(128)} %pad_add_fusion.at_ref.refs_0_, bf16[256,5376]{1,0:T(8,128)(2,1)} %refs_1_.5), custom_call_target="tpu_custom_call" | custom-call | tf_op jit(solution)/shard_map/split_w_out/pallas_call | solution.py:349
  4.1 3.1 %collective-permute-start.13 = (bf16[4,256,384]{2,1,0:T(8,128)(2,1)}, bf16[4,256,384]{2,1,0:T(8,128)(2,1)}, u32[]{:S(2)}, u32[]{:S(2)}) collective-permute-start(bf16[4,256,384]{2,1,0:T(8,128)(2,1)} %split_w_out.1), channel_id=1, source_target_pairs={{0,1},{1,0},{2,3},{3,2},{4,5},{5,4},{6,7},{7,6},{8,9},{9,8},{10,11... | collective-permute-start | bytes 2359304 | tf_op jit(solution)/shard_map/ppermute | solution.py:598
  7.3 3.2 %collective-permute-start.5 = (bf16[400,256]{1,0:T(8,128)(2,1)S(1)}, bf16[400,256]{1,0:T(8,128)(2,1)S(1)}, u32[]{:S(2)}, u32[]{:S(2)}) collective-permute-start(bf16[400,256]{1,0:T(8,128)(2,1)S(1)} %fusion.2.refs_3_.refs_6_), channel_id=1, source_target_pairs={{0,64},{16,80},{32,96},{48,112},{64,128},{80,144},{96,160},{112,17... | collective-permute-start | bytes 614408 | tf_op jit(solution)/shard_map/ppermute | solution.py:606
  10.5 4.1 %collective-permute-start.2 = (bf16[400,256]{1,0:T(8,128)(2,1)S(1)}, bf16[400,256]{1,0:T(8,128)(2,1)S(1)}, u32[]{:S(2)}, u32[]{:S(2)}) collective-permute-start(bf16[400,256]{1,0:T(8,128)(2,1)S(1)} %fusion.2.refs_3_.refs_6_), channel_id=1, source_target_pairs={{0,32},{16,48},{32,64},{48,80},{64,96},{80,112},{96,128},{112,144}... | collective-permute-start | bytes 614408 | tf_op jit(solution)/shard_map/ppermute | solution.py:606
  14.7 2.0 collective-permute-start.8
  16.6 1.2 dynamic-slice_bitcast_fusion
  17.8 1.1 dynamic-slice_bitcast_fusion.1
  19.0 10.8 %collective-permute-done.5.refs_7_.refs_8_ = bf16[400,256]{1,0:T(8,128)(2,1)S(1)} collective-permute-done((bf16[400,256]{1,0:T(8,128)(2,1)S(1)}, bf16[400,256]{1,0:T(8,128)(2,1)S(1)}, u32[]{:S(2)}, u32[]{:S(2)}) %collective-permute-start.5) | collective-permute-done | bytes 204832 | tf_op jit(solution)/shard_map/ppermute | solution.py:606
  29.8 1.9 collective-permute-start.15
  31.7 0.1 pad_maximum_fusion
  31.8 2.5 %collective-permute-done.2.refs_4_.refs_7_ = bf16[400,256]{1,0:T(8,128)(2,1)S(1)} collective-permute-done((bf16[400,256]{1,0:T(8,128)(2,1)S(1)}, bf16[400,256]{1,0:T(8,128)(2,1)S(1)}, u32[]{:S(2)}, u32[]{:S(2)}) %collective-permute-start.2) | collective-permute-done | bytes 204832 | tf_op jit(solution)/shard_map/ppermute | solution.py:606
  34.3 0.5 collective-permute-start
  34.8 1.9 collective-permute-start.7
  36.8 1.8 collective-permute-done.8.refs_9_.refs_10_
  38.7 5.9 %collective-permute-start.16 = (bf16[336,384]{1,0:T(8,128)(2,1)S(1)}, bf16[336,384]{1,0:T(8,128)(2,1)S(1)}, u32[]{:S(2)}, u32[]{:S(2)}) collective-permute-start(bf16[336,384]{1,0:T(8,128)(2,1)S(1)} %bitcast.29), channel_id=1, source_target_pairs={{0,14},{2,0},{4,2},{6,4},{8,6},{10,8},{12,10},{14,12},{1,15},{3,1}... | collective-permute-start | bytes 774152 | tf_op jit(solution)/shard_map/ppermute | solution.py:614
  44.5 26.9 %collective-permute-done.7.refs_8_.refs_9_ = bf16[400,256]{1,0:T(8,128)(2,1)} collective-permute-done((bf16[400,256]{1,0:T(8,128)(2,1)S(1)}, bf16[400,256]{1,0:T(8,128)(2,1)}, u32[]{:S(2)}, u32[]{:S(2)}) %collective-permute-start.7) | collective-permute-done | bytes 204832 | tf_op jit(solution)/shard_map/ppermute | solution.py:606
  71.4 1.3 collective-permute-start.11
  72.8 5.9 %collective-permute-start.18 = (bf16[336,384]{1,0:T(8,128)(2,1)S(1)}, bf16[336,384]{1,0:T(8,128)(2,1)S(1)}, u32[]{:S(2)}, u32[]{:S(2)}) collective-permute-start(bf16[336,384]{1,0:T(8,128)(2,1)S(1)} %collective-permute-done.16.refs_6_), channel_id=1, source_target_pairs={{0,14},{2,0},{4,2},{6,4},{8,6},{10,8},{12,10},{14,12},{1,15},{3,1}... | collective-permute-start | bytes 774152 | tf_op jit(solution)/shard_map/ppermute | solution.py:614
  78.7 4.5 %collective-permute-done.18.refs_8_ = bf16[336,384]{1,0:T(8,128)(2,1)S(1)} collective-permute-done((bf16[336,384]{1,0:T(8,128)(2,1)S(1)}, bf16[336,384]{1,0:T(8,128)(2,1)S(1)}, u32[]{:S(2)}, u32[]{:S(2)}) %collective-permute-start.18) | collective-permute-done | bytes 258080 | tf_op jit(solution)/shard_map/ppermute | solution.py:614
  83.2 3.7 %collective-permute-start.20 = (bf16[336,384]{1,0:T(8,128)(2,1)S(1)}, bf16[336,384]{1,0:T(8,128)(2,1)S(1)}, u32[]{:S(2)}, u32[]{:S(2)}) collective-permute-start(bf16[336,384]{1,0:T(8,128)(2,1)S(1)} %collective-permute-done.18.refs_8_), channel_id=1, source_target_pairs={{0,14},{2,0},{4,2},{6,4},{8,6},{10,8},{12,10},{14,12},{1,15},{3,1}... | collective-permute-start | bytes 774152 | tf_op jit(solution)/shard_map/ppermute | solution.py:614
  87.1 3.7 %collective-permute-done.20.refs_10_ = bf16[336,384]{1,0:T(8,128)(2,1)S(1)} collective-permute-done((bf16[336,384]{1,0:T(8,128)(2,1)S(1)}, bf16[336,384]{1,0:T(8,128)(2,1)S(1)}, u32[]{:S(2)}, u32[]{:S(2)}) %collective-permute-start.20) | collective-permute-done | bytes 258080 | tf_op jit(solution)/shard_map/ppermute | solution.py:614
  90.8 3.7 %collective-permute-done.21.refs_11_ = bf16[336,384]{1,0:T(8,128)(2,1)S(1)} collective-permute-done((bf16[336,384]{1,0:T(8,128)(2,1)S(1)}, bf16[336,384]{1,0:T(8,128)(2,1)S(1)}, u32[]{:S(2)}, u32[]{:S(2)}) %collective-permute-start.21) | collective-permute-done | bytes 258080 | tf_op jit(solution)/shard_map/ppermute | solution.py:614
  94.5 0.7 copy-done.18
  95.3 6.4 %dout_parts.1 = (f32[256,384]{1,0:T(8,128)}, bf16[256,384]{1,0:T(8,128)(2,1)}) custom-call(s32[3]{0:T(128)} %pad_add_fusion.at_ref.refs_0_, bf16[256,5376]{1,0:T(8,128)(2,1)} %refs_1_.5, bf16[4,256,384]{2,1,0:T(8,128)(2,1)} %collective-permute-done.13.refs_2_, bf16[4,256,384]{2,1,0:T(8,128)(2,1)} %collective-permute-done.14.refs_3_, ...), custom_call_target="tpu_custom_call" | custom-call | tf_op jit(solution)/shard_map/dout_parts/pallas_call | solution.py:407
  101.8 0.6 collective-permute-start.22
  102.4 0.6 broadcast_in_dim.8.refs_1_
  102.9 6.3 %stats_near.1 = (f32[1,768]{1,0:T(1,128)}, f32[1,768]{1,0:T(1,128)}, f32[128,768]{1,0:T(8,128)}, s32[1,384]{1,0:T(1,128)}) custom-call(s32[1]{0:T(128)} %bitcast.9.refs_0_.own_ref, s32[1,384]{1,0:T(1,128)} %broadcast_in_dim.8.refs_1_, bf16[384,256]{1,0:T(8,128)(2,1)} %refs_1_.6, bf16[400,256]{1,0:T(8,128)(2,1)} %copy-done.2, bf16[400,256]{1,0:T(8,128)(2,1)} %copy-done.4, ...), custom_call_target="tpu_custom_call" | custom-call | tf_op jit(solution)/shard_map/stats_near/pallas_call | solution.py:285
  109.3 5.8 %stats_far.1 = (f32[1,768]{1,0:T(1,128)}, f32[128,768]{1,0:T(8,128)}, s32[1,384]{1,0:T(1,128)}, s32[1]{0:T(128)}) custom-call(s32[1]{0:T(128)} %bitcast.9.refs_0_.own_ref, s32[1,384]{1,0:T(1,128)} %broadcast_in_dim.8.refs_1_, bf16[384,256]{1,0:T(8,128)(2,1)} %refs_1_.6, f32[1,768]{1,0:T(1,128)} %get-tuple-element.39.refs_3_, ...), custom_call_target="tpu_custom_call" | custom-call | tf_op jit(solution)/shard_map/stats_far/pallas_call | solution.py:285
  115.1 12.4 %attention_grads.1 = (bf16[256,384]{1,0:T(8,128)(2,1)}, bf16[5,384,256]{2,1,0:T(8,128)(2,1)}, bf16[5,384,256]{2,1,0:T(8,128)(2,1)}) custom-call(s32[1]{0:T(128)} %bitcast.9.refs_0_.own_ref, s32[1]{0:T(128)} %get-tuple-element.43.low_ref, s32[1,384]{1,0:T(1,128)} %get-tuple-element.44.refs_0_, bf16[384,256]{1,0:T(8,128)(2,1)} %refs_1_.6, ...), custom_call_target="tpu_custom_call" | custom-call | tf_op jit(solution)/shard_map/attention_grads/pallas_call | solution.py:299
  127.5 2.1 collective-permute-start.23
  129.7 2.4 %collective-permute-done.23.got_ref = bf16[5,384,256]{2,1,0:T(8,128)(2,1)} collective-permute-done((bf16[5,384,256]{2,1,0:T(8,128)(2,1)}, bf16[5,384,256]{2,1,0:T(8,128)(2,1)}, u32[]{:S(2)}, u32[]{:S(2)}) %collective-permute-start.23) | collective-permute-done | bytes 983072 | tf_op jit(solution)/shard_map/ppermute | solution.py:598
  132.1 2.6 %join_partials.1 = (f32[384,256]{1,0:T(8,128)}, bf16[384,256]{1,0:T(8,128)(2,1)}, bf16[384,256]{1,0:T(8,128)(2,1)}, bf16[384,256]{1,0:T(8,128)(2,1)}, bf16[384,2...) custom-call(s32[1]{0:T(128)} %bitcast.2.core_ref, bf16[5,384,256]{2,1,0:T(8,128)(2,1)} %get-tuple-element.49.mine_ref, ...), custom_call_target="tpu_custom_call" | custom-call | tf_op jit(solution)/shard_map/join_partials/pallas_call | solution.py:462
  134.7 0.7 collective-permute-start.24
  135.4 1.3 collective-permute-start.25
  136.7 1.9 collective-permute-start.26
  138.6 1.9 collective-permute-start.27
  140.5 1.9 collective-permute-start.28
  142.5 2.2 %collective-permute-done.25.refs_1_ = bf16[384,256]{1,0:T(8,128)(2,1)S(1)} collective-permute-done((bf16[384,256]{1,0:T(8,128)(2,1)}, bf16[384,256]{1,0:T(8,128)(2,1)S(1)}, u32[]{:S(2)}, u32[]{:S(2)}) %collective-permute-start.25) | collective-permute-done | bytes 196640 | tf_op jit(solution)/shard_map/ppermute | solution.py:610
  144.7 3.0 %collective-permute-start.30 = (bf16[256,384]{1,0:T(8,128)(2,1)S(1)}, bf16[256,384]{1,0:T(8,128)(2,1)S(1)}, u32[]{:S(2)}, u32[]{:S(2)}) collective-permute-start(bf16[256,384]{1,0:T(8,128)(2,1)S(1)} %copy-done.19), channel_id=1, source_target_pairs={{0,1},{1,0},{2,3},{3,2},{4,5},{5,4},{6,7},{7,6},{8,9},{9,8},{10,11... | collective-permute-start | bytes 589832 | tf_op jit(solution)/shard_map/ppermute | solution.py:598
  147.7 4.8 %collective-permute-done.27.refs_3_ = bf16[384,256]{1,0:T(8,128)(2,1)S(1)} collective-permute-done((bf16[384,256]{1,0:T(8,128)(2,1)}, bf16[384,256]{1,0:T(8,128)(2,1)S(1)}, u32[]{:S(2)}, u32[]{:S(2)}) %collective-permute-start.27) | collective-permute-done | bytes 196640 | tf_op jit(solution)/shard_map/ppermute | solution.py:610
  152.5 2.5 %collective-permute-done.28.refs_4_ = bf16[384,256]{1,0:T(8,128)(2,1)S(1)} collective-permute-done((bf16[384,256]{1,0:T(8,128)(2,1)}, bf16[384,256]{1,0:T(8,128)(2,1)S(1)}, u32[]{:S(2)}, u32[]{:S(2)}) %collective-permute-start.28) | collective-permute-done | bytes 196640 | tf_op jit(solution)/shard_map/ppermute | solution.py:610
  155.0 2.2 %total_partials.1.refs_5_ = bf16[256,384]{1,0:T(8,128)(2,1)} custom-call(f32[384,256]{1,0:T(8,128)} %get-tuple-element.51.own_ref, bf16[384,256]{1,0:T(8,128)(2,1)S(1)} %collective-permute-done.24.refs_0_, bf16[384,256]{1,0:T(8,128)(2,1)S(1)} %collective-permute-done.25.refs_1_, bf16[384,256]{1,0:T(8,128)(2,1)S(1)} %collective-permute-done.26.refs_2_, ...), custom_call_target="tpu_custom_call" | custom-call | tf_op jit(solution)/shard_map/total_partials/pallas_call | solution.py:496
  157.2 3.3 %collective-permute-start.29 = (bf16[256,384]{1,0:T(8,128)(2,1)}, bf16[256,384]{1,0:T(8,128)(2,1)S(1)}, u32[]{:S(2)}, u32[]{:S(2)}) collective-permute-start(bf16[256,384]{1,0:T(8,128)(2,1)} %total_partials.1.refs_5_), channel_id=1, source_target_pairs={{0,1},{1,0},{2,3},{3,2},{4,5},{5,4},{6,7},{7,6},{8,9},{9,8},{10,11... | collective-permute-start | bytes 589832 | tf_op jit(solution)/shard_map/ppermute | solution.py:598
  160.6 5.8 %project.3 = (f32[336,384]{1,0:T(8,128)}, f32[336,384]{1,0:T(8,128)}, f32[336,384]{1,0:T(8,128)}, f32[336,384]{1,0:T(8,128)}, f32[336,384]{1,0:T(8,128)}, /*inde...) custom-call(s32[3]{0:T(128)} %pad_add_fusion.at_ref.refs_0_, bf16[5376,256]{1,0:T(8,128)(2,1)} %refs_1_.7, ...), custom_call_target="tpu_custom_call" | custom-call | tf_op jit(solution)/shard_map/project/pallas_call | solution.py:575
  166.4 3.2 %project.5 = bf16[336,384]{1,0:T(8,128)(2,1)} custom-call(s32[3]{0:T(128)} %pad_add_fusion.at_ref.refs_0_, bf16[5376,128]{1,0:T(8,128)(2,1)} %refs_1_.9, bf16[5376,128]{1,0:T(8,128)(2,1)} %refs_2_.7, bf16[4,336,512]{2,1,0:T(8,128)(2,1)} %copy-done, bf16[4,336,512]{2,1,0:T(8,128)(2,1)} %collective-permute-done.1.refs_3_.refs_4_, ...), custom_call_target="tpu_custom_call" | custom-call | tf_op jit(solution)/shard_map/project/pallas_call | solution.py:575
  169.6 0.9 slice.9
  170.5 0.3 collective-permute-start.35
  170.8 0.9 slice.8
  171.7 1.9 collective-permute-start.31
  173.6 5.7 %project.4 = (f32[336,384]{1,0:T(8,128)}, f32[336,384]{1,0:T(8,128)}, f32[336,384]{1,0:T(8,128)}, f32[336,384]{1,0:T(8,128)}, f32[336,384]{1,0:T(8,128)}, /*index=5*/f32[336,384]{1,0:T(8,128)}, f32[336,384]{1,0:T(8,128)}) custom-call(s32[3]{0:T(128)} %pad_add_fusion.at_ref.refs_0_, bf16[5376,128]{1,0:T(8,128)(2,1)} %refs_1_.9, bf16[5376,128]{1,0:T(8,128)(2,1)} %refs_2_.7, ...), custom_call_target="tpu_custom_call" | custom-call | tf_op jit(solution)/shard_map/project/pallas_call | solution.py:575
  179.4 1.2 add_convert_fusion.3
  180.5 1.5 collective-permute-start.36
  182.0 1.1 add_convert_fusion.6
  183.1 0.7 collective-permute-start.32
  183.9 3.4 %collective-permute-done.36 = bf16[336,384]{1,0:T(8,128)(2,1)S(1)} collective-permute-done((bf16[336,384]{1,0:T(8,128)(2,1)S(1)}, bf16[336,384]{1,0:T(8,128)(2,1)S(1)}, u32[]{:S(2)}, u32[]{:S(2)}) %collective-permute-start.36) | collective-permute-done | bytes 258080 | tf_op jit(solution)/shard_map/ppermute | solution.py:614
  187.3 2.4 %collective-permute-start.37 = (bf16[336,384]{1,0:T(8,128)(2,1)S(1)}, bf16[336,384]{1,0:T(8,128)(2,1)S(1)}, u32[]{:S(2)}, u32[]{:S(2)}) collective-permute-start(bf16[336,384]{1,0:T(8,128)(2,1)S(1)} %add_convert_fusion.2), channel_id=1, source_target_pairs={{0,14},{2,0},{4,2},{6,4},{8,6},{10,8},{12,10},{14,12},{1,15},{3,1}... | collective-permute-start | bytes 774152 | tf_op jit(solution)/shard_map/ppermute | solution.py:614
  189.7 1.1 collective-permute-done.32
  190.9 4.0 %collective-permute-done.37 = bf16[336,384]{1,0:T(8,128)(2,1)S(1)} collective-permute-done((bf16[336,384]{1,0:T(8,128)(2,1)S(1)}, bf16[336,384]{1,0:T(8,128)(2,1)S(1)}, u32[]{:S(2)}, u32[]{:S(2)}) %collective-permute-start.37) | collective-permute-done | bytes 258080 | tf_op jit(solution)/shard_map/ppermute | solution.py:614
  195.0 2.5 %collective-permute-start.38 = (bf16[336,384]{1,0:T(8,128)(2,1)S(1)}, bf16[336,384]{1,0:T(8,128)(2,1)S(1)}, u32[]{:S(2)}, u32[]{:S(2)}) collective-permute-start(bf16[336,384]{1,0:T(8,128)(2,1)S(1)} %add_convert_fusion.1), channel_id=1, source_target_pairs={{0,14},{2,0},{4,2},{6,4},{8,6},{10,8},{12,10},{14,12},{1,15},{3,1}... | collective-permute-start | bytes 774152 | tf_op jit(solution)/shard_map/ppermute | solution.py:614
  197.5 1.4 collective-permute-done.33
  199.0 2.3 %collective-permute-done.38 = bf16[336,384]{1,0:T(8,128)(2,1)S(1)} collective-permute-done((bf16[336,384]{1,0:T(8,128)(2,1)S(1)}, bf16[336,384]{1,0:T(8,128)(2,1)S(1)}, u32[]{:S(2)}, u32[]{:S(2)}) %collective-permute-start.38) | collective-permute-done | bytes 258080 | tf_op jit(solution)/shard_map/ppermute | solution.py:614
  201.4 5.2 %collective-permute-done.34 = bf16[336,384]{1,0:T(8,128)(2,1)S(1)} collective-permute-done((bf16[336,384]{1,0:T(8,128)(2,1)S(1)}, bf16[336,384]{1,0:T(8,128)(2,1)S(1)}, u32[]{:S(2)}, u32[]{:S(2)}) %collective-permute-start.34) | collective-permute-done | bytes 258080 | tf_op jit(solution)/shard_map/ppermute | solution.py:614
  206.6 0.8 fusion.1
  (86 shorter events, 1.2 us)
Async XLA Ops:
  0.7 6.6 %copy-start.22 = (s32[384]{0:T(512)S(1)}, s32[384]{0:T(512)}, u32[]{:S(2)}) copy-start(s32[384]{0:T(512)} %param.13) | copy-start | bytes 4612
  0.7 6.6 %copy-start.20 = (bf16[384,128]{1,0:T(8,128)(2,1)S(1)}, bf16[384,128]{1,0:T(8,128)(2,1)}, u32[]{:S(2)}) copy-start(bf16[384,128]{1,0:T(8,128)(2,1)} %param.11) | copy-start | bytes 294916
  0.7 6.6 %copy-start.21 = (bf16[384,128]{1,0:T(8,128)(2,1)S(1)}, bf16[384,128]{1,0:T(8,128)(2,1)}, u32[]{:S(2)}) copy-start(bf16[384,128]{1,0:T(8,128)(2,1)} %param.10) | copy-start | bytes 294916
  4.1 32.6 %collective-permute-start.13 = (bf16[4,256,384]{2,1,0:T(8,128)(2,1)}, bf16[4,256,384]{2,1,0:T(8,128)(2,1)}, u32[]{:S(2)}, u32[]{:S(2)}) collective-permute-start(bf16[4,256,384]{2,1,0:T(8,128)(2,1)} %split_w_out.1), channel_id=1, source_target_pairs={{0,1},{1,0},{2,3},{3,2},{4,5},{5,4},{6,7},{7,6},{8,9},{9,8},{10,11... | collective-permute-start | bytes 2359304 | tf_op jit(solution)/shard_map/ppermute | solution.py:598
  7.3 64.1 %copy-start.2 = (bf16[400,256]{1,0:T(8,128)(2,1)}, bf16[400,256]{1,0:T(8,128)(2,1)S(1)}, u32[]{:S(2)}) copy-start(bf16[400,256]{1,0:T(8,128)(2,1)S(1)} %fusion.2.refs_3_.refs_6_) | copy-start | bytes 614404
  7.3 22.5 %collective-permute-start.5 = (bf16[400,256]{1,0:T(8,128)(2,1)S(1)}, bf16[400,256]{1,0:T(8,128)(2,1)S(1)}, u32[]{:S(2)}, u32[]{:S(2)}) collective-permute-start(bf16[400,256]{1,0:T(8,128)(2,1)S(1)} %fusion.2.refs_3_.refs_6_), channel_id=1, source_target_pairs={{0,64},{16,80},{32,96},{48,112},{64,128},{80,144},{96,160},{112,17... | collective-permute-start | bytes 614408 | tf_op jit(solution)/shard_map/ppermute | solution.py:606
  10.5 23.8 %collective-permute-start.2 = (bf16[400,256]{1,0:T(8,128)(2,1)S(1)}, bf16[400,256]{1,0:T(8,128)(2,1)S(1)}, u32[]{:S(2)}, u32[]{:S(2)}) collective-permute-start(bf16[400,256]{1,0:T(8,128)(2,1)S(1)} %fusion.2.refs_3_.refs_6_), channel_id=1, source_target_pairs={{0,32},{16,48},{32,64},{48,80},{64,96},{80,112},{96,128},{112,144}... | collective-permute-start | bytes 614408 | tf_op jit(solution)/shard_map/ppermute | solution.py:606
  14.6 20.2 %collective-permute-start.3 = (bf16[400,256]{1,0:T(8,128)(2,1)S(1)}, bf16[400,256]{1,0:T(8,128)(2,1)}, u32[]{:S(2)}, u32[]{:S(2)}) collective-permute-start(bf16[400,256]{1,0:T(8,128)(2,1)S(1)} %fusion.2.refs_3_.refs_6_), channel_id=1, source_target_pairs={{0,16},{16,0},{1,17},{17,1},{2,18},{18,2},{3,19},{19,3},{4,20},{20... | collective-permute-start | bytes 614408 | tf_op jit(solution)/shard_map/ppermute | solution.py:598
  14.7 24.0 %collective-permute-start.8 = (bf16[400,256]{1,0:T(8,128)(2,1)S(1)}, bf16[400,256]{1,0:T(8,128)(2,1)}, u32[]{:S(2)}, u32[]{:S(2)}) collective-permute-start(bf16[400,256]{1,0:T(8,128)(2,1)S(1)} %fusion.2.refs_3_.refs_6_), channel_id=1, source_target_pairs={{0,128},{16,144},{32,160},{48,176},{64,192},{80,208},{96,224},{112... | collective-permute-start | bytes 614408 | tf_op jit(solution)/shard_map/ppermute | solution.py:606
  16.6 13.1 %copy-start.11 = (bf16[384,336]{0,1:T(8,128)(2,1)S(1)}, bf16[384,336]{0,1:T(8,128)(2,1)}, u32[]{:S(2)}) copy-start(bf16[384,336]{0,1:T(8,128)(2,1)} %param.12) | copy-start | bytes 774148
  29.8 48.9 %copy-start.3 = (bf16[400,256]{1,0:T(8,128)(2,1)}, bf16[400,256]{1,0:T(8,128)(2,1)S(1)}, u32[]{:S(2)}) copy-start(bf16[400,256]{1,0:T(8,128)(2,1)S(1)} %collective-permute-done.5.refs_7_.refs_8_) | copy-start | bytes 614404
  29.8 14.8 %collective-permute-start.15 = (bf16[336,384]{1,0:T(8,128)(2,1)S(1)}, bf16[336,384]{1,0:T(8,128)(2,1)S(1)}, u32[]{:S(2)}, u32[]{:S(2)}) collective-permute-start(bf16[336,384]{1,0:T(8,128)(2,1)S(1)} %bitcast.28), channel_id=1, source_target_pairs={{0,2},{2,4},{4,6},{6,8},{8,10},{10,12},{12,14},{14,0},{1,3},{3,5},... | collective-permute-start | bytes 774152 | tf_op jit(solution)/shard_map/ppermute | solution.py:614
  34.3 67.5 %copy-start.4 = (bf16[400,256]{1,0:T(8,128)(2,1)}, bf16[400,256]{1,0:T(8,128)(2,1)S(1)}, u32[]{:S(2)}) copy-start(bf16[400,256]{1,0:T(8,128)(2,1)S(1)} %collective-permute-done.2.refs_4_.refs_7_) | copy-start | bytes 614404
  34.3 95.3 %collective-permute-start = (bf16[4,336,512]{2,1,0:T(8,128)(2,1)S(1)}, bf16[4,336,512]{2,1,0:T(8,128)(2,1)S(1)}, u32[]{:S(2)}, u32[]{:S(2)}) collective-permute-start(bf16[4,336,512]{2,1,0:T(8,128)(2,1)S(1)} %pad_maximum_fusion), channel_id=1, source_target_pairs={{0,1},{1,0},{2,3},{3,2},{4,5},{5,4},{6,7},{7,6},{8,9},{9,8},{10,11... | collective-permute-start | bytes 4128776 | tf_op jit(solution)/shard_map/ppermute | solution.py:598
  34.8 36.6 %collective-permute-start.7 = (bf16[400,256]{1,0:T(8,128)(2,1)S(1)}, bf16[400,256]{1,0:T(8,128)(2,1)}, u32[]{:S(2)}, u32[]{:S(2)}) collective-permute-start(bf16[400,256]{1,0:T(8,128)(2,1)S(1)} %fusion.2.refs_3_.refs_6_), channel_id=1, source_target_pairs={{0,96},{16,112},{32,128},{48,144},{64,160},{80,176},{96,192},{112,... | collective-permute-start | bytes 614408 | tf_op jit(solution)/shard_map/ppermute | solution.py:606
  36.7 57.8 %collective-permute-start.14 = (bf16[4,256,384]{2,1,0:T(8,128)(2,1)}, bf16[4,256,384]{2,1,0:T(8,128)(2,1)}, u32[]{:S(2)}, u32[]{:S(2)}) collective-permute-start(bf16[4,256,384]{2,1,0:T(8,128)(2,1)} %collective-permute-done.13.refs_2_), channel_id=1, source_target_pairs={{0,16},{16,0},{1,17},{17,1},{2,18},{18,2},{3,19},{19,3},{4,20},{20... | collective-permute-start | bytes 2359304 | tf_op jit(solution)/shard_map/ppermute | solution.py:598
  38.7 34.1 %collective-permute-start.16 = (bf16[336,384]{1,0:T(8,128)(2,1)S(1)}, bf16[336,384]{1,0:T(8,128)(2,1)S(1)}, u32[]{:S(2)}, u32[]{:S(2)}) collective-permute-start(bf16[336,384]{1,0:T(8,128)(2,1)S(1)} %bitcast.29), channel_id=1, source_target_pairs={{0,14},{2,0},{4,2},{6,4},{8,6},{10,8},{12,10},{14,12},{1,15},{3,1}... | collective-permute-start | bytes 774152 | tf_op jit(solution)/shard_map/ppermute | solution.py:614
  44.5 42.4 %copy-start.12 = (bf16[336,384]{1,0:T(8,128)(2,1)}, bf16[336,384]{1,0:T(8,128)(2,1)S(1)}, u32[]{:S(2)}) copy-start(bf16[336,384]{1,0:T(8,128)(2,1)S(1)} %collective-permute-done.15.refs_5_) | copy-start | bytes 774148
  44.5 34.1 %collective-permute-start.17 = (bf16[336,384]{1,0:T(8,128)(2,1)S(1)}, bf16[336,384]{1,0:T(8,128)(2,1)S(1)}, u32[]{:S(2)}, u32[]{:S(2)}) collective-permute-start(bf16[336,384]{1,0:T(8,128)(2,1)S(1)} %collective-permute-done.15.refs_5_), channel_id=1, source_target_pairs={{0,2},{2,4},{4,6},{6,8},{8,10},{10,12},{12,14},{14,0},{1,3},{3,5},... | collective-permute-start | bytes 774152 | tf_op jit(solution)/shard_map/ppermute | solution.py:614
  71.4 7.2 %collective-permute-start.11 = (bf16[400,256]{1,0:T(8,128)(2,1)S(1)}, bf16[400,256]{1,0:T(8,128)(2,1)}, u32[]{:S(2)}, u32[]{:S(2)}) collective-permute-start(bf16[400,256]{1,0:T(8,128)(2,1)S(1)} %fusion.2.refs_3_.refs_6_), channel_id=1, source_target_pairs={{16,176},{48,208},{80,240},{17,177},{49,209},{81,241},{18,178},{50... | collective-permute-start | bytes 614408 | tf_op jit(solution)/shard_map/ppermute | solution.py:606
  72.8 14.3 %copy-start.13 = (bf16[336,384]{1,0:T(8,128)(2,1)}, bf16[336,384]{1,0:T(8,128)(2,1)S(1)}, u32[]{:S(2)}) copy-start(bf16[336,384]{1,0:T(8,128)(2,1)S(1)} %collective-permute-done.16.refs_6_) | copy-start | bytes 774148
  72.8 10.5 %collective-permute-start.18 = (bf16[336,384]{1,0:T(8,128)(2,1)S(1)}, bf16[336,384]{1,0:T(8,128)(2,1)S(1)}, u32[]{:S(2)}, u32[]{:S(2)}) collective-permute-start(bf16[336,384]{1,0:T(8,128)(2,1)S(1)} %collective-permute-done.16.refs_6_), channel_id=1, source_target_pairs={{0,14},{2,0},{4,2},{6,4},{8,6},{10,8},{12,10},{14,12},{1,15},{3,1}... | collective-permute-start | bytes 774152 | tf_op jit(solution)/shard_map/ppermute | solution.py:614
  78.6 12.2 %copy-start.14 = (bf16[336,384]{1,0:T(8,128)(2,1)}, bf16[336,384]{1,0:T(8,128)(2,1)S(1)}, u32[]{:S(2)}) copy-start(bf16[336,384]{1,0:T(8,128)(2,1)S(1)} %collective-permute-done.17.refs_7_) | copy-start | bytes 774148
  78.6 8.3 %collective-permute-start.19 = (bf16[336,384]{1,0:T(8,128)(2,1)S(1)}, bf16[336,384]{1,0:T(8,128)(2,1)S(1)}, u32[]{:S(2)}, u32[]{:S(2)}) collective-permute-start(bf16[336,384]{1,0:T(8,128)(2,1)S(1)} %collective-permute-done.17.refs_7_), channel_id=1, source_target_pairs={{0,2},{2,4},{4,6},{6,8},{8,10},{10,12},{12,14},{14,0},{1,3},{3,5},... | collective-permute-start | bytes 774152 | tf_op jit(solution)/shard_map/ppermute | solution.py:614
  78.6 8.3 %collective-permute-start.6 = (bf16[400,256]{1,0:T(8,128)(2,1)S(1)}, bf16[400,256]{1,0:T(8,128)(2,1)S(1)}, u32[]{:S(2)}, u32[]{:S(2)}) collective-permute-start(bf16[400,256]{1,0:T(8,128)(2,1)S(1)} %collective-permute-done.5.refs_7_.refs_8_), channel_id=1, source_target_pairs={{0,16},{16,0},{1,17},{17,1},{2,18},{18,2},{3,19},{19,3},{4,20},{20... | collective-permute-start | bytes 614408 | tf_op jit(solution)/shard_map/ppermute | solution.py:598
  83.2 7.6 %copy-start.15 = (bf16[336,384]{1,0:T(8,128)(2,1)}, bf16[336,384]{1,0:T(8,128)(2,1)S(1)}, u32[]{:S(2)}) copy-start(bf16[336,384]{1,0:T(8,128)(2,1)S(1)} %collective-permute-done.18.refs_8_) | copy-start | bytes 774148
  83.2 7.5 %collective-permute-start.20 = (bf16[336,384]{1,0:T(8,128)(2,1)S(1)}, bf16[336,384]{1,0:T(8,128)(2,1)S(1)}, u32[]{:S(2)}, u32[]{:S(2)}) collective-permute-start(bf16[336,384]{1,0:T(8,128)(2,1)S(1)} %collective-permute-done.18.refs_8_), channel_id=1, source_target_pairs={{0,14},{2,0},{4,2},{6,4},{8,6},{10,8},{12,10},{14,12},{1,15},{3,1}... | collective-permute-start | bytes 774152 | tf_op jit(solution)/shard_map/ppermute | solution.py:614
  86.9 7.5 %copy-start.16 = (bf16[336,384]{1,0:T(8,128)(2,1)}, bf16[336,384]{1,0:T(8,128)(2,1)S(1)}, u32[]{:S(2)}) copy-start(bf16[336,384]{1,0:T(8,128)(2,1)S(1)} %collective-permute-done.19.refs_9_) | copy-start | bytes 774148
  86.9 7.5 %collective-permute-start.21 = (bf16[336,384]{1,0:T(8,128)(2,1)S(1)}, bf16[336,384]{1,0:T(8,128)(2,1)S(1)}, u32[]{:S(2)}, u32[]{:S(2)}) collective-permute-start(bf16[336,384]{1,0:T(8,128)(2,1)S(1)} %collective-permute-done.19.refs_9_), channel_id=1, source_target_pairs={{0,2},{2,4},{4,6},{6,8},{8,10},{10,12},{12,14},{14,0},{1,3},{3,5},... | collective-permute-start | bytes 774152 | tf_op jit(solution)/shard_map/ppermute | solution.py:614
  87.0 14.8 %copy-start.1 = (bf16[400,256]{1,0:T(8,128)(2,1)}, bf16[400,256]{1,0:T(8,128)(2,1)S(1)}, u32[]{:S(2)}) copy-start(bf16[400,256]{1,0:T(8,128)(2,1)S(1)} %collective-permute-done.6.refs_7_.refs_10_.refs_13_) | copy-start | bytes 614404
  87.0 14.8 %collective-permute-start.4 = (bf16[400,256]{1,0:T(8,128)(2,1)S(1)}, bf16[400,256]{1,0:T(8,128)(2,1)S(1)}, u32[]{:S(2)}, u32[]{:S(2)}) collective-permute-start(bf16[400,256]{1,0:T(8,128)(2,1)S(1)} %collective-permute-done.2.refs_4_.refs_7_), channel_id=1, source_target_pairs={{0,16},{16,0},{1,17},{17,1},{2,18},{18,2},{3,19},{19,3},{4,20},{20... | collective-permute-start | bytes 614408 | tf_op jit(solution)/shard_map/ppermute | solution.py:598
  90.8 3.7 %copy-start.17 = (bf16[336,384]{1,0:T(8,128)(2,1)}, bf16[336,384]{1,0:T(8,128)(2,1)S(1)}, u32[]{:S(2)}) copy-start(bf16[336,384]{1,0:T(8,128)(2,1)S(1)} %collective-permute-done.20.refs_10_) | copy-start | bytes 774148
  90.8 18.5 %collective-permute-start.10 = (bf16[400,256]{1,0:T(8,128)(2,1)}, bf16[400,256]{1,0:T(8,128)(2,1)}, u32[]{:S(2)}, u32[]{:S(2)}) collective-permute-start(bf16[400,256]{1,0:T(8,128)(2,1)} %collective-permute-done.8.refs_9_.refs_10_), channel_id=1, source_target_pairs={{0,16},{16,0},{1,17},{17,1},{2,18},{18,2},{3,19},{19,3},{4,20},{20... | collective-permute-start | bytes 614408 | tf_op jit(solution)/shard_map/ppermute | solution.py:598
  94.5 0.7 copy-start.18
  94.5 14.8 %collective-permute-start.9 = (bf16[400,256]{1,0:T(8,128)(2,1)}, bf16[400,256]{1,0:T(8,128)(2,1)}, u32[]{:S(2)}, u32[]{:S(2)}) collective-permute-start(bf16[400,256]{1,0:T(8,128)(2,1)} %collective-permute-done.7.refs_8_.refs_9_), channel_id=1, source_target_pairs={{0,16},{16,0},{1,17},{17,1},{2,18},{18,2},{3,19},{19,3},{4,20},{20... | collective-permute-start | bytes 614408 | tf_op jit(solution)/shard_map/ppermute | solution.py:598
  95.2 14.1 %collective-permute-start.12 = (bf16[400,256]{1,0:T(8,128)(2,1)}, bf16[400,256]{1,0:T(8,128)(2,1)}, u32[]{:S(2)}, u32[]{:S(2)}) collective-permute-start(bf16[400,256]{1,0:T(8,128)(2,1)} %collective-permute-done.11), channel_id=1, source_target_pairs={{0,16},{16,0},{1,17},{17,1},{2,18},{18,2},{3,19},{19,3},{4,20},{20... | collective-permute-start | bytes 614408 | tf_op jit(solution)/shard_map/ppermute | solution.py:598
  101.7 1.2 copy-start.5
  101.8 13.3 %collective-permute-start.22 = (bf16[256,384]{1,0:T(8,128)(2,1)}, bf16[256,384]{1,0:T(8,128)(2,1)S(1)}, u32[]{:S(2)}, u32[]{:S(2)}) collective-permute-start(bf16[256,384]{1,0:T(8,128)(2,1)} %get-tuple-element.46), channel_id=1, source_target_pairs={{0,1},{1,0},{2,3},{3,2},{4,5},{5,4},{6,7},{7,6},{8,9},{9,8},{10,11... | collective-permute-start | bytes 589832 | tf_op jit(solution)/shard_map/ppermute | solution.py:598
  127.5 17.2 %copy-start.19 = (bf16[256,384]{1,0:T(8,128)(2,1)S(1)}, bf16[256,384]{1,0:T(8,128)(2,1)}, u32[]{:S(2)}) copy-start(bf16[256,384]{1,0:T(8,128)(2,1)} %get-tuple-element.57.refs_4_) | copy-start | bytes 589828
  127.5 4.6 %collective-permute-start.23 = (bf16[5,384,256]{2,1,0:T(8,128)(2,1)}, bf16[5,384,256]{2,1,0:T(8,128)(2,1)}, u32[]{:S(2)}, u32[]{:S(2)}) collective-permute-start(bf16[5,384,256]{2,1,0:T(8,128)(2,1)} %get-tuple-element.50), channel_id=1, source_target_pairs={{0,16},{16,0},{1,17},{17,1},{2,18},{18,2},{3,19},{19,3},{4,20},{20... | collective-permute-start | bytes 2949128 | tf_op jit(solution)/shard_map/ppermute | solution.py:598
  129.6 27.7 %copy-start = (bf16[4,336,512]{2,1,0:T(8,128)(2,1)}, bf16[4,336,512]{2,1,0:T(8,128)(2,1)S(1)}, u32[]{:S(2)}) copy-start(bf16[4,336,512]{2,1,0:T(8,128)(2,1)S(1)} %collective-permute-done.refs_2_.refs_3_) | copy-start | bytes 4128772
  129.6 31.0 %collective-permute-start.1 = (bf16[4,336,512]{2,1,0:T(8,128)(2,1)S(1)}, bf16[4,336,512]{2,1,0:T(8,128)(2,1)}, u32[]{:S(2)}, u32[]{:S(2)}) collective-permute-start(bf16[4,336,512]{2,1,0:T(8,128)(2,1)S(1)} %collective-permute-done.refs_2_.refs_3_), channel_id=1, source_target_pairs={{0,16},{16,0},{1,17},{17,1},{2,18},{18,2},{3,19},{19,3},{4,20},{20... | collective-permute-start | bytes 4128776 | tf_op jit(solution)/shard_map/ppermute | solution.py:598
  134.7 5.8 %collective-permute-start.24 = (bf16[384,256]{1,0:T(8,128)(2,1)}, bf16[384,256]{1,0:T(8,128)(2,1)S(1)}, u32[]{:S(2)}, u32[]{:S(2)}) collective-permute-start(bf16[384,256]{1,0:T(8,128)(2,1)} %get-tuple-element.52), channel_id=1, source_target_pairs={{176,16},{208,48},{240,80},{177,17},{209,49},{241,81},{178,18},{21... | collective-permute-start | bytes 589832 | tf_op jit(solution)/shard_map/ppermute | solution.py:610
  135.4 9.3 %collective-permute-start.25 = (bf16[384,256]{1,0:T(8,128)(2,1)}, bf16[384,256]{1,0:T(8,128)(2,1)S(1)}, u32[]{:S(2)}, u32[]{:S(2)}) collective-permute-start(bf16[384,256]{1,0:T(8,128)(2,1)} %get-tuple-element.53), channel_id=1, source_target_pairs={{128,0},{144,16},{160,32},{176,48},{192,64},{208,80},{224,96},{240... | collective-permute-start | bytes 589832 | tf_op jit(solution)/shard_map/ppermute | solution.py:610
  136.7 11.0 %collective-permute-start.26 = (bf16[384,256]{1,0:T(8,128)(2,1)}, bf16[384,256]{1,0:T(8,128)(2,1)S(1)}, u32[]{:S(2)}, u32[]{:S(2)}) collective-permute-start(bf16[384,256]{1,0:T(8,128)(2,1)} %get-tuple-element.54), channel_id=1, source_target_pairs={{96,0},{112,16},{128,32},{144,48},{160,64},{176,80},{192,96},{208,... | collective-permute-start | bytes 589832 | tf_op jit(solution)/shard_map/ppermute | solution.py:610
  138.6 13.9 %collective-permute-start.27 = (bf16[384,256]{1,0:T(8,128)(2,1)}, bf16[384,256]{1,0:T(8,128)(2,1)S(1)}, u32[]{:S(2)}, u32[]{:S(2)}) collective-permute-start(bf16[384,256]{1,0:T(8,128)(2,1)} %get-tuple-element.55), channel_id=1, source_target_pairs={{64,0},{80,16},{96,32},{112,48},{128,64},{144,80},{160,96},{176,11... | collective-permute-start | bytes 589832 | tf_op jit(solution)/shard_map/ppermute | solution.py:610
  140.5 14.5 %collective-permute-start.28 = (bf16[384,256]{1,0:T(8,128)(2,1)}, bf16[384,256]{1,0:T(8,128)(2,1)S(1)}, u32[]{:S(2)}, u32[]{:S(2)}) collective-permute-start(bf16[384,256]{1,0:T(8,128)(2,1)} %get-tuple-element.56), channel_id=1, source_target_pairs={{32,0},{48,16},{64,32},{80,48},{96,64},{112,80},{128,96},{144,112}... | collective-permute-start | bytes 589832 | tf_op jit(solution)/shard_map/ppermute | solution.py:610
  144.7 15.9 %collective-permute-start.30 = (bf16[256,384]{1,0:T(8,128)(2,1)S(1)}, bf16[256,384]{1,0:T(8,128)(2,1)S(1)}, u32[]{:S(2)}, u32[]{:S(2)}) collective-permute-start(bf16[256,384]{1,0:T(8,128)(2,1)S(1)} %copy-done.19), channel_id=1, source_target_pairs={{0,1},{1,0},{2,3},{3,2},{4,5},{5,4},{6,7},{7,6},{8,9},{9,8},{10,11... | collective-permute-start | bytes 589832 | tf_op jit(solution)/shard_map/ppermute | solution.py:598
  157.2 9.2 %collective-permute-start.29 = (bf16[256,384]{1,0:T(8,128)(2,1)}, bf16[256,384]{1,0:T(8,128)(2,1)S(1)}, u32[]{:S(2)}, u32[]{:S(2)}) collective-permute-start(bf16[256,384]{1,0:T(8,128)(2,1)} %total_partials.1.refs_5_), channel_id=1, source_target_pairs={{0,1},{1,0},{2,3},{3,2},{4,5},{5,4},{6,7},{7,6},{8,9},{9,8},{10,11... | collective-permute-start | bytes 589832 | tf_op jit(solution)/shard_map/ppermute | solution.py:598
  170.5 8.8 %collective-permute-start.35 = (bf16[160,384]{1,0:T(8,128)(2,1)S(1)}, bf16[160,384]{1,0:T(8,128)(2,1)S(1)}, u32[]{:S(2)}, u32[]{:S(2)}) collective-permute-start(bf16[160,384]{1,0:T(8,128)(2,1)S(1)} %slice.9), channel_id=1, source_target_pairs={{0,14},{2,0},{4,2},{6,4},{8,6},{10,8},{12,10},{14,12},{1,15},{3,1}... | collective-permute-start | bytes 368648 | tf_op jit(solution)/shard_map/ppermute | solution.py:614
  171.7 10.3 %collective-permute-start.31 = (bf16[176,384]{1,0:T(8,128)(2,1)S(1)}, bf16[176,384]{1,0:T(8,128)(2,1)S(1)}, u32[]{:S(2)}, u32[]{:S(2)}) collective-permute-start(bf16[176,384]{1,0:T(8,128)(2,1)S(1)} %slice.8), channel_id=1, source_target_pairs={{0,2},{2,4},{4,6},{6,8},{8,10},{10,12},{12,14},{14,0},{1,3},{3,5},... | collective-permute-start | bytes 405512 | tf_op jit(solution)/shard_map/ppermute | solution.py:614
  179.3 7.9 %copy-start.10 = (f32[336,384]{1,0:T(8,128)S(1)}, f32[336,384]{1,0:T(8,128)}, u32[]{:S(2)}) copy-start(f32[336,384]{1,0:T(8,128)} %get-tuple-element.70) | copy-start | bytes 1548292
  179.4 11.4 %copy-start.9 = (f32[336,384]{1,0:T(8,128)S(1)}, f32[336,384]{1,0:T(8,128)}, u32[]{:S(2)}) copy-start(f32[336,384]{1,0:T(8,128)} %get-tuple-element.67) | copy-start | bytes 1548292
  180.5 6.7 %collective-permute-start.36 = (bf16[336,384]{1,0:T(8,128)(2,1)S(1)}, bf16[336,384]{1,0:T(8,128)(2,1)S(1)}, u32[]{:S(2)}, u32[]{:S(2)}) collective-permute-start(bf16[336,384]{1,0:T(8,128)(2,1)S(1)} %add_convert_fusion.3), channel_id=1, source_target_pairs={{0,14},{2,0},{4,2},{6,4},{8,6},{10,8},{12,10},{14,12},{1,15},{3,1}... | collective-permute-start | bytes 774152 | tf_op jit(solution)/shard_map/ppermute | solution.py:614
  182.0 12.9 %copy-start.8 = (f32[336,384]{1,0:T(8,128)S(1)}, f32[336,384]{1,0:T(8,128)}, u32[]{:S(2)}) copy-start(f32[336,384]{1,0:T(8,128)} %get-tuple-element.71) | copy-start | bytes 1548292
  183.1 7.6 %collective-permute-start.32 = (bf16[336,384]{1,0:T(8,128)(2,1)S(1)}, bf16[336,384]{1,0:T(8,128)(2,1)S(1)}, u32[]{:S(2)}, u32[]{:S(2)}) collective-permute-start(bf16[336,384]{1,0:T(8,128)(2,1)S(1)} %add_convert_fusion.6), channel_id=1, source_target_pairs={{0,2},{2,4},{4,6},{6,8},{8,10},{10,12},{12,14},{14,0},{1,3},{3,5},... | collective-permute-start | bytes 774152 | tf_op jit(solution)/shard_map/ppermute | solution.py:614
  187.3 11.6 %copy-start.7 = (f32[336,384]{1,0:T(8,128)S(1)}, f32[336,384]{1,0:T(8,128)}, u32[]{:S(2)}) copy-start(f32[336,384]{1,0:T(8,128)} %get-tuple-element.68) | copy-start | bytes 1548292
  187.3 7.6 %collective-permute-start.37 = (bf16[336,384]{1,0:T(8,128)(2,1)S(1)}, bf16[336,384]{1,0:T(8,128)(2,1)S(1)}, u32[]{:S(2)}, u32[]{:S(2)}) collective-permute-start(bf16[336,384]{1,0:T(8,128)(2,1)S(1)} %add_convert_fusion.2), channel_id=1, source_target_pairs={{0,14},{2,0},{4,2},{6,4},{8,6},{10,8},{12,10},{14,12},{1,15},{3,1}... | collective-permute-start | bytes 774152 | tf_op jit(solution)/shard_map/ppermute | solution.py:614
  190.8 15.8 %copy-start.6 = (f32[336,384]{1,0:T(8,128)S(1)}, f32[336,384]{1,0:T(8,128)}, u32[]{:S(2)}) copy-start(f32[336,384]{1,0:T(8,128)} %get-tuple-element.72) | copy-start | bytes 1548292
  190.8 8.0 %collective-permute-start.33 = (bf16[336,384]{1,0:T(8,128)(2,1)S(1)}, bf16[336,384]{1,0:T(8,128)(2,1)S(1)}, u32[]{:S(2)}, u32[]{:S(2)}) collective-permute-start(bf16[336,384]{1,0:T(8,128)(2,1)S(1)} %add_convert_fusion.5), channel_id=1, source_target_pairs={{0,2},{2,4},{4,6},{6,8},{8,10},{10,12},{12,14},{14,0},{1,3},{3,5},... | collective-permute-start | bytes 774152 | tf_op jit(solution)/shard_map/ppermute | solution.py:614
  195.0 6.4 %collective-permute-start.38 = (bf16[336,384]{1,0:T(8,128)(2,1)S(1)}, bf16[336,384]{1,0:T(8,128)(2,1)S(1)}, u32[]{:S(2)}, u32[]{:S(2)}) collective-permute-start(bf16[336,384]{1,0:T(8,128)(2,1)S(1)} %add_convert_fusion.1), channel_id=1, source_target_pairs={{0,14},{2,0},{4,2},{6,4},{8,6},{10,8},{12,10},{14,12},{1,15},{3,1}... | collective-permute-start | bytes 774152 | tf_op jit(solution)/shard_map/ppermute | solution.py:614
  198.9 7.6 %collective-permute-start.34 = (bf16[336,384]{1,0:T(8,128)(2,1)S(1)}, bf16[336,384]{1,0:T(8,128)(2,1)S(1)}, u32[]{:S(2)}, u32[]{:S(2)}) collective-permute-start(bf16[336,384]{1,0:T(8,128)(2,1)S(1)} %add_convert_fusion.4), channel_id=1, source_target_pairs={{0,2},{2,4},{4,6},{6,8},{8,10},{10,12},{12,14},{14,0},{1,3},{3,5},... | collective-permute-start | bytes 774152 | tf_op jit(solution)/shard_map/ppermute | solution.py:614

commit v3 on v2

--- a/solution.py
+++ b/solution.py
@@ -19,7 +19,6 @@
 SEG_ROWS = 16
 PACKED = ROWS + SEG_ROWS
 FEATS = 336
-UP_ROWS = 176
 CHUNK = 384
 WINDOW = 512
 BOTH = 2 * ROWS
@@ -507,11 +506,11 @@
     )(own, *parts)
 
 
-def project_kernel(deltas, own_lanes, far_lane, more, at_ref, *refs):
+def project_kernel(deltas, own_lanes, far, more, at_ref, *refs):
     n, k = len(deltas), len(own_lanes)
-    weights = refs[:k]
-    pa, pb, g_own, g_far = refs[k : k + 4]
-    refs = refs[k + 4 :]
+    weights, refs = refs[:k], refs[k:]
+    pa, pb, *grads = refs[: 2 + 1 + 2 * far]
+    refs = refs[3 + 2 * far :]
     sums, refs = (refs[:n], refs[n:]) if more else ((), refs)
     outs, refs = refs[:n], refs[n:]
     wbuf, gbuf, obuf, sem, g_sem, out_sem, *held = refs
@@ -519,7 +518,7 @@
     width = 2 * HD
     g_copies = [
         pltpu.make_async_copy(g, gbuf.at[width * i : width * (i + 1)], g_sem.at[i])
-        for i, g in enumerate((g_own, g_far))
+        for i, g in enumerate(grads)
     ]
     for c in g_copies:
         c.start()
@@ -535,24 +534,24 @@
             mine.append(pltpu.make_async_copy(sums[i], held[0].at[i], sem.at[i, k + 1]))
         for c in mine:
             c.start()
-        inner = lax.rem(chunk, RING // 2)
-        near, far = [
-            pltpu.make_async_copy(
-                p.at[inner, :, far_lane : far_lane + width], wbuf.at[i, :, width:], sem.at[i, k]
-            )
-            for p in (pa, pb)
-        ]
-        same = lax.div(chunk, RING // 2) == core
-
-        @pl.when(same)
-        def _(copy=near):
-            copy.start()
-
-        @pl.when(jnp.logical_not(same))
-        def _(copy=far):
-            copy.start()
-
-        copies.append(mine + [near])
+        if far:
+            inner = lax.rem(chunk, RING // 2)
+            near_rows, far_rows = [
+                pltpu.make_async_copy(p.at[inner], wbuf.at[i, :, width:], sem.at[i, k])
+                for p in (pa, pb)
+            ]
+            same = lax.div(chunk, RING // 2) == core
+
+            @pl.when(same)
+            def _(copy=near_rows):
+                copy.start()
+
+            @pl.when(jnp.logical_not(same))
+            def _(copy=far_rows):
+                copy.start()
+
+            mine.append(near_rows)
+        copies.append(mine)
     for c in g_copies:
         c.wait()
     results = []
@@ -569,25 +568,27 @@
         c.wait()
 
 
-def project(deltas, at, weights, own_lanes, far, far_lane, g_own, g_far, sums, kind):
+def project(deltas, at, weights, own_lanes, far_rows, grads, sums, kind):
     n, k = len(deltas), len(weights)
+    far = len(grads) > 1
     more = len(sums) > 0
+    depth = 2 * HD * len(grads)
     return pl.pallas_call(
-        lambda *refs: project_kernel(deltas, own_lanes, far_lane, more, *refs),
+        lambda *refs: project_kernel(deltas, own_lanes, far, more, *refs),
         name="project",
         out_shape=(jax.ShapeDtypeStruct((FEATS, ROWS), kind),) * n,
-        in_specs=[SMEM] + [ANY] * (k + 4 + len(sums)),
+        in_specs=[SMEM] + [ANY] * (k + 2 + len(grads) + len(sums)),
         out_specs=(ANY,) * n,
         scratch_shapes=[
-            pltpu.VMEM((n, FEATS, 4 * HD), BF16),
-            pltpu.VMEM((4 * HD, ROWS), BF16),
+            pltpu.VMEM((n, FEATS, depth), BF16),
+            pltpu.VMEM((depth, ROWS), BF16),
             pltpu.VMEM((n, FEATS, ROWS), kind),
             pltpu.SemaphoreType.DMA((n, k + 2)),
-            pltpu.SemaphoreType.DMA((2,)),
+            pltpu.SemaphoreType.DMA((len(grads),)),
             pltpu.SemaphoreType.DMA((n,)),
         ]
         + [pltpu.VMEM((n, FEATS, ROWS), F32)] * more,
-    )(at, *weights, *far, g_own, g_far, *sums)
+    )(at, *weights, *far_rows, *grads, *sums)
 
 
 def arrive(x):
@@ -652,32 +653,31 @@
     far = arrive(swapped(send, "xh"))
     stats = attention_stats(own, qseg, query, twins, others, 0, NEAR, state)
     gqt, mine, theirs = attention_grads(own, stats, query, near, far, twins, others)
-    got = swapped(theirs, "core")
+    got = arrive(swapped(theirs, "core"))
     gqt_far = arrive(swapped(gqt, "xh"))
     own_total, sends = join_partials(core[None], mine, got)
     parts = [chips_back(sends[d - 1], d) for d in range(HALF, 0, -1)]
     gkvt = total_partials(own_total, parts)
     gkvt_far = arrive(swapped(gkvt, "xh"))
 
-    deltas = (4, 3, -3, 2, -2, 1, -1, 0)
-    far_rows = (far_mine, far_other)
+    deltas = (4, -3, 3, -2, 2, -1, 1, 0)
     q_lanes = ((0, 2 * HD),)
-    sums = project(deltas, at, (w_query,), q_lanes, far_rows, 0, gqt, gqt_far, (), F32)
+    unread = (w_query, w_query)
+    sums = project(deltas, at, (w_query,), q_lanes, unread, (gqt,), (), F32)
     kv = (w_key, w_value)
     kv_lanes = ((0, HD), (HD, HD))
-    args = (at, kv, kv_lanes, far_rows, 2 * HD, gkvt, gkvt_far)
-    (across,) = project(deltas[:1], *args, sums[:1], BF16)
-    rest = project(deltas[1:], *args, sums[1:], F32)
-    ahead = round_z(across[:UP_ROWS], 1).astype(F32)
-    behind = round_z(across[UP_ROWS:], -1).astype(F32)
-    ahead = rest[0] + jnp.pad(ahead, ((0, FEATS - UP_ROWS), (0, 0)))
-    behind = rest[1] + jnp.pad(behind, ((UP_ROWS, 0), (0, 0)))
-    for k in (2, 3, 4):
-        ahead = round_z(ahead.astype(BF16), 1).astype(F32)
-        behind = round_z(behind.astype(BF16), -1).astype(F32)
-        if k < 4:
-            ahead, behind = ahead + rest[2 * k - 2], behind + rest[2 * k - 1]
-    result = (ahead + behind + rest[6]).astype(BF16)
+    args = (at, kv, kv_lanes, (far_mine, far_other), (gkvt, gqt_far, gkvt_far))
+    ahead, behind = project(deltas[:2], *args, sums[:2], BF16)
+    rest = project(deltas[2:4], *args, sums[2:4], F32)
+    rest += project(deltas[4:], *args, sums[4:], F32)
+    ahead = round_z(ahead, 1)
+    behind = round_z(behind, -1)
+    for k in (2, 3):
+        add_ahead, add_behind = rest[2 * k - 4], rest[2 * k - 3]
+        ahead = round_z((ahead.astype(F32) + add_ahead).astype(BF16), 1)
+        behind = round_z((behind.astype(F32) + add_behind).astype(BF16), -1)
+    ahead = round_z((ahead.astype(F32) + rest[4]).astype(BF16), 1)
+    result = (ahead.astype(F32) + behind.astype(F32) + rest[5]).astype(BF16)
     return result.T
 
 

time: 208 us -> 206 us (level)
  waiting for transfers between devices: 83.2 us -> 77.2 us
  Pallas kernels: 53.8 us -> 58.5 us
    ppermute x15 -> x14, waiting for transfers between devices: 29.2 us -> 23.9 us  [round_z(): return lax.ppermute(x, 'z', [(i, (i + step) % RING) for i in range(RING)])]
    pallas_call x3 -> x4, Pallas kernels: 14.7 us -> 18.8 us  [project(): pl.pallas_call(lambda *refs: project_kernel(deltas, own_lanes, far, more,...]
    ppermute x15 -> x14, starting transfers between devices: 26.8 us -> 27.9 us  [round_z(): return lax.ppermute(x, 'z', [(i, (i + step) % RING) for i in range(RING)])]
  transfers between devices with their start and end apart: 39 -> 38, of which waited for: 17 -> 15; matrix products, arithmetic and copies ran while one was open for 3% -> 3% of each run, Pallas kernels for 23% -> 25%
where the time goes in v3:
time: 206 us
  waiting for transfers between devices  77.2 us (37%)
  starting transfers between devices  60.7 us (29%)
  Pallas kernels  58.5 us (28%)
  local copies, waits for them, and re-layouts  4.46 us (2%)
  other arithmetic  4.05 us (2%)
    ppermute x5, waiting for transfers between devices, chips_on(): return lax.ppermute(x, AA, chip_pairs(d))  41.5 us
    ppermute x14, starting transfers between devices, round_z(): return lax.ppermute(x, 'z', [(i, (i + step) % RING) for i in range(RING)])  27.9 us
    ppermute x14, waiting for transfers between devices, round_z(): return lax.ppermute(x, 'z', [(i, (i + step) % RING) for i in range(RING)])  23.9 us
    pallas_call x4, Pallas kernels, project(): pl.pallas_call(lambda *refs: project_kernel(deltas, own_lanes, far, more,...  18.8 us
    ppermute x14, starting transfers between devices, swapped(): return lax.ppermute(x, axis, [(0, 1), (1, 0)])  13.2 us
    pallas_call x1, Pallas kernels, attention_grads(): pl.pallas_call(grads_kernel, name='attention_grads', out_shape=(jax.Shape...  12.3 us
    pallas_call x2, Pallas kernels, attention_stats(): pl.pallas_call(lambda *refs: stats_kernel(low, high, *refs), name='stats_...  12.1 us
    ppermute x5, starting transfers between devices, chips_on(): return lax.ppermute(x, AA, chip_pairs(d))  11.8 us
  transfers between devices with their start and end apart: 38, of which 15 were waited for; matrix products, arithmetic and copies ran while one was open for 3% of the time, Pallas kernels for 25%

profile of v3, /device:TPU:24, one launch (start us, length us, event | category | flops | bytes accessed | tf_op | source)
XLA Modules:
  0.0 205.6 jit_solution(8386935439922731825)
XLA Ops:
  0.0 0.6 pad_add_fusion.at_ref.refs_0_
  0.6 3.5 %split_w_out.1 = bf16[4,256,384]{2,1,0:T(8,128)(2,1)} custom-call(s32[3]{0:T(128)} %pad_add_fusion.at_ref.refs_0_, bf16[256,5376]{1,0:T(8,128)(2,1)} %refs_1_.6), custom_call_target="tpu_custom_call" | custom-call | tf_op jit(solution)/shard_map/split_w_out/pallas_call | solution.py:348
  4.1 3.1 %collective-permute-start.13 = (bf16[4,256,384]{2,1,0:T(8,128)(2,1)}, bf16[4,256,384]{2,1,0:T(8,128)(2,1)}, u32[]{:S(2)}, u32[]{:S(2)}) collective-permute-start(bf16[4,256,384]{2,1,0:T(8,128)(2,1)} %split_w_out.1), channel_id=1, source_target_pairs={{0,1},{1,0},{2,3},{3,2},{4,5},{5,4},{6,7},{7,6},{8,9},{9,8},{10,11... | collective-permute-start | bytes 2359304 | tf_op jit(solution)/shard_map/ppermute | solution.py:599
  7.3 3.2 %collective-permute-start.5 = (bf16[400,256]{1,0:T(8,128)(2,1)S(1)}, bf16[400,256]{1,0:T(8,128)(2,1)S(1)}, u32[]{:S(2)}, u32[]{:S(2)}) collective-permute-start(bf16[400,256]{1,0:T(8,128)(2,1)S(1)} %fusion.2.refs_3_.refs_6_), channel_id=1, source_target_pairs={{0,64},{16,80},{32,96},{48,112},{64,128},{80,144},{96,160},{112,17... | collective-permute-start | bytes 614408 | tf_op jit(solution)/shard_map/ppermute | solution.py:607
  10.5 4.1 %collective-permute-start.2 = (bf16[400,256]{1,0:T(8,128)(2,1)S(1)}, bf16[400,256]{1,0:T(8,128)(2,1)S(1)}, u32[]{:S(2)}, u32[]{:S(2)}) collective-permute-start(bf16[400,256]{1,0:T(8,128)(2,1)S(1)} %fusion.2.refs_3_.refs_6_), channel_id=1, source_target_pairs={{0,32},{16,48},{32,64},{48,80},{64,96},{80,112},{96,128},{112,144}... | collective-permute-start | bytes 614408 | tf_op jit(solution)/shard_map/ppermute | solution.py:607
  14.6 0.1 collective-permute-start.3
  14.7 1.3 collective-permute-start.8
  16.0 1.2 dynamic-slice_bitcast_fusion
  17.2 1.1 dynamic-slice_bitcast_fusion.1
  18.3 11.4 %collective-permute-done.5.refs_7_.refs_8_ = bf16[400,256]{1,0:T(8,128)(2,1)S(1)} collective-permute-done((bf16[400,256]{1,0:T(8,128)(2,1)S(1)}, bf16[400,256]{1,0:T(8,128)(2,1)S(1)}, u32[]{:S(2)}, u32[]{:S(2)}) %collective-permute-start.5) | collective-permute-done | bytes 204832 | tf_op jit(solution)/shard_map/ppermute | solution.py:607
  29.7 1.9 collective-permute-start.15
  31.7 1.3 pad_maximum_fusion
  32.9 1.3 collective-permute-done.2.refs_4_.refs_7_
  34.3 0.5 collective-permute-start
  34.8 1.9 collective-permute-start.7
  36.7 0.1 collective-permute-start.14
  36.8 1.8 collective-permute-done.8.refs_9_.refs_10_
  38.6 5.9 %collective-permute-start.16 = (bf16[336,384]{1,0:T(8,128)(2,1)S(1)}, bf16[336,384]{1,0:T(8,128)(2,1)S(1)}, u32[]{:S(2)}, u32[]{:S(2)}) collective-permute-start(bf16[336,384]{1,0:T(8,128)(2,1)S(1)} %bitcast.29), channel_id=1, source_target_pairs={{0,14},{2,0},{4,2},{6,4},{8,6},{10,8},{12,10},{14,12},{1,15},{3,1}... | collective-permute-start | bytes 774152 | tf_op jit(solution)/shard_map/ppermute | solution.py:615
  44.5 26.9 %collective-permute-done.7.refs_8_.refs_9_ = bf16[400,256]{1,0:T(8,128)(2,1)S(1)} collective-permute-done((bf16[400,256]{1,0:T(8,128)(2,1)S(1)}, bf16[400,256]{1,0:T(8,128)(2,1)S(1)}, u32[]{:S(2)}, u32[]{:S(2)}) %collective-permute-start.7) | collective-permute-done | bytes 204832 | tf_op jit(solution)/shard_map/ppermute | solution.py:607
  71.4 1.3 collective-permute-start.11
  72.7 5.9 %collective-permute-start.18 = (bf16[336,384]{1,0:T(8,128)(2,1)S(1)}, bf16[336,384]{1,0:T(8,128)(2,1)S(1)}, u32[]{:S(2)}, u32[]{:S(2)}) collective-permute-start(bf16[336,384]{1,0:T(8,128)(2,1)S(1)} %collective-permute-done.16.refs_6_), channel_id=1, source_target_pairs={{0,14},{2,0},{4,2},{6,4},{8,6},{10,8},{12,10},{14,12},{1,15},{3,1}... | collective-permute-start | bytes 774152 | tf_op jit(solution)/shard_map/ppermute | solution.py:615
  78.6 0.1 collective-permute-start.6
  78.7 4.5 %collective-permute-done.18.refs_8_ = bf16[336,384]{1,0:T(8,128)(2,1)S(1)} collective-permute-done((bf16[336,384]{1,0:T(8,128)(2,1)S(1)}, bf16[336,384]{1,0:T(8,128)(2,1)S(1)}, u32[]{:S(2)}, u32[]{:S(2)}) %collective-permute-start.18) | collective-permute-done | bytes 258080 | tf_op jit(solution)/shard_map/ppermute | solution.py:615
  83.2 3.7 %collective-permute-start.20 = (bf16[336,384]{1,0:T(8,128)(2,1)S(1)}, bf16[336,384]{1,0:T(8,128)(2,1)S(1)}, u32[]{:S(2)}, u32[]{:S(2)}) collective-permute-start(bf16[336,384]{1,0:T(8,128)(2,1)S(1)} %collective-permute-done.18.refs_8_), channel_id=1, source_target_pairs={{0,14},{2,0},{4,2},{6,4},{8,6},{10,8},{12,10},{14,12},{1,15},{3,1}... | collective-permute-start | bytes 774152 | tf_op jit(solution)/shard_map/ppermute | solution.py:615
  87.0 0.1 collective-permute-start.4
  87.1 3.7 %collective-permute-done.20.refs_10_ = bf16[336,384]{1,0:T(8,128)(2,1)S(1)} collective-permute-done((bf16[336,384]{1,0:T(8,128)(2,1)S(1)}, bf16[336,384]{1,0:T(8,128)(2,1)S(1)}, u32[]{:S(2)}, u32[]{:S(2)}) %collective-permute-start.20) | collective-permute-done | bytes 258080 | tf_op jit(solution)/shard_map/ppermute | solution.py:615
  90.8 3.7 %collective-permute-done.21.refs_11_ = bf16[336,384]{1,0:T(8,128)(2,1)S(1)} collective-permute-done((bf16[336,384]{1,0:T(8,128)(2,1)S(1)}, bf16[336,384]{1,0:T(8,128)(2,1)S(1)}, u32[]{:S(2)}, u32[]{:S(2)}) %collective-permute-start.21) | collective-permute-done | bytes 258080 | tf_op jit(solution)/shard_map/ppermute | solution.py:615
  94.5 0.7 copy-done.24
  95.2 0.1 collective-permute-start.12
  95.3 6.4 %dout_parts.1 = (f32[256,384]{1,0:T(8,128)}, bf16[256,384]{1,0:T(8,128)(2,1)}) custom-call(s32[3]{0:T(128)} %pad_add_fusion.at_ref.refs_0_, bf16[256,5376]{1,0:T(8,128)(2,1)} %refs_1_.6, bf16[4,256,384]{2,1,0:T(8,128)(2,1)} %collective-permute-done.13.refs_2_, bf16[4,256,384]{2,1,0:T(8,128)(2,1)} %collective-permute-done.14.refs_3_, ...), custom_call_target="tpu_custom_call" | custom-call | tf_op jit(solution)/shard_map/dout_parts/pallas_call | solution.py:406
  101.8 0.6 collective-permute-start.22
  102.4 0.6 broadcast_in_dim.8.refs_1_
  103.0 6.3 %stats_near.1 = (f32[1,768]{1,0:T(1,128)}, f32[1,768]{1,0:T(1,128)}, f32[128,768]{1,0:T(8,128)}, s32[1,384]{1,0:T(1,128)}) custom-call(s32[1]{0:T(128)} %bitcast.9.refs_0_.own_ref, s32[1,384]{1,0:T(1,128)} %broadcast_in_dim.8.refs_1_, bf16[384,256]{1,0:T(8,128)(2,1)} %refs_1_.7, bf16[400,256]{1,0:T(8,128)(2,1)} %copy-done.2, bf16[400,256]{1,0:T(8,128)(2,1)} %copy-done.4, ...), custom_call_target="tpu_custom_call" | custom-call | tf_op jit(solution)/shard_map/stats_near/pallas_call | solution.py:284
  109.3 0.6 copy-done.9
  110.1 5.8 %stats_far.1 = (f32[1,768]{1,0:T(1,128)}, f32[128,768]{1,0:T(8,128)}, s32[1,384]{1,0:T(1,128)}, s32[1]{0:T(128)}) custom-call(s32[1]{0:T(128)} %bitcast.9.refs_0_.own_ref, s32[1,384]{1,0:T(1,128)} %broadcast_in_dim.8.refs_1_, bf16[384,256]{1,0:T(8,128)(2,1)} %refs_1_.7, f32[1,768]{1,0:T(1,128)} %get-tuple-element.40.refs_3_, ...), custom_call_target="tpu_custom_call" | custom-call | tf_op jit(solution)/shard_map/stats_far/pallas_call | solution.py:284
  115.9 12.3 %attention_grads.1 = (bf16[256,384]{1,0:T(8,128)(2,1)}, bf16[5,384,256]{2,1,0:T(8,128)(2,1)}, bf16[5,384,256]{2,1,0:T(8,128)(2,1)}) custom-call(s32[1]{0:T(128)} %bitcast.9.refs_0_.own_ref, s32[1]{0:T(128)} %get-tuple-element.44.low_ref, s32[1,384]{1,0:T(1,128)} %get-tuple-element.45.refs_0_, bf16[384,256]{1,0:T(8,128)(2,1)} %refs_1_.7, ...), custom_call_target="tpu_custom_call" | custom-call | tf_op jit(solution)/shard_map/attention_grads/pallas_call | solution.py:298
  128.3 2.0 collective-permute-start.23
  130.3 0.1 collective-permute-start.1
  130.4 2.3 %collective-permute-done.23.got_ref = bf16[5,384,256]{2,1,0:T(8,128)(2,1)S(1)} collective-permute-done((bf16[5,384,256]{2,1,0:T(8,128)(2,1)}, bf16[5,384,256]{2,1,0:T(8,128)(2,1)S(1)}, u32[]{:S(2)}, u32[]{:S(2)}) %collective-permute-start.23) | collective-permute-done | bytes 983072 | tf_op jit(solution)/shard_map/ppermute | solution.py:599
  132.7 3.2 %join_partials.1 = (f32[384,256]{1,0:T(8,128)}, bf16[384,256]{1,0:T(8,128)(2,1)}, bf16[384,256]{1,0:T(8,128)(2,1)}, bf16[384,256]{1,0:T(8,128)(2,1)}, bf16[384,2...) custom-call(s32[1]{0:T(128)} %bitcast.2.core_ref, bf16[5,384,256]{2,1,0:T(8,128)(2,1)} %get-tuple-element.50.mine_ref, ...), custom_call_target="tpu_custom_call" | custom-call | tf_op jit(solution)/shard_map/join_partials/pallas_call | solution.py:461
  136.0 0.7 collective-permute-start.24
  136.6 1.3 collective-permute-start.25
  137.9 1.9 collective-permute-start.26
  139.9 1.9 collective-permute-start.27
  141.8 1.9 collective-permute-start.28
  143.7 2.2 %collective-permute-done.25.refs_1_ = bf16[384,256]{1,0:T(8,128)(2,1)S(1)} collective-permute-done((bf16[384,256]{1,0:T(8,128)(2,1)}, bf16[384,256]{1,0:T(8,128)(2,1)S(1)}, u32[]{:S(2)}, u32[]{:S(2)}) %collective-permute-start.25) | collective-permute-done | bytes 196640 | tf_op jit(solution)/shard_map/ppermute | solution.py:611
  145.9 3.0 %collective-permute-start.29 = (bf16[256,384]{1,0:T(8,128)(2,1)S(1)}, bf16[256,384]{1,0:T(8,128)(2,1)S(1)}, u32[]{:S(2)}, u32[]{:S(2)}) collective-permute-start(bf16[256,384]{1,0:T(8,128)(2,1)S(1)} %copy-done.25), channel_id=1, source_target_pairs={{0,1},{1,0},{2,3},{3,2},{4,5},{5,4},{6,7},{7,6},{8,9},{9,8},{10,11... | collective-permute-start | bytes 589832 | tf_op jit(solution)/shard_map/ppermute | solution.py:599
  148.9 4.8 %collective-permute-done.27.refs_3_ = bf16[384,256]{1,0:T(8,128)(2,1)S(1)} collective-permute-done((bf16[384,256]{1,0:T(8,128)(2,1)}, bf16[384,256]{1,0:T(8,128)(2,1)S(1)}, u32[]{:S(2)}, u32[]{:S(2)}) %collective-permute-start.27) | collective-permute-done | bytes 196640 | tf_op jit(solution)/shard_map/ppermute | solution.py:611
  153.8 2.5 %collective-permute-done.28.refs_4_ = bf16[384,256]{1,0:T(8,128)(2,1)S(1)} collective-permute-done((bf16[384,256]{1,0:T(8,128)(2,1)}, bf16[384,256]{1,0:T(8,128)(2,1)S(1)}, u32[]{:S(2)}, u32[]{:S(2)}) %collective-permute-start.28) | collective-permute-done | bytes 196640 | tf_op jit(solution)/shard_map/ppermute | solution.py:611
  156.3 2.2 %total_partials.1.refs_5_ = bf16[256,384]{1,0:T(8,128)(2,1)} custom-call(f32[384,256]{1,0:T(8,128)} %get-tuple-element.52.own_ref, bf16[384,256]{1,0:T(8,128)(2,1)S(1)} %collective-permute-done.24.refs_0_, bf16[384,256]{1,0:T(8,128)(2,1)S(1)} %collective-permute-done.25.refs_1_, bf16[384,256]{1,0:T(8,128)(2,1)S(1)} %collective-permute-done.26.refs_2_, ...), custom_call_target="tpu_custom_call" | custom-call | tf_op jit(solution)/shard_map/total_partials/pallas_call | solution.py:495
  158.5 3.3 %collective-permute-start.30 = (bf16[256,384]{1,0:T(8,128)(2,1)}, bf16[256,384]{1,0:T(8,128)(2,1)S(1)}, u32[]{:S(2)}, u32[]{:S(2)}) collective-permute-start(bf16[256,384]{1,0:T(8,128)(2,1)} %total_partials.1.refs_5_), channel_id=1, source_target_pairs={{0,1},{1,0},{2,3},{3,2},{4,5},{5,4},{6,7},{7,6},{8,9},{9,8},{10,11... | collective-permute-start | bytes 589832 | tf_op jit(solution)/shard_map/ppermute | solution.py:599
  161.8 5.2 %project.4 = (f32[336,384]{1,0:T(8,128)}, f32[336,384]{1,0:T(8,128)}, f32[336,384]{1,0:T(8,128)}, f32[336,384]{1,0:T(8,128)}, f32[336,384]{1,0:T(8,128)}, /*inde...) custom-call(s32[3]{0:T(128)} %pad_add_fusion.at_ref.refs_0_, bf16[5376,256]{1,0:T(8,128)(2,1)} %refs_3_.1, ...), custom_call_target="tpu_custom_call" | custom-call | tf_op jit(solution)/shard_map/project/pallas_call | solution.py:576
  167.0 4.1 %project.5 = (bf16[336,384]{1,0:T(8,128)(2,1)}, bf16[336,384]{1,0:T(8,128)(2,1)}) custom-call(s32[3]{0:T(128)} %pad_add_fusion.at_ref.refs_0_, bf16[5376,128]{1,0:T(8,128)(2,1)} %refs_1_.11, bf16[5376,128]{1,0:T(8,128)(2,1)} %refs_2_.11, bf16[4,336,512]{2,1,0:T(8,128)(2,1)} %copy-done, bf16[4,336,512]{2,1,0:T(8,128)(2,1)} %collective-permute-done.1.refs_4_, ...), custom_call_target="tpu_custom_call" | custom-call | tf_op jit(solution)/shard_map/project/pallas_call | solution.py:576
  171.2 3.2 %collective-permute-start.35 = (bf16[336,384]{1,0:T(8,128)(2,1)}, bf16[336,384]{1,0:T(8,128)(2,1)S(1)}, u32[]{:S(2)}, u32[]{:S(2)}) collective-permute-start(bf16[336,384]{1,0:T(8,128)(2,1)} %get-tuple-element.71), channel_id=1, source_target_pairs={{0,14},{2,0},{4,2},{6,4},{8,6},{10,8},{12,10},{14,12},{1,15},{3,1}... | collective-permute-start | bytes 774152 | tf_op jit(solution)/shard_map/ppermute | solution.py:615
  174.5 4.2 %project.6 = (f32[336,384]{1,0:T(8,128)}, f32[336,384]{1,0:T(8,128)}) custom-call(s32[3]{0:T(128)} %pad_add_fusion.at_ref.refs_0_, bf16[5376,128]{1,0:T(8,128)(2,1)} %refs_1_.11, bf16[5376,128]{1,0:T(8,128)(2,1)} %refs_2_.11, bf16[4,336,512]{2,1,0:T(8,128)(2,1)} %copy-done, bf16[4,336,512]{2,1,0:T(8,128)(2,1)} %collective-permute-done.1.refs_4_, ...), custom_call_target="tpu_custom_call" | custom-call | tf_op jit(solution)/shard_map/project/pallas_call | solution.py:576
  178.7 0.7 collective-permute-done.31
  179.4 1.1 add_convert_fusion.5
  180.6 5.3 %project.7 = (f32[336,384]{1,0:T(8,128)}, f32[336,384]{1,0:T(8,128)}, f32[336,384]{1,0:T(8,128)}, f32[336,384]{1,0:T(8,128)}) custom-call(s32[3]{0:T(128)} %pad_add_fusion.at_ref.refs_0_, bf16[5376,128]{1,0:T(8,128)(2,1)} %refs_1_.11, bf16[5376,128]{1,0:T(8,128)(2,1)} %refs_2_.11, bf16[4,336,512]{2,1,0:T(8,128)(2,1)} %copy-done, ...), custom_call_target="tpu_custom_call" | custom-call | tf_op jit(solution)/shard_map/project/pallas_call | solution.py:576
  186.1 3.3 %collective-permute-start.36 = (bf16[336,384]{1,0:T(8,128)(2,1)S(1)}, bf16[336,384]{1,0:T(8,128)(2,1)S(1)}, u32[]{:S(2)}, u32[]{:S(2)}) collective-permute-start(bf16[336,384]{1,0:T(8,128)(2,1)S(1)} %add_convert_fusion.2), channel_id=1, source_target_pairs={{0,14},{2,0},{4,2},{6,4},{8,6},{10,8},{12,10},{14,12},{1,15},{3,1}... | collective-permute-start | bytes 774152 | tf_op jit(solution)/shard_map/ppermute | solution.py:615
  189.5 3.7 %collective-permute-done.36 = bf16[336,384]{1,0:T(8,128)(2,1)S(1)} collective-permute-done((bf16[336,384]{1,0:T(8,128)(2,1)S(1)}, bf16[336,384]{1,0:T(8,128)(2,1)S(1)}, u32[]{:S(2)}, u32[]{:S(2)}) %collective-permute-start.36) | collective-permute-done | bytes 258080 | tf_op jit(solution)/shard_map/ppermute | solution.py:615
  193.3 3.8 %collective-permute-start.37 = (bf16[336,384]{1,0:T(8,128)(2,1)S(1)}, bf16[336,384]{1,0:T(8,128)(2,1)S(1)}, u32[]{:S(2)}, u32[]{:S(2)}) collective-permute-start(bf16[336,384]{1,0:T(8,128)(2,1)S(1)} %add_convert_fusion.1), channel_id=1, source_target_pairs={{0,14},{2,0},{4,2},{6,4},{8,6},{10,8},{12,10},{14,12},{1,15},{3,1}... | collective-permute-start | bytes 774152 | tf_op jit(solution)/shard_map/ppermute | solution.py:615
  197.2 3.7 %collective-permute-done.37 = bf16[336,384]{1,0:T(8,128)(2,1)S(1)} collective-permute-done((bf16[336,384]{1,0:T(8,128)(2,1)S(1)}, bf16[336,384]{1,0:T(8,128)(2,1)S(1)}, u32[]{:S(2)}, u32[]{:S(2)}) %collective-permute-start.37) | collective-permute-done | bytes 258080 | tf_op jit(solution)/shard_map/ppermute | solution.py:615
  200.9 3.8 %collective-permute-done.34 = bf16[336,384]{1,0:T(8,128)(2,1)S(1)} collective-permute-done((bf16[336,384]{1,0:T(8,128)(2,1)S(1)}, bf16[336,384]{1,0:T(8,128)(2,1)S(1)}, u32[]{:S(2)}, u32[]{:S(2)}) %collective-permute-start.34) | collective-permute-done | bytes 258080 | tf_op jit(solution)/shard_map/ppermute | solution.py:615
  204.8 0.8 fusion.1
  (94 shorter events, 0.9 us)
Async XLA Ops:
  0.6 6.6 %copy-start.28 = (s32[384]{0:T(512)S(1)}, s32[384]{0:T(512)}, u32[]{:S(2)}) copy-start(s32[384]{0:T(512)} %param.13) | copy-start | bytes 4612
  0.6 6.6 %copy-start.26 = (bf16[384,128]{1,0:T(8,128)(2,1)S(1)}, bf16[384,128]{1,0:T(8,128)(2,1)}, u32[]{:S(2)}) copy-start(bf16[384,128]{1,0:T(8,128)(2,1)} %param.11) | copy-start | bytes 294916
  0.6 6.6 %copy-start.27 = (bf16[384,128]{1,0:T(8,128)(2,1)S(1)}, bf16[384,128]{1,0:T(8,128)(2,1)}, u32[]{:S(2)}) copy-start(bf16[384,128]{1,0:T(8,128)(2,1)} %param.10) | copy-start | bytes 294916
  4.1 32.6 %collective-permute-start.13 = (bf16[4,256,384]{2,1,0:T(8,128)(2,1)}, bf16[4,256,384]{2,1,0:T(8,128)(2,1)}, u32[]{:S(2)}, u32[]{:S(2)}) collective-permute-start(bf16[4,256,384]{2,1,0:T(8,128)(2,1)} %split_w_out.1), channel_id=1, source_target_pairs={{0,1},{1,0},{2,3},{3,2},{4,5},{5,4},{6,7},{7,6},{8,9},{9,8},{10,11... | collective-permute-start | bytes 2359304 | tf_op jit(solution)/shard_map/ppermute | solution.py:599
  7.3 64.1 %copy-start.2 = (bf16[400,256]{1,0:T(8,128)(2,1)}, bf16[400,256]{1,0:T(8,128)(2,1)S(1)}, u32[]{:S(2)}) copy-start(bf16[400,256]{1,0:T(8,128)(2,1)S(1)} %fusion.2.refs_3_.refs_6_) | copy-start | bytes 614404
  7.3 22.5 %collective-permute-start.5 = (bf16[400,256]{1,0:T(8,128)(2,1)S(1)}, bf16[400,256]{1,0:T(8,128)(2,1)S(1)}, u32[]{:S(2)}, u32[]{:S(2)}) collective-permute-start(bf16[400,256]{1,0:T(8,128)(2,1)S(1)} %fusion.2.refs_3_.refs_6_), channel_id=1, source_target_pairs={{0,64},{16,80},{32,96},{48,112},{64,128},{80,144},{96,160},{112,17... | collective-permute-start | bytes 614408 | tf_op jit(solution)/shard_map/ppermute | solution.py:607
  10.5 23.8 %collective-permute-start.2 = (bf16[400,256]{1,0:T(8,128)(2,1)S(1)}, bf16[400,256]{1,0:T(8,128)(2,1)S(1)}, u32[]{:S(2)}, u32[]{:S(2)}) collective-permute-start(bf16[400,256]{1,0:T(8,128)(2,1)S(1)} %fusion.2.refs_3_.refs_6_), channel_id=1, source_target_pairs={{0,32},{16,48},{32,64},{48,80},{64,96},{80,112},{96,128},{112,144}... | collective-permute-start | bytes 614408 | tf_op jit(solution)/shard_map/ppermute | solution.py:607
  14.6 20.2 %collective-permute-start.3 = (bf16[400,256]{1,0:T(8,128)(2,1)S(1)}, bf16[400,256]{1,0:T(8,128)(2,1)S(1)}, u32[]{:S(2)}, u32[]{:S(2)}) collective-permute-start(bf16[400,256]{1,0:T(8,128)(2,1)S(1)} %fusion.2.refs_3_.refs_6_), channel_id=1, source_target_pairs={{0,16},{16,0},{1,17},{17,1},{2,18},{18,2},{3,19},{19,3},{4,20},{20... | collective-permute-start | bytes 614408 | tf_op jit(solution)/shard_map/ppermute | solution.py:599
  14.7 24.0 %collective-permute-start.8 = (bf16[400,256]{1,0:T(8,128)(2,1)S(1)}, bf16[400,256]{1,0:T(8,128)(2,1)S(1)}, u32[]{:S(2)}, u32[]{:S(2)}) collective-permute-start(bf16[400,256]{1,0:T(8,128)(2,1)S(1)} %fusion.2.refs_3_.refs_6_), channel_id=1, source_target_pairs={{0,128},{16,144},{32,160},{48,176},{64,192},{80,208},{96,224},{112... | collective-permute-start | bytes 614408 | tf_op jit(solution)/shard_map/ppermute | solution.py:607
  16.0 13.8 %copy-start.17 = (bf16[384,336]{0,1:T(8,128)(2,1)S(1)}, bf16[384,336]{0,1:T(8,128)(2,1)}, u32[]{:S(2)}) copy-start(bf16[384,336]{0,1:T(8,128)(2,1)} %param.12) | copy-start | bytes 774148
  29.7 48.9 %copy-start.3 = (bf16[400,256]{1,0:T(8,128)(2,1)}, bf16[400,256]{1,0:T(8,128)(2,1)S(1)}, u32[]{:S(2)}) copy-start(bf16[400,256]{1,0:T(8,128)(2,1)S(1)} %collective-permute-done.5.refs_7_.refs_8_) | copy-start | bytes 614404
  29.7 14.8 %collective-permute-start.15 = (bf16[336,384]{1,0:T(8,128)(2,1)S(1)}, bf16[336,384]{1,0:T(8,128)(2,1)S(1)}, u32[]{:S(2)}, u32[]{:S(2)}) collective-permute-start(bf16[336,384]{1,0:T(8,128)(2,1)S(1)} %bitcast.28), channel_id=1, source_target_pairs={{0,2},{2,4},{4,6},{6,8},{8,10},{10,12},{12,14},{14,0},{1,3},{3,5},... | collective-permute-start | bytes 774152 | tf_op jit(solution)/shard_map/ppermute | solution.py:615
  34.3 67.5 %copy-start.4 = (bf16[400,256]{1,0:T(8,128)(2,1)}, bf16[400,256]{1,0:T(8,128)(2,1)S(1)}, u32[]{:S(2)}) copy-start(bf16[400,256]{1,0:T(8,128)(2,1)S(1)} %collective-permute-done.2.refs_4_.refs_7_) | copy-start | bytes 614404
  34.3 96.1 %collective-permute-start = (bf16[4,336,512]{2,1,0:T(8,128)(2,1)}, bf16[4,336,512]{2,1,0:T(8,128)(2,1)S(1)}, u32[]{:S(2)}, u32[]{:S(2)}) collective-permute-start(bf16[4,336,512]{2,1,0:T(8,128)(2,1)} %pad_maximum_fusion), channel_id=1, source_target_pairs={{0,1},{1,0},{2,3},{3,2},{4,5},{5,4},{6,7},{7,6},{8,9},{9,8},{10,11... | collective-permute-start | bytes 4128776 | tf_op jit(solution)/shard_map/ppermute | solution.py:599
  34.8 67.0 %copy-start.5 = (bf16[400,256]{1,0:T(8,128)(2,1)}, bf16[400,256]{1,0:T(8,128)(2,1)S(1)}, u32[]{:S(2)}) copy-start(bf16[400,256]{1,0:T(8,128)(2,1)S(1)} %collective-permute-done.3.refs_5_.refs_11_) | copy-start | bytes 614404
  34.8 36.6 %collective-permute-start.7 = (bf16[400,256]{1,0:T(8,128)(2,1)S(1)}, bf16[400,256]{1,0:T(8,128)(2,1)S(1)}, u32[]{:S(2)}, u32[]{:S(2)}) collective-permute-start(bf16[400,256]{1,0:T(8,128)(2,1)S(1)} %fusion.2.refs_3_.refs_6_), channel_id=1, source_target_pairs={{0,96},{16,112},{32,128},{48,144},{64,160},{80,176},{96,192},{112,... | collective-permute-start | bytes 614408 | tf_op jit(solution)/shard_map/ppermute | solution.py:607
  36.7 57.8 %collective-permute-start.14 = (bf16[4,256,384]{2,1,0:T(8,128)(2,1)}, bf16[4,256,384]{2,1,0:T(8,128)(2,1)}, u32[]{:S(2)}, u32[]{:S(2)}) collective-permute-start(bf16[4,256,384]{2,1,0:T(8,128)(2,1)} %collective-permute-done.13.refs_2_), channel_id=1, source_target_pairs={{0,16},{16,0},{1,17},{17,1},{2,18},{18,2},{3,19},{19,3},{4,20},{20... | collective-permute-start | bytes 2359304 | tf_op jit(solution)/shard_map/ppermute | solution.py:599
  38.6 63.1 %copy-start.6 = (bf16[400,256]{1,0:T(8,128)(2,1)}, bf16[400,256]{1,0:T(8,128)(2,1)S(1)}, u32[]{:S(2)}) copy-start(bf16[400,256]{1,0:T(8,128)(2,1)S(1)} %collective-permute-done.8.refs_9_.refs_10_) | copy-start | bytes 614404
  38.6 34.1 %collective-permute-start.16 = (bf16[336,384]{1,0:T(8,128)(2,1)S(1)}, bf16[336,384]{1,0:T(8,128)(2,1)S(1)}, u32[]{:S(2)}, u32[]{:S(2)}) collective-permute-start(bf16[336,384]{1,0:T(8,128)(2,1)S(1)} %bitcast.29), channel_id=1, source_target_pairs={{0,14},{2,0},{4,2},{6,4},{8,6},{10,8},{12,10},{14,12},{1,15},{3,1}... | collective-permute-start | bytes 774152 | tf_op jit(solution)/shard_map/ppermute | solution.py:615
  44.5 42.4 %copy-start.18 = (bf16[336,384]{1,0:T(8,128)(2,1)}, bf16[336,384]{1,0:T(8,128)(2,1)S(1)}, u32[]{:S(2)}) copy-start(bf16[336,384]{1,0:T(8,128)(2,1)S(1)} %collective-permute-done.15.refs_5_) | copy-start | bytes 774148
  44.5 34.1 %collective-permute-start.17 = (bf16[336,384]{1,0:T(8,128)(2,1)S(1)}, bf16[336,384]{1,0:T(8,128)(2,1)S(1)}, u32[]{:S(2)}, u32[]{:S(2)}) collective-permute-start(bf16[336,384]{1,0:T(8,128)(2,1)S(1)} %collective-permute-done.15.refs_5_), channel_id=1, source_target_pairs={{0,2},{2,4},{4,6},{6,8},{8,10},{10,12},{12,14},{14,0},{1,3},{3,5},... | collective-permute-start | bytes 774152 | tf_op jit(solution)/shard_map/ppermute | solution.py:615
  71.4 30.4 %copy-start.7 = (bf16[400,256]{1,0:T(8,128)(2,1)}, bf16[400,256]{1,0:T(8,128)(2,1)S(1)}, u32[]{:S(2)}) copy-start(bf16[400,256]{1,0:T(8,128)(2,1)S(1)} %collective-permute-done.7.refs_8_.refs_9_) | copy-start | bytes 614404
  71.4 7.2 %collective-permute-start.11 = (bf16[400,256]{1,0:T(8,128)(2,1)S(1)}, bf16[400,256]{1,0:T(8,128)(2,1)}, u32[]{:S(2)}, u32[]{:S(2)}) collective-permute-start(bf16[400,256]{1,0:T(8,128)(2,1)S(1)} %fusion.2.refs_3_.refs_6_), channel_id=1, source_target_pairs={{16,176},{48,208},{80,240},{17,177},{49,209},{81,241},{18,178},{50... | collective-permute-start | bytes 614408 | tf_op jit(solution)/shard_map/ppermute | solution.py:607
  72.7 21.7 %copy-start.19 = (bf16[336,384]{1,0:T(8,128)(2,1)}, bf16[336,384]{1,0:T(8,128)(2,1)S(1)}, u32[]{:S(2)}) copy-start(bf16[336,384]{1,0:T(8,128)(2,1)S(1)} %collective-permute-done.16.refs_6_) | copy-start | bytes 774148
  72.7 10.5 %collective-permute-start.18 = (bf16[336,384]{1,0:T(8,128)(2,1)S(1)}, bf16[336,384]{1,0:T(8,128)(2,1)S(1)}, u32[]{:S(2)}, u32[]{:S(2)}) collective-permute-start(bf16[336,384]{1,0:T(8,128)(2,1)S(1)} %collective-permute-done.16.refs_6_), channel_id=1, source_target_pairs={{0,14},{2,0},{4,2},{6,4},{8,6},{10,8},{12,10},{14,12},{1,15},{3,1}... | collective-permute-start | bytes 774152 | tf_op jit(solution)/shard_map/ppermute | solution.py:615
  78.6 15.9 %copy-start.20 = (bf16[336,384]{1,0:T(8,128)(2,1)}, bf16[336,384]{1,0:T(8,128)(2,1)S(1)}, u32[]{:S(2)}) copy-start(bf16[336,384]{1,0:T(8,128)(2,1)S(1)} %collective-permute-done.17.refs_7_) | copy-start | bytes 774148
  78.6 8.3 %collective-permute-start.19 = (bf16[336,384]{1,0:T(8,128)(2,1)S(1)}, bf16[336,384]{1,0:T(8,128)(2,1)S(1)}, u32[]{:S(2)}, u32[]{:S(2)}) collective-permute-start(bf16[336,384]{1,0:T(8,128)(2,1)S(1)} %collective-permute-done.17.refs_7_), channel_id=1, source_target_pairs={{0,2},{2,4},{4,6},{6,8},{8,10},{10,12},{12,14},{14,0},{1,3},{3,5},... | collective-permute-start | bytes 774152 | tf_op jit(solution)/shard_map/ppermute | solution.py:615
  78.6 8.3 %collective-permute-start.6 = (bf16[400,256]{1,0:T(8,128)(2,1)S(1)}, bf16[400,256]{1,0:T(8,128)(2,1)S(1)}, u32[]{:S(2)}, u32[]{:S(2)}) collective-permute-start(bf16[400,256]{1,0:T(8,128)(2,1)S(1)} %collective-permute-done.5.refs_7_.refs_8_), channel_id=1, source_target_pairs={{0,16},{16,0},{1,17},{17,1},{2,18},{18,2},{3,19},{19,3},{4,20},{20... | collective-permute-start | bytes 614408 | tf_op jit(solution)/shard_map/ppermute | solution.py:599
  83.2 12.1 %copy-start.21 = (bf16[336,384]{1,0:T(8,128)(2,1)}, bf16[336,384]{1,0:T(8,128)(2,1)S(1)}, u32[]{:S(2)}) copy-start(bf16[336,384]{1,0:T(8,128)(2,1)S(1)} %collective-permute-done.18.refs_8_) | copy-start | bytes 774148
  83.2 7.5 %collective-permute-start.20 = (bf16[336,384]{1,0:T(8,128)(2,1)S(1)}, bf16[336,384]{1,0:T(8,128)(2,1)S(1)}, u32[]{:S(2)}, u32[]{:S(2)}) collective-permute-start(bf16[336,384]{1,0:T(8,128)(2,1)S(1)} %collective-permute-done.18.refs_8_), channel_id=1, source_target_pairs={{0,14},{2,0},{4,2},{6,4},{8,6},{10,8},{12,10},{14,12},{1,15},{3,1}... | collective-permute-start | bytes 774152 | tf_op jit(solution)/shard_map/ppermute | solution.py:615
  86.9 7.6 %copy-start.22 = (bf16[336,384]{1,0:T(8,128)(2,1)}, bf16[336,384]{1,0:T(8,128)(2,1)S(1)}, u32[]{:S(2)}) copy-start(bf16[336,384]{1,0:T(8,128)(2,1)S(1)} %collective-permute-done.19.refs_9_) | copy-start | bytes 774148
  86.9 7.5 %collective-permute-start.21 = (bf16[336,384]{1,0:T(8,128)(2,1)S(1)}, bf16[336,384]{1,0:T(8,128)(2,1)S(1)}, u32[]{:S(2)}, u32[]{:S(2)}) collective-permute-start(bf16[336,384]{1,0:T(8,128)(2,1)S(1)} %collective-permute-done.19.refs_9_), channel_id=1, source_target_pairs={{0,2},{2,4},{4,6},{6,8},{8,10},{10,12},{12,14},{14,0},{1,3},{3,5},... | collective-permute-start | bytes 774152 | tf_op jit(solution)/shard_map/ppermute | solution.py:615
  87.0 14.8 %copy-start.1 = (bf16[400,256]{1,0:T(8,128)(2,1)}, bf16[400,256]{1,0:T(8,128)(2,1)S(1)}, u32[]{:S(2)}) copy-start(bf16[400,256]{1,0:T(8,128)(2,1)S(1)} %collective-permute-done.6.refs_7_.refs_10_.refs_13_) | copy-start | bytes 614404
  87.0 14.8 %collective-permute-start.4 = (bf16[400,256]{1,0:T(8,128)(2,1)S(1)}, bf16[400,256]{1,0:T(8,128)(2,1)S(1)}, u32[]{:S(2)}, u32[]{:S(2)}) collective-permute-start(bf16[400,256]{1,0:T(8,128)(2,1)S(1)} %collective-permute-done.2.refs_4_.refs_7_), channel_id=1, source_target_pairs={{0,16},{16,0},{1,17},{17,1},{2,18},{18,2},{3,19},{19,3},{4,20},{20... | collective-permute-start | bytes 614408 | tf_op jit(solution)/shard_map/ppermute | solution.py:599
  90.8 3.7 %copy-start.23 = (bf16[336,384]{1,0:T(8,128)(2,1)}, bf16[336,384]{1,0:T(8,128)(2,1)S(1)}, u32[]{:S(2)}) copy-start(bf16[336,384]{1,0:T(8,128)(2,1)S(1)} %collective-permute-done.20.refs_10_) | copy-start | bytes 774148
  90.8 18.5 %collective-permute-start.10 = (bf16[400,256]{1,0:T(8,128)(2,1)S(1)}, bf16[400,256]{1,0:T(8,128)(2,1)S(1)}, u32[]{:S(2)}, u32[]{:S(2)}) collective-permute-start(bf16[400,256]{1,0:T(8,128)(2,1)S(1)} %collective-permute-done.8.refs_9_.refs_10_), channel_id=1, source_target_pairs={{0,16},{16,0},{1,17},{17,1},{2,18},{18,2},{3,19},{19,3},{4,20},{20... | collective-permute-start | bytes 614408 | tf_op jit(solution)/shard_map/ppermute | solution.py:599
  94.5 14.8 %collective-permute-start.9 = (bf16[400,256]{1,0:T(8,128)(2,1)S(1)}, bf16[400,256]{1,0:T(8,128)(2,1)S(1)}, u32[]{:S(2)}, u32[]{:S(2)}) collective-permute-start(bf16[400,256]{1,0:T(8,128)(2,1)S(1)} %collective-permute-done.7.refs_8_.refs_9_), channel_id=1, source_target_pairs={{0,16},{16,0},{1,17},{17,1},{2,18},{18,2},{3,19},{19,3},{4,20},{20... | collective-permute-start | bytes 614408 | tf_op jit(solution)/shard_map/ppermute | solution.py:599
  95.2 14.1 %collective-permute-start.12 = (bf16[400,256]{1,0:T(8,128)(2,1)}, bf16[400,256]{1,0:T(8,128)(2,1)S(1)}, u32[]{:S(2)}, u32[]{:S(2)}) collective-permute-start(bf16[400,256]{1,0:T(8,128)(2,1)} %collective-permute-done.11), channel_id=1, source_target_pairs={{0,16},{16,0},{1,17},{17,1},{2,18},{18,2},{3,19},{19,3},{4,20},{20... | collective-permute-start | bytes 614408 | tf_op jit(solution)/shard_map/ppermute | solution.py:599
  101.8 1.2 copy-start.8
  101.8 14.1 %collective-permute-start.22 = (bf16[256,384]{1,0:T(8,128)(2,1)}, bf16[256,384]{1,0:T(8,128)(2,1)S(1)}, u32[]{:S(2)}, u32[]{:S(2)}) collective-permute-start(bf16[256,384]{1,0:T(8,128)(2,1)} %get-tuple-element.47), channel_id=1, source_target_pairs={{0,1},{1,0},{2,3},{3,2},{4,5},{5,4},{6,7},{7,6},{8,9},{9,8},{10,11... | collective-permute-start | bytes 589832 | tf_op jit(solution)/shard_map/ppermute | solution.py:599
  109.3 0.8 copy-start.11
  128.3 17.7 %copy-start.25 = (bf16[256,384]{1,0:T(8,128)(2,1)S(1)}, bf16[256,384]{1,0:T(8,128)(2,1)}, u32[]{:S(2)}) copy-start(bf16[256,384]{1,0:T(8,128)(2,1)} %get-tuple-element.58.refs_4_) | copy-start | bytes 589828
  128.3 4.5 %collective-permute-start.23 = (bf16[5,384,256]{2,1,0:T(8,128)(2,1)}, bf16[5,384,256]{2,1,0:T(8,128)(2,1)S(1)}, u32[]{:S(2)}, u32[]{:S(2)}) collective-permute-start(bf16[5,384,256]{2,1,0:T(8,128)(2,1)} %get-tuple-element.51), channel_id=1, source_target_pairs={{0,16},{16,0},{1,17},{17,1},{2,18},{18,2},{3,19},{19,3},{4,20},{20... | collective-permute-start | bytes 2949128 | tf_op jit(solution)/shard_map/ppermute | solution.py:599
  130.3 28.2 %copy-start = (bf16[4,336,512]{2,1,0:T(8,128)(2,1)}, bf16[4,336,512]{2,1,0:T(8,128)(2,1)S(1)}, u32[]{:S(2)}) copy-start(bf16[4,336,512]{2,1,0:T(8,128)(2,1)S(1)} %collective-permute-done.refs_3_) | copy-start | bytes 4128772
  130.3 36.7 %collective-permute-start.1 = (bf16[4,336,512]{2,1,0:T(8,128)(2,1)S(1)}, bf16[4,336,512]{2,1,0:T(8,128)(2,1)}, u32[]{:S(2)}, u32[]{:S(2)}) collective-permute-start(bf16[4,336,512]{2,1,0:T(8,128)(2,1)S(1)} %collective-permute-done.refs_3_), channel_id=1, source_target_pairs={{0,16},{16,0},{1,17},{17,1},{2,18},{18,2},{3,19},{19,3},{4,20},{20... | collective-permute-start | bytes 4128776 | tf_op jit(solution)/shard_map/ppermute | solution.py:599
  136.0 5.8 %collective-permute-start.24 = (bf16[384,256]{1,0:T(8,128)(2,1)}, bf16[384,256]{1,0:T(8,128)(2,1)S(1)}, u32[]{:S(2)}, u32[]{:S(2)}) collective-permute-start(bf16[384,256]{1,0:T(8,128)(2,1)} %get-tuple-element.53), channel_id=1, source_target_pairs={{176,16},{208,48},{240,80},{177,17},{209,49},{241,81},{178,18},{21... | collective-permute-start | bytes 589832 | tf_op jit(solution)/shard_map/ppermute | solution.py:611
  136.6 9.3 %collective-permute-start.25 = (bf16[384,256]{1,0:T(8,128)(2,1)}, bf16[384,256]{1,0:T(8,128)(2,1)S(1)}, u32[]{:S(2)}, u32[]{:S(2)}) collective-permute-start(bf16[384,256]{1,0:T(8,128)(2,1)} %get-tuple-element.54), channel_id=1, source_target_pairs={{128,0},{144,16},{160,32},{176,48},{192,64},{208,80},{224,96},{240... | collective-permute-start | bytes 589832 | tf_op jit(solution)/shard_map/ppermute | solution.py:611
  137.9 11.0 %collective-permute-start.26 = (bf16[384,256]{1,0:T(8,128)(2,1)}, bf16[384,256]{1,0:T(8,128)(2,1)S(1)}, u32[]{:S(2)}, u32[]{:S(2)}) collective-permute-start(bf16[384,256]{1,0:T(8,128)(2,1)} %get-tuple-element.55), channel_id=1, source_target_pairs={{96,0},{112,16},{128,32},{144,48},{160,64},{176,80},{192,96},{208,... | collective-permute-start | bytes 589832 | tf_op jit(solution)/shard_map/ppermute | solution.py:611
  139.9 13.9 %collective-permute-start.27 = (bf16[384,256]{1,0:T(8,128)(2,1)}, bf16[384,256]{1,0:T(8,128)(2,1)S(1)}, u32[]{:S(2)}, u32[]{:S(2)}) collective-permute-start(bf16[384,256]{1,0:T(8,128)(2,1)} %get-tuple-element.56), channel_id=1, source_target_pairs={{64,0},{80,16},{96,32},{112,48},{128,64},{144,80},{160,96},{176,11... | collective-permute-start | bytes 589832 | tf_op jit(solution)/shard_map/ppermute | solution.py:611
  141.8 14.5 %collective-permute-start.28 = (bf16[384,256]{1,0:T(8,128)(2,1)}, bf16[384,256]{1,0:T(8,128)(2,1)S(1)}, u32[]{:S(2)}, u32[]{:S(2)}) collective-permute-start(bf16[384,256]{1,0:T(8,128)(2,1)} %get-tuple-element.57), channel_id=1, source_target_pairs={{32,0},{48,16},{64,32},{80,48},{96,64},{112,80},{128,96},{144,112}... | collective-permute-start | bytes 589832 | tf_op jit(solution)/shard_map/ppermute | solution.py:611
  145.9 21.1 %collective-permute-start.29 = (bf16[256,384]{1,0:T(8,128)(2,1)S(1)}, bf16[256,384]{1,0:T(8,128)(2,1)S(1)}, u32[]{:S(2)}, u32[]{:S(2)}) collective-permute-start(bf16[256,384]{1,0:T(8,128)(2,1)S(1)} %copy-done.25), channel_id=1, source_target_pairs={{0,1},{1,0},{2,3},{3,2},{4,5},{5,4},{6,7},{7,6},{8,9},{9,8},{10,11... | collective-permute-start | bytes 589832 | tf_op jit(solution)/shard_map/ppermute | solution.py:599
  158.5 8.5 %collective-permute-start.30 = (bf16[256,384]{1,0:T(8,128)(2,1)}, bf16[256,384]{1,0:T(8,128)(2,1)S(1)}, u32[]{:S(2)}, u32[]{:S(2)}) collective-permute-start(bf16[256,384]{1,0:T(8,128)(2,1)} %total_partials.1.refs_5_), channel_id=1, source_target_pairs={{0,1},{1,0},{2,3},{3,2},{4,5},{5,4},{6,7},{7,6},{8,9},{9,8},{10,11... | collective-permute-start | bytes 589832 | tf_op jit(solution)/shard_map/ppermute | solution.py:599
  171.1 8.3 %collective-permute-start.31 = (bf16[336,384]{1,0:T(8,128)(2,1)}, bf16[336,384]{1,0:T(8,128)(2,1)S(1)}, u32[]{:S(2)}, u32[]{:S(2)}) collective-permute-start(bf16[336,384]{1,0:T(8,128)(2,1)} %get-tuple-element.61), channel_id=1, source_target_pairs={{0,2},{2,4},{4,6},{6,8},{8,10},{10,12},{12,14},{14,0},{1,3},{3,5},... | collective-permute-start | bytes 774152 | tf_op jit(solution)/shard_map/ppermute | solution.py:615
  171.2 14.8 %collective-permute-start.35 = (bf16[336,384]{1,0:T(8,128)(2,1)}, bf16[336,384]{1,0:T(8,128)(2,1)S(1)}, u32[]{:S(2)}, u32[]{:S(2)}) collective-permute-start(bf16[336,384]{1,0:T(8,128)(2,1)} %get-tuple-element.71), channel_id=1, source_target_pairs={{0,14},{2,0},{4,2},{6,4},{8,6},{10,8},{12,10},{14,12},{1,15},{3,1}... | collective-permute-start | bytes 774152 | tf_op jit(solution)/shard_map/ppermute | solution.py:615
  180.5 8.9 %collective-permute-start.32 = (bf16[336,384]{1,0:T(8,128)(2,1)S(1)}, bf16[336,384]{1,0:T(8,128)(2,1)S(1)}, u32[]{:S(2)}, u32[]{:S(2)}) collective-permute-start(bf16[336,384]{1,0:T(8,128)(2,1)S(1)} %add_convert_fusion.5), channel_id=1, source_target_pairs={{0,2},{2,4},{4,6},{6,8},{8,10},{10,12},{12,14},{14,0},{1,3},{3,5},... | collective-permute-start | bytes 774152 | tf_op jit(solution)/shard_map/ppermute | solution.py:615
  180.6 5.4 %copy-start.15 = (f32[336,384]{1,0:T(8,128)S(1)}, f32[336,384]{1,0:T(8,128)}, u32[]{:S(2)}) copy-start(f32[336,384]{1,0:T(8,128)} %get-tuple-element.72) | copy-start | bytes 1548292
  186.0 3.4 %copy-start.16 = (f32[336,384]{1,0:T(8,128)S(1)}, f32[336,384]{1,0:T(8,128)}, u32[]{:S(2)}) copy-start(f32[336,384]{1,0:T(8,128)} %get-tuple-element.69) | copy-start | bytes 1548292
  186.0 7.2 %copy-start.14 = (f32[336,384]{1,0:T(8,128)S(1)}, f32[336,384]{1,0:T(8,128)}, u32[]{:S(2)}) copy-start(f32[336,384]{1,0:T(8,128)} %get-tuple-element.73) | copy-start | bytes 1548292
  186.0 11.1 %copy-start.13 = (f32[336,384]{1,0:T(8,128)S(1)}, f32[336,384]{1,0:T(8,128)}, u32[]{:S(2)}) copy-start(f32[336,384]{1,0:T(8,128)} %get-tuple-element.70) | copy-start | bytes 1548292
  186.1 7.1 %collective-permute-start.36 = (bf16[336,384]{1,0:T(8,128)(2,1)S(1)}, bf16[336,384]{1,0:T(8,128)(2,1)S(1)}, u32[]{:S(2)}, u32[]{:S(2)}) collective-permute-start(bf16[336,384]{1,0:T(8,128)(2,1)S(1)} %add_convert_fusion.2), channel_id=1, source_target_pairs={{0,14},{2,0},{4,2},{6,4},{8,6},{10,8},{12,10},{14,12},{1,15},{3,1}... | collective-permute-start | bytes 774152 | tf_op jit(solution)/shard_map/ppermute | solution.py:615
  189.4 15.4 %copy-start.12 = (f32[336,384]{1,0:T(8,128)S(1)}, f32[336,384]{1,0:T(8,128)}, u32[]{:S(2)}) copy-start(f32[336,384]{1,0:T(8,128)} %get-tuple-element.74) | copy-start | bytes 1548292
  189.5 7.6 %collective-permute-start.33 = (bf16[336,384]{1,0:T(8,128)(2,1)S(1)}, bf16[336,384]{1,0:T(8,128)(2,1)S(1)}, u32[]{:S(2)}, u32[]{:S(2)}) collective-permute-start(bf16[336,384]{1,0:T(8,128)(2,1)S(1)} %add_convert_fusion.4), channel_id=1, source_target_pairs={{0,2},{2,4},{4,6},{6,8},{8,10},{10,12},{12,14},{14,0},{1,3},{3,5},... | collective-permute-start | bytes 774152 | tf_op jit(solution)/shard_map/ppermute | solution.py:615
  193.3 7.6 %collective-permute-start.37 = (bf16[336,384]{1,0:T(8,128)(2,1)S(1)}, bf16[336,384]{1,0:T(8,128)(2,1)S(1)}, u32[]{:S(2)}, u32[]{:S(2)}) collective-permute-start(bf16[336,384]{1,0:T(8,128)(2,1)S(1)} %add_convert_fusion.1), channel_id=1, source_target_pairs={{0,14},{2,0},{4,2},{6,4},{8,6},{10,8},{12,10},{14,12},{1,15},{3,1}... | collective-permute-start | bytes 774152 | tf_op jit(solution)/shard_map/ppermute | solution.py:615
  197.1 7.6 %collective-permute-start.34 = (bf16[336,384]{1,0:T(8,128)(2,1)S(1)}, bf16[336,384]{1,0:T(8,128)(2,1)S(1)}, u32[]{:S(2)}, u32[]{:S(2)}) collective-permute-start(bf16[336,384]{1,0:T(8,128)(2,1)S(1)} %add_convert_fusion.3), channel_id=1, source_target_pairs={{0,2},{2,4},{4,6},{6,8},{8,10},{10,12},{12,14},{14,0},{1,3},{3,5},... | collective-permute-start | bytes 774152 | tf_op jit(solution)/shard_map/ppermute | solution.py:615
  (3 other events, 2.1 us)

commit v4 on v3

--- a/solution.py
+++ b/solution.py
@@ -360,15 +360,13 @@
 
 def dout_kernel(deltas, at_ref, w_ref, pa, pb, *refs):
     shards = refs[:RING]
-    near_ref, send_ref, wbuf, fbuf, gbuf, hbuf, sem = refs[RING:]
+    near_ref, send_ref, wbuf, fbuf, gbuf, hbuf, far_acc, sem = refs[RING:]
     z, xh, core = at_ref[0], at_ref[1], at_ref[2]
-    copies = []
     for i in range(RING):
         chunk = lax.rem(z + deltas[i] + RING, RING)
         half = lax.div(chunk, RING // 2)
         inner = lax.rem(chunk, RING // 2)
-        lanes, skip = column_window(2 * chunk + xh)
-        place = pl.ds(pl.multiple_of(skip, 16), FEATS)
+        lanes, _ = column_window(2 * chunk + xh)
         far = pltpu.make_async_copy(pa.at[inner], fbuf.at[i], sem.at[i, 1])
         far_too = pltpu.make_async_copy(pb.at[inner], fbuf.at[i], sem.at[i, 1])
         pltpu.make_async_copy(w_ref.at[:, lanes], wbuf.at[i], sem.at[i, 0]).start()
@@ -381,27 +379,31 @@
         def _(copy=far_too):
             copy.start()
 
-        gbuf[i] = jnp.zeros((WINDOW, ROWS), BF16)
+        pltpu.make_async_copy(shards[i], hbuf.at[i, :FEATS], sem.at[i, 2]).start()
         hbuf[i, FEATS:] = jnp.zeros((CHUNK - FEATS, ROWS), BF16)
-        to_far = pltpu.make_async_copy(shards[i], hbuf.at[i, :FEATS], sem.at[i, 2])
-        to_far.start()
-        own_rows = pltpu.make_async_copy(w_ref.at[:, lanes], wbuf.at[i], sem.at[i, 0])
-        copies.append((own_rows, far, to_far, place))
-    near = far = None
-    for i in range(RING):
-        for c in copies[i][:3]:
-            c.wait()
-        gbuf[i, copies[i][3], :] = hbuf[i, :FEATS]
-        add_far = dot(fbuf[i], hbuf[i])
-        add_near = dot(wbuf[i], gbuf[i])
-        far = add_far if i == 0 else far + add_far
-        near = add_near if i == 0 else near + add_near
-    near_ref[...] = near
-    send_ref[...] = far.astype(BF16)
+    near_ref[...] = jnp.zeros(near_ref.shape, F32)
+    far_acc[...] = jnp.zeros(far_acc.shape, F32)
+
+    def one_chunk(i, carry):
+        pltpu.make_async_copy(w_ref.at[:, :WINDOW], wbuf.at[i], sem.at[i, 0]).wait()
+        pltpu.make_async_copy(pa.at[0], fbuf.at[i], sem.at[i, 1]).wait()
+        pltpu.make_async_copy(shards[0], hbuf.at[i, :FEATS], sem.at[i, 2]).wait()
+        delta = jnp.where(lax.rem(i, 2) == 1, -lax.div(i + 1, 2), lax.div(i, 2))
+        chunk = lax.rem(z + delta + RING, RING)
+        _, skip = column_window(2 * chunk + xh)
+        gbuf[...] = jnp.zeros((WINDOW, ROWS), BF16)
+        gbuf[pl.ds(pl.multiple_of(skip, 16), FEATS), :] = hbuf[i, :FEATS]
+        far_acc[...] += dot(fbuf[i], hbuf[i])
+        near_ref[...] += dot(wbuf[i], gbuf[...])
+        return carry
+
+    lax.fori_loop(0, RING, one_chunk, 0)
+    send_ref[...] = far_acc[...].astype(BF16)
 
 
 def dout_parts(at, w_out, far_w, shards):
     deltas = tuple(shards)
+    assert deltas == (0, -1, 1, -2, 2, -3, 3, -4)
     half = (2 * HD, ROWS)
     return pl.pallas_call(
         lambda *refs: dout_kernel(deltas, *refs),
@@ -412,48 +414,27 @@
         scratch_shapes=[
             pltpu.VMEM((RING, 2 * HD, WINDOW), BF16),
             pltpu.VMEM((RING, 2 * HD, CHUNK), BF16),
-            pltpu.VMEM((RING, WINDOW, ROWS), BF16),
+            pltpu.VMEM((WINDOW, ROWS), BF16),
             pltpu.VMEM((RING, CHUNK, ROWS), BF16),
+            pltpu.VMEM(half, F32),
             pltpu.SemaphoreType.DMA((RING, 3)),
         ],
     )(at, w_out, *far_w, *shards.values())
 
 
-def join_kernel(core_ref, mine_ref, got_ref, own_ref, *refs):
-    send_refs = refs[:HALF]
-    mine, got, own, made, in_sem, out_sem = refs[HALF:]
+def join_kernel(core_ref, mine_ref, got_ref, own_ref, *send_refs):
     core = core_ref[0]
-    arrivals = []
-    for d in reversed(range(HALF)):
-        pair = [
-            pltpu.make_async_copy(x.at[d], y.at[d], in_sem.at[i, d])
-            for i, (x, y) in enumerate(((got_ref, got), (mine_ref, mine)))
-        ]
-        for c in pair:
-            c.start()
-        arrivals.append(pair)
-    arrivals.reverse()
-    departures = []
-    for d in reversed(range(HALF + 1)):
-        if d > 0:
-            for c in arrivals[d - 1]:
-                c.wait()
+    for d in range(HALF + 1):
         at = d - core
         inside = (at >= 0) & (at < HALF)
-        total = jnp.where(inside, got[jnp.clip(at, 0, HALF - 1)].astype(F32), 0.0)
+        other = got_ref[jnp.clip(at, 0, HALF - 1)].astype(F32)
+        total = jnp.where(inside, other, 0.0)
         if d < HALF:
-            total = total + mine[d].astype(F32)
+            total = total + mine_ref[d].astype(F32)
         if d == 0:
-            own[...] = total
-            departures.append(pltpu.make_async_copy(own, own_ref, out_sem.at[d]))
+            own_ref[...] = total
         else:
-            made[d - 1] = total.astype(BF16)
-            departures.append(
-                pltpu.make_async_copy(made.at[d - 1], send_refs[d - 1], out_sem.at[d])
-            )
-        departures[-1].start()
-    for c in departures:
-        c.wait()
+            send_refs[d - 1][...] = total.astype(BF16)
 
 
 def join_partials(core, mine, got):
@@ -462,55 +443,34 @@
         join_kernel,
         name="join_partials",
         out_shape=(jax.ShapeDtypeStruct(shape, F32),) + (jax.ShapeDtypeStruct(shape, BF16),) * HALF,
-        in_specs=[SMEM, ANY, ANY],
-        out_specs=(ANY,) * (HALF + 1),
-        scratch_shapes=[
-            pltpu.VMEM((HALF, *shape), BF16),
-            pltpu.VMEM((HALF, *shape), BF16),
-            pltpu.VMEM(shape, F32),
-            pltpu.VMEM((HALF, *shape), BF16),
-            pltpu.SemaphoreType.DMA((2, HALF)),
-            pltpu.SemaphoreType.DMA((HALF + 1,)),
-        ],
+        in_specs=[SMEM, VMEM, VMEM],
+        out_specs=(VMEM,) * (HALF + 1),
     )(core, mine, got)
     return result[0], result[1:]
 
 
 def total_kernel(own_ref, *refs):
-    part_refs, (out_ref, own, parts, sem) = refs[:HALF], refs[HALF:]
-    copies = [pltpu.make_async_copy(own_ref, own, sem.at[HALF])]
-    copies += [pltpu.make_async_copy(x, parts.at[i], sem.at[i]) for i, x in enumerate(part_refs)]
-    for c in copies:
-        c.start()
-    for c in copies:
-        c.wait()
-    total = own[...]
-    for i in range(HALF):
-        total = total + parts[i].astype(F32)
-    out_ref[...] = total.astype(BF16).T
+    total = own_ref[...]
+    for ref in refs[:HALF]:
+        total = total + ref[...].astype(F32)
+    refs[HALF][...] = total.astype(BF16).T
 
 
 def total_partials(own, parts):
-    shape = (ROWS, 2 * HD)
     return pl.pallas_call(
         total_kernel,
         name="total_partials",
         out_shape=jax.ShapeDtypeStruct((2 * HD, ROWS), BF16),
-        in_specs=[ANY] * (HALF + 1),
+        in_specs=[VMEM] * (HALF + 1),
         out_specs=VMEM,
-        scratch_shapes=[
-            pltpu.VMEM(shape, F32),
-            pltpu.VMEM((HALF, *shape), BF16),
-            pltpu.SemaphoreType.DMA((HALF + 1,)),
-        ],
     )(own, *parts)
 
 
-def project_kernel(deltas, own_lanes, far, more, at_ref, *refs):
+def project_kernel(deltas, own_lanes, far, grad_count, more, at_ref, *refs):
     n, k = len(deltas), len(own_lanes)
     weights, refs = refs[:k], refs[k:]
-    pa, pb, *grads = refs[: 2 + 1 + 2 * far]
-    refs = refs[3 + 2 * far :]
+    grads, refs = refs[:grad_count], refs[grad_count:]
+    far_refs, refs = (refs[:4], refs[4:]) if far else ((), refs)
     sums, refs = (refs[:n], refs[n:]) if more else ((), refs)
     outs, refs = refs[:n], refs[n:]
     wbuf, gbuf, obuf, sem, g_sem, out_sem, *held = refs
@@ -535,22 +495,22 @@
         for c in mine:
             c.start()
         if far:
-            inner = lax.rem(chunk, RING // 2)
-            near_rows, far_rows = [
-                pltpu.make_async_copy(p.at[inner], wbuf.at[i, :, width:], sem.at[i, k])
-                for p in (pa, pb)
-            ]
-            same = lax.div(chunk, RING // 2) == core
-
-            @pl.when(same)
-            def _(copy=near_rows):
-                copy.start()
-
-            @pl.when(jnp.logical_not(same))
-            def _(copy=far_rows):
-                copy.start()
-
-            mine.append(near_rows)
+            first, size, lane = far
+            part = lax.div(lax.rem(chunk, RING // 2), 2)
+            other = lax.div(chunk, RING // 2) != core
+            source = 2 * other.astype(jnp.int32) + part
+            for j, ref in enumerate(far_refs):
+                copy = pltpu.make_async_copy(
+                    ref.at[lax.rem(chunk, 2), :, first : first + size],
+                    wbuf.at[i, :, lane : lane + size],
+                    sem.at[i, k],
+                )
+
+                @pl.when(source == j)
+                def _(copy=copy):
+                    copy.start()
+
+            mine.append(copy)
         copies.append(mine)
     for c in g_copies:
         c.wait()
@@ -568,16 +528,15 @@
         c.wait()
 
 
-def project(deltas, at, weights, own_lanes, far_rows, grads, sums, kind):
+def project(deltas, at, weights, own_lanes, far, far_rows, grads, sums, kind):
     n, k = len(deltas), len(weights)
-    far = len(grads) > 1
     more = len(sums) > 0
     depth = 2 * HD * len(grads)
     return pl.pallas_call(
-        lambda *refs: project_kernel(deltas, own_lanes, far, more, *refs),
+        lambda *refs: project_kernel(deltas, own_lanes, far, len(grads), more, *refs),
         name="project",
         out_shape=(jax.ShapeDtypeStruct((FEATS, ROWS), kind),) * n,
-        in_specs=[SMEM] + [ANY] * (k + 2 + len(grads) + len(sums)),
+        in_specs=[SMEM] + [ANY] * (k + len(grads) + len(far_rows) + len(sums)),
         out_specs=(ANY,) * n,
         scratch_shapes=[
             pltpu.VMEM((n, FEATS, depth), BF16),
@@ -588,7 +547,7 @@
             pltpu.SemaphoreType.DMA((n,)),
         ]
         + [pltpu.VMEM((n, FEATS, ROWS), F32)] * more,
-    )(at, *weights, *far_rows, *grads, *sums)
+    )(at, *weights, *grads, *far_rows, *sums)
 
 
 def arrive(x):
@@ -608,7 +567,7 @@
 
 
 def chips_back(x, d):
-    return arrive(lax.ppermute(x, AA, [(j, i) for i, j in chip_pairs(d)]))
+    return lax.ppermute(x, AA, [(j, i) for i, j in chip_pairs(d)])
 
 
 def round_z(x, step):
@@ -636,16 +595,18 @@
     block = jnp.concatenate((jnp.concatenate((keys, values), axis=1), ids), axis=0)
     twins = [block] + [chips_on(block, d) for d in range(1, HALF + 1)]
     others = [swapped(twins[d], "core") for d in range(HALF + 1)]
-    wanted = [
-        lax.dynamic_index_in_dim(
-            w.reshape(2, RING // 2, 2, FEATS, -1), core, 0, keepdims=False
-        )
-        for w in (w_query, w_key, w_value)
-    ]
-    wanted = [lax.dynamic_index_in_dim(w, 1 - xh, 1, keepdims=False) for w in wanted]
-    wanted = jnp.concatenate(wanted, axis=2)
-    far_mine = swapped(wanted, "xh")
-    far_other = swapped(far_mine, "core")
+    arrivals = []
+    for half in range(2):
+        wanted = [
+            lax.dynamic_index_in_dim(w.reshape(2, 2, 2, 2, FEATS, -1), core, 0, keepdims=False)
+            for w in (w_query, w_key, w_value)
+        ]
+        wanted = [
+            lax.dynamic_index_in_dim(w[half], 1 - xh, 1, keepdims=False) for w in wanted
+        ]
+        wanted = jnp.concatenate(wanted, axis=2)
+        arrivals.append(swapped(wanted, "xh"))
+    far_rows = (*arrivals, *(swapped(arrivals[h], "core") for h in range(2)))
 
     qseg = segment_ids[None, :]
     state = attention_stats(own, qseg, query, twins, others, NEAR, BLOCKS)
@@ -661,15 +622,23 @@
     gkvt_far = arrive(swapped(gkvt, "xh"))
 
     deltas = (4, -3, 3, -2, 2, -1, 1, 0)
-    q_lanes = ((0, 2 * HD),)
-    unread = (w_query, w_query)
-    sums = project(deltas, at, (w_query,), q_lanes, unread, (gqt,), (), F32)
+    wide = 2 * HD
+    q_lanes = ((0, wide),)
+    kv_lanes = ((0, HD), (HD, HD))
     kv = (w_key, w_value)
-    kv_lanes = ((0, HD), (HD, HD))
-    args = (at, kv, kv_lanes, (far_mine, far_other), (gkvt, gqt_far, gkvt_far))
-    ahead, behind = project(deltas[:2], *args, sums[:2], BF16)
-    rest = project(deltas[2:4], *args, sums[2:4], F32)
-    rest += project(deltas[4:], *args, sums[4:], F32)
+    sums = project(deltas, at, (w_query,), q_lanes, (), (), (gqt,), (), F32)
+    first = project(
+        deltas[:2], at, kv, kv_lanes, (0, wide, wide), far_rows,
+        (gkvt, gqt_far), sums[:2], F32,
+    )
+    ahead, behind = project(
+        deltas[:2], at, (), (), (wide, wide, 0), far_rows,
+        (gkvt_far,), first, BF16,
+    )
+    rest = project(
+        deltas[2:], at, kv, kv_lanes, (0, 2 * wide, wide), far_rows,
+        (gkvt, gqt_far, gkvt_far), sums[2:], F32,
+    )
     ahead = round_z(ahead, 1)
     behind = round_z(behind, -1)
     for k in (2, 3):

time: 206 us -> 217 us (1.053)
  waiting for transfers between devices: 77.2 us -> 83 us
  starting transfers between devices: 60.7 us -> 65.2 us
  local copies, waits for them, and re-layouts: 4.46 us -> 6.72 us
    ppermute x5, waiting for transfers between devices: 41.5 us -> 4.05 us  [chips_on(): return lax.ppermute(x, AA, chip_pairs(d))]
    ppermute x14 -> x16, waiting for transfers between devices: 2.32 us -> 36.1 us  [swapped(): return lax.ppermute(x, axis, [(0, 1), (1, 0)])]
    ppermute x5, waiting for transfers between devices: 9.55 us -> 14.7 us  [chips_back(): return lax.ppermute(x, AA, [(j, i) for i, j in chip_pairs(d)])]
    ppermute x5, starting transfers between devices: 11.8 us -> 16.2 us  [chips_on(): return lax.ppermute(x, AA, chip_pairs(d))]
    ppermute x14, waiting for transfers between devices: 23.9 us -> 28.1 us  [round_z(): return lax.ppermute(x, 'z', [(i, (i + step) % RING) for i in range(RING)])]
    ppermute x14 -> x16, starting transfers between devices: 13.2 us -> 15.7 us  [swapped(): return lax.ppermute(x, axis, [(0, 1), (1, 0)])]
    ppermute x14, starting transfers between devices: 27.9 us -> 25.6 us  [round_z(): return lax.ppermute(x, 'z', [(i, (i + step) % RING) for i in range(RING)])]
  transfers between devices with their start and end apart: 38 -> 40, of which waited for: 15 -> 14; matrix products, arithmetic and copies ran while one was open for 3% -> 2% of each run, Pallas kernels for 25% -> 18%
where the time goes in v4:
time: 217 us; the launch traced here: 216 us
  waiting for transfers between devices  83 us (38%)
  starting transfers between devices  65.2 us (30%)
  Pallas kernels  57.5 us (26%)
  local copies, waits for them, and re-layouts  6.72 us (3%)
  other arithmetic  3.02 us (1%)
    ppermute x16, waiting for transfers between devices, swapped(): return lax.ppermute(x, axis, [(0, 1), (1, 0)])  36.1 us
    ppermute x14, waiting for transfers between devices, round_z(): return lax.ppermute(x, 'z', [(i, (i + step) % RING) for i in range(RING)])  28.1 us
    ppermute x14, starting transfers between devices, round_z(): return lax.ppermute(x, 'z', [(i, (i + step) % RING) for i in range(RING)])  25.6 us
    pallas_call x4, Pallas kernels, project(): pl.pallas_call(lambda *refs: project_kernel(deltas, own_lanes, far, len(g...  18.4 us
    ppermute x5, starting transfers between devices, chips_on(): return lax.ppermute(x, AA, chip_pairs(d))  16.2 us
    ppermute x16, starting transfers between devices, swapped(): return lax.ppermute(x, axis, [(0, 1), (1, 0)])  15.7 us
    ppermute x5, waiting for transfers between devices, chips_back(): return lax.ppermute(x, AA, [(j, i) for i, j in chip_pairs(d)])  14.7 us
    pallas_call x1, Pallas kernels, attention_grads(): pl.pallas_call(grads_kernel, name='attention_grads', out_shape=(jax.Shape...  12.5 us
  transfers between devices with their start and end apart: 40, of which 14 were waited for; matrix products, arithmetic and copies ran while one was open for 2% of the time, Pallas kernels for 18%

profile of v4, /device:TPU:24, one launch (start us, length us, event | category | flops | bytes accessed | tf_op | source)
XLA Modules:
  0.0 216.1 jit_solution(11867714952838991002)
XLA Ops:
  0.0 0.6 pad_add_fusion.at_ref.refs_0_
  0.6 3.5 %split_w_out.1 = bf16[4,256,384]{2,1,0:T(8,128)(2,1)} custom-call(s32[3]{0:T(128)} %pad_add_fusion.at_ref.refs_0_, bf16[256,5376]{1,0:T(8,128)(2,1)} %refs_1_.5), custom_call_target="tpu_custom_call" | custom-call | tf_op jit(solution)/shard_map/split_w_out/pallas_call | solution.py:348
  4.1 3.1 %collective-permute-start.11 = (bf16[4,256,384]{2,1,0:T(8,128)(2,1)}, bf16[4,256,384]{2,1,0:T(8,128)(2,1)S(1)}, u32[]{:S(2)}, u32[]{:S(2)}) collective-permute-start(bf16[4,256,384]{2,1,0:T(8,128)(2,1)} %split_w_out.1), channel_id=1, source_target_pairs={{0,1},{1,0},{2,3},{3,2},{4,5},{5,4},{6,7},{7,6},{8,9},{9,8},{10,11... | collective-permute-start | bytes 2359304 | tf_op jit(solution)/shard_map/ppermute | solution.py:558
  7.2 1.9 collective-permute-start.13
  9.1 3.9 %collective-permute-start.14 = (bf16[336,384]{1,0:T(8,128)(2,1)S(1)}, bf16[336,384]{1,0:T(8,128)(2,1)S(1)}, u32[]{:S(2)}, u32[]{:S(2)}) collective-permute-start(bf16[336,384]{1,0:T(8,128)(2,1)S(1)} %bitcast.41), channel_id=1, source_target_pairs={{0,14},{2,0},{4,2},{6,4},{8,6},{10,8},{12,10},{14,12},{1,15},{3,1}... | collective-permute-start | bytes 774152 | tf_op jit(solution)/shard_map/ppermute | solution.py:574
  13.1 5.9 %collective-permute-done.13.refs_5_ = bf16[336,384]{1,0:T(8,128)(2,1)S(1)} collective-permute-done((bf16[336,384]{1,0:T(8,128)(2,1)S(1)}, bf16[336,384]{1,0:T(8,128)(2,1)S(1)}, u32[]{:S(2)}, u32[]{:S(2)}) %collective-permute-start.13) | collective-permute-done | bytes 258080 | tf_op jit(solution)/shard_map/ppermute | solution.py:574
  19.0 6.2 %collective-permute-done.11.refs_2_ = bf16[4,256,384]{2,1,0:T(8,128)(2,1)S(1)} collective-permute-done((bf16[4,256,384]{2,1,0:T(8,128)(2,1)}, bf16[4,256,384]{2,1,0:T(8,128)(2,1)S(1)}, u32[]{:S(2)}, u32[]{:S(2)}) %collective-permute-start.11) | collective-permute-done | bytes 786464 | tf_op jit(solution)/shard_map/ppermute | solution.py:558
  25.2 5.9 %collective-permute-start.16 = (bf16[336,384]{1,0:T(8,128)(2,1)S(1)}, bf16[336,384]{1,0:T(8,128)(2,1)S(1)}, u32[]{:S(2)}, u32[]{:S(2)}) collective-permute-start(bf16[336,384]{1,0:T(8,128)(2,1)S(1)} %collective-permute-done.14.refs_6_), channel_id=1, source_target_pairs={{0,14},{2,0},{4,2},{6,4},{8,6},{10,8},{12,10},{14,12},{1,15},{3,1}... | collective-permute-start | bytes 774152 | tf_op jit(solution)/shard_map/ppermute | solution.py:574
  31.2 6.0 %collective-permute-done.16.refs_8_ = bf16[336,384]{1,0:T(8,128)(2,1)S(1)} collective-permute-done((bf16[336,384]{1,0:T(8,128)(2,1)S(1)}, bf16[336,384]{1,0:T(8,128)(2,1)S(1)}, u32[]{:S(2)}, u32[]{:S(2)}) %collective-permute-start.16) | collective-permute-done | bytes 258080 | tf_op jit(solution)/shard_map/ppermute | solution.py:574
  37.2 3.7 %collective-permute-start.18 = (bf16[336,384]{1,0:T(8,128)(2,1)S(1)}, bf16[336,384]{1,0:T(8,128)(2,1)S(1)}, u32[]{:S(2)}, u32[]{:S(2)}) collective-permute-start(bf16[336,384]{1,0:T(8,128)(2,1)S(1)} %collective-permute-done.16.refs_8_), channel_id=1, source_target_pairs={{0,14},{2,0},{4,2},{6,4},{8,6},{10,8},{12,10},{14,12},{1,15},{3,1}... | collective-permute-start | bytes 774152 | tf_op jit(solution)/shard_map/ppermute | solution.py:574
  41.0 4.1 %collective-permute-start.3 = (bf16[400,256]{1,0:T(8,128)(2,1)S(1)}, bf16[400,256]{1,0:T(8,128)(2,1)S(1)}, u32[]{:S(2)}, u32[]{:S(2)}) collective-permute-start(bf16[400,256]{1,0:T(8,128)(2,1)S(1)} %fusion.2.refs_3_.refs_6_), channel_id=1, source_target_pairs={{0,64},{16,80},{32,96},{48,112},{64,128},{80,144},{96,160},{112,17... | collective-permute-start | bytes 614408 | tf_op jit(solution)/shard_map/ppermute | solution.py:566
  45.0 4.1 %collective-permute-start = (bf16[400,256]{1,0:T(8,128)(2,1)S(1)}, bf16[400,256]{1,0:T(8,128)(2,1)S(1)}, u32[]{:S(2)}, u32[]{:S(2)}) collective-permute-start(bf16[400,256]{1,0:T(8,128)(2,1)S(1)} %fusion.2.refs_3_.refs_6_), channel_id=1, source_target_pairs={{0,32},{16,48},{32,64},{48,80},{64,96},{80,112},{96,128},{112,144}... | collective-permute-start | bytes 614408 | tf_op jit(solution)/shard_map/ppermute | solution.py:566
  49.1 1.5 collective-permute-done.3.refs_7_.refs_8_
  50.6 2.6 %collective-permute-done.refs_4_.refs_7_ = bf16[400,256]{1,0:T(8,128)(2,1)S(1)} collective-permute-done((bf16[400,256]{1,0:T(8,128)(2,1)S(1)}, bf16[400,256]{1,0:T(8,128)(2,1)S(1)}, u32[]{:S(2)}, u32[]{:S(2)}) %collective-permute-start) | collective-permute-done | bytes 204832 | tf_op jit(solution)/shard_map/ppermute | solution.py:566
  53.2 5.4 %collective-permute-start.5 = (bf16[400,256]{1,0:T(8,128)(2,1)S(1)}, bf16[400,256]{1,0:T(8,128)(2,1)S(1)}, u32[]{:S(2)}, u32[]{:S(2)}) collective-permute-start(bf16[400,256]{1,0:T(8,128)(2,1)S(1)} %fusion.2.refs_3_.refs_6_), channel_id=1, source_target_pairs={{0,96},{16,112},{32,128},{48,144},{64,160},{80,176},{96,192},{112,... | collective-permute-start | bytes 614408 | tf_op jit(solution)/shard_map/ppermute | solution.py:566
  58.6 1.3 collective-permute-start.6
  59.9 1.3 collective-permute-start.9
  61.3 0.9 copy-done.14
  62.2 0.5 broadcast_in_dim.8.refs_1_
  62.7 6.2 %dout_parts.1 = (f32[256,384]{1,0:T(8,128)}, bf16[256,384]{1,0:T(8,128)(2,1)}) custom-call(s32[3]{0:T(128)} %pad_add_fusion.at_ref.refs_0_, bf16[256,5376]{1,0:T(8,128)(2,1)} %refs_1_.5, bf16[4,256,384]{2,1,0:T(8,128)(2,1)} %copy-done.13, bf16[4,256,384]{2,1,0:T(8,128)(2,1)} %copy-done.14, bf16[336,384]{1,0:T(8,128)(2,1)} %bitcast.39, ...), custom_call_target="tpu_custom_call" | custom-call | tf_op jit(solution)/shard_map/dout_parts/pallas_call | solution.py:408
  69.0 0.6 collective-permute-start.2
  69.6 0.1 collective-permute-start.7
  69.8 0.4 collective-permute-start.8
  70.2 0.1 collective-permute-start.10
  70.3 2.9 %collective-permute-start.20 = (bf16[256,384]{1,0:T(8,128)(2,1)}, bf16[256,384]{1,0:T(8,128)(2,1)S(1)}, u32[]{:S(2)}, u32[]{:S(2)}) collective-permute-start(bf16[256,384]{1,0:T(8,128)(2,1)} %get-tuple-element.49), channel_id=1, source_target_pairs={{0,1},{1,0},{2,3},{3,2},{4,5},{5,4},{6,7},{7,6},{8,9},{9,8},{10,11... | collective-permute-start | bytes 589832 | tf_op jit(solution)/shard_map/ppermute | solution.py:558
  73.2 1.1 dynamic-slice_bitcast_fusion
  74.3 1.9 dynamic-slice_bitcast_fusion.2
  76.2 0.7 copy-done.9
  76.9 6.3 %stats_near.1 = (f32[1,768]{1,0:T(1,128)}, f32[1,768]{1,0:T(1,128)}, f32[128,768]{1,0:T(8,128)}, s32[1,384]{1,0:T(1,128)}) custom-call(s32[1]{0:T(128)} %bitcast.3.refs_0_.own_ref, s32[1,384]{1,0:T(1,128)} %broadcast_in_dim.8.refs_1_, bf16[384,256]{1,0:T(8,128)(2,1)} %refs_1_.6, bf16[400,256]{1,0:T(8,128)(2,1)} %copy-done.3, bf16[400,256]{1,0:T(8,128)(2,1)} %copy-done.5, ...), custom_call_target="tpu_custom_call" | custom-call | tf_op jit(solution)/shard_map/stats_near/pallas_call | solution.py:284
  83.3 0.7 copy-done.10
  84.1 5.8 %stats_far.1 = (f32[1,768]{1,0:T(1,128)}, f32[128,768]{1,0:T(8,128)}, s32[1,384]{1,0:T(1,128)}, s32[1]{0:T(128)}) custom-call(s32[1]{0:T(128)} %bitcast.3.refs_0_.own_ref, s32[1,384]{1,0:T(1,128)} %broadcast_in_dim.8.refs_1_, bf16[384,256]{1,0:T(8,128)(2,1)} %refs_1_.6, f32[1,768]{1,0:T(1,128)} %get-tuple-element.42.refs_3_, ...), custom_call_target="tpu_custom_call" | custom-call | tf_op jit(solution)/shard_map/stats_far/pallas_call | solution.py:284
  89.9 12.5 %attention_grads.1 = (bf16[256,384]{1,0:T(8,128)(2,1)}, bf16[5,384,256]{2,1,0:T(8,128)(2,1)}, bf16[5,384,256]{2,1,0:T(8,128)(2,1)}) custom-call(s32[1]{0:T(128)} %bitcast.3.refs_0_.own_ref, s32[1]{0:T(128)} %get-tuple-element.46.low_ref, s32[1,384]{1,0:T(1,128)} %get-tuple-element.47.refs_0_, bf16[384,256]{1,0:T(8,128)(2,1)} %refs_1_.6, ...), custom_call_target="tpu_custom_call" | custom-call | tf_op jit(solution)/shard_map/attention_grads/pallas_call | solution.py:298
  102.4 1.9 collective-permute-start.21
  104.3 0.9 collective-permute-start.28
  105.3 2.8 %collective-permute-start.29 = (bf16[2,336,512]{2,1,0:T(8,128)(2,1)S(1)}, bf16[2,336,512]{2,1,0:T(8,128)(2,1)S(1)}, u32[]{:S(2)}, u32[]{:S(2)}) collective-permute-start(bf16[2,336,512]{2,1,0:T(8,128)(2,1)S(1)} %pad_maximum_fusion.1), channel_id=1, source_target_pairs={{0,1},{1,0},{2,3},{3,2},{4,5},{5,4},{6,7},{7,6},{8,9},{9,8},{10,11... | collective-permute-start | bytes 2064392 | tf_op jit(solution)/shard_map/ppermute | solution.py:558
  108.1 16.1 %collective-permute-done.28.refs_5_.refs_2_.refs_6_ = bf16[2,336,512]{2,1,0:T(8,128)(2,1)S(1)} collective-permute-done((bf16[2,336,512]{2,1,0:T(8,128)(2,1)S(1)}, bf16[2,336,512]{2,1,0:T(8,128)(2,1)S(1)}, u32[]{:S(2)}, u32[]{:S(2)}) %collective-permute-start.28) | collective-permute-done | bytes 688160 | tf_op jit(solution)/shard_map/ppermute | solution.py:558
  124.2 13.8 %collective-permute-done.29.refs_6_.refs_3_.refs_7_ = bf16[2,336,512]{2,1,0:T(8,128)(2,1)S(1)} collective-permute-done((bf16[2,336,512]{2,1,0:T(8,128)(2,1)S(1)}, bf16[2,336,512]{2,1,0:T(8,128)(2,1)S(1)}, u32[]{:S(2)}, u32[]{:S(2)}) %collective-permute-start.29) | collective-permute-done | bytes 688160 | tf_op jit(solution)/shard_map/ppermute | solution.py:558
  138.1 2.6 %join_partials.1 = (f32[384,256]{1,0:T(8,128)}, bf16[384,256]{1,0:T(8,128)(2,1)}, bf16[384,256]{1,0:T(8,128)(2,1)}, bf16[384,256]{1,0:T(8,128)(2,1)}, bf16[384,2...) custom-call(s32[1]{0:T(128)} %bitcast.2.core_ref, bf16[5,384,256]{2,1,0:T(8,128)(2,1)} %get-tuple-element.52.mine_ref, ...), custom_call_target="tpu_custom_call" | custom-call | tf_op jit(solution)/shard_map/join_partials/pallas_call | solution.py:442
  140.7 0.7 collective-permute-start.22
  141.4 1.3 collective-permute-start.23
  142.7 1.9 collective-permute-start.24
  144.6 1.9 collective-permute-start.25
  146.5 4.0 %collective-permute-done.23.refs_1_ = bf16[384,256]{1,0:T(8,128)(2,1)S(1)} collective-permute-done((bf16[384,256]{1,0:T(8,128)(2,1)}, bf16[384,256]{1,0:T(8,128)(2,1)S(1)}, u32[]{:S(2)}, u32[]{:S(2)}) %collective-permute-start.23) | collective-permute-done | bytes 196640 | tf_op jit(solution)/shard_map/ppermute | solution.py:570
  150.5 1.9 collective-permute-start.26
  152.4 0.4 collective-permute-done.24.refs_2_
  152.8 0.8 collective-permute-start.32
  153.6 3.3 %collective-permute-done.25.refs_3_ = bf16[384,256]{1,0:T(8,128)(2,1)S(1)} collective-permute-done((bf16[384,256]{1,0:T(8,128)(2,1)}, bf16[384,256]{1,0:T(8,128)(2,1)S(1)}, u32[]{:S(2)}, u32[]{:S(2)}) %collective-permute-start.25) | collective-permute-done | bytes 196640 | tf_op jit(solution)/shard_map/ppermute | solution.py:570
  156.9 7.1 %collective-permute-done.26.refs_4_ = bf16[384,256]{1,0:T(8,128)(2,1)S(1)} collective-permute-done((bf16[384,256]{1,0:T(8,128)(2,1)}, bf16[384,256]{1,0:T(8,128)(2,1)S(1)}, u32[]{:S(2)}, u32[]{:S(2)}) %collective-permute-start.26) | collective-permute-done | bytes 196640 | tf_op jit(solution)/shard_map/ppermute | solution.py:570
  164.0 0.7 copy-done.34
  164.7 2.2 %total_partials.1.refs_3_ = bf16[256,384]{1,0:T(8,128)(2,1)} custom-call(f32[384,256]{1,0:T(8,128)} %get-tuple-element.54.own_ref, bf16[384,256]{1,0:T(8,128)(2,1)} %copy-done.30, bf16[384,256]{1,0:T(8,128)(2,1)} %copy-done.31, bf16[384,256]{1,0:T(8,128)(2,1)} %copy-done.32, bf16[384,256]{1,0:T(8,128)(2,1)} %copy-done.33, bf16[384,256]{1,0:T(8,128)(2,1)} %copy-done.34), custom_call_target="tpu_custom_call" | custom-call | tf_op jit(solution)/shard_map/total_partials/pallas_call | solution.py:460
  166.9 2.1 collective-permute-start.27
  169.0 5.1 %project.4 = (f32[336,384]{1,0:T(8,128)}, f32[336,384]{1,0:T(8,128)}, f32[336,384]{1,0:T(8,128)}, f32[336,384]{1,0:T(8,128)}, f32[336,384]{1,0:T(8,128)}, /*inde...) custom-call(s32[3]{0:T(128)} %pad_add_fusion.at_ref.refs_0_, bf16[5376,256]{1,0:T(8,128)(2,1)} %refs_1_.7, ...), custom_call_target="tpu_custom_call" | custom-call | tf_op jit(solution)/shard_map/project/pallas_call | solution.py:535
  174.2 3.7 %project.5 = (f32[336,384]{1,0:T(8,128)}, f32[336,384]{1,0:T(8,128)}) custom-call(s32[3]{0:T(128)} %pad_add_fusion.at_ref.refs_0_, bf16[5376,128]{1,0:T(8,128)(2,1)} %refs_1_.9, bf16[5376,128]{1,0:T(8,128)(2,1)} %refs_2_.7, bf16[256,384]{1,0:T(8,128)(2,1)} %total_partials.1.refs_3_, bf16[256,384]{1,0:T(8,128)(2,1)S(1)} %collective-permute-done.32.refs_4_, ...), custom_call_target="tpu_custom_call" | custom-call | tf_op jit(solution)/shard_map/project/pallas_call | solution.py:535
  177.9 3.3 %project.6 = (bf16[336,384]{1,0:T(8,128)(2,1)}, bf16[336,384]{1,0:T(8,128)(2,1)}) custom-call(s32[3]{0:T(128)} %pad_add_fusion.at_ref.refs_0_, bf16[256,384]{1,0:T(8,128)(2,1)S(1)} %collective-permute-done.27.refs_1_.refs_5_, bf16[2,336,512]{2,1,0:T(8,128)(2,1)} %copy-done, bf16[2,336,512]{2,1,0:T(8,128)(2,1)} %copy-done.1, ...), custom_call_target="tpu_custom_call" | custom-call | tf_op jit(solution)/shard_map/project/pallas_call | solution.py:535
  181.3 3.2 %collective-permute-start.37 = (bf16[336,384]{1,0:T(8,128)(2,1)}, bf16[336,384]{1,0:T(8,128)(2,1)S(1)}, u32[]{:S(2)}, u32[]{:S(2)}) collective-permute-start(bf16[336,384]{1,0:T(8,128)(2,1)} %get-tuple-element.75), channel_id=1, source_target_pairs={{0,14},{2,0},{4,2},{6,4},{8,6},{10,8},{12,10},{14,12},{1,15},{3,1}... | collective-permute-start | bytes 774152 | tf_op jit(solution)/shard_map/ppermute | solution.py:574
  184.5 6.2 %project.7 = (f32[336,384]{1,0:T(8,128)}, f32[336,384]{1,0:T(8,128)}, f32[336,384]{1,0:T(8,128)}, f32[336,384]{1,0:T(8,128)}, f32[336,384]{1,0:T(8,128)}, /*index=5*/f32[336,384]{1,0:T(8,128)}) custom-call(s32[3]{0:T(128)} %pad_add_fusion.at_ref.refs_0_, bf16[5376,128]{1,0:T(8,128)(2,1)} %refs_1_.9, bf16[5376,128]{1,0:T(8,128)(2,1)} %refs_2_.7, ...), custom_call_target="tpu_custom_call" | custom-call | tf_op jit(solution)/shard_map/project/pallas_call | solution.py:535
  190.8 1.2 add_convert_fusion.5
  192.0 0.1 collective-permute-start.34
  192.2 3.3 %collective-permute-start.38 = (bf16[336,384]{1,0:T(8,128)(2,1)S(1)}, bf16[336,384]{1,0:T(8,128)(2,1)S(1)}, u32[]{:S(2)}, u32[]{:S(2)}) collective-permute-start(bf16[336,384]{1,0:T(8,128)(2,1)S(1)} %add_convert_fusion.2), channel_id=1, source_target_pairs={{0,14},{2,0},{4,2},{6,4},{8,6},{10,8},{12,10},{14,12},{1,15},{3,1}... | collective-permute-start | bytes 774152 | tf_op jit(solution)/shard_map/ppermute | solution.py:574
  195.5 4.4 %collective-permute-done.34 = bf16[336,384]{1,0:T(8,128)(2,1)S(1)} collective-permute-done((bf16[336,384]{1,0:T(8,128)(2,1)S(1)}, bf16[336,384]{1,0:T(8,128)(2,1)S(1)}, u32[]{:S(2)}, u32[]{:S(2)}) %collective-permute-start.34) | collective-permute-done | bytes 258080 | tf_op jit(solution)/shard_map/ppermute | solution.py:574
  200.2 3.3 %collective-permute-start.39 = (bf16[336,384]{1,0:T(8,128)(2,1)S(1)}, bf16[336,384]{1,0:T(8,128)(2,1)S(1)}, u32[]{:S(2)}, u32[]{:S(2)}) collective-permute-start(bf16[336,384]{1,0:T(8,128)(2,1)S(1)} %add_convert_fusion.1), channel_id=1, source_target_pairs={{0,14},{2,0},{4,2},{6,4},{8,6},{10,8},{12,10},{14,12},{1,15},{3,1}... | collective-permute-start | bytes 774152 | tf_op jit(solution)/shard_map/ppermute | solution.py:574
  203.5 4.2 %collective-permute-done.35 = bf16[336,384]{1,0:T(8,128)(2,1)S(1)} collective-permute-done((bf16[336,384]{1,0:T(8,128)(2,1)S(1)}, bf16[336,384]{1,0:T(8,128)(2,1)S(1)}, u32[]{:S(2)}, u32[]{:S(2)}) %collective-permute-start.35) | collective-permute-done | bytes 258080 | tf_op jit(solution)/shard_map/ppermute | solution.py:574
  207.8 7.5 %collective-permute-done.36 = bf16[336,384]{1,0:T(8,128)(2,1)S(1)} collective-permute-done((bf16[336,384]{1,0:T(8,128)(2,1)S(1)}, bf16[336,384]{1,0:T(8,128)(2,1)S(1)}, u32[]{:S(2)}, u32[]{:S(2)}) %collective-permute-start.36) | collective-permute-done | bytes 258080 | tf_op jit(solution)/shard_map/ppermute | solution.py:574
  215.3 0.8 fusion.1
  (117 shorter events, 1.0 us)
Async XLA Ops:
  0.6 30.5 %copy-start.37 = (s32[384]{0:T(512)S(1)}, s32[384]{0:T(512)}, u32[]{:S(2)}) copy-start(s32[384]{0:T(512)} %param.13) | copy-start | bytes 4612
  0.6 40.3 %copy-start.35 = (bf16[384,128]{1,0:T(8,128)(2,1)S(1)}, bf16[384,128]{1,0:T(8,128)(2,1)}, u32[]{:S(2)}) copy-start(bf16[384,128]{1,0:T(8,128)(2,1)} %param.11) | copy-start | bytes 294916
  0.6 40.3 %copy-start.36 = (bf16[384,128]{1,0:T(8,128)(2,1)S(1)}, bf16[384,128]{1,0:T(8,128)(2,1)}, u32[]{:S(2)}) copy-start(bf16[384,128]{1,0:T(8,128)(2,1)} %param.10) | copy-start | bytes 294916
  4.1 21.1 %collective-permute-start.11 = (bf16[4,256,384]{2,1,0:T(8,128)(2,1)}, bf16[4,256,384]{2,1,0:T(8,128)(2,1)S(1)}, u32[]{:S(2)}, u32[]{:S(2)}) collective-permute-start(bf16[4,256,384]{2,1,0:T(8,128)(2,1)} %split_w_out.1), channel_id=1, source_target_pairs={{0,1},{1,0},{2,3},{3,2},{4,5},{5,4},{6,7},{7,6},{8,9},{9,8},{10,11... | collective-permute-start | bytes 2359304 | tf_op jit(solution)/shard_map/ppermute | solution.py:558
  7.2 11.8 %collective-permute-start.13 = (bf16[336,384]{1,0:T(8,128)(2,1)S(1)}, bf16[336,384]{1,0:T(8,128)(2,1)S(1)}, u32[]{:S(2)}, u32[]{:S(2)}) collective-permute-start(bf16[336,384]{1,0:T(8,128)(2,1)S(1)} %bitcast.40), channel_id=1, source_target_pairs={{0,2},{2,4},{4,6},{6,8},{8,10},{10,12},{12,14},{14,0},{1,3},{3,5},... | collective-permute-start | bytes 774152 | tf_op jit(solution)/shard_map/ppermute | solution.py:574
  9.1 16.1 %collective-permute-start.14 = (bf16[336,384]{1,0:T(8,128)(2,1)S(1)}, bf16[336,384]{1,0:T(8,128)(2,1)S(1)}, u32[]{:S(2)}, u32[]{:S(2)}) collective-permute-start(bf16[336,384]{1,0:T(8,128)(2,1)S(1)} %bitcast.41), channel_id=1, source_target_pairs={{0,14},{2,0},{4,2},{6,4},{8,6},{10,8},{12,10},{14,12},{1,15},{3,1}... | collective-permute-start | bytes 774152 | tf_op jit(solution)/shard_map/ppermute | solution.py:574
  19.0 43.7 %copy-start.22 = (bf16[336,384]{1,0:T(8,128)(2,1)}, bf16[336,384]{1,0:T(8,128)(2,1)S(1)}, u32[]{:S(2)}) copy-start(bf16[336,384]{1,0:T(8,128)(2,1)S(1)} %collective-permute-done.13.refs_5_) | copy-start | bytes 774148
  19.0 12.1 %collective-permute-start.15 = (bf16[336,384]{1,0:T(8,128)(2,1)S(1)}, bf16[336,384]{1,0:T(8,128)(2,1)S(1)}, u32[]{:S(2)}, u32[]{:S(2)}) collective-permute-start(bf16[336,384]{1,0:T(8,128)(2,1)S(1)} %collective-permute-done.13.refs_5_), channel_id=1, source_target_pairs={{0,2},{2,4},{4,6},{6,8},{8,10},{10,12},{12,14},{14,0},{1,3},{3,5},... | collective-permute-start | bytes 774152 | tf_op jit(solution)/shard_map/ppermute | solution.py:574
  25.2 37.5 %copy-start.13 = (bf16[4,256,384]{2,1,0:T(8,128)(2,1)}, bf16[4,256,384]{2,1,0:T(8,128)(2,1)S(1)}, u32[]{:S(2)}) copy-start(bf16[4,256,384]{2,1,0:T(8,128)(2,1)S(1)} %collective-permute-done.11.refs_2_) | copy-start | bytes 2359300
  25.2 36.1 %collective-permute-start.12 = (bf16[4,256,384]{2,1,0:T(8,128)(2,1)S(1)}, bf16[4,256,384]{2,1,0:T(8,128)(2,1)S(1)}, u32[]{:S(2)}, u32[]{:S(2)}) collective-permute-start(bf16[4,256,384]{2,1,0:T(8,128)(2,1)S(1)} %collective-permute-done.11.refs_2_), channel_id=1, source_target_pairs={{0,16},{16,0},{1,17},{17,1},{2,18},{18,2},{3,19},{19,3},{4,20},{20... | collective-permute-start | bytes 2359304 | tf_op jit(solution)/shard_map/ppermute | solution.py:558
  25.2 37.5 %copy-start.23 = (bf16[336,384]{1,0:T(8,128)(2,1)}, bf16[336,384]{1,0:T(8,128)(2,1)S(1)}, u32[]{:S(2)}) copy-start(bf16[336,384]{1,0:T(8,128)(2,1)S(1)} %collective-permute-done.14.refs_6_) | copy-start | bytes 774148
  25.2 12.0 %collective-permute-start.16 = (bf16[336,384]{1,0:T(8,128)(2,1)S(1)}, bf16[336,384]{1,0:T(8,128)(2,1)S(1)}, u32[]{:S(2)}, u32[]{:S(2)}) collective-permute-start(bf16[336,384]{1,0:T(8,128)(2,1)S(1)} %collective-permute-done.14.refs_6_), channel_id=1, source_target_pairs={{0,14},{2,0},{4,2},{6,4},{8,6},{10,8},{12,10},{14,12},{1,15},{3,1}... | collective-permute-start | bytes 774152 | tf_op jit(solution)/shard_map/ppermute | solution.py:574
  31.1 31.6 %copy-start.24 = (bf16[336,384]{1,0:T(8,128)(2,1)}, bf16[336,384]{1,0:T(8,128)(2,1)S(1)}, u32[]{:S(2)}) copy-start(bf16[336,384]{1,0:T(8,128)(2,1)S(1)} %collective-permute-done.15.refs_7_) | copy-start | bytes 774148
  31.1 9.8 %collective-permute-start.17 = (bf16[336,384]{1,0:T(8,128)(2,1)S(1)}, bf16[336,384]{1,0:T(8,128)(2,1)S(1)}, u32[]{:S(2)}, u32[]{:S(2)}) collective-permute-start(bf16[336,384]{1,0:T(8,128)(2,1)S(1)} %collective-permute-done.15.refs_7_), channel_id=1, source_target_pairs={{0,2},{2,4},{4,6},{6,8},{8,10},{10,12},{12,14},{14,0},{1,3},{3,5},... | collective-permute-start | bytes 774152 | tf_op jit(solution)/shard_map/ppermute | solution.py:574
  37.2 25.5 %copy-start.25 = (bf16[336,384]{1,0:T(8,128)(2,1)}, bf16[336,384]{1,0:T(8,128)(2,1)S(1)}, u32[]{:S(2)}) copy-start(bf16[336,384]{1,0:T(8,128)(2,1)S(1)} %collective-permute-done.16.refs_8_) | copy-start | bytes 774148
  37.2 21.4 %collective-permute-start.18 = (bf16[336,384]{1,0:T(8,128)(2,1)S(1)}, bf16[336,384]{1,0:T(8,128)(2,1)S(1)}, u32[]{:S(2)}, u32[]{:S(2)}) collective-permute-start(bf16[336,384]{1,0:T(8,128)(2,1)S(1)} %collective-permute-done.16.refs_8_), channel_id=1, source_target_pairs={{0,14},{2,0},{4,2},{6,4},{8,6},{10,8},{12,10},{14,12},{1,15},{3,1}... | collective-permute-start | bytes 774152 | tf_op jit(solution)/shard_map/ppermute | solution.py:574
  40.9 21.8 %copy-start.26 = (bf16[336,384]{1,0:T(8,128)(2,1)}, bf16[336,384]{1,0:T(8,128)(2,1)S(1)}, u32[]{:S(2)}) copy-start(bf16[336,384]{1,0:T(8,128)(2,1)S(1)} %collective-permute-done.17.refs_9_) | copy-start | bytes 774148
  40.9 19.0 %collective-permute-start.19 = (bf16[336,384]{1,0:T(8,128)(2,1)S(1)}, bf16[336,384]{1,0:T(8,128)(2,1)S(1)}, u32[]{:S(2)}, u32[]{:S(2)}) collective-permute-start(bf16[336,384]{1,0:T(8,128)(2,1)S(1)} %collective-permute-done.17.refs_9_), channel_id=1, source_target_pairs={{0,2},{2,4},{4,6},{6,8},{8,10},{10,12},{12,14},{14,0},{1,3},{3,5},... | collective-permute-start | bytes 774152 | tf_op jit(solution)/shard_map/ppermute | solution.py:574
  41.0 28.0 %copy-start.3 = (bf16[400,256]{1,0:T(8,128)(2,1)}, bf16[400,256]{1,0:T(8,128)(2,1)S(1)}, u32[]{:S(2)}) copy-start(bf16[400,256]{1,0:T(8,128)(2,1)S(1)} %fusion.2.refs_3_.refs_6_) | copy-start | bytes 614404
  41.0 9.7 %collective-permute-start.3 = (bf16[400,256]{1,0:T(8,128)(2,1)S(1)}, bf16[400,256]{1,0:T(8,128)(2,1)S(1)}, u32[]{:S(2)}, u32[]{:S(2)}) collective-permute-start(bf16[400,256]{1,0:T(8,128)(2,1)S(1)} %fusion.2.refs_3_.refs_6_), channel_id=1, source_target_pairs={{0,64},{16,80},{32,96},{48,112},{64,128},{80,144},{96,160},{112,17... | collective-permute-start | bytes 614408 | tf_op jit(solution)/shard_map/ppermute | solution.py:566
  45.0 8.1 %collective-permute-start = (bf16[400,256]{1,0:T(8,128)(2,1)S(1)}, bf16[400,256]{1,0:T(8,128)(2,1)S(1)}, u32[]{:S(2)}, u32[]{:S(2)}) collective-permute-start(bf16[400,256]{1,0:T(8,128)(2,1)S(1)} %fusion.2.refs_3_.refs_6_), channel_id=1, source_target_pairs={{0,32},{16,48},{32,64},{48,80},{64,96},{80,112},{96,128},{112,144}... | collective-permute-start | bytes 614408 | tf_op jit(solution)/shard_map/ppermute | solution.py:566
  50.6 18.4 %copy-start.4 = (bf16[400,256]{1,0:T(8,128)(2,1)}, bf16[400,256]{1,0:T(8,128)(2,1)S(1)}, u32[]{:S(2)}) copy-start(bf16[400,256]{1,0:T(8,128)(2,1)S(1)} %collective-permute-done.3.refs_7_.refs_8_) | copy-start | bytes 614404
  50.6 18.4 %collective-permute-start.1 = (bf16[400,256]{1,0:T(8,128)(2,1)S(1)}, bf16[400,256]{1,0:T(8,128)(2,1)S(1)}, u32[]{:S(2)}, u32[]{:S(2)}) collective-permute-start(bf16[400,256]{1,0:T(8,128)(2,1)S(1)} %fusion.2.refs_3_.refs_6_), channel_id=1, source_target_pairs={{0,16},{16,0},{1,17},{17,1},{2,18},{18,2},{3,19},{19,3},{4,20},{20... | collective-permute-start | bytes 614408 | tf_op jit(solution)/shard_map/ppermute | solution.py:558
  53.2 15.8 %copy-start.5 = (bf16[400,256]{1,0:T(8,128)(2,1)}, bf16[400,256]{1,0:T(8,128)(2,1)S(1)}, u32[]{:S(2)}) copy-start(bf16[400,256]{1,0:T(8,128)(2,1)S(1)} %collective-permute-done.refs_4_.refs_7_) | copy-start | bytes 614404
  53.2 16.4 %collective-permute-start.5 = (bf16[400,256]{1,0:T(8,128)(2,1)S(1)}, bf16[400,256]{1,0:T(8,128)(2,1)S(1)}, u32[]{:S(2)}, u32[]{:S(2)}) collective-permute-start(bf16[400,256]{1,0:T(8,128)(2,1)S(1)} %fusion.2.refs_3_.refs_6_), channel_id=1, source_target_pairs={{0,96},{16,112},{32,128},{48,144},{64,160},{80,176},{96,192},{112,... | collective-permute-start | bytes 614408 | tf_op jit(solution)/shard_map/ppermute | solution.py:566
  58.6 11.1 %collective-permute-start.6 = (bf16[400,256]{1,0:T(8,128)(2,1)S(1)}, bf16[400,256]{1,0:T(8,128)(2,1)S(1)}, u32[]{:S(2)}, u32[]{:S(2)}) collective-permute-start(bf16[400,256]{1,0:T(8,128)(2,1)S(1)} %fusion.2.refs_3_.refs_6_), channel_id=1, source_target_pairs={{0,128},{16,144},{32,160},{48,176},{64,192},{80,208},{96,224},{112... | collective-permute-start | bytes 614408 | tf_op jit(solution)/shard_map/ppermute | solution.py:566
  59.9 10.2 %collective-permute-start.9 = (bf16[400,256]{1,0:T(8,128)(2,1)S(1)}, bf16[400,256]{1,0:T(8,128)(2,1)}, u32[]{:S(2)}, u32[]{:S(2)}) collective-permute-start(bf16[400,256]{1,0:T(8,128)(2,1)S(1)} %fusion.2.refs_3_.refs_6_), channel_id=1, source_target_pairs={{16,176},{48,208},{80,240},{17,177},{49,209},{81,241},{18,178},{50... | collective-permute-start | bytes 614408 | tf_op jit(solution)/shard_map/ppermute | solution.py:566
  62.2 8.1 %collective-permute-start.4 = (bf16[400,256]{1,0:T(8,128)(2,1)S(1)}, bf16[400,256]{1,0:T(8,128)(2,1)S(1)}, u32[]{:S(2)}, u32[]{:S(2)}) collective-permute-start(bf16[400,256]{1,0:T(8,128)(2,1)S(1)} %collective-permute-done.3.refs_7_.refs_8_), channel_id=1, source_target_pairs={{0,16},{16,0},{1,17},{17,1},{2,18},{18,2},{3,19},{19,3},{4,20},{20... | collective-permute-start | bytes 614408 | tf_op jit(solution)/shard_map/ppermute | solution.py:558
  69.0 7.2 %copy-start.6 = (bf16[400,256]{1,0:T(8,128)(2,1)}, bf16[400,256]{1,0:T(8,128)(2,1)S(1)}, u32[]{:S(2)}) copy-start(bf16[400,256]{1,0:T(8,128)(2,1)S(1)} %collective-permute-done.1.refs_5_.refs_11_) | copy-start | bytes 614404
  69.0 7.2 %collective-permute-start.2 = (bf16[400,256]{1,0:T(8,128)(2,1)S(1)}, bf16[400,256]{1,0:T(8,128)(2,1)S(1)}, u32[]{:S(2)}, u32[]{:S(2)}) collective-permute-start(bf16[400,256]{1,0:T(8,128)(2,1)S(1)} %collective-permute-done.refs_4_.refs_7_), channel_id=1, source_target_pairs={{0,16},{16,0},{1,17},{17,1},{2,18},{18,2},{3,19},{19,3},{4,20},{20... | collective-permute-start | bytes 614408 | tf_op jit(solution)/shard_map/ppermute | solution.py:558
  69.6 13.6 %collective-permute-start.7 = (bf16[400,256]{1,0:T(8,128)(2,1)S(1)}, bf16[400,256]{1,0:T(8,128)(2,1)S(1)}, u32[]{:S(2)}, u32[]{:S(2)}) collective-permute-start(bf16[400,256]{1,0:T(8,128)(2,1)S(1)} %collective-permute-done.5.refs_8_.refs_9_), channel_id=1, source_target_pairs={{0,16},{16,0},{1,17},{17,1},{2,18},{18,2},{3,19},{19,3},{4,20},{20... | collective-permute-start | bytes 614408 | tf_op jit(solution)/shard_map/ppermute | solution.py:558
  69.8 13.5 %collective-permute-start.8 = (bf16[400,256]{1,0:T(8,128)(2,1)S(1)}, bf16[400,256]{1,0:T(8,128)(2,1)S(1)}, u32[]{:S(2)}, u32[]{:S(2)}) collective-permute-start(bf16[400,256]{1,0:T(8,128)(2,1)S(1)} %collective-permute-done.6.refs_9_.refs_10_), channel_id=1, source_target_pairs={{0,16},{16,0},{1,17},{17,1},{2,18},{18,2},{3,19},{19,3},{4,20},{20... | collective-permute-start | bytes 614408 | tf_op jit(solution)/shard_map/ppermute | solution.py:558
  70.2 13.1 %collective-permute-start.10 = (bf16[400,256]{1,0:T(8,128)(2,1)}, bf16[400,256]{1,0:T(8,128)(2,1)S(1)}, u32[]{:S(2)}, u32[]{:S(2)}) collective-permute-start(bf16[400,256]{1,0:T(8,128)(2,1)} %collective-permute-done.9), channel_id=1, source_target_pairs={{0,16},{16,0},{1,17},{17,1},{2,18},{18,2},{3,19},{19,3},{4,20},{20... | collective-permute-start | bytes 614408 | tf_op jit(solution)/shard_map/ppermute | solution.py:558
  70.3 19.6 %collective-permute-start.20 = (bf16[256,384]{1,0:T(8,128)(2,1)}, bf16[256,384]{1,0:T(8,128)(2,1)S(1)}, u32[]{:S(2)}, u32[]{:S(2)}) collective-permute-start(bf16[256,384]{1,0:T(8,128)(2,1)} %get-tuple-element.49), channel_id=1, source_target_pairs={{0,1},{1,0},{2,3},{3,2},{4,5},{5,4},{6,7},{7,6},{8,9},{9,8},{10,11... | collective-permute-start | bytes 589832 | tf_op jit(solution)/shard_map/ppermute | solution.py:558
  89.9 14.4 %copy-start.15 = (bf16[2,336,128]{2,1,0:T(8,128)(2,1)S(1)}, bf16[2,336,128]{2,1,0:T(8,128)(2,1)}, u32[]{:S(2)}) copy-start(bf16[2,336,128]{2,1,0:T(8,128)(2,1)} %get-tuple-element.85) | copy-start | bytes 516100
  102.4 35.7 %collective-permute-start.21 = (bf16[5,384,256]{2,1,0:T(8,128)(2,1)}, bf16[5,384,256]{2,1,0:T(8,128)(2,1)S(1)}, u32[]{:S(2)}, u32[]{:S(2)}) collective-permute-start(bf16[5,384,256]{2,1,0:T(8,128)(2,1)} %get-tuple-element.53), channel_id=1, source_target_pairs={{0,16},{16,0},{1,17},{17,1},{2,18},{18,2},{3,19},{19,3},{4,20},{20... | collective-permute-start | bytes 2949128 | tf_op jit(solution)/shard_map/ppermute | solution.py:558
  104.3 19.9 %collective-permute-start.28 = (bf16[2,336,512]{2,1,0:T(8,128)(2,1)S(1)}, bf16[2,336,512]{2,1,0:T(8,128)(2,1)S(1)}, u32[]{:S(2)}, u32[]{:S(2)}) collective-permute-start(bf16[2,336,512]{2,1,0:T(8,128)(2,1)S(1)} %pad_maximum_fusion), channel_id=1, source_target_pairs={{0,1},{1,0},{2,3},{3,2},{4,5},{5,4},{6,7},{7,6},{8,9},{9,8},{10,11... | collective-permute-start | bytes 2064392 | tf_op jit(solution)/shard_map/ppermute | solution.py:558
  105.2 47.6 %copy-start.29 = (bf16[256,384]{1,0:T(8,128)(2,1)S(1)}, bf16[256,384]{1,0:T(8,128)(2,1)}, u32[]{:S(2)}) copy-start(bf16[256,384]{1,0:T(8,128)(2,1)} %get-tuple-element.60.refs_2_) | copy-start | bytes 589828
  105.3 32.7 %collective-permute-start.29 = (bf16[2,336,512]{2,1,0:T(8,128)(2,1)S(1)}, bf16[2,336,512]{2,1,0:T(8,128)(2,1)S(1)}, u32[]{:S(2)}, u32[]{:S(2)}) collective-permute-start(bf16[2,336,512]{2,1,0:T(8,128)(2,1)S(1)} %pad_maximum_fusion.1), channel_id=1, source_target_pairs={{0,1},{1,0},{2,3},{3,2},{4,5},{5,4},{6,7},{7,6},{8,9},{9,8},{10,11... | collective-permute-start | bytes 2064392 | tf_op jit(solution)/shard_map/ppermute | solution.py:558
  124.2 42.7 %copy-start = (bf16[2,336,512]{2,1,0:T(8,128)(2,1)}, bf16[2,336,512]{2,1,0:T(8,128)(2,1)S(1)}, u32[]{:S(2)}) copy-start(bf16[2,336,512]{2,1,0:T(8,128)(2,1)S(1)} %collective-permute-done.28.refs_5_.refs_2_.refs_6_) | copy-start | bytes 2064388
  124.2 49.9 %collective-permute-start.30 = (bf16[2,336,512]{2,1,0:T(8,128)(2,1)S(1)}, bf16[2,336,512]{2,1,0:T(8,128)(2,1)}, u32[]{:S(2)}, u32[]{:S(2)}) collective-permute-start(bf16[2,336,512]{2,1,0:T(8,128)(2,1)S(1)} %collective-permute-done.28.refs_5_.refs_2_.refs_6_), channel_id=1, source_target_pairs={{0,16},{16,0},{1,17},{17,1},{2,18},{18,2},{3,19},{19,3},{4,20},{20... | collective-permute-start | bytes 2064392 | tf_op jit(solution)/shard_map/ppermute | solution.py:558
  138.0 28.9 %copy-start.1 = (bf16[2,336,512]{2,1,0:T(8,128)(2,1)}, bf16[2,336,512]{2,1,0:T(8,128)(2,1)S(1)}, u32[]{:S(2)}) copy-start(bf16[2,336,512]{2,1,0:T(8,128)(2,1)S(1)} %collective-permute-done.29.refs_6_.refs_3_.refs_7_) | copy-start | bytes 2064388
  138.0 36.1 %collective-permute-start.31 = (bf16[2,336,512]{2,1,0:T(8,128)(2,1)S(1)}, bf16[2,336,512]{2,1,0:T(8,128)(2,1)}, u32[]{:S(2)}, u32[]{:S(2)}) collective-permute-start(bf16[2,336,512]{2,1,0:T(8,128)(2,1)S(1)} %collective-permute-done.29.refs_6_.refs_3_.refs_7_), channel_id=1, source_target_pairs={{0,16},{16,0},{1,17},{17,1},{2,18},{18,2},{3,19},{19,3},{4,20},{20... | collective-permute-start | bytes 2064392 | tf_op jit(solution)/shard_map/ppermute | solution.py:558
  140.7 3.9 %collective-permute-start.22 = (bf16[384,256]{1,0:T(8,128)(2,1)}, bf16[384,256]{1,0:T(8,128)(2,1)S(1)}, u32[]{:S(2)}, u32[]{:S(2)}) collective-permute-start(bf16[384,256]{1,0:T(8,128)(2,1)} %get-tuple-element.55), channel_id=1, source_target_pairs={{176,16},{208,48},{240,80},{177,17},{209,49},{241,81},{178,18},{21... | collective-permute-start | bytes 589832 | tf_op jit(solution)/shard_map/ppermute | solution.py:570
  141.4 9.2 %collective-permute-start.23 = (bf16[384,256]{1,0:T(8,128)(2,1)}, bf16[384,256]{1,0:T(8,128)(2,1)S(1)}, u32[]{:S(2)}, u32[]{:S(2)}) collective-permute-start(bf16[384,256]{1,0:T(8,128)(2,1)} %get-tuple-element.56), channel_id=1, source_target_pairs={{128,0},{144,16},{160,32},{176,48},{192,64},{208,80},{224,96},{240... | collective-permute-start | bytes 589832 | tf_op jit(solution)/shard_map/ppermute | solution.py:570
  142.7 10.2 %collective-permute-start.24 = (bf16[384,256]{1,0:T(8,128)(2,1)}, bf16[384,256]{1,0:T(8,128)(2,1)S(1)}, u32[]{:S(2)}, u32[]{:S(2)}) collective-permute-start(bf16[384,256]{1,0:T(8,128)(2,1)} %get-tuple-element.57), channel_id=1, source_target_pairs={{96,0},{112,16},{128,32},{144,48},{160,64},{176,80},{192,96},{208,... | collective-permute-start | bytes 589832 | tf_op jit(solution)/shard_map/ppermute | solution.py:570
  144.6 19.4 %copy-start.30 = (bf16[384,256]{1,0:T(8,128)(2,1)}, bf16[384,256]{1,0:T(8,128)(2,1)S(1)}, u32[]{:S(2)}) copy-start(bf16[384,256]{1,0:T(8,128)(2,1)S(1)} %collective-permute-done.22.refs_0_) | copy-start | bytes 589828
  144.6 12.3 %collective-permute-start.25 = (bf16[384,256]{1,0:T(8,128)(2,1)}, bf16[384,256]{1,0:T(8,128)(2,1)S(1)}, u32[]{:S(2)}, u32[]{:S(2)}) collective-permute-start(bf16[384,256]{1,0:T(8,128)(2,1)} %get-tuple-element.58), channel_id=1, source_target_pairs={{64,0},{80,16},{96,32},{112,48},{128,64},{144,80},{160,96},{176,11... | collective-permute-start | bytes 589832 | tf_op jit(solution)/shard_map/ppermute | solution.py:570
  150.5 13.5 %copy-start.31 = (bf16[384,256]{1,0:T(8,128)(2,1)}, bf16[384,256]{1,0:T(8,128)(2,1)S(1)}, u32[]{:S(2)}) copy-start(bf16[384,256]{1,0:T(8,128)(2,1)S(1)} %collective-permute-done.23.refs_1_) | copy-start | bytes 589828
  150.5 13.5 %collective-permute-start.26 = (bf16[384,256]{1,0:T(8,128)(2,1)}, bf16[384,256]{1,0:T(8,128)(2,1)S(1)}, u32[]{:S(2)}, u32[]{:S(2)}) collective-permute-start(bf16[384,256]{1,0:T(8,128)(2,1)} %get-tuple-element.59), channel_id=1, source_target_pairs={{32,0},{48,16},{64,32},{80,48},{96,64},{112,80},{128,96},{144,112}... | collective-permute-start | bytes 589832 | tf_op jit(solution)/shard_map/ppermute | solution.py:570
  152.8 11.2 %copy-start.32 = (bf16[384,256]{1,0:T(8,128)(2,1)}, bf16[384,256]{1,0:T(8,128)(2,1)S(1)}, u32[]{:S(2)}) copy-start(bf16[384,256]{1,0:T(8,128)(2,1)S(1)} %collective-permute-done.24.refs_2_) | copy-start | bytes 589828
  152.8 21.4 %collective-permute-start.32 = (bf16[256,384]{1,0:T(8,128)(2,1)S(1)}, bf16[256,384]{1,0:T(8,128)(2,1)S(1)}, u32[]{:S(2)}, u32[]{:S(2)}) collective-permute-start(bf16[256,384]{1,0:T(8,128)(2,1)S(1)} %copy-done.29), channel_id=1, source_target_pairs={{0,1},{1,0},{2,3},{3,2},{4,5},{5,4},{6,7},{7,6},{8,9},{9,8},{10,11... | collective-permute-start | bytes 589832 | tf_op jit(solution)/shard_map/ppermute | solution.py:558
  166.9 11.0 %collective-permute-start.27 = (bf16[256,384]{1,0:T(8,128)(2,1)}, bf16[256,384]{1,0:T(8,128)(2,1)S(1)}, u32[]{:S(2)}, u32[]{:S(2)}) collective-permute-start(bf16[256,384]{1,0:T(8,128)(2,1)} %total_partials.1.refs_3_), channel_id=1, source_target_pairs={{0,1},{1,0},{2,3},{3,2},{4,5},{5,4},{6,7},{7,6},{8,9},{9,8},{10,11... | collective-permute-start | bytes 589832 | tf_op jit(solution)/shard_map/ppermute | solution.py:558
  181.2 9.6 %collective-permute-start.33 = (bf16[336,384]{1,0:T(8,128)(2,1)}, bf16[336,384]{1,0:T(8,128)(2,1)S(1)}, u32[]{:S(2)}, u32[]{:S(2)}) collective-permute-start(bf16[336,384]{1,0:T(8,128)(2,1)} %get-tuple-element.65), channel_id=1, source_target_pairs={{0,2},{2,4},{4,6},{6,8},{8,10},{10,12},{12,14},{14,0},{1,3},{3,5},... | collective-permute-start | bytes 774152 | tf_op jit(solution)/shard_map/ppermute | solution.py:574
  181.3 10.8 %collective-permute-start.37 = (bf16[336,384]{1,0:T(8,128)(2,1)}, bf16[336,384]{1,0:T(8,128)(2,1)S(1)}, u32[]{:S(2)}, u32[]{:S(2)}) collective-permute-start(bf16[336,384]{1,0:T(8,128)(2,1)} %get-tuple-element.75), channel_id=1, source_target_pairs={{0,14},{2,0},{4,2},{6,4},{8,6},{10,8},{12,10},{14,12},{1,15},{3,1}... | collective-permute-start | bytes 774152 | tf_op jit(solution)/shard_map/ppermute | solution.py:574
  190.8 9.1 %copy-start.19 = (f32[336,384]{1,0:T(8,128)S(1)}, f32[336,384]{1,0:T(8,128)}, u32[]{:S(2)}) copy-start(f32[336,384]{1,0:T(8,128)} %get-tuple-element.73) | copy-start | bytes 1548292
  190.8 9.3 %copy-start.18 = (f32[336,384]{1,0:T(8,128)S(1)}, f32[336,384]{1,0:T(8,128)}, u32[]{:S(2)}) copy-start(f32[336,384]{1,0:T(8,128)} %get-tuple-element.77) | copy-start | bytes 1548292
  192.0 7.9 %collective-permute-start.34 = (bf16[336,384]{1,0:T(8,128)(2,1)S(1)}, bf16[336,384]{1,0:T(8,128)(2,1)S(1)}, u32[]{:S(2)}, u32[]{:S(2)}) collective-permute-start(bf16[336,384]{1,0:T(8,128)(2,1)S(1)} %add_convert_fusion.5), channel_id=1, source_target_pairs={{0,2},{2,4},{4,6},{6,8},{8,10},{10,12},{12,14},{14,0},{1,3},{3,5},... | collective-permute-start | bytes 774152 | tf_op jit(solution)/shard_map/ppermute | solution.py:574
  192.1 15.5 %copy-start.17 = (f32[336,384]{1,0:T(8,128)S(1)}, f32[336,384]{1,0:T(8,128)}, u32[]{:S(2)}) copy-start(f32[336,384]{1,0:T(8,128)} %get-tuple-element.74) | copy-start | bytes 1548292
  192.2 7.9 %collective-permute-start.38 = (bf16[336,384]{1,0:T(8,128)(2,1)S(1)}, bf16[336,384]{1,0:T(8,128)(2,1)S(1)}, u32[]{:S(2)}, u32[]{:S(2)}) collective-permute-start(bf16[336,384]{1,0:T(8,128)(2,1)S(1)} %add_convert_fusion.2), channel_id=1, source_target_pairs={{0,14},{2,0},{4,2},{6,4},{8,6},{10,8},{12,10},{14,12},{1,15},{3,1}... | collective-permute-start | bytes 774152 | tf_op jit(solution)/shard_map/ppermute | solution.py:574
  199.9 15.4 %copy-start.16 = (f32[336,384]{1,0:T(8,128)S(1)}, f32[336,384]{1,0:T(8,128)}, u32[]{:S(2)}) copy-start(f32[336,384]{1,0:T(8,128)} %get-tuple-element.78) | copy-start | bytes 1548292
  200.0 7.6 %collective-permute-start.35 = (bf16[336,384]{1,0:T(8,128)(2,1)S(1)}, bf16[336,384]{1,0:T(8,128)(2,1)S(1)}, u32[]{:S(2)}, u32[]{:S(2)}) collective-permute-start(bf16[336,384]{1,0:T(8,128)(2,1)S(1)} %add_convert_fusion.4), channel_id=1, source_target_pairs={{0,2},{2,4},{4,6},{6,8},{8,10},{10,12},{12,14},{14,0},{1,3},{3,5},... | collective-permute-start | bytes 774152 | tf_op jit(solution)/shard_map/ppermute | solution.py:574
  200.2 7.6 %collective-permute-start.39 = (bf16[336,384]{1,0:T(8,128)(2,1)S(1)}, bf16[336,384]{1,0:T(8,128)(2,1)S(1)}, u32[]{:S(2)}, u32[]{:S(2)}) collective-permute-start(bf16[336,384]{1,0:T(8,128)(2,1)S(1)} %add_convert_fusion.1), channel_id=1, source_target_pairs={{0,14},{2,0},{4,2},{6,4},{8,6},{10,8},{12,10},{14,12},{1,15},{3,1}... | collective-permute-start | bytes 774152 | tf_op jit(solution)/shard_map/ppermute | solution.py:574
  207.7 7.6 %collective-permute-start.36 = (bf16[336,384]{1,0:T(8,128)(2,1)S(1)}, bf16[336,384]{1,0:T(8,128)(2,1)S(1)}, u32[]{:S(2)}, u32[]{:S(2)}) collective-permute-start(bf16[336,384]{1,0:T(8,128)(2,1)S(1)} %add_convert_fusion.3), channel_id=1, source_target_pairs={{0,2},{2,4},{4,6},{6,8},{8,10},{10,12},{12,14},{14,0},{1,3},{3,5},... | collective-permute-start | bytes 774152 | tf_op jit(solution)/shard_map/ppermute | solution.py:574
  (14 other events, 42.6 us)

commit v5 on v4

--- a/solution.py
+++ b/solution.py
@@ -496,9 +496,9 @@
             c.start()
         if far:
             first, size, lane = far
-            part = lax.div(lax.rem(chunk, RING // 2), 2)
+            other_y = lax.rem(lax.div(chunk, 2), 2) != at_ref[3]
             other = lax.div(chunk, RING // 2) != core
-            source = 2 * other.astype(jnp.int32) + part
+            source = 2 * other.astype(jnp.int32) + other_y.astype(jnp.int32)
             for j, ref in enumerate(far_refs):
                 copy = pltpu.make_async_copy(
                     ref.at[lax.rem(chunk, 2), :, first : first + size],
@@ -558,6 +558,10 @@
     return lax.ppermute(x, axis, [(0, 1), (1, 0)])
 
 
+def next_y(x):
+    return lax.ppermute(x, "y", [(0, 1), (1, 0), (2, 3), (3, 2)])
+
+
 def chip_pairs(d):
     return [(i, i + 2 * d) for i in range(lax.axis_size(AA) - 2 * d) if d < HALF or i % 2]
 
@@ -567,7 +571,7 @@
 
 
 def chips_back(x, d):
-    return lax.ppermute(x, AA, [(j, i) for i, j in chip_pairs(d)])
+    return arrive(lax.ppermute(x, AA, [(j, i) for i, j in chip_pairs(d)]))
 
 
 def round_z(x, step):
@@ -579,7 +583,8 @@
     z = lax.axis_index("z")
     xh = lax.axis_index("xh")
     own = lax.axis_index(AA)[None]
-    at = jnp.stack((z, xh, core))
+    pair = lax.axis_index("y") % 2
+    at = jnp.stack((z, xh, core, pair))
     shards = {0: grad_out.T}
     for k in range(1, RING // 2 + 1):
         shards[-k] = round_z(shards[1 - k], 1)
@@ -587,7 +592,7 @@
             shards[k] = round_z(shards[k - 1], -1)
     send_w = split_w_out(at, w_out)
     far_w = swapped(send_w, "xh")
-    far_w = (far_w, swapped(far_w, "core"))
+    far_w = (far_w, arrive(swapped(far_w, "core")))
     ids = jnp.pad(
         segment_ids.astype(BF16).reshape(ROWS // HD, HD),
         ((0, SEG_ROWS - ROWS // HD), (0, HD)),
@@ -595,17 +600,15 @@
     block = jnp.concatenate((jnp.concatenate((keys, values), axis=1), ids), axis=0)
     twins = [block] + [chips_on(block, d) for d in range(1, HALF + 1)]
     others = [swapped(twins[d], "core") for d in range(HALF + 1)]
-    arrivals = []
-    for half in range(2):
-        wanted = [
-            lax.dynamic_index_in_dim(w.reshape(2, 2, 2, 2, FEATS, -1), core, 0, keepdims=False)
-            for w in (w_query, w_key, w_value)
-        ]
-        wanted = [
-            lax.dynamic_index_in_dim(w[half], 1 - xh, 1, keepdims=False) for w in wanted
-        ]
-        wanted = jnp.concatenate(wanted, axis=2)
-        arrivals.append(swapped(wanted, "xh"))
+    wanted = []
+    for w in (w_query, w_key, w_value):
+        w = w.reshape(2, 2, 2, 2, FEATS, -1)
+        w = lax.dynamic_index_in_dim(w, core, 0, keepdims=False)
+        w = lax.dynamic_index_in_dim(w, pair, 0, keepdims=False)
+        wanted.append(lax.dynamic_index_in_dim(w, 1 - xh, 1, keepdims=False))
+    wanted = jnp.concatenate(wanted, axis=2)
+    arrivals = [swapped(wanted, "xh")]
+    arrivals.append(next_y(arrivals[0]))
     far_rows = (*arrivals, *(swapped(arrivals[h], "core") for h in range(2)))
 
     qseg = segment_ids[None, :]
@@ -635,10 +638,12 @@
         deltas[:2], at, (), (), (wide, wide, 0), far_rows,
         (gkvt_far,), first, BF16,
     )
-    rest = project(
-        deltas[2:], at, kv, kv_lanes, (0, 2 * wide, wide), far_rows,
-        (gkvt, gqt_far, gkvt_far), sums[2:], F32,
-    )
+    rest = ()
+    for some in (slice(2, 6), slice(6, 8)):
+        rest += project(
+            deltas[some], at, kv, kv_lanes, (0, 2 * wide, wide), far_rows,
+            (gkvt, gqt_far, gkvt_far), sums[some], F32,
+        )
     ahead = round_z(ahead, 1)
     behind = round_z(behind, -1)
     for k in (2, 3):

time: 217 us -> 203 us (0.935)
  starting transfers between devices: 65.2 us -> 56.5 us
  waiting for transfers between devices: 83 us -> 76 us
  Pallas kernels: 57.5 us -> 60.6 us
    ppermute x16 -> x15, waiting for transfers between devices: 36.1 us -> 0.04 us  [swapped(): return lax.ppermute(x, axis, [(0, 1), (1, 0)])]
    ppermute x5 -> x6, waiting for transfers between devices: 14.7 us -> 35 us  [the longest x5 17.7 us: chips_back(): return arrive(lax.ppermute(x, AA, [(j, i) for i, j in chip_pairs(d)]))]
    ppermute x5, waiting for transfers between devices: 4.05 us -> 19.4 us  [chips_on(): return lax.ppermute(x, AA, chip_pairs(d))]
    ppermute x14, waiting for transfers between devices: 28.1 us -> 21.6 us  [round_z(): return lax.ppermute(x, 'z', [(i, (i + step) % RING) for i in range(RING)])]
    ppermute x5, starting transfers between devices: 16.2 us -> 11.8 us  [chips_on(): return lax.ppermute(x, AA, chip_pairs(d))]
    ppermute x16 -> x15, starting transfers between devices: 15.7 us -> 11.9 us  [swapped(): return lax.ppermute(x, axis, [(0, 1), (1, 0)])]
    pallas_call x4 -> x5, Pallas kernels: 18.4 us -> 21.7 us  [project(): pl.pallas_call(lambda *refs: project_kernel(deltas, own_lanes, far, len(g...]
    ppermute x5 -> x6, starting transfers between devices: 7.7 us -> 8.13 us  [the longest x5 7.97 us: chips_back(): return arrive(lax.ppermute(x, AA, [(j, i) for i, j in chip_pairs(d)]))]
  transfers between devices with their start and end apart: 40 -> 40, of which waited for: 14 -> 14; matrix products, arithmetic and copies ran while one was open for 2% -> 2% of each run, Pallas kernels for 18% -> 27%
where the time goes in v5:
time: 203 us
  waiting for transfers between devices  76 us (37%)
  Pallas kernels  60.6 us (30%)
  starting transfers between devices  56.5 us (28%)
  local copies, waits for them, and re-layouts  4.94 us (2%)
  other arithmetic  3.83 us (2%)
    ppermute x14, starting transfers between devices, round_z(): return lax.ppermute(x, 'z', [(i, (i + step) % RING) for i in range(RING)])  24.6 us
    pallas_call x5, Pallas kernels, project(): pl.pallas_call(lambda *refs: project_kernel(deltas, own_lanes, far, len(g...  21.7 us
    ppermute x14, waiting for transfers between devices, round_z(): return lax.ppermute(x, 'z', [(i, (i + step) % RING) for i in range(RING)])  21.6 us
    ppermute x5, waiting for transfers between devices, chips_on(): return lax.ppermute(x, AA, chip_pairs(d))  19.4 us
    ppermute x5, waiting for transfers between devices, chips_back(): return arrive(lax.ppermute(x, AA, [(j, i) for i, j in chip_pairs(d)]))  17.7 us
    ppermute x1, waiting for transfers between devices, next_y(): return lax.ppermute(x, 'y', [(0, 1), (1, 0), (2, 3), (3, 2)])  17.2 us
    pallas_call x1, Pallas kernels, attention_grads(): pl.pallas_call(grads_kernel, name='attention_grads', out_shape=(jax.Shape...  12.4 us
    pallas_call x2, Pallas kernels, attention_stats(): pl.pallas_call(lambda *refs: stats_kernel(low, high, *refs), name='stats_...  12.1 us
  transfers between devices with their start and end apart: 40, of which 14 were waited for; matrix products, arithmetic and copies ran while one was open for 2% of the time, Pallas kernels for 27%

profile of v5, /device:TPU:24, one launch (start us, length us, event | category | flops | bytes accessed | tf_op | source)
XLA Modules:
  0.0 202.5 jit_solution(3900228154065938673)
XLA Ops:
  0.0 0.7 pad_add_fusion.at_ref.refs_0_
  0.7 3.5 %split_w_out.1 = bf16[4,256,384]{2,1,0:T(8,128)(2,1)} custom-call(s32[4]{0:T(128)} %pad_add_fusion.at_ref.refs_0_, bf16[256,5376]{1,0:T(8,128)(2,1)} %refs_1_.6), custom_call_target="tpu_custom_call" | custom-call | tf_op jit(solution)/shard_map/split_w_out/pallas_call | solution.py:348
  4.1 3.1 %collective-permute-start.11 = (bf16[4,256,384]{2,1,0:T(8,128)(2,1)}, bf16[4,256,384]{2,1,0:T(8,128)(2,1)}, u32[]{:S(2)}, u32[]{:S(2)}) collective-permute-start(bf16[4,256,384]{2,1,0:T(8,128)(2,1)} %split_w_out.1), channel_id=1, source_target_pairs={{0,1},{1,0},{2,3},{3,2},{4,5},{5,4},{6,7},{7,6},{8,9},{9,8},{10,11... | collective-permute-start | bytes 2359304 | tf_op jit(solution)/shard_map/ppermute | solution.py:558
  7.3 1.9 collective-permute-start.13
  9.2 3.2 %collective-permute-start.3 = (bf16[400,256]{1,0:T(8,128)(2,1)S(1)}, bf16[400,256]{1,0:T(8,128)(2,1)S(1)}, u32[]{:S(2)}, u32[]{:S(2)}) collective-permute-start(bf16[400,256]{1,0:T(8,128)(2,1)S(1)} %fusion.2.refs_3_.refs_6_), channel_id=1, source_target_pairs={{0,64},{16,80},{32,96},{48,112},{64,128},{80,144},{96,160},{112,17... | collective-permute-start | bytes 614408 | tf_op jit(solution)/shard_map/ppermute | solution.py:570
  12.4 4.1 %collective-permute-start = (bf16[400,256]{1,0:T(8,128)(2,1)S(1)}, bf16[400,256]{1,0:T(8,128)(2,1)S(1)}, u32[]{:S(2)}, u32[]{:S(2)}) collective-permute-start(bf16[400,256]{1,0:T(8,128)(2,1)S(1)} %fusion.2.refs_3_.refs_6_), channel_id=1, source_target_pairs={{0,32},{16,48},{32,64},{48,80},{64,96},{80,112},{96,128},{112,144}... | collective-permute-start | bytes 614408 | tf_op jit(solution)/shard_map/ppermute | solution.py:570
  16.5 0.1 collective-permute-start.1
  16.6 13.2 %collective-permute-done.3.refs_7_.refs_8_ = bf16[400,256]{1,0:T(8,128)(2,1)S(1)} collective-permute-done((bf16[400,256]{1,0:T(8,128)(2,1)S(1)}, bf16[400,256]{1,0:T(8,128)(2,1)S(1)}, u32[]{:S(2)}, u32[]{:S(2)}) %collective-permute-start.3) | collective-permute-done | bytes 204832 | tf_op jit(solution)/shard_map/ppermute | solution.py:570
  29.8 5.9 %collective-permute-start.14 = (bf16[336,384]{1,0:T(8,128)(2,1)S(1)}, bf16[336,384]{1,0:T(8,128)(2,1)}, u32[]{:S(2)}, u32[]{:S(2)}) collective-permute-start(bf16[336,384]{1,0:T(8,128)(2,1)S(1)} %bitcast.30), channel_id=1, source_target_pairs={{0,14},{2,0},{4,2},{6,4},{8,6},{10,8},{12,10},{14,12},{1,15},{3,1}... | collective-permute-start | bytes 774152 | tf_op jit(solution)/shard_map/ppermute | solution.py:578
  35.7 0.1 collective-permute-start.12
  35.8 1.9 collective-permute-start.5
  37.8 1.3 collective-permute-start.6
  39.1 1.0 dynamic-slice_bitcast_fusion
  40.1 6.3 %collective-permute-done.5.refs_8_.refs_9_ = bf16[400,256]{1,0:T(8,128)(2,1)S(1)} collective-permute-done((bf16[400,256]{1,0:T(8,128)(2,1)S(1)}, bf16[400,256]{1,0:T(8,128)(2,1)S(1)}, u32[]{:S(2)}, u32[]{:S(2)}) %collective-permute-start.5) | collective-permute-done | bytes 204832 | tf_op jit(solution)/shard_map/ppermute | solution.py:570
  46.4 1.3 collective-permute-start.9
  47.7 3.1 %collective-permute-start.16 = (bf16[336,384]{1,0:T(8,128)(2,1)}, bf16[336,384]{1,0:T(8,128)(2,1)S(1)}, u32[]{:S(2)}, u32[]{:S(2)}) collective-permute-start(bf16[336,384]{1,0:T(8,128)(2,1)} %collective-permute-done.14.refs_6_), channel_id=1, source_target_pairs={{0,14},{2,0},{4,2},{6,4},{8,6},{10,8},{12,10},{14,12},{1,15},{3,1}... | collective-permute-start | bytes 774152 | tf_op jit(solution)/shard_map/ppermute | solution.py:578
  50.8 1.0 dynamic-slice_bitcast_fusion.1
  51.9 0.1 collective-permute-start.4
  52.0 0.9 pad_maximum_fusion
  52.9 0.6 collective-permute-start.28
  53.5 2.8 %collective-permute-done.16.refs_8_ = bf16[336,384]{1,0:T(8,128)(2,1)S(1)} collective-permute-done((bf16[336,384]{1,0:T(8,128)(2,1)}, bf16[336,384]{1,0:T(8,128)(2,1)S(1)}, u32[]{:S(2)}, u32[]{:S(2)}) %collective-permute-start.16) | collective-permute-done | bytes 258080 | tf_op jit(solution)/shard_map/ppermute | solution.py:578
  56.3 3.6 %collective-permute-start.18 = (bf16[336,384]{1,0:T(8,128)(2,1)S(1)}, bf16[336,384]{1,0:T(8,128)(2,1)S(1)}, u32[]{:S(2)}, u32[]{:S(2)}) collective-permute-start(bf16[336,384]{1,0:T(8,128)(2,1)S(1)} %collective-permute-done.16.refs_8_), channel_id=1, source_target_pairs={{0,14},{2,0},{4,2},{6,4},{8,6},{10,8},{12,10},{14,12},{1,15},{3,1}... | collective-permute-start | bytes 774152 | tf_op jit(solution)/shard_map/ppermute | solution.py:578
  59.9 0.1 collective-permute-start.2
  60.0 4.2 %collective-permute-done.18.refs_10_ = bf16[336,384]{1,0:T(8,128)(2,1)S(1)} collective-permute-done((bf16[336,384]{1,0:T(8,128)(2,1)S(1)}, bf16[336,384]{1,0:T(8,128)(2,1)S(1)}, u32[]{:S(2)}, u32[]{:S(2)}) %collective-permute-start.18) | collective-permute-done | bytes 258080 | tf_op jit(solution)/shard_map/ppermute | solution.py:578
  64.2 0.7 copy-done.22
  64.9 2.7 %collective-permute-done.19.refs_11_ = bf16[336,384]{1,0:T(8,128)(2,1)S(1)} collective-permute-done((bf16[336,384]{1,0:T(8,128)(2,1)S(1)}, bf16[336,384]{1,0:T(8,128)(2,1)S(1)}, u32[]{:S(2)}, u32[]{:S(2)}) %collective-permute-start.19) | collective-permute-done | bytes 258080 | tf_op jit(solution)/shard_map/ppermute | solution.py:578
  67.7 0.7 copy-done.23
  68.4 6.4 %dout_parts.1 = (f32[256,384]{1,0:T(8,128)}, bf16[256,384]{1,0:T(8,128)(2,1)}) custom-call(s32[4]{0:T(128)} %pad_add_fusion.at_ref.refs_0_, bf16[256,5376]{1,0:T(8,128)(2,1)} %refs_1_.6, bf16[4,256,384]{2,1,0:T(8,128)(2,1)} %collective-permute-done.11.refs_2_, bf16[4,256,384]{2,1,0:T(8,128)(2,1)S(1)} %collective-permute-done.12.refs_3_, ...), custom_call_target="tpu_custom_call" | custom-call | tf_op jit(solution)/shard_map/dout_parts/pallas_call | solution.py:408
  74.8 1.5 collective-permute-start.20
  76.3 0.6 broadcast_in_dim.8.refs_1_
  76.9 6.3 %stats_near.1 = (f32[1,768]{1,0:T(1,128)}, f32[1,768]{1,0:T(1,128)}, f32[128,768]{1,0:T(8,128)}, s32[1,384]{1,0:T(1,128)}) custom-call(s32[1]{0:T(128)} %bitcast.4.refs_0_.own_ref, s32[1,384]{1,0:T(1,128)} %broadcast_in_dim.8.refs_1_, bf16[384,256]{1,0:T(8,128)(2,1)} %refs_1_.7, bf16[400,256]{1,0:T(8,128)(2,1)} %copy-done.3, bf16[400,256]{1,0:T(8,128)(2,1)} %copy-done.5, ...), custom_call_target="tpu_custom_call" | custom-call | tf_op jit(solution)/shard_map/stats_near/pallas_call | solution.py:284
  83.3 0.6 copy-done.10
  84.0 0.1 copy-done.12
  84.1 5.8 %stats_far.1 = (f32[1,768]{1,0:T(1,128)}, f32[128,768]{1,0:T(8,128)}, s32[1,384]{1,0:T(1,128)}, s32[1]{0:T(128)}) custom-call(s32[1]{0:T(128)} %bitcast.4.refs_0_.own_ref, s32[1,384]{1,0:T(1,128)} %broadcast_in_dim.8.refs_1_, bf16[384,256]{1,0:T(8,128)(2,1)} %refs_1_.7, f32[1,768]{1,0:T(1,128)} %get-tuple-element.42.refs_3_, ...), custom_call_target="tpu_custom_call" | custom-call | tf_op jit(solution)/shard_map/stats_far/pallas_call | solution.py:284
  89.9 12.4 %attention_grads.1 = (bf16[256,384]{1,0:T(8,128)(2,1)}, bf16[5,384,256]{2,1,0:T(8,128)(2,1)}, bf16[5,384,256]{2,1,0:T(8,128)(2,1)}) custom-call(s32[1]{0:T(128)} %bitcast.4.refs_0_.own_ref, s32[1]{0:T(128)} %get-tuple-element.46.low_ref, s32[1,384]{1,0:T(1,128)} %get-tuple-element.47.refs_0_, bf16[384,256]{1,0:T(8,128)(2,1)} %refs_1_.7, ...), custom_call_target="tpu_custom_call" | custom-call | tf_op jit(solution)/shard_map/attention_grads/pallas_call | solution.py:298
  102.3 2.1 %collective-permute-start.21 = (bf16[5,384,256]{2,1,0:T(8,128)(2,1)}, bf16[5,384,256]{2,1,0:T(8,128)(2,1)S(1)}, u32[]{:S(2)}, u32[]{:S(2)}) collective-permute-start(bf16[5,384,256]{2,1,0:T(8,128)(2,1)} %get-tuple-element.53), channel_id=1, source_target_pairs={{0,16},{16,0},{1,17},{17,1},{2,18},{18,2},{3,19},{19,3},{4,20},{20... | collective-permute-start | bytes 2949128 | tf_op jit(solution)/shard_map/ppermute | solution.py:558
  104.5 0.2 collective-permute-start.29
  104.7 17.2 %collective-permute-done.29.refs_6_.refs_3_.refs_7_ = bf16[2,336,512]{2,1,0:T(8,128)(2,1)S(1)} collective-permute-done((bf16[2,336,512]{2,1,0:T(8,128)(2,1)S(1)}, bf16[2,336,512]{2,1,0:T(8,128)(2,1)S(1)}, u32[]{:S(2)}, u32[]{:S(2)}) %collective-permute-start.29) | collective-permute-done | bytes 688160 | tf_op jit(solution)/shard_map/ppermute | solution.py:562
  122.0 2.7 %join_partials.1 = (f32[384,256]{1,0:T(8,128)}, bf16[384,256]{1,0:T(8,128)(2,1)}, bf16[384,256]{1,0:T(8,128)(2,1)}, bf16[384,256]{1,0:T(8,128)(2,1)}, bf16[384,2...) custom-call(s32[1]{0:T(128)} %bitcast.2.core_ref, bf16[5,384,256]{2,1,0:T(8,128)(2,1)} %get-tuple-element.52.mine_ref, ...), custom_call_target="tpu_custom_call" | custom-call | tf_op jit(solution)/shard_map/join_partials/pallas_call | solution.py:442
  124.6 0.7 collective-permute-start.22
  125.3 1.3 collective-permute-start.23
  126.6 1.9 collective-permute-start.24
  128.5 1.9 collective-permute-start.25
  130.4 4.7 %collective-permute-done.23.refs_1_ = bf16[384,256]{1,0:T(8,128)(2,1)S(1)} collective-permute-done((bf16[384,256]{1,0:T(8,128)(2,1)}, bf16[384,256]{1,0:T(8,128)(2,1)S(1)}, u32[]{:S(2)}, u32[]{:S(2)}) %collective-permute-start.23) | collective-permute-done | bytes 196640 | tf_op jit(solution)/shard_map/ppermute | solution.py:574
  135.2 2.2 %collective-permute-start.26 = (bf16[384,256]{1,0:T(8,128)(2,1)}, bf16[384,256]{1,0:T(8,128)(2,1)S(1)}, u32[]{:S(2)}, u32[]{:S(2)}) collective-permute-start(bf16[384,256]{1,0:T(8,128)(2,1)} %get-tuple-element.59), channel_id=1, source_target_pairs={{32,0},{48,16},{64,32},{80,48},{96,64},{112,80},{128,96},{144,112}... | collective-permute-start | bytes 589832 | tf_op jit(solution)/shard_map/ppermute | solution.py:574
  137.3 1.7 collective-permute-done.24.refs_2_
  139.0 2.8 %collective-permute-start.32 = (bf16[256,384]{1,0:T(8,128)(2,1)S(1)}, bf16[256,384]{1,0:T(8,128)(2,1)S(1)}, u32[]{:S(2)}, u32[]{:S(2)}) collective-permute-start(bf16[256,384]{1,0:T(8,128)(2,1)S(1)} %copy-done.24), channel_id=1, source_target_pairs={{0,1},{1,0},{2,3},{3,2},{4,5},{5,4},{6,7},{7,6},{8,9},{9,8},{10,11... | collective-permute-start | bytes 589832 | tf_op jit(solution)/shard_map/ppermute | solution.py:558
  141.8 6.0 %collective-permute-done.25.refs_3_ = bf16[384,256]{1,0:T(8,128)(2,1)S(1)} collective-permute-done((bf16[384,256]{1,0:T(8,128)(2,1)}, bf16[384,256]{1,0:T(8,128)(2,1)S(1)}, u32[]{:S(2)}, u32[]{:S(2)}) %collective-permute-start.25) | collective-permute-done | bytes 196640 | tf_op jit(solution)/shard_map/ppermute | solution.py:574
  147.8 5.4 %collective-permute-done.26.refs_4_ = bf16[384,256]{1,0:T(8,128)(2,1)S(1)} collective-permute-done((bf16[384,256]{1,0:T(8,128)(2,1)}, bf16[384,256]{1,0:T(8,128)(2,1)S(1)}, u32[]{:S(2)}, u32[]{:S(2)}) %collective-permute-start.26) | collective-permute-done | bytes 196640 | tf_op jit(solution)/shard_map/ppermute | solution.py:574
  153.2 1.9 total_partials.1.refs_3_
  155.1 1.3 collective-permute-start.27
  156.4 5.1 %project.5 = (f32[336,384]{1,0:T(8,128)}, f32[336,384]{1,0:T(8,128)}, f32[336,384]{1,0:T(8,128)}, f32[336,384]{1,0:T(8,128)}, f32[336,384]{1,0:T(8,128)}, /*inde...) custom-call(s32[4]{0:T(128)} %pad_add_fusion.at_ref.refs_0_, bf16[5376,256]{1,0:T(8,128)(2,1)} %refs_1_.8, ...), custom_call_target="tpu_custom_call" | custom-call | tf_op jit(solution)/shard_map/project/pallas_call | solution.py:535
  161.6 3.7 %project.6 = (f32[336,384]{1,0:T(8,128)}, f32[336,384]{1,0:T(8,128)}) custom-call(s32[4]{0:T(128)} %pad_add_fusion.at_ref.refs_0_, bf16[5376,128]{1,0:T(8,128)(2,1)} %refs_1_.11, bf16[5376,128]{1,0:T(8,128)(2,1)} %refs_2_.9, bf16[256,384]{1,0:T(8,128)(2,1)} %total_partials.1.refs_3_, bf16[256,384]{1,0:T(8,128)(2,1)S(1)} %collective-permute-done.32.refs_4_, ...), custom_call_target="tpu_custom_call" | custom-call | tf_op jit(solution)/shard_map/project/pallas_call | solution.py:535
  165.3 3.3 %project.7 = (bf16[336,384]{1,0:T(8,128)(2,1)}, bf16[336,384]{1,0:T(8,128)(2,1)}) custom-call(s32[4]{0:T(128)} %pad_add_fusion.at_ref.refs_0_, bf16[256,384]{1,0:T(8,128)(2,1)S(1)} %collective-permute-done.27.refs_1_.refs_5_, bf16[2,336,512]{2,1,0:T(8,128)(2,1)} %copy-done, bf16[2,336,512]{2,1,0:T(8,128)(2,1)} %copy-done.1, ...), custom_call_target="tpu_custom_call" | custom-call | tf_op jit(solution)/shard_map/project/pallas_call | solution.py:535
  168.7 3.2 %collective-permute-start.37 = (bf16[336,384]{1,0:T(8,128)(2,1)}, bf16[336,384]{1,0:T(8,128)(2,1)S(1)}, u32[]{:S(2)}, u32[]{:S(2)}) collective-permute-start(bf16[336,384]{1,0:T(8,128)(2,1)} %get-tuple-element.75), channel_id=1, source_target_pairs={{0,14},{2,0},{4,2},{6,4},{8,6},{10,8},{12,10},{14,12},{1,15},{3,1}... | collective-permute-start | bytes 774152 | tf_op jit(solution)/shard_map/ppermute | solution.py:578
  171.9 5.2 %project.8 = (f32[336,384]{1,0:T(8,128)}, f32[336,384]{1,0:T(8,128)}, f32[336,384]{1,0:T(8,128)}, f32[336,384]{1,0:T(8,128)}) custom-call(s32[4]{0:T(128)} %pad_add_fusion.at_ref.refs_0_, bf16[5376,128]{1,0:T(8,128)(2,1)} %refs_1_.11, bf16[5376,128]{1,0:T(8,128)(2,1)} %refs_2_.9, bf16[256,384]{1,0:T(8,128)(2,1)} %total_partials.1.refs_3_, ...), custom_call_target="tpu_custom_call" | custom-call | tf_op jit(solution)/shard_map/project/pallas_call | solution.py:535
  177.2 1.2 add_convert_fusion.5
  178.5 3.3 %collective-permute-start.38 = (bf16[336,384]{1,0:T(8,128)(2,1)S(1)}, bf16[336,384]{1,0:T(8,128)(2,1)S(1)}, u32[]{:S(2)}, u32[]{:S(2)}) collective-permute-start(bf16[336,384]{1,0:T(8,128)(2,1)S(1)} %add_convert_fusion.2), channel_id=1, source_target_pairs={{0,14},{2,0},{4,2},{6,4},{8,6},{10,8},{12,10},{14,12},{1,15},{3,1}... | collective-permute-start | bytes 774152 | tf_op jit(solution)/shard_map/ppermute | solution.py:578
  181.8 4.3 %collective-permute-done.34 = bf16[336,384]{1,0:T(8,128)(2,1)S(1)} collective-permute-done((bf16[336,384]{1,0:T(8,128)(2,1)S(1)}, bf16[336,384]{1,0:T(8,128)(2,1)S(1)}, u32[]{:S(2)}, u32[]{:S(2)}) %collective-permute-start.34) | collective-permute-done | bytes 258080 | tf_op jit(solution)/shard_map/ppermute | solution.py:578
  186.3 4.3 %project.9 = (f32[336,384]{1,0:T(8,128)}, f32[336,384]{1,0:T(8,128)}) custom-call(s32[4]{0:T(128)} %pad_add_fusion.at_ref.refs_0_, bf16[5376,128]{1,0:T(8,128)(2,1)} %refs_1_.11, bf16[5376,128]{1,0:T(8,128)(2,1)} %refs_2_.9, bf16[256,384]{1,0:T(8,128)(2,1)} %total_partials.1.refs_3_, bf16[256,384]{1,0:T(8,128)(2,1)S(1)} %collective-permute-done.32.refs_4_, ...), custom_call_target="tpu_custom_call" | custom-call | tf_op jit(solution)/shard_map/project/pallas_call | solution.py:535
  190.8 3.3 %collective-permute-start.39 = (bf16[336,384]{1,0:T(8,128)(2,1)S(1)}, bf16[336,384]{1,0:T(8,128)(2,1)S(1)}, u32[]{:S(2)}, u32[]{:S(2)}) collective-permute-start(bf16[336,384]{1,0:T(8,128)(2,1)S(1)} %add_convert_fusion.1), channel_id=1, source_target_pairs={{0,14},{2,0},{4,2},{6,4},{8,6},{10,8},{12,10},{14,12},{1,15},{3,1}... | collective-permute-start | bytes 774152 | tf_op jit(solution)/shard_map/ppermute | solution.py:578
  194.2 3.7 %collective-permute-done.39 = bf16[336,384]{1,0:T(8,128)(2,1)S(1)} collective-permute-done((bf16[336,384]{1,0:T(8,128)(2,1)S(1)}, bf16[336,384]{1,0:T(8,128)(2,1)S(1)}, u32[]{:S(2)}, u32[]{:S(2)}) %collective-permute-start.39) | collective-permute-done | bytes 258080 | tf_op jit(solution)/shard_map/ppermute | solution.py:578
  197.9 3.8 %collective-permute-done.36 = bf16[336,384]{1,0:T(8,128)(2,1)S(1)} collective-permute-done((bf16[336,384]{1,0:T(8,128)(2,1)S(1)}, bf16[336,384]{1,0:T(8,128)(2,1)S(1)}, u32[]{:S(2)}, u32[]{:S(2)}) %collective-permute-start.36) | collective-permute-done | bytes 258080 | tf_op jit(solution)/shard_map/ppermute | solution.py:578
  201.7 0.8 fusion.1
  (97 shorter events, 1.0 us)
Async XLA Ops:
  0.7 6.6 %copy-start.18 = (bf16[384,336]{0,1:T(8,128)(2,1)S(1)}, bf16[384,336]{0,1:T(8,128)(2,1)}, u32[]{:S(2)}) copy-start(bf16[384,336]{0,1:T(8,128)(2,1)} %param.12) | copy-start | bytes 774148
  0.7 8.5 %copy-start.27 = (s32[384]{0:T(512)S(1)}, s32[384]{0:T(512)}, u32[]{:S(2)}) copy-start(s32[384]{0:T(512)} %param.13) | copy-start | bytes 4612
  0.7 8.5 %copy-start.25 = (bf16[384,128]{1,0:T(8,128)(2,1)S(1)}, bf16[384,128]{1,0:T(8,128)(2,1)}, u32[]{:S(2)}) copy-start(bf16[384,128]{1,0:T(8,128)(2,1)} %param.11) | copy-start | bytes 294916
  0.7 8.5 %copy-start.26 = (bf16[384,128]{1,0:T(8,128)(2,1)S(1)}, bf16[384,128]{1,0:T(8,128)(2,1)}, u32[]{:S(2)}) copy-start(bf16[384,128]{1,0:T(8,128)(2,1)} %param.10) | copy-start | bytes 294916
  4.1 31.5 %collective-permute-start.11 = (bf16[4,256,384]{2,1,0:T(8,128)(2,1)}, bf16[4,256,384]{2,1,0:T(8,128)(2,1)}, u32[]{:S(2)}, u32[]{:S(2)}) collective-permute-start(bf16[4,256,384]{2,1,0:T(8,128)(2,1)} %split_w_out.1), channel_id=1, source_target_pairs={{0,1},{1,0},{2,3},{3,2},{4,5},{5,4},{6,7},{7,6},{8,9},{9,8},{10,11... | collective-permute-start | bytes 2359304 | tf_op jit(solution)/shard_map/ppermute | solution.py:558
  7.3 28.4 %collective-permute-start.13 = (bf16[336,384]{1,0:T(8,128)(2,1)S(1)}, bf16[336,384]{1,0:T(8,128)(2,1)S(1)}, u32[]{:S(2)}, u32[]{:S(2)}) collective-permute-start(bf16[336,384]{1,0:T(8,128)(2,1)S(1)} %bitcast.29), channel_id=1, source_target_pairs={{0,2},{2,4},{4,6},{6,8},{8,10},{10,12},{12,14},{14,0},{1,3},{3,5},... | collective-permute-start | bytes 774152 | tf_op jit(solution)/shard_map/ppermute | solution.py:578
  9.2 43.7 %copy-start.3 = (bf16[400,256]{1,0:T(8,128)(2,1)}, bf16[400,256]{1,0:T(8,128)(2,1)S(1)}, u32[]{:S(2)}) copy-start(bf16[400,256]{1,0:T(8,128)(2,1)S(1)} %fusion.2.refs_3_.refs_6_) | copy-start | bytes 614404
  9.2 20.5 %collective-permute-start.3 = (bf16[400,256]{1,0:T(8,128)(2,1)S(1)}, bf16[400,256]{1,0:T(8,128)(2,1)S(1)}, u32[]{:S(2)}, u32[]{:S(2)}) collective-permute-start(bf16[400,256]{1,0:T(8,128)(2,1)S(1)} %fusion.2.refs_3_.refs_6_), channel_id=1, source_target_pairs={{0,64},{16,80},{32,96},{48,112},{64,128},{80,144},{96,160},{112,17... | collective-permute-start | bytes 614408 | tf_op jit(solution)/shard_map/ppermute | solution.py:570
  12.4 23.3 %collective-permute-start = (bf16[400,256]{1,0:T(8,128)(2,1)S(1)}, bf16[400,256]{1,0:T(8,128)(2,1)S(1)}, u32[]{:S(2)}, u32[]{:S(2)}) collective-permute-start(bf16[400,256]{1,0:T(8,128)(2,1)S(1)} %fusion.2.refs_3_.refs_6_), channel_id=1, source_target_pairs={{0,32},{16,48},{32,64},{48,80},{64,96},{80,112},{96,128},{112,144}... | collective-permute-start | bytes 614408 | tf_op jit(solution)/shard_map/ppermute | solution.py:570
  16.5 21.2 %collective-permute-start.1 = (bf16[400,256]{1,0:T(8,128)(2,1)S(1)}, bf16[400,256]{1,0:T(8,128)(2,1)S(1)}, u32[]{:S(2)}, u32[]{:S(2)}) collective-permute-start(bf16[400,256]{1,0:T(8,128)(2,1)S(1)} %fusion.2.refs_3_.refs_6_), channel_id=1, source_target_pairs={{0,16},{16,0},{1,17},{17,1},{2,18},{18,2},{3,19},{19,3},{4,20},{20... | collective-permute-start | bytes 614408 | tf_op jit(solution)/shard_map/ppermute | solution.py:558
  29.8 23.1 %copy-start.4 = (bf16[400,256]{1,0:T(8,128)(2,1)}, bf16[400,256]{1,0:T(8,128)(2,1)S(1)}, u32[]{:S(2)}) copy-start(bf16[400,256]{1,0:T(8,128)(2,1)S(1)} %collective-permute-done.3.refs_7_.refs_8_) | copy-start | bytes 614404
  29.8 17.9 %collective-permute-start.14 = (bf16[336,384]{1,0:T(8,128)(2,1)S(1)}, bf16[336,384]{1,0:T(8,128)(2,1)}, u32[]{:S(2)}, u32[]{:S(2)}) collective-permute-start(bf16[336,384]{1,0:T(8,128)(2,1)S(1)} %bitcast.30), channel_id=1, source_target_pairs={{0,14},{2,0},{4,2},{6,4},{8,6},{10,8},{12,10},{14,12},{1,15},{3,1}... | collective-permute-start | bytes 774152 | tf_op jit(solution)/shard_map/ppermute | solution.py:578
  35.7 15.2 %copy-start.19 = (bf16[336,384]{1,0:T(8,128)(2,1)}, bf16[336,384]{1,0:T(8,128)(2,1)S(1)}, u32[]{:S(2)}) copy-start(bf16[336,384]{1,0:T(8,128)(2,1)S(1)} %collective-permute-done.13.refs_5_) | copy-start | bytes 774148
  35.7 15.2 %collective-permute-start.15 = (bf16[336,384]{1,0:T(8,128)(2,1)S(1)}, bf16[336,384]{1,0:T(8,128)(2,1)}, u32[]{:S(2)}, u32[]{:S(2)}) collective-permute-start(bf16[336,384]{1,0:T(8,128)(2,1)S(1)} %collective-permute-done.13.refs_5_), channel_id=1, source_target_pairs={{0,2},{2,4},{4,6},{6,8},{8,10},{10,12},{12,14},{14,0},{1,3},{3,5},... | collective-permute-start | bytes 774152 | tf_op jit(solution)/shard_map/ppermute | solution.py:578
  35.7 32.0 %collective-permute-start.12 = (bf16[4,256,384]{2,1,0:T(8,128)(2,1)}, bf16[4,256,384]{2,1,0:T(8,128)(2,1)S(1)}, u32[]{:S(2)}, u32[]{:S(2)}) collective-permute-start(bf16[4,256,384]{2,1,0:T(8,128)(2,1)} %collective-permute-done.11.refs_2_), channel_id=1, source_target_pairs={{0,16},{16,0},{1,17},{17,1},{2,18},{18,2},{3,19},{19,3},{4,20},{20... | collective-permute-start | bytes 2359304 | tf_op jit(solution)/shard_map/ppermute | solution.py:558
  35.8 24.1 %copy-start.5 = (bf16[400,256]{1,0:T(8,128)(2,1)}, bf16[400,256]{1,0:T(8,128)(2,1)S(1)}, u32[]{:S(2)}) copy-start(bf16[400,256]{1,0:T(8,128)(2,1)S(1)} %collective-permute-done.refs_4_.refs_7_) | copy-start | bytes 614404
  35.8 10.6 %collective-permute-start.5 = (bf16[400,256]{1,0:T(8,128)(2,1)S(1)}, bf16[400,256]{1,0:T(8,128)(2,1)S(1)}, u32[]{:S(2)}, u32[]{:S(2)}) collective-permute-start(bf16[400,256]{1,0:T(8,128)(2,1)S(1)} %fusion.2.refs_3_.refs_6_), channel_id=1, source_target_pairs={{0,96},{16,112},{32,128},{48,144},{64,160},{80,176},{96,192},{112,... | collective-permute-start | bytes 614408 | tf_op jit(solution)/shard_map/ppermute | solution.py:570
  37.8 15.2 %copy-start.6 = (bf16[400,256]{1,0:T(8,128)(2,1)}, bf16[400,256]{1,0:T(8,128)(2,1)S(1)}, u32[]{:S(2)}) copy-start(bf16[400,256]{1,0:T(8,128)(2,1)S(1)} %collective-permute-done.1.refs_5_.refs_11_) | copy-start | bytes 614404
  37.8 14.1 %collective-permute-start.6 = (bf16[400,256]{1,0:T(8,128)(2,1)S(1)}, bf16[400,256]{1,0:T(8,128)(2,1)S(1)}, u32[]{:S(2)}, u32[]{:S(2)}) collective-permute-start(bf16[400,256]{1,0:T(8,128)(2,1)S(1)} %fusion.2.refs_3_.refs_6_), channel_id=1, source_target_pairs={{0,128},{16,144},{32,160},{48,176},{64,192},{80,208},{96,224},{112... | collective-permute-start | bytes 614408 | tf_op jit(solution)/shard_map/ppermute | solution.py:570
  46.3 28.4 %copy-start.7 = (bf16[400,256]{1,0:T(8,128)(2,1)}, bf16[400,256]{1,0:T(8,128)(2,1)S(1)}, u32[]{:S(2)}) copy-start(bf16[400,256]{1,0:T(8,128)(2,1)S(1)} %collective-permute-done.5.refs_8_.refs_9_) | copy-start | bytes 614404
  46.4 6.6 %collective-permute-start.9 = (bf16[400,256]{1,0:T(8,128)(2,1)S(1)}, bf16[400,256]{1,0:T(8,128)(2,1)}, u32[]{:S(2)}, u32[]{:S(2)}) collective-permute-start(bf16[400,256]{1,0:T(8,128)(2,1)S(1)} %fusion.2.refs_3_.refs_6_), channel_id=1, source_target_pairs={{16,176},{48,208},{80,240},{17,177},{49,209},{81,241},{18,178},{50... | collective-permute-start | bytes 614408 | tf_op jit(solution)/shard_map/ppermute | solution.py:570
  47.7 8.6 %collective-permute-start.16 = (bf16[336,384]{1,0:T(8,128)(2,1)}, bf16[336,384]{1,0:T(8,128)(2,1)S(1)}, u32[]{:S(2)}, u32[]{:S(2)}) collective-permute-start(bf16[336,384]{1,0:T(8,128)(2,1)} %collective-permute-done.14.refs_6_), channel_id=1, source_target_pairs={{0,14},{2,0},{4,2},{6,4},{8,6},{10,8},{12,10},{14,12},{1,15},{3,1}... | collective-permute-start | bytes 774152 | tf_op jit(solution)/shard_map/ppermute | solution.py:578
  50.8 9.1 %collective-permute-start.17 = (bf16[336,384]{1,0:T(8,128)(2,1)}, bf16[336,384]{1,0:T(8,128)(2,1)S(1)}, u32[]{:S(2)}, u32[]{:S(2)}) collective-permute-start(bf16[336,384]{1,0:T(8,128)(2,1)} %collective-permute-done.15.refs_7_), channel_id=1, source_target_pairs={{0,2},{2,4},{4,6},{6,8},{8,10},{10,12},{12,14},{14,0},{1,3},{3,5},... | collective-permute-start | bytes 774152 | tf_op jit(solution)/shard_map/ppermute | solution.py:578
  51.9 22.9 %copy-start.8 = (bf16[400,256]{1,0:T(8,128)(2,1)}, bf16[400,256]{1,0:T(8,128)(2,1)S(1)}, u32[]{:S(2)}) copy-start(bf16[400,256]{1,0:T(8,128)(2,1)S(1)} %collective-permute-done.6.refs_9_.refs_10_) | copy-start | bytes 614404
  51.9 8.0 %collective-permute-start.4 = (bf16[400,256]{1,0:T(8,128)(2,1)S(1)}, bf16[400,256]{1,0:T(8,128)(2,1)S(1)}, u32[]{:S(2)}, u32[]{:S(2)}) collective-permute-start(bf16[400,256]{1,0:T(8,128)(2,1)S(1)} %collective-permute-done.3.refs_7_.refs_8_), channel_id=1, source_target_pairs={{0,16},{16,0},{1,17},{17,1},{2,18},{18,2},{3,19},{19,3},{4,20},{20... | collective-permute-start | bytes 614408 | tf_op jit(solution)/shard_map/ppermute | solution.py:558
  52.9 51.6 %collective-permute-start.28 = (bf16[2,336,512]{2,1,0:T(8,128)(2,1)}, bf16[2,336,512]{2,1,0:T(8,128)(2,1)S(1)}, u32[]{:S(2)}, u32[]{:S(2)}) collective-permute-start(bf16[2,336,512]{2,1,0:T(8,128)(2,1)} %pad_maximum_fusion), channel_id=1, source_target_pairs={{0,1},{1,0},{2,3},{3,2},{4,5},{5,4},{6,7},{7,6},{8,9},{9,8},{10,11... | collective-permute-start | bytes 2064392 | tf_op jit(solution)/shard_map/ppermute | solution.py:558
  56.3 12.0 %copy-start.20 = (bf16[336,384]{1,0:T(8,128)(2,1)}, bf16[336,384]{1,0:T(8,128)(2,1)S(1)}, u32[]{:S(2)}) copy-start(bf16[336,384]{1,0:T(8,128)(2,1)S(1)} %collective-permute-done.16.refs_8_) | copy-start | bytes 774148
  56.3 7.9 %collective-permute-start.18 = (bf16[336,384]{1,0:T(8,128)(2,1)S(1)}, bf16[336,384]{1,0:T(8,128)(2,1)S(1)}, u32[]{:S(2)}, u32[]{:S(2)}) collective-permute-start(bf16[336,384]{1,0:T(8,128)(2,1)S(1)} %collective-permute-done.16.refs_8_), channel_id=1, source_target_pairs={{0,14},{2,0},{4,2},{6,4},{8,6},{10,8},{12,10},{14,12},{1,15},{3,1}... | collective-permute-start | bytes 774152 | tf_op jit(solution)/shard_map/ppermute | solution.py:578
  59.9 7.7 %copy-start.21 = (bf16[336,384]{1,0:T(8,128)(2,1)}, bf16[336,384]{1,0:T(8,128)(2,1)S(1)}, u32[]{:S(2)}) copy-start(bf16[336,384]{1,0:T(8,128)(2,1)S(1)} %collective-permute-done.17.refs_9_) | copy-start | bytes 774148
  59.9 7.7 %collective-permute-start.19 = (bf16[336,384]{1,0:T(8,128)(2,1)S(1)}, bf16[336,384]{1,0:T(8,128)(2,1)S(1)}, u32[]{:S(2)}, u32[]{:S(2)}) collective-permute-start(bf16[336,384]{1,0:T(8,128)(2,1)S(1)} %collective-permute-done.17.refs_9_), channel_id=1, source_target_pairs={{0,2},{2,4},{4,6},{6,8},{8,10},{10,12},{12,14},{14,0},{1,3},{3,5},... | collective-permute-start | bytes 774152 | tf_op jit(solution)/shard_map/ppermute | solution.py:578
  59.9 14.9 %copy-start.2 = (bf16[400,256]{1,0:T(8,128)(2,1)}, bf16[400,256]{1,0:T(8,128)(2,1)S(1)}, u32[]{:S(2)}) copy-start(bf16[400,256]{1,0:T(8,128)(2,1)S(1)} %collective-permute-done.4.refs_7_.refs_10_.refs_13_) | copy-start | bytes 614404
  59.9 14.9 %collective-permute-start.2 = (bf16[400,256]{1,0:T(8,128)(2,1)S(1)}, bf16[400,256]{1,0:T(8,128)(2,1)S(1)}, u32[]{:S(2)}, u32[]{:S(2)}) collective-permute-start(bf16[400,256]{1,0:T(8,128)(2,1)S(1)} %collective-permute-done.refs_4_.refs_7_), channel_id=1, source_target_pairs={{0,16},{16,0},{1,17},{17,1},{2,18},{18,2},{3,19},{19,3},{4,20},{20... | collective-permute-start | bytes 614408 | tf_op jit(solution)/shard_map/ppermute | solution.py:558
  64.2 19.0 %collective-permute-start.7 = (bf16[400,256]{1,0:T(8,128)(2,1)S(1)}, bf16[400,256]{1,0:T(8,128)(2,1)S(1)}, u32[]{:S(2)}, u32[]{:S(2)}) collective-permute-start(bf16[400,256]{1,0:T(8,128)(2,1)S(1)} %collective-permute-done.5.refs_8_.refs_9_), channel_id=1, source_target_pairs={{0,16},{16,0},{1,17},{17,1},{2,18},{18,2},{3,19},{19,3},{4,20},{20... | collective-permute-start | bytes 614408 | tf_op jit(solution)/shard_map/ppermute | solution.py:558
  67.6 15.6 %collective-permute-start.8 = (bf16[400,256]{1,0:T(8,128)(2,1)S(1)}, bf16[400,256]{1,0:T(8,128)(2,1)S(1)}, u32[]{:S(2)}, u32[]{:S(2)}) collective-permute-start(bf16[400,256]{1,0:T(8,128)(2,1)S(1)} %collective-permute-done.6.refs_9_.refs_10_), channel_id=1, source_target_pairs={{0,16},{16,0},{1,17},{17,1},{2,18},{18,2},{3,19},{19,3},{4,20},{20... | collective-permute-start | bytes 614408 | tf_op jit(solution)/shard_map/ppermute | solution.py:558
  68.4 14.9 %collective-permute-start.10 = (bf16[400,256]{1,0:T(8,128)(2,1)}, bf16[400,256]{1,0:T(8,128)(2,1)S(1)}, u32[]{:S(2)}, u32[]{:S(2)}) collective-permute-start(bf16[400,256]{1,0:T(8,128)(2,1)} %collective-permute-done.9), channel_id=1, source_target_pairs={{0,16},{16,0},{1,17},{17,1},{2,18},{18,2},{3,19},{19,3},{4,20},{20... | collective-permute-start | bytes 614408 | tf_op jit(solution)/shard_map/ppermute | solution.py:558
  74.8 2.1 %copy-start.9 = (bf16[400,256]{1,0:T(8,128)(2,1)}, bf16[400,256]{1,0:T(8,128)(2,1)S(1)}, u32[]{:S(2)}) copy-start(bf16[400,256]{1,0:T(8,128)(2,1)S(1)} %collective-permute-done.2.refs_6_.refs_12_) | copy-start | bytes 614404
  74.8 15.0 %collective-permute-start.20 = (bf16[256,384]{1,0:T(8,128)(2,1)}, bf16[256,384]{1,0:T(8,128)(2,1)S(1)}, u32[]{:S(2)}, u32[]{:S(2)}) collective-permute-start(bf16[256,384]{1,0:T(8,128)(2,1)} %get-tuple-element.49), channel_id=1, source_target_pairs={{0,1},{1,0},{2,3},{3,2},{4,5},{5,4},{6,7},{7,6},{8,9},{9,8},{10,11... | collective-permute-start | bytes 589832 | tf_op jit(solution)/shard_map/ppermute | solution.py:558
  83.3 0.8 copy-start.12
  102.3 36.7 %copy-start.24 = (bf16[256,384]{1,0:T(8,128)(2,1)S(1)}, bf16[256,384]{1,0:T(8,128)(2,1)}, u32[]{:S(2)}) copy-start(bf16[256,384]{1,0:T(8,128)(2,1)} %get-tuple-element.60.refs_2_) | copy-start | bytes 589828
  102.3 19.6 %collective-permute-start.21 = (bf16[5,384,256]{2,1,0:T(8,128)(2,1)}, bf16[5,384,256]{2,1,0:T(8,128)(2,1)S(1)}, u32[]{:S(2)}, u32[]{:S(2)}) collective-permute-start(bf16[5,384,256]{2,1,0:T(8,128)(2,1)} %get-tuple-element.53), channel_id=1, source_target_pairs={{0,16},{16,0},{1,17},{17,1},{2,18},{18,2},{3,19},{19,3},{4,20},{20... | collective-permute-start | bytes 2949128 | tf_op jit(solution)/shard_map/ppermute | solution.py:558
  104.5 50.6 %copy-start = (bf16[2,336,512]{2,1,0:T(8,128)(2,1)}, bf16[2,336,512]{2,1,0:T(8,128)(2,1)S(1)}, u32[]{:S(2)}) copy-start(bf16[2,336,512]{2,1,0:T(8,128)(2,1)S(1)} %collective-permute-done.28.refs_5_.refs_2_.refs_6_) | copy-start | bytes 2064388
  104.5 17.5 %collective-permute-start.29 = (bf16[2,336,512]{2,1,0:T(8,128)(2,1)S(1)}, bf16[2,336,512]{2,1,0:T(8,128)(2,1)S(1)}, u32[]{:S(2)}, u32[]{:S(2)}) collective-permute-start(bf16[2,336,512]{2,1,0:T(8,128)(2,1)S(1)} %collective-permute-done.28.refs_5_.refs_2_.refs_6_), channel_id=1, source_target_pairs={{0,32},{32,0},{64,96},{96,64},{1,33},{33,1},{65,97},{97,65},{2,34}... | collective-permute-start | bytes 2064392 | tf_op jit(solution)/shard_map/ppermute | solution.py:562
  104.6 56.9 %collective-permute-start.30 = (bf16[2,336,512]{2,1,0:T(8,128)(2,1)S(1)}, bf16[2,336,512]{2,1,0:T(8,128)(2,1)}, u32[]{:S(2)}, u32[]{:S(2)}) collective-permute-start(bf16[2,336,512]{2,1,0:T(8,128)(2,1)S(1)} %collective-permute-done.28.refs_5_.refs_2_.refs_6_), channel_id=1, source_target_pairs={{0,16},{16,0},{1,17},{17,1},{2,18},{18,2},{3,19},{19,3},{4,20},{20... | collective-permute-start | bytes 2064392 | tf_op jit(solution)/shard_map/ppermute | solution.py:558
  121.9 33.1 %copy-start.1 = (bf16[2,336,512]{2,1,0:T(8,128)(2,1)}, bf16[2,336,512]{2,1,0:T(8,128)(2,1)S(1)}, u32[]{:S(2)}) copy-start(bf16[2,336,512]{2,1,0:T(8,128)(2,1)S(1)} %collective-permute-done.29.refs_6_.refs_3_.refs_7_) | copy-start | bytes 2064388
  122.0 39.6 %collective-permute-start.31 = (bf16[2,336,512]{2,1,0:T(8,128)(2,1)S(1)}, bf16[2,336,512]{2,1,0:T(8,128)(2,1)}, u32[]{:S(2)}, u32[]{:S(2)}) collective-permute-start(bf16[2,336,512]{2,1,0:T(8,128)(2,1)S(1)} %collective-permute-done.29.refs_6_.refs_3_.refs_7_), channel_id=1, source_target_pairs={{0,16},{16,0},{1,17},{17,1},{2,18},{18,2},{3,19},{19,3},{4,20},{20... | collective-permute-start | bytes 2064392 | tf_op jit(solution)/shard_map/ppermute | solution.py:558
  124.6 3.9 %collective-permute-start.22 = (bf16[384,256]{1,0:T(8,128)(2,1)}, bf16[384,256]{1,0:T(8,128)(2,1)S(1)}, u32[]{:S(2)}, u32[]{:S(2)}) collective-permute-start(bf16[384,256]{1,0:T(8,128)(2,1)} %get-tuple-element.55), channel_id=1, source_target_pairs={{176,16},{208,48},{240,80},{177,17},{209,49},{241,81},{178,18},{21... | collective-permute-start | bytes 589832 | tf_op jit(solution)/shard_map/ppermute | solution.py:574
  125.3 9.9 %collective-permute-start.23 = (bf16[384,256]{1,0:T(8,128)(2,1)}, bf16[384,256]{1,0:T(8,128)(2,1)S(1)}, u32[]{:S(2)}, u32[]{:S(2)}) collective-permute-start(bf16[384,256]{1,0:T(8,128)(2,1)} %get-tuple-element.56), channel_id=1, source_target_pairs={{128,0},{144,16},{160,32},{176,48},{192,64},{208,80},{224,96},{240... | collective-permute-start | bytes 589832 | tf_op jit(solution)/shard_map/ppermute | solution.py:574
  126.6 12.4 %collective-permute-start.24 = (bf16[384,256]{1,0:T(8,128)(2,1)}, bf16[384,256]{1,0:T(8,128)(2,1)S(1)}, u32[]{:S(2)}, u32[]{:S(2)}) collective-permute-start(bf16[384,256]{1,0:T(8,128)(2,1)} %get-tuple-element.57), channel_id=1, source_target_pairs={{96,0},{112,16},{128,32},{144,48},{160,64},{176,80},{192,96},{208,... | collective-permute-start | bytes 589832 | tf_op jit(solution)/shard_map/ppermute | solution.py:574
  128.5 19.3 %collective-permute-start.25 = (bf16[384,256]{1,0:T(8,128)(2,1)}, bf16[384,256]{1,0:T(8,128)(2,1)S(1)}, u32[]{:S(2)}, u32[]{:S(2)}) collective-permute-start(bf16[384,256]{1,0:T(8,128)(2,1)} %get-tuple-element.58), channel_id=1, source_target_pairs={{64,0},{80,16},{96,32},{112,48},{128,64},{144,80},{160,96},{176,11... | collective-permute-start | bytes 589832 | tf_op jit(solution)/shard_map/ppermute | solution.py:574
  135.2 18.0 %collective-permute-start.26 = (bf16[384,256]{1,0:T(8,128)(2,1)}, bf16[384,256]{1,0:T(8,128)(2,1)S(1)}, u32[]{:S(2)}, u32[]{:S(2)}) collective-permute-start(bf16[384,256]{1,0:T(8,128)(2,1)} %get-tuple-element.59), channel_id=1, source_target_pairs={{32,0},{48,16},{64,32},{80,48},{96,64},{112,80},{128,96},{144,112}... | collective-permute-start | bytes 589832 | tf_op jit(solution)/shard_map/ppermute | solution.py:574
  139.0 22.5 %collective-permute-start.32 = (bf16[256,384]{1,0:T(8,128)(2,1)S(1)}, bf16[256,384]{1,0:T(8,128)(2,1)S(1)}, u32[]{:S(2)}, u32[]{:S(2)}) collective-permute-start(bf16[256,384]{1,0:T(8,128)(2,1)S(1)} %copy-done.24), channel_id=1, source_target_pairs={{0,1},{1,0},{2,3},{3,2},{4,5},{5,4},{6,7},{7,6},{8,9},{9,8},{10,11... | collective-permute-start | bytes 589832 | tf_op jit(solution)/shard_map/ppermute | solution.py:558
  155.1 10.2 %collective-permute-start.27 = (bf16[256,384]{1,0:T(8,128)(2,1)}, bf16[256,384]{1,0:T(8,128)(2,1)S(1)}, u32[]{:S(2)}, u32[]{:S(2)}) collective-permute-start(bf16[256,384]{1,0:T(8,128)(2,1)} %total_partials.1.refs_3_), channel_id=1, source_target_pairs={{0,1},{1,0},{2,3},{3,2},{4,5},{5,4},{6,7},{7,6},{8,9},{9,8},{10,11... | collective-permute-start | bytes 589832 | tf_op jit(solution)/shard_map/ppermute | solution.py:558
  168.6 8.6 %collective-permute-start.33 = (bf16[336,384]{1,0:T(8,128)(2,1)}, bf16[336,384]{1,0:T(8,128)(2,1)S(1)}, u32[]{:S(2)}, u32[]{:S(2)}) collective-permute-start(bf16[336,384]{1,0:T(8,128)(2,1)} %get-tuple-element.65), channel_id=1, source_target_pairs={{0,2},{2,4},{4,6},{6,8},{8,10},{10,12},{12,14},{14,0},{1,3},{3,5},... | collective-permute-start | bytes 774152 | tf_op jit(solution)/shard_map/ppermute | solution.py:578
  168.7 9.8 %collective-permute-start.37 = (bf16[336,384]{1,0:T(8,128)(2,1)}, bf16[336,384]{1,0:T(8,128)(2,1)S(1)}, u32[]{:S(2)}, u32[]{:S(2)}) collective-permute-start(bf16[336,384]{1,0:T(8,128)(2,1)} %get-tuple-element.75), channel_id=1, source_target_pairs={{0,14},{2,0},{4,2},{6,4},{8,6},{10,8},{12,10},{14,12},{1,15},{3,1}... | collective-permute-start | bytes 774152 | tf_op jit(solution)/shard_map/ppermute | solution.py:578
  177.1 1.4 copy-start.17
  177.1 9.0 %copy-start.15 = (f32[336,384]{1,0:T(8,128)S(1)}, f32[336,384]{1,0:T(8,128)}, u32[]{:S(2)}) copy-start(f32[336,384]{1,0:T(8,128)} %get-tuple-element.71) | copy-start | bytes 1548292
  178.4 7.8 %collective-permute-start.34 = (bf16[336,384]{1,0:T(8,128)(2,1)S(1)}, bf16[336,384]{1,0:T(8,128)(2,1)S(1)}, u32[]{:S(2)}, u32[]{:S(2)}) collective-permute-start(bf16[336,384]{1,0:T(8,128)(2,1)S(1)} %add_convert_fusion.5), channel_id=1, source_target_pairs={{0,2},{2,4},{4,6},{6,8},{8,10},{10,12},{12,14},{14,0},{1,3},{3,5},... | collective-permute-start | bytes 774152 | tf_op jit(solution)/shard_map/ppermute | solution.py:578
  178.5 12.1 %collective-permute-start.38 = (bf16[336,384]{1,0:T(8,128)(2,1)S(1)}, bf16[336,384]{1,0:T(8,128)(2,1)S(1)}, u32[]{:S(2)}, u32[]{:S(2)}) collective-permute-start(bf16[336,384]{1,0:T(8,128)(2,1)S(1)} %add_convert_fusion.2), channel_id=1, source_target_pairs={{0,14},{2,0},{4,2},{6,4},{8,6},{10,8},{12,10},{14,12},{1,15},{3,1}... | collective-permute-start | bytes 774152 | tf_op jit(solution)/shard_map/ppermute | solution.py:578
  186.2 7.8 %collective-permute-start.35 = (bf16[336,384]{1,0:T(8,128)(2,1)S(1)}, bf16[336,384]{1,0:T(8,128)(2,1)S(1)}, u32[]{:S(2)}, u32[]{:S(2)}) collective-permute-start(bf16[336,384]{1,0:T(8,128)(2,1)S(1)} %add_convert_fusion.4), channel_id=1, source_target_pairs={{0,2},{2,4},{4,6},{6,8},{8,10},{10,12},{12,14},{14,0},{1,3},{3,5},... | collective-permute-start | bytes 774152 | tf_op jit(solution)/shard_map/ppermute | solution.py:578
  186.3 4.4 %copy-start.14 = (f32[336,384]{1,0:T(8,128)S(1)}, f32[336,384]{1,0:T(8,128)}, u32[]{:S(2)}) copy-start(f32[336,384]{1,0:T(8,128)} %get-tuple-element.77) | copy-start | bytes 1548292
  190.7 3.4 %copy-start.16 = (f32[336,384]{1,0:T(8,128)S(1)}, f32[336,384]{1,0:T(8,128)}, u32[]{:S(2)}) copy-start(f32[336,384]{1,0:T(8,128)} %get-tuple-element.74) | copy-start | bytes 1548292
  190.7 11.1 %copy-start.13 = (f32[336,384]{1,0:T(8,128)S(1)}, f32[336,384]{1,0:T(8,128)}, u32[]{:S(2)}) copy-start(f32[336,384]{1,0:T(8,128)} %get-tuple-element.78) | copy-start | bytes 1548292
  190.8 7.1 %collective-permute-start.39 = (bf16[336,384]{1,0:T(8,128)(2,1)S(1)}, bf16[336,384]{1,0:T(8,128)(2,1)S(1)}, u32[]{:S(2)}, u32[]{:S(2)}) collective-permute-start(bf16[336,384]{1,0:T(8,128)(2,1)S(1)} %add_convert_fusion.1), channel_id=1, source_target_pairs={{0,14},{2,0},{4,2},{6,4},{8,6},{10,8},{12,10},{14,12},{1,15},{3,1}... | collective-permute-start | bytes 774152 | tf_op jit(solution)/shard_map/ppermute | solution.py:578
  194.1 7.6 %collective-permute-start.36 = (bf16[336,384]{1,0:T(8,128)(2,1)S(1)}, bf16[336,384]{1,0:T(8,128)(2,1)S(1)}, u32[]{:S(2)}, u32[]{:S(2)}) collective-permute-start(bf16[336,384]{1,0:T(8,128)(2,1)S(1)} %add_convert_fusion.3), channel_id=1, source_target_pairs={{0,2},{2,4},{4,6},{6,8},{8,10},{10,12},{12,14},{14,0},{1,3},{3,5},... | collective-permute-start | bytes 774152 | tf_op jit(solution)/shard_map/ppermute | solution.py:578
  (4 other events, 2.9 us)

commit v6 on v5

--- a/solution.py
+++ b/solution.py
@@ -470,7 +470,7 @@
     n, k = len(deltas), len(own_lanes)
     weights, refs = refs[:k], refs[k:]
     grads, refs = refs[:grad_count], refs[grad_count:]
-    far_refs, refs = (refs[:4], refs[4:]) if far else ((), refs)
+    far_refs, refs = (refs[:RING], refs[RING:]) if far else ((), refs)
     sums, refs = (refs[:n], refs[n:]) if more else ((), refs)
     outs, refs = refs[:n], refs[n:]
     wbuf, gbuf, obuf, sem, g_sem, out_sem, *held = refs
@@ -498,10 +498,11 @@
             first, size, lane = far
             other_y = lax.rem(lax.div(chunk, 2), 2) != at_ref[3]
             other = lax.div(chunk, RING // 2) != core
-            source = 2 * other.astype(jnp.int32) + other_y.astype(jnp.int32)
+            source = 4 * other.astype(jnp.int32) + 2 * other_y.astype(jnp.int32)
+            source = source + lax.rem(chunk, 2)
             for j, ref in enumerate(far_refs):
                 copy = pltpu.make_async_copy(
-                    ref.at[lax.rem(chunk, 2), :, first : first + size],
+                    ref.at[:, first : first + size],
                     wbuf.at[i, :, lane : lane + size],
                     sem.at[i, k],
                 )
@@ -600,16 +601,19 @@
     block = jnp.concatenate((jnp.concatenate((keys, values), axis=1), ids), axis=0)
     twins = [block] + [chips_on(block, d) for d in range(1, HALF + 1)]
     others = [swapped(twins[d], "core") for d in range(HALF + 1)]
-    wanted = []
-    for w in (w_query, w_key, w_value):
-        w = w.reshape(2, 2, 2, 2, FEATS, -1)
-        w = lax.dynamic_index_in_dim(w, core, 0, keepdims=False)
-        w = lax.dynamic_index_in_dim(w, pair, 0, keepdims=False)
-        wanted.append(lax.dynamic_index_in_dim(w, 1 - xh, 1, keepdims=False))
-    wanted = jnp.concatenate(wanted, axis=2)
-    arrivals = [swapped(wanted, "xh")]
-    arrivals.append(next_y(arrivals[0]))
-    far_rows = (*arrivals, *(swapped(arrivals[h], "core") for h in range(2)))
+    mine, theirs = [], []
+    for k in range(2):
+        wanted = []
+        for w in (w_query, w_key, w_value):
+            w = w.reshape(2, 2, 2, 2, FEATS, -1)
+            w = lax.dynamic_index_in_dim(w, core, 0, keepdims=False)
+            w = lax.dynamic_index_in_dim(w, pair, 0, keepdims=False)
+            wanted.append(lax.dynamic_index_in_dim(w[k], 1 - xh, 0, keepdims=False))
+        wanted = jnp.concatenate(wanted, axis=1)
+        mine.append(swapped(wanted, "xh"))
+        theirs.append(next_y(mine[k]))
+    far_rows = (*mine, *theirs)
+    far_rows += tuple(swapped(x, "core") for x in far_rows)
 
     qseg = segment_ids[None, :]
     state = attention_stats(own, qseg, query, twins, others, NEAR, BLOCKS)

time: 203 us -> 199 us (0.980)
  waiting for transfers between devices: 76 us -> 65.9 us
  starting transfers between devices: 56.5 us -> 63.2 us
    ppermute x15 -> x18, waiting for transfers between devices: 0.04 us -> 29.2 us  [swapped(): return lax.ppermute(x, axis, [(0, 1), (1, 0)])]
    ppermute x5, waiting for transfers between devices: 19.4 us -> 0.51 us  [chips_on(): return lax.ppermute(x, AA, chip_pairs(d))]
    ppermute x1 -> x2, waiting for transfers between devices: 17.2 us -> 0.77 us  [next_y(): return lax.ppermute(x, 'y', [(0, 1), (1, 0), (2, 3), (3, 2)])]
    ppermute x15 -> x18, starting transfers between devices: 11.9 us -> 17.3 us  [swapped(): return lax.ppermute(x, axis, [(0, 1), (1, 0)])]
    ppermute x5, waiting for transfers between devices: 17.7 us -> 13 us  [chips_back(): return arrive(lax.ppermute(x, AA, [(j, i) for i, j in chip_pairs(d)]))]
    ppermute x5, starting transfers between devices: 7.97 us -> 10.4 us  [chips_back(): return arrive(lax.ppermute(x, AA, [(j, i) for i, j in chip_pairs(d)]))]
  transfers between devices with their start and end apart: 40 -> 44, of which waited for: 14 -> 15; matrix products, arithmetic and copies ran while one was open for 2% -> 2% of each run, Pallas kernels for 27% -> 21%
where the time goes in v6:
time: 199 us; the launch traced here: 198 us
  waiting for transfers between devices  65.9 us (33%)
  starting transfers between devices  63.2 us (32%)
  Pallas kernels  60.2 us (30%)
  local copies, waits for them, and re-layouts  4.81 us (2%)
  other arithmetic  2.98 us (1%)
    ppermute x18, waiting for transfers between devices, swapped(): return lax.ppermute(x, axis, [(0, 1), (1, 0)])  29.2 us
    ppermute x14, starting transfers between devices, round_z(): return lax.ppermute(x, 'z', [(i, (i + step) % RING) for i in range(RING)])  25.3 us
    ppermute x14, waiting for transfers between devices, round_z(): return lax.ppermute(x, 'z', [(i, (i + step) % RING) for i in range(RING)])  22.5 us
    pallas_call x5, Pallas kernels, project(): pl.pallas_call(lambda *refs: project_kernel(deltas, own_lanes, far, len(g...  21.8 us
    ppermute x18, starting transfers between devices, swapped(): return lax.ppermute(x, axis, [(0, 1), (1, 0)])  17.3 us
    ppermute x5, waiting for transfers between devices, chips_back(): return arrive(lax.ppermute(x, AA, [(j, i) for i, j in chip_pairs(d)]))  13 us
    pallas_call x1, Pallas kernels, attention_grads(): pl.pallas_call(grads_kernel, name='attention_grads', out_shape=(jax.Shape...  12.3 us
    pallas_call x2, Pallas kernels, attention_stats(): pl.pallas_call(lambda *refs: stats_kernel(low, high, *refs), name='stats_...  12.1 us
  transfers between devices with their start and end apart: 44, of which 15 were waited for; matrix products, arithmetic and copies ran while one was open for 2% of the time, Pallas kernels for 21%

profile of v6, /device:TPU:24, one launch (start us, length us, event | category | flops | bytes accessed | tf_op | source)
XLA Modules:
  0.0 197.9 jit_solution(9787939756863814250)
XLA Ops:
  0.0 0.7 pad_add_fusion.at_ref.refs_0_
  0.7 3.5 %split_w_out.1 = bf16[4,256,384]{2,1,0:T(8,128)(2,1)} custom-call(s32[4]{0:T(128)} %pad_add_fusion.at_ref.refs_0_, bf16[256,5376]{1,0:T(8,128)(2,1)} %refs_1_.6), custom_call_target="tpu_custom_call" | custom-call | tf_op jit(solution)/shard_map/split_w_out/pallas_call | solution.py:348
  4.1 3.1 %collective-permute-start.11 = (bf16[4,256,384]{2,1,0:T(8,128)(2,1)}, bf16[4,256,384]{2,1,0:T(8,128)(2,1)S(1)}, u32[]{:S(2)}, u32[]{:S(2)}) collective-permute-start(bf16[4,256,384]{2,1,0:T(8,128)(2,1)} %split_w_out.1), channel_id=1, source_target_pairs={{0,1},{1,0},{2,3},{3,2},{4,5},{5,4},{6,7},{7,6},{8,9},{9,8},{10,11... | collective-permute-start | bytes 2359304 | tf_op jit(solution)/shard_map/ppermute | solution.py:559
  7.2 1.9 collective-permute-start.13
  9.2 3.2 %collective-permute-start.3 = (bf16[400,256]{1,0:T(8,128)(2,1)S(1)}, bf16[400,256]{1,0:T(8,128)(2,1)S(1)}, u32[]{:S(2)}, u32[]{:S(2)}) collective-permute-start(bf16[400,256]{1,0:T(8,128)(2,1)S(1)} %fusion.2.refs_3_.refs_6_), channel_id=1, source_target_pairs={{0,64},{16,80},{32,96},{48,112},{64,128},{80,144},{96,160},{112,17... | collective-permute-start | bytes 614408 | tf_op jit(solution)/shard_map/ppermute | solution.py:571
  12.4 13.9 %collective-permute-done.11.refs_2_ = bf16[4,256,384]{2,1,0:T(8,128)(2,1)S(1)} collective-permute-done((bf16[4,256,384]{2,1,0:T(8,128)(2,1)}, bf16[4,256,384]{2,1,0:T(8,128)(2,1)S(1)}, u32[]{:S(2)}, u32[]{:S(2)}) %collective-permute-start.11) | collective-permute-done | bytes 786464 | tf_op jit(solution)/shard_map/ppermute | solution.py:559
  26.4 5.9 %collective-permute-start.14 = (bf16[336,384]{1,0:T(8,128)(2,1)S(1)}, bf16[336,384]{1,0:T(8,128)(2,1)S(1)}, u32[]{:S(2)}, u32[]{:S(2)}) collective-permute-start(bf16[336,384]{1,0:T(8,128)(2,1)S(1)} %bitcast.30), channel_id=1, source_target_pairs={{0,14},{2,0},{4,2},{6,4},{8,6},{10,8},{12,10},{14,12},{1,15},{3,1}... | collective-permute-start | bytes 774152 | tf_op jit(solution)/shard_map/ppermute | solution.py:579
  32.2 1.9 collective-permute-start
  34.2 0.3 collective-permute-start.1
  34.5 3.9 %collective-permute-done.14.refs_6_ = bf16[336,384]{1,0:T(8,128)(2,1)S(1)} collective-permute-done((bf16[336,384]{1,0:T(8,128)(2,1)S(1)}, bf16[336,384]{1,0:T(8,128)(2,1)S(1)}, u32[]{:S(2)}, u32[]{:S(2)}) %collective-permute-start.14) | collective-permute-done | bytes 258080 | tf_op jit(solution)/shard_map/ppermute | solution.py:579
  38.4 3.7 %collective-permute-start.16 = (bf16[336,384]{1,0:T(8,128)(2,1)S(1)}, bf16[336,384]{1,0:T(8,128)(2,1)S(1)}, u32[]{:S(2)}, u32[]{:S(2)}) collective-permute-start(bf16[336,384]{1,0:T(8,128)(2,1)S(1)} %collective-permute-done.14.refs_6_), channel_id=1, source_target_pairs={{0,14},{2,0},{4,2},{6,4},{8,6},{10,8},{12,10},{14,12},{1,15},{3,1}... | collective-permute-start | bytes 774152 | tf_op jit(solution)/shard_map/ppermute | solution.py:579
  42.1 2.4 %collective-permute-start.5 = (bf16[400,256]{1,0:T(8,128)(2,1)S(1)}, bf16[400,256]{1,0:T(8,128)(2,1)S(1)}, u32[]{:S(2)}, u32[]{:S(2)}) collective-permute-start(bf16[400,256]{1,0:T(8,128)(2,1)S(1)} %fusion.2.refs_3_.refs_6_), channel_id=1, source_target_pairs={{0,96},{16,112},{32,128},{48,144},{64,160},{80,176},{96,192},{112,... | collective-permute-start | bytes 614408 | tf_op jit(solution)/shard_map/ppermute | solution.py:571
  44.6 1.3 collective-permute-start.6
  45.9 1.5 collective-permute-done.16.refs_8_
  47.3 3.7 %collective-permute-start.18 = (bf16[336,384]{1,0:T(8,128)(2,1)S(1)}, bf16[336,384]{1,0:T(8,128)(2,1)S(1)}, u32[]{:S(2)}, u32[]{:S(2)}) collective-permute-start(bf16[336,384]{1,0:T(8,128)(2,1)S(1)} %collective-permute-done.16.refs_8_), channel_id=1, source_target_pairs={{0,14},{2,0},{4,2},{6,4},{8,6},{10,8},{12,10},{14,12},{1,15},{3,1}... | collective-permute-start | bytes 774152 | tf_op jit(solution)/shard_map/ppermute | solution.py:579
  51.0 0.5 collective-permute-done.5.refs_8_.refs_9_
  51.6 1.3 collective-permute-start.9
  52.9 0.5 collective-permute-start.2
  53.4 2.1 %collective-permute-done.18.refs_10_ = bf16[336,384]{1,0:T(8,128)(2,1)S(1)} collective-permute-done((bf16[336,384]{1,0:T(8,128)(2,1)S(1)}, bf16[336,384]{1,0:T(8,128)(2,1)S(1)}, u32[]{:S(2)}, u32[]{:S(2)}) %collective-permute-start.18) | collective-permute-done | bytes 258080 | tf_op jit(solution)/shard_map/ppermute | solution.py:579
  55.5 3.4 %collective-permute-done.19.refs_11_ = bf16[336,384]{1,0:T(8,128)(2,1)S(1)} collective-permute-done((bf16[336,384]{1,0:T(8,128)(2,1)S(1)}, bf16[336,384]{1,0:T(8,128)(2,1)S(1)}, u32[]{:S(2)}, u32[]{:S(2)}) %collective-permute-start.19) | collective-permute-done | bytes 258080 | tf_op jit(solution)/shard_map/ppermute | solution.py:579
  58.9 0.6 copy-done.29
  59.6 6.3 %dout_parts.1 = (f32[256,384]{1,0:T(8,128)}, bf16[256,384]{1,0:T(8,128)(2,1)}) custom-call(s32[4]{0:T(128)} %pad_add_fusion.at_ref.refs_0_, bf16[256,5376]{1,0:T(8,128)(2,1)} %refs_1_.6, bf16[4,256,384]{2,1,0:T(8,128)(2,1)} %copy-done.16, bf16[4,256,384]{2,1,0:T(8,128)(2,1)S(1)} %collective-permute-done.12.refs_3_, bf16[336,384]{1,0:T(8,128)(2,1)} %bitcast.28, ...), custom_call_target="tpu_custom_call" | custom-call | tf_op jit(solution)/shard_map/dout_parts/pallas_call | solution.py:408
  65.9 3.3 %collective-permute-start.20 = (bf16[256,384]{1,0:T(8,128)(2,1)}, bf16[256,384]{1,0:T(8,128)(2,1)S(1)}, u32[]{:S(2)}, u32[]{:S(2)}) collective-permute-start(bf16[256,384]{1,0:T(8,128)(2,1)} %get-tuple-element.49), channel_id=1, source_target_pairs={{0,1},{1,0},{2,3},{3,2},{4,5},{5,4},{6,7},{7,6},{8,9},{9,8},{10,11... | collective-permute-start | bytes 589832 | tf_op jit(solution)/shard_map/ppermute | solution.py:559
  69.2 0.5 broadcast_in_dim.8.refs_1_
  69.8 1.0 dynamic-slice_bitcast_fusion
  70.8 0.7 copy-done.12
  71.5 6.3 %stats_near.1 = (f32[1,768]{1,0:T(1,128)}, f32[1,768]{1,0:T(1,128)}, f32[128,768]{1,0:T(8,128)}, s32[1,384]{1,0:T(1,128)}) custom-call(s32[1]{0:T(128)} %bitcast.4.refs_0_.own_ref, s32[1,384]{1,0:T(1,128)} %broadcast_in_dim.8.refs_1_, bf16[384,256]{1,0:T(8,128)(2,1)} %refs_1_.7, bf16[400,256]{1,0:T(8,128)(2,1)} %copy-done.6, bf16[400,256]{1,0:T(8,128)(2,1)} %copy-done.8, ...), custom_call_target="tpu_custom_call" | custom-call | tf_op jit(solution)/shard_map/stats_near/pallas_call | solution.py:284
  77.8 0.6 copy-done.13
  78.6 5.8 %stats_far.1 = (f32[1,768]{1,0:T(1,128)}, f32[128,768]{1,0:T(8,128)}, s32[1,384]{1,0:T(1,128)}, s32[1]{0:T(128)}) custom-call(s32[1]{0:T(128)} %bitcast.4.refs_0_.own_ref, s32[1,384]{1,0:T(1,128)} %broadcast_in_dim.8.refs_1_, bf16[384,256]{1,0:T(8,128)(2,1)} %refs_1_.7, f32[1,768]{1,0:T(1,128)} %get-tuple-element.42.refs_3_, ...), custom_call_target="tpu_custom_call" | custom-call | tf_op jit(solution)/shard_map/stats_far/pallas_call | solution.py:284
  84.4 12.3 %attention_grads.1 = (bf16[256,384]{1,0:T(8,128)(2,1)}, bf16[5,384,256]{2,1,0:T(8,128)(2,1)}, bf16[5,384,256]{2,1,0:T(8,128)(2,1)}) custom-call(s32[1]{0:T(128)} %bitcast.4.refs_0_.own_ref, s32[1]{0:T(128)} %get-tuple-element.46.low_ref, s32[1,384]{1,0:T(1,128)} %get-tuple-element.47.refs_0_, bf16[384,256]{1,0:T(8,128)(2,1)} %refs_1_.7, ...), custom_call_target="tpu_custom_call" | custom-call | tf_op jit(solution)/shard_map/attention_grads/pallas_call | solution.py:298
  96.7 2.2 %collective-permute-start.21 = (bf16[5,384,256]{2,1,0:T(8,128)(2,1)}, bf16[5,384,256]{2,1,0:T(8,128)(2,1)S(1)}, u32[]{:S(2)}, u32[]{:S(2)}) collective-permute-start(bf16[5,384,256]{2,1,0:T(8,128)(2,1)} %get-tuple-element.53), channel_id=1, source_target_pairs={{0,16},{16,0},{1,17},{17,1},{2,18},{18,2},{3,19},{19,3},{4,20},{20... | collective-permute-start | bytes 2949128 | tf_op jit(solution)/shard_map/ppermute | solution.py:559
  98.9 1.0 dynamic-slice_bitcast_fusion.2
  100.0 0.6 collective-permute-start.28
  100.6 3.1 %collective-permute-start.29 = (bf16[336,512]{1,0:T(8,128)(2,1)S(1)}, bf16[336,512]{1,0:T(8,128)(2,1)S(1)}, u32[]{:S(2)}, u32[]{:S(2)}) collective-permute-start(bf16[336,512]{1,0:T(8,128)(2,1)S(1)} %pad_maximum_fusion.1), channel_id=1, source_target_pairs={{0,1},{1,0},{2,3},{3,2},{4,5},{5,4},{6,7},{7,6},{8,9},{9,8},{10,11... | collective-permute-start | bytes 1032200 | tf_op jit(solution)/shard_map/ppermute | solution.py:559
  103.8 8.8 %collective-permute-done.28.refs_5_.refs_2_.refs_6_ = bf16[336,512]{1,0:T(8,128)(2,1)S(1)} collective-permute-done((bf16[336,512]{1,0:T(8,128)(2,1)S(1)}, bf16[336,512]{1,0:T(8,128)(2,1)S(1)}, u32[]{:S(2)}, u32[]{:S(2)}) %collective-permute-start.28) | collective-permute-done | bytes 344096 | tf_op jit(solution)/shard_map/ppermute | solution.py:559
  112.5 6.4 %collective-permute-done.29.refs_6_.refs_3_.refs_7_ = bf16[336,512]{1,0:T(8,128)(2,1)S(1)} collective-permute-done((bf16[336,512]{1,0:T(8,128)(2,1)S(1)}, bf16[336,512]{1,0:T(8,128)(2,1)S(1)}, u32[]{:S(2)}, u32[]{:S(2)}) %collective-permute-start.29) | collective-permute-done | bytes 344096 | tf_op jit(solution)/shard_map/ppermute | solution.py:559
  119.0 2.5 %join_partials.1 = (f32[384,256]{1,0:T(8,128)}, bf16[384,256]{1,0:T(8,128)(2,1)}, bf16[384,256]{1,0:T(8,128)(2,1)}, bf16[384,256]{1,0:T(8,128)(2,1)}, bf16[384,2...) custom-call(s32[1]{0:T(128)} %bitcast.2.core_ref, bf16[5,384,256]{2,1,0:T(8,128)(2,1)} %get-tuple-element.52.mine_ref, ...), custom_call_target="tpu_custom_call" | custom-call | tf_op jit(solution)/shard_map/join_partials/pallas_call | solution.py:442
  121.5 0.7 collective-permute-start.22
  122.2 1.3 collective-permute-start.23
  123.5 1.9 collective-permute-start.24
  125.4 1.9 collective-permute-start.25
  127.4 0.8 collective-permute-done.31.refs_8_.refs_5_.refs_9_
  128.1 4.6 %collective-permute-start.26 = (bf16[384,256]{1,0:T(8,128)(2,1)}, bf16[384,256]{1,0:T(8,128)(2,1)S(1)}, u32[]{:S(2)}, u32[]{:S(2)}) collective-permute-start(bf16[384,256]{1,0:T(8,128)(2,1)} %get-tuple-element.59), channel_id=1, source_target_pairs={{32,0},{48,16},{64,32},{80,48},{96,64},{112,80},{128,96},{144,112}... | collective-permute-start | bytes 589832 | tf_op jit(solution)/shard_map/ppermute | solution.py:575
  132.8 0.3 collective-permute-start.33
  133.1 3.2 %collective-permute-done.24.refs_2_ = bf16[384,256]{1,0:T(8,128)(2,1)S(1)} collective-permute-done((bf16[384,256]{1,0:T(8,128)(2,1)}, bf16[384,256]{1,0:T(8,128)(2,1)S(1)}, u32[]{:S(2)}, u32[]{:S(2)}) %collective-permute-start.24) | collective-permute-done | bytes 196640 | tf_op jit(solution)/shard_map/ppermute | solution.py:575
  136.2 8.0 %collective-permute-done.25.refs_3_ = bf16[384,256]{1,0:T(8,128)(2,1)S(1)} collective-permute-done((bf16[384,256]{1,0:T(8,128)(2,1)}, bf16[384,256]{1,0:T(8,128)(2,1)S(1)}, u32[]{:S(2)}, u32[]{:S(2)}) %collective-permute-start.25) | collective-permute-done | bytes 196640 | tf_op jit(solution)/shard_map/ppermute | solution.py:575
  144.3 1.8 collective-permute-done.26.refs_4_
  146.1 2.0 collective-permute-start.36
  148.0 1.9 total_partials.1.refs_3_
  149.9 1.9 collective-permute-start.27
  151.8 5.2 %project.5 = (f32[336,384]{1,0:T(8,128)}, f32[336,384]{1,0:T(8,128)}, f32[336,384]{1,0:T(8,128)}, f32[336,384]{1,0:T(8,128)}, f32[336,384]{1,0:T(8,128)}, /*inde...) custom-call(s32[4]{0:T(128)} %pad_add_fusion.at_ref.refs_0_, bf16[5376,256]{1,0:T(8,128)(2,1)} %refs_1_.8, ...), custom_call_target="tpu_custom_call" | custom-call | tf_op jit(solution)/shard_map/project/pallas_call | solution.py:536
  157.1 3.7 %project.6 = (f32[336,384]{1,0:T(8,128)}, f32[336,384]{1,0:T(8,128)}) custom-call(s32[4]{0:T(128)} %pad_add_fusion.at_ref.refs_0_, bf16[5376,128]{1,0:T(8,128)(2,1)} %refs_1_.11, bf16[5376,128]{1,0:T(8,128)(2,1)} %refs_2_.9, bf16[256,384]{1,0:T(8,128)(2,1)} %total_partials.1.refs_3_, bf16[256,384]{1,0:T(8,128)(2,1)S(1)} %collective-permute-done.36.refs_4_, ...), custom_call_target="tpu_custom_call" | custom-call | tf_op jit(solution)/shard_map/project/pallas_call | solution.py:536
  160.8 3.3 %project.7 = (bf16[336,384]{1,0:T(8,128)(2,1)}, bf16[336,384]{1,0:T(8,128)(2,1)}) custom-call(s32[4]{0:T(128)} %pad_add_fusion.at_ref.refs_0_, bf16[256,384]{1,0:T(8,128)(2,1)S(1)} %collective-permute-done.27.refs_1_.refs_5_, bf16[336,512]{1,0:T(8,128)(2,1)} %copy-done, bf16[336,512]{1,0:T(8,128)(2,1)} %copy-done.1, bf16[336,512]{1,0:T(8,128)(2,1)} %copy-done.2, ...), custom_call_target="tpu_custom_call" | custom-call | tf_op jit(solution)/shard_map/project/pallas_call | solution.py:536
  164.2 3.2 %collective-permute-start.41 = (bf16[336,384]{1,0:T(8,128)(2,1)}, bf16[336,384]{1,0:T(8,128)(2,1)S(1)}, u32[]{:S(2)}, u32[]{:S(2)}) collective-permute-start(bf16[336,384]{1,0:T(8,128)(2,1)} %get-tuple-element.75), channel_id=1, source_target_pairs={{0,14},{2,0},{4,2},{6,4},{8,6},{10,8},{12,10},{14,12},{1,15},{3,1}... | collective-permute-start | bytes 774152 | tf_op jit(solution)/shard_map/ppermute | solution.py:579
  167.4 5.3 %project.8 = (f32[336,384]{1,0:T(8,128)}, f32[336,384]{1,0:T(8,128)}, f32[336,384]{1,0:T(8,128)}, f32[336,384]{1,0:T(8,128)}) custom-call(s32[4]{0:T(128)} %pad_add_fusion.at_ref.refs_0_, bf16[5376,128]{1,0:T(8,128)(2,1)} %refs_1_.11, bf16[5376,128]{1,0:T(8,128)(2,1)} %refs_2_.9, bf16[256,384]{1,0:T(8,128)(2,1)} %total_partials.1.refs_3_, ...), custom_call_target="tpu_custom_call" | custom-call | tf_op jit(solution)/shard_map/project/pallas_call | solution.py:536
  172.7 1.2 add_convert_fusion.5
  173.9 0.1 collective-permute-start.38
  174.1 3.3 %collective-permute-start.42 = (bf16[336,384]{1,0:T(8,128)(2,1)S(1)}, bf16[336,384]{1,0:T(8,128)(2,1)S(1)}, u32[]{:S(2)}, u32[]{:S(2)}) collective-permute-start(bf16[336,384]{1,0:T(8,128)(2,1)S(1)} %add_convert_fusion.2), channel_id=1, source_target_pairs={{0,14},{2,0},{4,2},{6,4},{8,6},{10,8},{12,10},{14,12},{1,15},{3,1}... | collective-permute-start | bytes 774152 | tf_op jit(solution)/shard_map/ppermute | solution.py:579
  177.4 4.2 %collective-permute-done.38 = bf16[336,384]{1,0:T(8,128)(2,1)S(1)} collective-permute-done((bf16[336,384]{1,0:T(8,128)(2,1)S(1)}, bf16[336,384]{1,0:T(8,128)(2,1)S(1)}, u32[]{:S(2)}, u32[]{:S(2)}) %collective-permute-start.38) | collective-permute-done | bytes 258080 | tf_op jit(solution)/shard_map/ppermute | solution.py:579
  181.7 4.3 %project.9 = (f32[336,384]{1,0:T(8,128)}, f32[336,384]{1,0:T(8,128)}) custom-call(s32[4]{0:T(128)} %pad_add_fusion.at_ref.refs_0_, bf16[5376,128]{1,0:T(8,128)(2,1)} %refs_1_.11, bf16[5376,128]{1,0:T(8,128)(2,1)} %refs_2_.9, bf16[256,384]{1,0:T(8,128)(2,1)} %total_partials.1.refs_3_, bf16[256,384]{1,0:T(8,128)(2,1)S(1)} %collective-permute-done.36.refs_4_, ...), custom_call_target="tpu_custom_call" | custom-call | tf_op jit(solution)/shard_map/project/pallas_call | solution.py:536
  186.1 3.3 %collective-permute-start.43 = (bf16[336,384]{1,0:T(8,128)(2,1)S(1)}, bf16[336,384]{1,0:T(8,128)(2,1)S(1)}, u32[]{:S(2)}, u32[]{:S(2)}) collective-permute-start(bf16[336,384]{1,0:T(8,128)(2,1)S(1)} %add_convert_fusion.1), channel_id=1, source_target_pairs={{0,14},{2,0},{4,2},{6,4},{8,6},{10,8},{12,10},{14,12},{1,15},{3,1}... | collective-permute-start | bytes 774152 | tf_op jit(solution)/shard_map/ppermute | solution.py:579
  189.6 3.7 %collective-permute-done.43 = bf16[336,384]{1,0:T(8,128)(2,1)S(1)} collective-permute-done((bf16[336,384]{1,0:T(8,128)(2,1)S(1)}, bf16[336,384]{1,0:T(8,128)(2,1)S(1)}, u32[]{:S(2)}, u32[]{:S(2)}) %collective-permute-start.43) | collective-permute-done | bytes 258080 | tf_op jit(solution)/shard_map/ppermute | solution.py:579
  193.2 3.8 %collective-permute-done.40 = bf16[336,384]{1,0:T(8,128)(2,1)S(1)} collective-permute-done((bf16[336,384]{1,0:T(8,128)(2,1)S(1)}, bf16[336,384]{1,0:T(8,128)(2,1)S(1)}, u32[]{:S(2)}, u32[]{:S(2)}) %collective-permute-start.40) | collective-permute-done | bytes 258080 | tf_op jit(solution)/shard_map/ppermute | solution.py:579
  197.1 0.8 fusion.1
  (118 shorter events, 1.0 us)
Async XLA Ops:
  0.7 8.5 %copy-start.31 = (bf16[384,128]{1,0:T(8,128)(2,1)S(1)}, bf16[384,128]{1,0:T(8,128)(2,1)}, u32[]{:S(2)}) copy-start(bf16[384,128]{1,0:T(8,128)(2,1)} %param.11) | copy-start | bytes 294916
  0.7 8.5 %copy-start.32 = (bf16[384,128]{1,0:T(8,128)(2,1)S(1)}, bf16[384,128]{1,0:T(8,128)(2,1)}, u32[]{:S(2)}) copy-start(bf16[384,128]{1,0:T(8,128)(2,1)} %param.10) | copy-start | bytes 294916
  4.1 22.2 %collective-permute-start.11 = (bf16[4,256,384]{2,1,0:T(8,128)(2,1)}, bf16[4,256,384]{2,1,0:T(8,128)(2,1)S(1)}, u32[]{:S(2)}, u32[]{:S(2)}) collective-permute-start(bf16[4,256,384]{2,1,0:T(8,128)(2,1)} %split_w_out.1), channel_id=1, source_target_pairs={{0,1},{1,0},{2,3},{3,2},{4,5},{5,4},{6,7},{7,6},{8,9},{9,8},{10,11... | collective-permute-start | bytes 2359304 | tf_op jit(solution)/shard_map/ppermute | solution.py:559
  7.2 25.0 %collective-permute-start.13 = (bf16[336,384]{1,0:T(8,128)(2,1)S(1)}, bf16[336,384]{1,0:T(8,128)(2,1)S(1)}, u32[]{:S(2)}, u32[]{:S(2)}) collective-permute-start(bf16[336,384]{1,0:T(8,128)(2,1)S(1)} %bitcast.29), channel_id=1, source_target_pairs={{0,2},{2,4},{4,6},{6,8},{8,10},{10,12},{12,14},{14,0},{1,3},{3,5},... | collective-permute-start | bytes 774152 | tf_op jit(solution)/shard_map/ppermute | solution.py:579
  9.2 56.6 %copy-start.6 = (bf16[400,256]{1,0:T(8,128)(2,1)}, bf16[400,256]{1,0:T(8,128)(2,1)S(1)}, u32[]{:S(2)}) copy-start(bf16[400,256]{1,0:T(8,128)(2,1)S(1)} %fusion.2.refs_3_.refs_6_) | copy-start | bytes 614404
  9.2 24.9 %collective-permute-start.3 = (bf16[400,256]{1,0:T(8,128)(2,1)S(1)}, bf16[400,256]{1,0:T(8,128)(2,1)S(1)}, u32[]{:S(2)}, u32[]{:S(2)}) collective-permute-start(bf16[400,256]{1,0:T(8,128)(2,1)S(1)} %fusion.2.refs_3_.refs_6_), channel_id=1, source_target_pairs={{0,64},{16,80},{32,96},{48,112},{64,128},{80,144},{96,160},{112,17... | collective-permute-start | bytes 614408 | tf_op jit(solution)/shard_map/ppermute | solution.py:571
  26.3 32.6 %copy-start.16 = (bf16[4,256,384]{2,1,0:T(8,128)(2,1)}, bf16[4,256,384]{2,1,0:T(8,128)(2,1)S(1)}, u32[]{:S(2)}) copy-start(bf16[4,256,384]{2,1,0:T(8,128)(2,1)S(1)} %collective-permute-done.11.refs_2_) | copy-start | bytes 2359300
  26.3 32.5 %collective-permute-start.12 = (bf16[4,256,384]{2,1,0:T(8,128)(2,1)S(1)}, bf16[4,256,384]{2,1,0:T(8,128)(2,1)S(1)}, u32[]{:S(2)}, u32[]{:S(2)}) collective-permute-start(bf16[4,256,384]{2,1,0:T(8,128)(2,1)S(1)} %collective-permute-done.11.refs_2_), channel_id=1, source_target_pairs={{0,16},{16,0},{1,17},{17,1},{2,18},{18,2},{3,19},{19,3},{4,20},{20... | collective-permute-start | bytes 2359304 | tf_op jit(solution)/shard_map/ppermute | solution.py:559
  26.4 12.0 %collective-permute-start.14 = (bf16[336,384]{1,0:T(8,128)(2,1)S(1)}, bf16[336,384]{1,0:T(8,128)(2,1)S(1)}, u32[]{:S(2)}, u32[]{:S(2)}) collective-permute-start(bf16[336,384]{1,0:T(8,128)(2,1)S(1)} %bitcast.30), channel_id=1, source_target_pairs={{0,14},{2,0},{4,2},{6,4},{8,6},{10,8},{12,10},{14,12},{1,15},{3,1}... | collective-permute-start | bytes 774152 | tf_op jit(solution)/shard_map/ppermute | solution.py:579
  32.2 9.9 %copy-start.23 = (bf16[336,384]{1,0:T(8,128)(2,1)}, bf16[336,384]{1,0:T(8,128)(2,1)S(1)}, u32[]{:S(2)}) copy-start(bf16[336,384]{1,0:T(8,128)(2,1)S(1)} %collective-permute-done.13.refs_5_) | copy-start | bytes 774148
  32.2 9.8 %collective-permute-start.15 = (bf16[336,384]{1,0:T(8,128)(2,1)S(1)}, bf16[336,384]{1,0:T(8,128)(2,1)S(1)}, u32[]{:S(2)}, u32[]{:S(2)}) collective-permute-start(bf16[336,384]{1,0:T(8,128)(2,1)S(1)} %collective-permute-done.13.refs_5_), channel_id=1, source_target_pairs={{0,2},{2,4},{4,6},{6,8},{8,10},{10,12},{12,14},{14,0},{1,3},{3,5},... | collective-permute-start | bytes 774152 | tf_op jit(solution)/shard_map/ppermute | solution.py:579
  32.2 9.9 %collective-permute-start = (bf16[400,256]{1,0:T(8,128)(2,1)S(1)}, bf16[400,256]{1,0:T(8,128)(2,1)S(1)}, u32[]{:S(2)}, u32[]{:S(2)}) collective-permute-start(bf16[400,256]{1,0:T(8,128)(2,1)S(1)} %fusion.2.refs_3_.refs_6_), channel_id=1, source_target_pairs={{0,32},{16,48},{32,64},{48,80},{64,96},{80,112},{96,128},{112,144}... | collective-permute-start | bytes 614408 | tf_op jit(solution)/shard_map/ppermute | solution.py:571
  34.2 31.7 %copy-start.7 = (bf16[400,256]{1,0:T(8,128)(2,1)}, bf16[400,256]{1,0:T(8,128)(2,1)S(1)}, u32[]{:S(2)}) copy-start(bf16[400,256]{1,0:T(8,128)(2,1)S(1)} %collective-permute-done.3.refs_7_.refs_8_) | copy-start | bytes 614404
  34.2 10.4 %collective-permute-start.1 = (bf16[400,256]{1,0:T(8,128)(2,1)S(1)}, bf16[400,256]{1,0:T(8,128)(2,1)S(1)}, u32[]{:S(2)}, u32[]{:S(2)}) collective-permute-start(bf16[400,256]{1,0:T(8,128)(2,1)S(1)} %fusion.2.refs_3_.refs_6_), channel_id=1, source_target_pairs={{0,16},{16,0},{1,17},{17,1},{2,18},{18,2},{3,19},{19,3},{4,20},{20... | collective-permute-start | bytes 614408 | tf_op jit(solution)/shard_map/ppermute | solution.py:559
  38.4 15.0 %copy-start.24 = (bf16[336,384]{1,0:T(8,128)(2,1)}, bf16[336,384]{1,0:T(8,128)(2,1)S(1)}, u32[]{:S(2)}) copy-start(bf16[336,384]{1,0:T(8,128)(2,1)S(1)} %collective-permute-done.14.refs_6_) | copy-start | bytes 774148
  38.4 9.0 %collective-permute-start.16 = (bf16[336,384]{1,0:T(8,128)(2,1)S(1)}, bf16[336,384]{1,0:T(8,128)(2,1)S(1)}, u32[]{:S(2)}, u32[]{:S(2)}) collective-permute-start(bf16[336,384]{1,0:T(8,128)(2,1)S(1)} %collective-permute-done.14.refs_6_), channel_id=1, source_target_pairs={{0,14},{2,0},{4,2},{6,4},{8,6},{10,8},{12,10},{14,12},{1,15},{3,1}... | collective-permute-start | bytes 774152 | tf_op jit(solution)/shard_map/ppermute | solution.py:579
  42.1 13.4 %copy-start.25 = (bf16[336,384]{1,0:T(8,128)(2,1)}, bf16[336,384]{1,0:T(8,128)(2,1)S(1)}, u32[]{:S(2)}) copy-start(bf16[336,384]{1,0:T(8,128)(2,1)S(1)} %collective-permute-done.15.refs_7_) | copy-start | bytes 774148
  42.1 9.0 %collective-permute-start.17 = (bf16[336,384]{1,0:T(8,128)(2,1)S(1)}, bf16[336,384]{1,0:T(8,128)(2,1)S(1)}, u32[]{:S(2)}, u32[]{:S(2)}) collective-permute-start(bf16[336,384]{1,0:T(8,128)(2,1)S(1)} %collective-permute-done.15.refs_7_), channel_id=1, source_target_pairs={{0,2},{2,4},{4,6},{6,8},{8,10},{10,12},{12,14},{14,0},{1,3},{3,5},... | collective-permute-start | bytes 774152 | tf_op jit(solution)/shard_map/ppermute | solution.py:579
  42.1 23.8 %copy-start.8 = (bf16[400,256]{1,0:T(8,128)(2,1)}, bf16[400,256]{1,0:T(8,128)(2,1)S(1)}, u32[]{:S(2)}) copy-start(bf16[400,256]{1,0:T(8,128)(2,1)S(1)} %collective-permute-done.refs_4_.refs_7_) | copy-start | bytes 614404
  42.1 9.5 %collective-permute-start.5 = (bf16[400,256]{1,0:T(8,128)(2,1)S(1)}, bf16[400,256]{1,0:T(8,128)(2,1)S(1)}, u32[]{:S(2)}, u32[]{:S(2)}) collective-permute-start(bf16[400,256]{1,0:T(8,128)(2,1)S(1)} %fusion.2.refs_3_.refs_6_), channel_id=1, source_target_pairs={{0,96},{16,112},{32,128},{48,144},{64,160},{80,176},{96,192},{112,... | collective-permute-start | bytes 614408 | tf_op jit(solution)/shard_map/ppermute | solution.py:571
  44.6 21.3 %copy-start.9 = (bf16[400,256]{1,0:T(8,128)(2,1)}, bf16[400,256]{1,0:T(8,128)(2,1)S(1)}, u32[]{:S(2)}) copy-start(bf16[400,256]{1,0:T(8,128)(2,1)S(1)} %collective-permute-done.1.refs_5_.refs_11_) | copy-start | bytes 614404
  44.6 8.3 %collective-permute-start.6 = (bf16[400,256]{1,0:T(8,128)(2,1)S(1)}, bf16[400,256]{1,0:T(8,128)(2,1)S(1)}, u32[]{:S(2)}, u32[]{:S(2)}) collective-permute-start(bf16[400,256]{1,0:T(8,128)(2,1)S(1)} %fusion.2.refs_3_.refs_6_), channel_id=1, source_target_pairs={{0,128},{16,144},{32,160},{48,176},{64,192},{80,208},{96,224},{112... | collective-permute-start | bytes 614408 | tf_op jit(solution)/shard_map/ppermute | solution.py:571
  47.3 12.2 %copy-start.26 = (bf16[336,384]{1,0:T(8,128)(2,1)}, bf16[336,384]{1,0:T(8,128)(2,1)S(1)}, u32[]{:S(2)}) copy-start(bf16[336,384]{1,0:T(8,128)(2,1)S(1)} %collective-permute-done.16.refs_8_) | copy-start | bytes 774148
  47.3 8.1 %collective-permute-start.18 = (bf16[336,384]{1,0:T(8,128)(2,1)S(1)}, bf16[336,384]{1,0:T(8,128)(2,1)S(1)}, u32[]{:S(2)}, u32[]{:S(2)}) collective-permute-start(bf16[336,384]{1,0:T(8,128)(2,1)S(1)} %collective-permute-done.16.refs_8_), channel_id=1, source_target_pairs={{0,14},{2,0},{4,2},{6,4},{8,6},{10,8},{12,10},{14,12},{1,15},{3,1}... | collective-permute-start | bytes 774152 | tf_op jit(solution)/shard_map/ppermute | solution.py:579
  51.0 7.8 %collective-permute-start.19 = (bf16[336,384]{1,0:T(8,128)(2,1)S(1)}, bf16[336,384]{1,0:T(8,128)(2,1)S(1)}, u32[]{:S(2)}, u32[]{:S(2)}) collective-permute-start(bf16[336,384]{1,0:T(8,128)(2,1)S(1)} %collective-permute-done.17.refs_9_), channel_id=1, source_target_pairs={{0,2},{2,4},{4,6},{6,8},{8,10},{10,12},{12,14},{14,0},{1,3},{3,5},... | collective-permute-start | bytes 774152 | tf_op jit(solution)/shard_map/ppermute | solution.py:579
  51.5 14.3 %copy-start.10 = (bf16[400,256]{1,0:T(8,128)(2,1)}, bf16[400,256]{1,0:T(8,128)(2,1)S(1)}, u32[]{:S(2)}) copy-start(bf16[400,256]{1,0:T(8,128)(2,1)S(1)} %collective-permute-done.5.refs_8_.refs_9_) | copy-start | bytes 614404
  51.6 1.3 collective-permute-start.9
  52.9 13.0 %copy-start.11 = (bf16[400,256]{1,0:T(8,128)(2,1)}, bf16[400,256]{1,0:T(8,128)(2,1)S(1)}, u32[]{:S(2)}) copy-start(bf16[400,256]{1,0:T(8,128)(2,1)S(1)} %collective-permute-done.6.refs_9_.refs_10_) | copy-start | bytes 614404
  52.9 13.0 %collective-permute-start.4 = (bf16[400,256]{1,0:T(8,128)(2,1)S(1)}, bf16[400,256]{1,0:T(8,128)(2,1)S(1)}, u32[]{:S(2)}, u32[]{:S(2)}) collective-permute-start(bf16[400,256]{1,0:T(8,128)(2,1)S(1)} %collective-permute-done.3.refs_7_.refs_8_), channel_id=1, source_target_pairs={{0,16},{16,0},{1,17},{17,1},{2,18},{18,2},{3,19},{19,3},{4,20},{20... | collective-permute-start | bytes 614408 | tf_op jit(solution)/shard_map/ppermute | solution.py:559
  52.9 17.9 %collective-permute-start.2 = (bf16[400,256]{1,0:T(8,128)(2,1)S(1)}, bf16[400,256]{1,0:T(8,128)(2,1)S(1)}, u32[]{:S(2)}, u32[]{:S(2)}) collective-permute-start(bf16[400,256]{1,0:T(8,128)(2,1)S(1)} %collective-permute-done.refs_4_.refs_7_), channel_id=1, source_target_pairs={{0,16},{16,0},{1,17},{17,1},{2,18},{18,2},{3,19},{19,3},{4,20},{20... | collective-permute-start | bytes 614408 | tf_op jit(solution)/shard_map/ppermute | solution.py:559
  55.5 22.3 %collective-permute-start.7 = (bf16[400,256]{1,0:T(8,128)(2,1)S(1)}, bf16[400,256]{1,0:T(8,128)(2,1)S(1)}, u32[]{:S(2)}, u32[]{:S(2)}) collective-permute-start(bf16[400,256]{1,0:T(8,128)(2,1)S(1)} %collective-permute-done.5.refs_8_.refs_9_), channel_id=1, source_target_pairs={{0,16},{16,0},{1,17},{17,1},{2,18},{18,2},{3,19},{19,3},{4,20},{20... | collective-permute-start | bytes 614408 | tf_op jit(solution)/shard_map/ppermute | solution.py:559
  58.9 18.9 %collective-permute-start.8 = (bf16[400,256]{1,0:T(8,128)(2,1)S(1)}, bf16[400,256]{1,0:T(8,128)(2,1)S(1)}, u32[]{:S(2)}, u32[]{:S(2)}) collective-permute-start(bf16[400,256]{1,0:T(8,128)(2,1)S(1)} %collective-permute-done.6.refs_9_.refs_10_), channel_id=1, source_target_pairs={{0,16},{16,0},{1,17},{17,1},{2,18},{18,2},{3,19},{19,3},{4,20},{20... | collective-permute-start | bytes 614408 | tf_op jit(solution)/shard_map/ppermute | solution.py:559
  59.6 18.2 %collective-permute-start.10 = (bf16[400,256]{1,0:T(8,128)(2,1)}, bf16[400,256]{1,0:T(8,128)(2,1)S(1)}, u32[]{:S(2)}, u32[]{:S(2)}) collective-permute-start(bf16[400,256]{1,0:T(8,128)(2,1)} %collective-permute-done.9), channel_id=1, source_target_pairs={{0,16},{16,0},{1,17},{17,1},{2,18},{18,2},{3,19},{19,3},{4,20},{20... | collective-permute-start | bytes 614408 | tf_op jit(solution)/shard_map/ppermute | solution.py:559
  65.9 18.5 %collective-permute-start.20 = (bf16[256,384]{1,0:T(8,128)(2,1)}, bf16[256,384]{1,0:T(8,128)(2,1)S(1)}, u32[]{:S(2)}, u32[]{:S(2)}) collective-permute-start(bf16[256,384]{1,0:T(8,128)(2,1)} %get-tuple-element.49), channel_id=1, source_target_pairs={{0,1},{1,0},{2,3},{3,2},{4,5},{5,4},{6,7},{7,6},{8,9},{9,8},{10,11... | collective-permute-start | bytes 589832 | tf_op jit(solution)/shard_map/ppermute | solution.py:559
  96.7 22.3 %collective-permute-start.21 = (bf16[5,384,256]{2,1,0:T(8,128)(2,1)}, bf16[5,384,256]{2,1,0:T(8,128)(2,1)S(1)}, u32[]{:S(2)}, u32[]{:S(2)}) collective-permute-start(bf16[5,384,256]{2,1,0:T(8,128)(2,1)} %get-tuple-element.53), channel_id=1, source_target_pairs={{0,16},{16,0},{1,17},{17,1},{2,18},{18,2},{3,19},{19,3},{4,20},{20... | collective-permute-start | bytes 2949128 | tf_op jit(solution)/shard_map/ppermute | solution.py:559
  100.0 46.1 %copy-start.30 = (bf16[256,384]{1,0:T(8,128)(2,1)S(1)}, bf16[256,384]{1,0:T(8,128)(2,1)}, u32[]{:S(2)}) copy-start(bf16[256,384]{1,0:T(8,128)(2,1)} %get-tuple-element.60.refs_2_) | copy-start | bytes 589828
  100.0 12.5 %collective-permute-start.28 = (bf16[336,512]{1,0:T(8,128)(2,1)S(1)}, bf16[336,512]{1,0:T(8,128)(2,1)S(1)}, u32[]{:S(2)}, u32[]{:S(2)}) collective-permute-start(bf16[336,512]{1,0:T(8,128)(2,1)S(1)} %pad_maximum_fusion), channel_id=1, source_target_pairs={{0,1},{1,0},{2,3},{3,2},{4,5},{5,4},{6,7},{7,6},{8,9},{9,8},{10,11... | collective-permute-start | bytes 1032200 | tf_op jit(solution)/shard_map/ppermute | solution.py:559
  100.6 18.3 %collective-permute-start.29 = (bf16[336,512]{1,0:T(8,128)(2,1)S(1)}, bf16[336,512]{1,0:T(8,128)(2,1)S(1)}, u32[]{:S(2)}, u32[]{:S(2)}) collective-permute-start(bf16[336,512]{1,0:T(8,128)(2,1)S(1)} %pad_maximum_fusion.1), channel_id=1, source_target_pairs={{0,1},{1,0},{2,3},{3,2},{4,5},{5,4},{6,7},{7,6},{8,9},{9,8},{10,11... | collective-permute-start | bytes 1032200 | tf_op jit(solution)/shard_map/ppermute | solution.py:559
  112.5 37.4 %copy-start = (bf16[336,512]{1,0:T(8,128)(2,1)}, bf16[336,512]{1,0:T(8,128)(2,1)S(1)}, u32[]{:S(2)}) copy-start(bf16[336,512]{1,0:T(8,128)(2,1)S(1)} %collective-permute-done.28.refs_5_.refs_2_.refs_6_) | copy-start | bytes 1032196
  112.5 12.9 %collective-permute-start.30 = (bf16[336,512]{1,0:T(8,128)(2,1)S(1)}, bf16[336,512]{1,0:T(8,128)(2,1)S(1)}, u32[]{:S(2)}, u32[]{:S(2)}) collective-permute-start(bf16[336,512]{1,0:T(8,128)(2,1)S(1)} %collective-permute-done.28.refs_5_.refs_2_.refs_6_), channel_id=1, source_target_pairs={{0,32},{32,0},{64,96},{96,64},{1,33},{33,1},{65,97},{97,65},{2,34}... | collective-permute-start | bytes 1032200 | tf_op jit(solution)/shard_map/ppermute | solution.py:563
  119.0 31.0 %copy-start.1 = (bf16[336,512]{1,0:T(8,128)(2,1)}, bf16[336,512]{1,0:T(8,128)(2,1)S(1)}, u32[]{:S(2)}) copy-start(bf16[336,512]{1,0:T(8,128)(2,1)S(1)} %collective-permute-done.29.refs_6_.refs_3_.refs_7_) | copy-start | bytes 1032196
  119.0 9.1 %collective-permute-start.31 = (bf16[336,512]{1,0:T(8,128)(2,1)S(1)}, bf16[336,512]{1,0:T(8,128)(2,1)S(1)}, u32[]{:S(2)}, u32[]{:S(2)}) collective-permute-start(bf16[336,512]{1,0:T(8,128)(2,1)S(1)} %collective-permute-done.29.refs_6_.refs_3_.refs_7_), channel_id=1, source_target_pairs={{0,32},{32,0},{64,96},{96,64},{1,33},{33,1},{65,97},{97,65},{2,34}... | collective-permute-start | bytes 1032200 | tf_op jit(solution)/shard_map/ppermute | solution.py:563
  121.5 6.6 %collective-permute-start.22 = (bf16[384,256]{1,0:T(8,128)(2,1)}, bf16[384,256]{1,0:T(8,128)(2,1)S(1)}, u32[]{:S(2)}, u32[]{:S(2)}) collective-permute-start(bf16[384,256]{1,0:T(8,128)(2,1)} %get-tuple-element.55), channel_id=1, source_target_pairs={{176,16},{208,48},{240,80},{177,17},{209,49},{241,81},{178,18},{21... | collective-permute-start | bytes 589832 | tf_op jit(solution)/shard_map/ppermute | solution.py:575
  122.2 10.6 %collective-permute-start.23 = (bf16[384,256]{1,0:T(8,128)(2,1)}, bf16[384,256]{1,0:T(8,128)(2,1)S(1)}, u32[]{:S(2)}, u32[]{:S(2)}) collective-permute-start(bf16[384,256]{1,0:T(8,128)(2,1)} %get-tuple-element.56), channel_id=1, source_target_pairs={{128,0},{144,16},{160,32},{176,48},{192,64},{208,80},{224,96},{240... | collective-permute-start | bytes 589832 | tf_op jit(solution)/shard_map/ppermute | solution.py:575
  123.5 12.8 %collective-permute-start.24 = (bf16[384,256]{1,0:T(8,128)(2,1)}, bf16[384,256]{1,0:T(8,128)(2,1)S(1)}, u32[]{:S(2)}, u32[]{:S(2)}) collective-permute-start(bf16[384,256]{1,0:T(8,128)(2,1)} %get-tuple-element.57), channel_id=1, source_target_pairs={{96,0},{112,16},{128,32},{144,48},{160,64},{176,80},{192,96},{208,... | collective-permute-start | bytes 589832 | tf_op jit(solution)/shard_map/ppermute | solution.py:575
  125.4 31.6 %copy-start.2 = (bf16[336,512]{1,0:T(8,128)(2,1)}, bf16[336,512]{1,0:T(8,128)(2,1)S(1)}, u32[]{:S(2)}) copy-start(bf16[336,512]{1,0:T(8,128)(2,1)S(1)} %collective-permute-done.30.refs_7_.refs_4_.refs_8_) | copy-start | bytes 1032196
  125.4 18.9 %collective-permute-start.25 = (bf16[384,256]{1,0:T(8,128)(2,1)}, bf16[384,256]{1,0:T(8,128)(2,1)S(1)}, u32[]{:S(2)}, u32[]{:S(2)}) collective-permute-start(bf16[384,256]{1,0:T(8,128)(2,1)} %get-tuple-element.58), channel_id=1, source_target_pairs={{64,0},{80,16},{96,32},{112,48},{128,64},{144,80},{160,96},{176,11... | collective-permute-start | bytes 589832 | tf_op jit(solution)/shard_map/ppermute | solution.py:575
  128.1 28.9 %copy-start.3 = (bf16[336,512]{1,0:T(8,128)(2,1)}, bf16[336,512]{1,0:T(8,128)(2,1)S(1)}, u32[]{:S(2)}) copy-start(bf16[336,512]{1,0:T(8,128)(2,1)S(1)} %collective-permute-done.31.refs_8_.refs_5_.refs_9_) | copy-start | bytes 1032196
  128.1 21.8 %collective-permute-start.32 = (bf16[336,512]{1,0:T(8,128)(2,1)S(1)}, bf16[336,512]{1,0:T(8,128)(2,1)S(1)}, u32[]{:S(2)}, u32[]{:S(2)}) collective-permute-start(bf16[336,512]{1,0:T(8,128)(2,1)S(1)} %collective-permute-done.28.refs_5_.refs_2_.refs_6_), channel_id=1, source_target_pairs={{0,16},{16,0},{1,17},{17,1},{2,18},{18,2},{3,19},{19,3},{4,20},{20... | collective-permute-start | bytes 1032200 | tf_op jit(solution)/shard_map/ppermute | solution.py:559
  128.1 18.0 %collective-permute-start.26 = (bf16[384,256]{1,0:T(8,128)(2,1)}, bf16[384,256]{1,0:T(8,128)(2,1)S(1)}, u32[]{:S(2)}, u32[]{:S(2)}) collective-permute-start(bf16[384,256]{1,0:T(8,128)(2,1)} %get-tuple-element.59), channel_id=1, source_target_pairs={{32,0},{48,16},{64,32},{80,48},{96,64},{112,80},{128,96},{144,112}... | collective-permute-start | bytes 589832 | tf_op jit(solution)/shard_map/ppermute | solution.py:575
  132.8 24.2 %collective-permute-start.33 = (bf16[336,512]{1,0:T(8,128)(2,1)S(1)}, bf16[336,512]{1,0:T(8,128)(2,1)}, u32[]{:S(2)}, u32[]{:S(2)}) collective-permute-start(bf16[336,512]{1,0:T(8,128)(2,1)S(1)} %collective-permute-done.29.refs_6_.refs_3_.refs_7_), channel_id=1, source_target_pairs={{0,16},{16,0},{1,17},{17,1},{2,18},{18,2},{3,19},{19,3},{4,20},{20... | collective-permute-start | bytes 1032200 | tf_op jit(solution)/shard_map/ppermute | solution.py:559
  136.2 20.8 %collective-permute-start.34 = (bf16[336,512]{1,0:T(8,128)(2,1)S(1)}, bf16[336,512]{1,0:T(8,128)(2,1)}, u32[]{:S(2)}, u32[]{:S(2)}) collective-permute-start(bf16[336,512]{1,0:T(8,128)(2,1)S(1)} %collective-permute-done.30.refs_7_.refs_4_.refs_8_), channel_id=1, source_target_pairs={{0,16},{16,0},{1,17},{17,1},{2,18},{18,2},{3,19},{19,3},{4,20},{20... | collective-permute-start | bytes 1032200 | tf_op jit(solution)/shard_map/ppermute | solution.py:559
  144.3 12.7 %collective-permute-start.35 = (bf16[336,512]{1,0:T(8,128)(2,1)S(1)}, bf16[336,512]{1,0:T(8,128)(2,1)}, u32[]{:S(2)}, u32[]{:S(2)}) collective-permute-start(bf16[336,512]{1,0:T(8,128)(2,1)S(1)} %collective-permute-done.31.refs_8_.refs_5_.refs_9_), channel_id=1, source_target_pairs={{0,16},{16,0},{1,17},{17,1},{2,18},{18,2},{3,19},{19,3},{4,20},{20... | collective-permute-start | bytes 1032200 | tf_op jit(solution)/shard_map/ppermute | solution.py:559
  146.1 11.0 %collective-permute-start.36 = (bf16[256,384]{1,0:T(8,128)(2,1)S(1)}, bf16[256,384]{1,0:T(8,128)(2,1)S(1)}, u32[]{:S(2)}, u32[]{:S(2)}) collective-permute-start(bf16[256,384]{1,0:T(8,128)(2,1)S(1)} %copy-done.30), channel_id=1, source_target_pairs={{0,1},{1,0},{2,3},{3,2},{4,5},{5,4},{6,7},{7,6},{8,9},{9,8},{10,11... | collective-permute-start | bytes 589832 | tf_op jit(solution)/shard_map/ppermute | solution.py:559
  149.9 10.8 %collective-permute-start.27 = (bf16[256,384]{1,0:T(8,128)(2,1)}, bf16[256,384]{1,0:T(8,128)(2,1)S(1)}, u32[]{:S(2)}, u32[]{:S(2)}) collective-permute-start(bf16[256,384]{1,0:T(8,128)(2,1)} %total_partials.1.refs_3_), channel_id=1, source_target_pairs={{0,1},{1,0},{2,3},{3,2},{4,5},{5,4},{6,7},{7,6},{8,9},{9,8},{10,11... | collective-permute-start | bytes 589832 | tf_op jit(solution)/shard_map/ppermute | solution.py:559
  164.1 8.6 %collective-permute-start.37 = (bf16[336,384]{1,0:T(8,128)(2,1)}, bf16[336,384]{1,0:T(8,128)(2,1)S(1)}, u32[]{:S(2)}, u32[]{:S(2)}) collective-permute-start(bf16[336,384]{1,0:T(8,128)(2,1)} %get-tuple-element.65), channel_id=1, source_target_pairs={{0,2},{2,4},{4,6},{6,8},{8,10},{10,12},{12,14},{14,0},{1,3},{3,5},... | collective-permute-start | bytes 774152 | tf_op jit(solution)/shard_map/ppermute | solution.py:579
  164.2 9.8 %collective-permute-start.41 = (bf16[336,384]{1,0:T(8,128)(2,1)}, bf16[336,384]{1,0:T(8,128)(2,1)S(1)}, u32[]{:S(2)}, u32[]{:S(2)}) collective-permute-start(bf16[336,384]{1,0:T(8,128)(2,1)} %get-tuple-element.75), channel_id=1, source_target_pairs={{0,14},{2,0},{4,2},{6,4},{8,6},{10,8},{12,10},{14,12},{1,15},{3,1}... | collective-permute-start | bytes 774152 | tf_op jit(solution)/shard_map/ppermute | solution.py:579
  172.7 8.8 %copy-start.20 = (f32[336,384]{1,0:T(8,128)S(1)}, f32[336,384]{1,0:T(8,128)}, u32[]{:S(2)}) copy-start(f32[336,384]{1,0:T(8,128)} %get-tuple-element.71) | copy-start | bytes 1548292
  173.9 7.6 %collective-permute-start.38 = (bf16[336,384]{1,0:T(8,128)(2,1)S(1)}, bf16[336,384]{1,0:T(8,128)(2,1)S(1)}, u32[]{:S(2)}, u32[]{:S(2)}) collective-permute-start(bf16[336,384]{1,0:T(8,128)(2,1)S(1)} %add_convert_fusion.5), channel_id=1, source_target_pairs={{0,2},{2,4},{4,6},{6,8},{8,10},{10,12},{12,14},{14,0},{1,3},{3,5},... | collective-permute-start | bytes 774152 | tf_op jit(solution)/shard_map/ppermute | solution.py:579
  174.1 12.0 %collective-permute-start.42 = (bf16[336,384]{1,0:T(8,128)(2,1)S(1)}, bf16[336,384]{1,0:T(8,128)(2,1)S(1)}, u32[]{:S(2)}, u32[]{:S(2)}) collective-permute-start(bf16[336,384]{1,0:T(8,128)(2,1)S(1)} %add_convert_fusion.2), channel_id=1, source_target_pairs={{0,14},{2,0},{4,2},{6,4},{8,6},{10,8},{12,10},{14,12},{1,15},{3,1}... | collective-permute-start | bytes 774152 | tf_op jit(solution)/shard_map/ppermute | solution.py:579
  181.6 7.8 %collective-permute-start.39 = (bf16[336,384]{1,0:T(8,128)(2,1)S(1)}, bf16[336,384]{1,0:T(8,128)(2,1)S(1)}, u32[]{:S(2)}, u32[]{:S(2)}) collective-permute-start(bf16[336,384]{1,0:T(8,128)(2,1)S(1)} %add_convert_fusion.4), channel_id=1, source_target_pairs={{0,2},{2,4},{4,6},{6,8},{8,10},{10,12},{12,14},{14,0},{1,3},{3,5},... | collective-permute-start | bytes 774152 | tf_op jit(solution)/shard_map/ppermute | solution.py:579
  186.0 11.1 %copy-start.17 = (f32[336,384]{1,0:T(8,128)S(1)}, f32[336,384]{1,0:T(8,128)}, u32[]{:S(2)}) copy-start(f32[336,384]{1,0:T(8,128)} %get-tuple-element.78) | copy-start | bytes 1548292
  186.1 7.1 %collective-permute-start.43 = (bf16[336,384]{1,0:T(8,128)(2,1)S(1)}, bf16[336,384]{1,0:T(8,128)(2,1)S(1)}, u32[]{:S(2)}, u32[]{:S(2)}) collective-permute-start(bf16[336,384]{1,0:T(8,128)(2,1)S(1)} %add_convert_fusion.1), channel_id=1, source_target_pairs={{0,14},{2,0},{4,2},{6,4},{8,6},{10,8},{12,10},{14,12},{1,15},{3,1}... | collective-permute-start | bytes 774152 | tf_op jit(solution)/shard_map/ppermute | solution.py:579
  189.5 7.6 %collective-permute-start.40 = (bf16[336,384]{1,0:T(8,128)(2,1)S(1)}, bf16[336,384]{1,0:T(8,128)(2,1)S(1)}, u32[]{:S(2)}, u32[]{:S(2)}) collective-permute-start(bf16[336,384]{1,0:T(8,128)(2,1)S(1)} %add_convert_fusion.3), channel_id=1, source_target_pairs={{0,2},{2,4},{4,6},{6,8},{8,10},{10,12},{12,14},{14,0},{1,3},{3,5},... | collective-permute-start | bytes 774152 | tf_op jit(solution)/shard_map/ppermute | solution.py:579
  (14 other events, 51.1 us)

commit v7 on v6

--- a/solution.py
+++ b/solution.py
@@ -408,7 +408,7 @@
     return pl.pallas_call(
         lambda *refs: dout_kernel(deltas, *refs),
         name="dout_parts",
-        out_shape=(jax.ShapeDtypeStruct(half, F32), jax.ShapeDtypeStruct(half, BF16)),
+        out_shape=(jax.ShapeDtypeStruct(half, F32), pltpu.VMEM(half, BF16)),
         in_specs=[SMEM] + [ANY] * (3 + RING),
         out_specs=(VMEM, VMEM),
         scratch_shapes=[
@@ -442,7 +442,7 @@
     result = pl.pallas_call(
         join_kernel,
         name="join_partials",
-        out_shape=(jax.ShapeDtypeStruct(shape, F32),) + (jax.ShapeDtypeStruct(shape, BF16),) * HALF,
+        out_shape=(jax.ShapeDtypeStruct(shape, F32),) + (pltpu.VMEM(shape, BF16),) * HALF,
         in_specs=[SMEM, VMEM, VMEM],
         out_specs=(VMEM,) * (HALF + 1),
     )(core, mine, got)
@@ -536,7 +536,7 @@
     return pl.pallas_call(
         lambda *refs: project_kernel(deltas, own_lanes, far, len(grads), more, *refs),
         name="project",
-        out_shape=(jax.ShapeDtypeStruct((FEATS, ROWS), kind),) * n,
+        out_shape=((jax.ShapeDtypeStruct if kind == F32 else pltpu.VMEM)((FEATS, ROWS), kind),) * n,
         in_specs=[SMEM] + [ANY] * (k + len(grads) + len(far_rows) + len(sums)),
         out_specs=(ANY,) * n,
         scratch_shapes=[

time: 199 us -> 199 us (level)
  transfers between devices with their start and end apart: 44 -> 44, of which waited for: 15 -> 15; matrix products, arithmetic and copies ran while one was open for 2% -> 2% of each run, Pallas kernels for 21% -> 20%
where the time goes in v7:
time: 199 us; the launch traced here: 198 us
  waiting for transfers between devices  66.5 us (33%)
  starting transfers between devices  62.7 us (32%)
  Pallas kernels  59.6 us (30%)
  local copies, waits for them, and re-layouts  5.76 us (3%)
  other arithmetic  2.96 us (1%)
    ppermute x18, waiting for transfers between devices, swapped(): return lax.ppermute(x, axis, [(0, 1), (1, 0)])  29.3 us
    ppermute x14, starting transfers between devices, round_z(): return lax.ppermute(x, 'z', [(i, (i + step) % RING) for i in range(RING)])  25.3 us
    ppermute x14, waiting for transfers between devices, round_z(): return lax.ppermute(x, 'z', [(i, (i + step) % RING) for i in range(RING)])  22.5 us
    pallas_call x5, Pallas kernels, project(): pl.pallas_call(lambda *refs: project_kernel(deltas, own_lanes, far, len(g...  21.7 us
    ppermute x18, starting transfers between devices, swapped(): return lax.ppermute(x, axis, [(0, 1), (1, 0)])  17.1 us
    pallas_call x1, Pallas kernels, attention_grads(): pl.pallas_call(grads_kernel, name='attention_grads', out_shape=(jax.Shape...  12.3 us
    pallas_call x2, Pallas kernels, attention_stats(): pl.pallas_call(lambda *refs: stats_kernel(low, high, *refs), name='stats_...  12.1 us
    ppermute x5, waiting for transfers between devices, chips_back(): return arrive(lax.ppermute(x, AA, [(j, i) for i, j in chip_pairs(d)]))  11.5 us
  transfers between devices with their start and end apart: 44, of which 15 were waited for; matrix products, arithmetic and copies ran while one was open for 2% of the time, Pallas kernels for 20%

profile of v7, /device:TPU:24, one launch (start us, length us, event | category | flops | bytes accessed | tf_op | source)
XLA Modules:
  0.0 198.3 jit_solution(5759744218910657154)
XLA Ops:
  0.0 0.7 pad_add_fusion.at_ref.refs_0_
  0.7 3.5 %split_w_out.1 = bf16[4,256,384]{2,1,0:T(8,128)(2,1)} custom-call(s32[4]{0:T(128)} %pad_add_fusion.at_ref.refs_0_, bf16[256,5376]{1,0:T(8,128)(2,1)} %refs_1_.6), custom_call_target="tpu_custom_call" | custom-call | tf_op jit(solution)/shard_map/split_w_out/pallas_call | solution.py:348
  4.1 3.1 %collective-permute-start.11 = (bf16[4,256,384]{2,1,0:T(8,128)(2,1)}, bf16[4,256,384]{2,1,0:T(8,128)(2,1)S(1)}, u32[]{:S(2)}, u32[]{:S(2)}) collective-permute-start(bf16[4,256,384]{2,1,0:T(8,128)(2,1)} %split_w_out.1), channel_id=1, source_target_pairs={{0,1},{1,0},{2,3},{3,2},{4,5},{5,4},{6,7},{7,6},{8,9},{9,8},{10,11... | collective-permute-start | bytes 2359304 | tf_op jit(solution)/shard_map/ppermute | solution.py:559
  7.2 1.9 collective-permute-start.13
  9.2 3.2 %collective-permute-start.3 = (bf16[400,256]{1,0:T(8,128)(2,1)S(1)}, bf16[400,256]{1,0:T(8,128)(2,1)S(1)}, u32[]{:S(2)}, u32[]{:S(2)}) collective-permute-start(bf16[400,256]{1,0:T(8,128)(2,1)S(1)} %fusion.2.refs_3_.refs_6_), channel_id=1, source_target_pairs={{0,64},{16,80},{32,96},{48,112},{64,128},{80,144},{96,160},{112,17... | collective-permute-start | bytes 614408 | tf_op jit(solution)/shard_map/ppermute | solution.py:571
  12.4 13.9 %collective-permute-done.11.refs_2_ = bf16[4,256,384]{2,1,0:T(8,128)(2,1)S(1)} collective-permute-done((bf16[4,256,384]{2,1,0:T(8,128)(2,1)}, bf16[4,256,384]{2,1,0:T(8,128)(2,1)S(1)}, u32[]{:S(2)}, u32[]{:S(2)}) %collective-permute-start.11) | collective-permute-done | bytes 786464 | tf_op jit(solution)/shard_map/ppermute | solution.py:559
  26.4 5.9 %collective-permute-start.14 = (bf16[336,384]{1,0:T(8,128)(2,1)S(1)}, bf16[336,384]{1,0:T(8,128)(2,1)S(1)}, u32[]{:S(2)}, u32[]{:S(2)}) collective-permute-start(bf16[336,384]{1,0:T(8,128)(2,1)S(1)} %bitcast.30), channel_id=1, source_target_pairs={{0,14},{2,0},{4,2},{6,4},{8,6},{10,8},{12,10},{14,12},{1,15},{3,1}... | collective-permute-start | bytes 774152 | tf_op jit(solution)/shard_map/ppermute | solution.py:579
  32.2 1.9 collective-permute-start
  34.2 0.3 collective-permute-start.1
  34.5 3.9 %collective-permute-done.14.refs_6_ = bf16[336,384]{1,0:T(8,128)(2,1)S(1)} collective-permute-done((bf16[336,384]{1,0:T(8,128)(2,1)S(1)}, bf16[336,384]{1,0:T(8,128)(2,1)S(1)}, u32[]{:S(2)}, u32[]{:S(2)}) %collective-permute-start.14) | collective-permute-done | bytes 258080 | tf_op jit(solution)/shard_map/ppermute | solution.py:579
  38.4 3.7 %collective-permute-start.16 = (bf16[336,384]{1,0:T(8,128)(2,1)S(1)}, bf16[336,384]{1,0:T(8,128)(2,1)S(1)}, u32[]{:S(2)}, u32[]{:S(2)}) collective-permute-start(bf16[336,384]{1,0:T(8,128)(2,1)S(1)} %collective-permute-done.14.refs_6_), channel_id=1, source_target_pairs={{0,14},{2,0},{4,2},{6,4},{8,6},{10,8},{12,10},{14,12},{1,15},{3,1}... | collective-permute-start | bytes 774152 | tf_op jit(solution)/shard_map/ppermute | solution.py:579
  42.1 2.4 %collective-permute-start.5 = (bf16[400,256]{1,0:T(8,128)(2,1)S(1)}, bf16[400,256]{1,0:T(8,128)(2,1)S(1)}, u32[]{:S(2)}, u32[]{:S(2)}) collective-permute-start(bf16[400,256]{1,0:T(8,128)(2,1)S(1)} %fusion.2.refs_3_.refs_6_), channel_id=1, source_target_pairs={{0,96},{16,112},{32,128},{48,144},{64,160},{80,176},{96,192},{112,... | collective-permute-start | bytes 614408 | tf_op jit(solution)/shard_map/ppermute | solution.py:571
  44.6 1.3 collective-permute-start.6
  45.9 1.5 collective-permute-done.16.refs_8_
  47.3 3.7 %collective-permute-start.18 = (bf16[336,384]{1,0:T(8,128)(2,1)S(1)}, bf16[336,384]{1,0:T(8,128)(2,1)S(1)}, u32[]{:S(2)}, u32[]{:S(2)}) collective-permute-start(bf16[336,384]{1,0:T(8,128)(2,1)S(1)} %collective-permute-done.16.refs_8_), channel_id=1, source_target_pairs={{0,14},{2,0},{4,2},{6,4},{8,6},{10,8},{12,10},{14,12},{1,15},{3,1}... | collective-permute-start | bytes 774152 | tf_op jit(solution)/shard_map/ppermute | solution.py:579
  51.1 0.5 collective-permute-done.5.refs_8_.refs_9_
  51.5 1.3 collective-permute-start.9
  52.9 0.5 collective-permute-start.2
  53.4 2.1 %collective-permute-done.18.refs_10_ = bf16[336,384]{1,0:T(8,128)(2,1)S(1)} collective-permute-done((bf16[336,384]{1,0:T(8,128)(2,1)S(1)}, bf16[336,384]{1,0:T(8,128)(2,1)S(1)}, u32[]{:S(2)}, u32[]{:S(2)}) %collective-permute-start.18) | collective-permute-done | bytes 258080 | tf_op jit(solution)/shard_map/ppermute | solution.py:579
  55.5 3.4 %collective-permute-done.19.refs_11_ = bf16[336,384]{1,0:T(8,128)(2,1)S(1)} collective-permute-done((bf16[336,384]{1,0:T(8,128)(2,1)S(1)}, bf16[336,384]{1,0:T(8,128)(2,1)S(1)}, u32[]{:S(2)}, u32[]{:S(2)}) %collective-permute-start.19) | collective-permute-done | bytes 258080 | tf_op jit(solution)/shard_map/ppermute | solution.py:579
  58.9 0.6 copy-done.29
  59.6 6.2 %dout_parts.1 = (f32[256,384]{1,0:T(8,128)}, bf16[256,384]{1,0:T(8,128)(2,1)S(1)}) custom-call(s32[4]{0:T(128)} %pad_add_fusion.at_ref.refs_0_, bf16[256,5376]{1,0:T(8,128)(2,1)} %refs_1_.6, bf16[4,256,384]{2,1,0:T(8,128)(2,1)} %copy-done.16, bf16[4,256,384]{2,1,0:T(8,128)(2,1)S(1)} %collective-permute-done.12.refs_3_, bf16[336,384]{1,0:T(8,128)(2,1)} %bitcast.28, ...), custom_call_target="tpu_custom_call" | custom-call | tf_op jit(solution)/shard_map/dout_parts/pallas_call | solution.py:408
  65.9 3.3 %collective-permute-start.20 = (bf16[256,384]{1,0:T(8,128)(2,1)S(1)}, bf16[256,384]{1,0:T(8,128)(2,1)S(1)}, u32[]{:S(2)}, u32[]{:S(2)}) collective-permute-start(bf16[256,384]{1,0:T(8,128)(2,1)S(1)} %get-tuple-element.49), channel_id=1, source_target_pairs={{0,1},{1,0},{2,3},{3,2},{4,5},{5,4},{6,7},{7,6},{8,9},{9,8},{10,11... | collective-permute-start | bytes 589832 | tf_op jit(solution)/shard_map/ppermute | solution.py:559
  69.1 0.5 broadcast_in_dim.8.refs_1_
  69.7 1.0 dynamic-slice_bitcast_fusion
  70.8 0.7 copy-done.12
  71.4 6.3 %stats_near.1 = (f32[1,768]{1,0:T(1,128)}, f32[1,768]{1,0:T(1,128)}, f32[128,768]{1,0:T(8,128)}, s32[1,384]{1,0:T(1,128)}) custom-call(s32[1]{0:T(128)} %bitcast.4.refs_0_.own_ref, s32[1,384]{1,0:T(1,128)} %broadcast_in_dim.8.refs_1_, bf16[384,256]{1,0:T(8,128)(2,1)} %refs_1_.7, bf16[400,256]{1,0:T(8,128)(2,1)} %copy-done.6, bf16[400,256]{1,0:T(8,128)(2,1)} %copy-done.8, ...), custom_call_target="tpu_custom_call" | custom-call | tf_op jit(solution)/shard_map/stats_near/pallas_call | solution.py:284
  77.8 0.6 copy-done.13
  78.5 5.8 %stats_far.1 = (f32[1,768]{1,0:T(1,128)}, f32[128,768]{1,0:T(8,128)}, s32[1,384]{1,0:T(1,128)}, s32[1]{0:T(128)}) custom-call(s32[1]{0:T(128)} %bitcast.4.refs_0_.own_ref, s32[1,384]{1,0:T(1,128)} %broadcast_in_dim.8.refs_1_, bf16[384,256]{1,0:T(8,128)(2,1)} %refs_1_.7, f32[1,768]{1,0:T(1,128)} %get-tuple-element.42.refs_3_, ...), custom_call_target="tpu_custom_call" | custom-call | tf_op jit(solution)/shard_map/stats_far/pallas_call | solution.py:284
  84.4 12.3 %attention_grads.1 = (bf16[256,384]{1,0:T(8,128)(2,1)}, bf16[5,384,256]{2,1,0:T(8,128)(2,1)}, bf16[5,384,256]{2,1,0:T(8,128)(2,1)}) custom-call(s32[1]{0:T(128)} %bitcast.4.refs_0_.own_ref, s32[1]{0:T(128)} %get-tuple-element.46.low_ref, s32[1,384]{1,0:T(1,128)} %get-tuple-element.47.refs_0_, bf16[384,256]{1,0:T(8,128)(2,1)} %refs_1_.7, ...), custom_call_target="tpu_custom_call" | custom-call | tf_op jit(solution)/shard_map/attention_grads/pallas_call | solution.py:298
  96.7 2.2 %collective-permute-start.21 = (bf16[5,384,256]{2,1,0:T(8,128)(2,1)}, bf16[5,384,256]{2,1,0:T(8,128)(2,1)S(1)}, u32[]{:S(2)}, u32[]{:S(2)}) collective-permute-start(bf16[5,384,256]{2,1,0:T(8,128)(2,1)} %get-tuple-element.53), channel_id=1, source_target_pairs={{0,16},{16,0},{1,17},{17,1},{2,18},{18,2},{3,19},{19,3},{4,20},{20... | collective-permute-start | bytes 2949128 | tf_op jit(solution)/shard_map/ppermute | solution.py:559
  98.9 1.0 dynamic-slice_bitcast_fusion.2
  100.0 0.6 collective-permute-start.28
  100.6 3.1 %collective-permute-start.29 = (bf16[336,512]{1,0:T(8,128)(2,1)S(1)}, bf16[336,512]{1,0:T(8,128)(2,1)}, u32[]{:S(2)}, u32[]{:S(2)}) collective-permute-start(bf16[336,512]{1,0:T(8,128)(2,1)S(1)} %pad_maximum_fusion.1), channel_id=1, source_target_pairs={{0,1},{1,0},{2,3},{3,2},{4,5},{5,4},{6,7},{7,6},{8,9},{9,8},{10,11... | collective-permute-start | bytes 1032200 | tf_op jit(solution)/shard_map/ppermute | solution.py:559
  103.7 8.8 %collective-permute-done.28.refs_5_.refs_2_.refs_6_ = bf16[336,512]{1,0:T(8,128)(2,1)S(1)} collective-permute-done((bf16[336,512]{1,0:T(8,128)(2,1)S(1)}, bf16[336,512]{1,0:T(8,128)(2,1)S(1)}, u32[]{:S(2)}, u32[]{:S(2)}) %collective-permute-start.28) | collective-permute-done | bytes 344096 | tf_op jit(solution)/shard_map/ppermute | solution.py:559
  112.5 6.5 %collective-permute-done.29.refs_6_.refs_3_.refs_7_ = bf16[336,512]{1,0:T(8,128)(2,1)} collective-permute-done((bf16[336,512]{1,0:T(8,128)(2,1)S(1)}, bf16[336,512]{1,0:T(8,128)(2,1)}, u32[]{:S(2)}, u32[]{:S(2)}) %collective-permute-start.29) | collective-permute-done | bytes 344096 | tf_op jit(solution)/shard_map/ppermute | solution.py:559
  119.0 2.0 %join_partials.1 = (f32[384,256]{1,0:T(8,128)}, bf16[384,256]{1,0:T(8,128)(2,1)S(1)}, bf16[384,256]{1,0:T(8,128)(2,1)S(1)}, bf16[384,256]{1,0:T(8,128)(2,1)S(1)}...) custom-call(s32[1]{0:T(128)} %bitcast.2.core_ref, bf16[5,384,256]{2,1,0:T(8,128)(2,1)} %get-tuple-element.52.mine_ref, ...), custom_call_target="tpu_custom_call" | custom-call | tf_op jit(solution)/shard_map/join_partials/pallas_call | solution.py:442
  121.0 0.7 collective-permute-start.22
  121.7 1.3 collective-permute-start.23
  123.0 1.9 collective-permute-start.24
  124.9 1.9 collective-permute-start.25
  126.9 2.7 %collective-permute-done.31.refs_8_.refs_5_.refs_9_ = bf16[336,512]{1,0:T(8,128)(2,1)} collective-permute-done((bf16[336,512]{1,0:T(8,128)(2,1)}, bf16[336,512]{1,0:T(8,128)(2,1)}, u32[]{:S(2)}, u32[]{:S(2)}) %collective-permute-start.31) | collective-permute-done | bytes 344096 | tf_op jit(solution)/shard_map/ppermute | solution.py:563
  129.5 4.4 %collective-permute-start.26 = (bf16[384,256]{1,0:T(8,128)(2,1)S(1)}, bf16[384,256]{1,0:T(8,128)(2,1)S(1)}, u32[]{:S(2)}, u32[]{:S(2)}) collective-permute-start(bf16[384,256]{1,0:T(8,128)(2,1)S(1)} %get-tuple-element.59), channel_id=1, source_target_pairs={{32,0},{48,16},{64,32},{80,48},{96,64},{112,80},{128,96},{144,112}... | collective-permute-start | bytes 589832 | tf_op jit(solution)/shard_map/ppermute | solution.py:575
  133.9 0.3 collective-permute-start.33
  134.2 1.4 collective-permute-done.24.refs_2_
  135.7 8.3 %collective-permute-done.25.refs_3_ = bf16[384,256]{1,0:T(8,128)(2,1)S(1)} collective-permute-done((bf16[384,256]{1,0:T(8,128)(2,1)S(1)}, bf16[384,256]{1,0:T(8,128)(2,1)S(1)}, u32[]{:S(2)}, u32[]{:S(2)}) %collective-permute-start.25) | collective-permute-done | bytes 196640 | tf_op jit(solution)/shard_map/ppermute | solution.py:575
  144.1 1.8 collective-permute-done.26.refs_4_
  145.8 1.9 collective-permute-start.36
  147.7 1.9 total_partials.1.refs_3_
  149.5 1.8 collective-permute-start.27
  151.3 5.1 %project.5 = (f32[336,384]{1,0:T(8,128)}, f32[336,384]{1,0:T(8,128)}, f32[336,384]{1,0:T(8,128)}, f32[336,384]{1,0:T(8,128)}, f32[336,384]{1,0:T(8,128)}, /*inde...) custom-call(s32[4]{0:T(128)} %pad_add_fusion.at_ref.refs_0_, bf16[5376,256]{1,0:T(8,128)(2,1)} %refs_1_.8, ...), custom_call_target="tpu_custom_call" | custom-call | tf_op jit(solution)/shard_map/project/pallas_call | solution.py:536
  156.5 0.7 copy-done.2
  157.5 3.7 %project.6 = (f32[336,384]{1,0:T(8,128)}, f32[336,384]{1,0:T(8,128)}) custom-call(s32[4]{0:T(128)} %pad_add_fusion.at_ref.refs_0_, bf16[5376,128]{1,0:T(8,128)(2,1)} %refs_1_.11, bf16[5376,128]{1,0:T(8,128)(2,1)} %refs_2_.9, bf16[256,384]{1,0:T(8,128)(2,1)} %total_partials.1.refs_3_, bf16[256,384]{1,0:T(8,128)(2,1)S(1)} %collective-permute-done.36.refs_4_, ...), custom_call_target="tpu_custom_call" | custom-call | tf_op jit(solution)/shard_map/project/pallas_call | solution.py:536
  161.2 3.3 %project.7 = (bf16[336,384]{1,0:T(8,128)(2,1)S(1)}, bf16[336,384]{1,0:T(8,128)(2,1)S(1)}) custom-call(s32[4]{0:T(128)} %pad_add_fusion.at_ref.refs_0_, bf16[256,384]{1,0:T(8,128)(2,1)S(1)} %collective-permute-done.27.refs_1_.refs_5_, bf16[336,512]{1,0:T(8,128)(2,1)} %copy-done, bf16[336,512]{1,0:T(8,128)(2,1)} %collective-permute-done.29.refs_6_.refs_3_.refs_7_, ...), custom_call_target="tpu_custom_call" | custom-call | tf_op jit(solution)/shard_map/project/pallas_call | solution.py:536
  164.6 3.2 %collective-permute-start.41 = (bf16[336,384]{1,0:T(8,128)(2,1)S(1)}, bf16[336,384]{1,0:T(8,128)(2,1)S(1)}, u32[]{:S(2)}, u32[]{:S(2)}) collective-permute-start(bf16[336,384]{1,0:T(8,128)(2,1)S(1)} %get-tuple-element.75), channel_id=1, source_target_pairs={{0,14},{2,0},{4,2},{6,4},{8,6},{10,8},{12,10},{14,12},{1,15},{3,1}... | collective-permute-start | bytes 774152 | tf_op jit(solution)/shard_map/ppermute | solution.py:579
  167.8 5.3 %project.8 = (f32[336,384]{1,0:T(8,128)}, f32[336,384]{1,0:T(8,128)}, f32[336,384]{1,0:T(8,128)}, f32[336,384]{1,0:T(8,128)}) custom-call(s32[4]{0:T(128)} %pad_add_fusion.at_ref.refs_0_, bf16[5376,128]{1,0:T(8,128)(2,1)} %refs_1_.11, bf16[5376,128]{1,0:T(8,128)(2,1)} %refs_2_.9, bf16[256,384]{1,0:T(8,128)(2,1)} %total_partials.1.refs_3_, ...), custom_call_target="tpu_custom_call" | custom-call | tf_op jit(solution)/shard_map/project/pallas_call | solution.py:536
  173.1 1.2 add_convert_fusion.5
  174.5 3.3 %collective-permute-start.42 = (bf16[336,384]{1,0:T(8,128)(2,1)S(1)}, bf16[336,384]{1,0:T(8,128)(2,1)S(1)}, u32[]{:S(2)}, u32[]{:S(2)}) collective-permute-start(bf16[336,384]{1,0:T(8,128)(2,1)S(1)} %add_convert_fusion.2), channel_id=1, source_target_pairs={{0,14},{2,0},{4,2},{6,4},{8,6},{10,8},{12,10},{14,12},{1,15},{3,1}... | collective-permute-start | bytes 774152 | tf_op jit(solution)/shard_map/ppermute | solution.py:579
  177.8 4.2 %collective-permute-done.38 = bf16[336,384]{1,0:T(8,128)(2,1)S(1)} collective-permute-done((bf16[336,384]{1,0:T(8,128)(2,1)S(1)}, bf16[336,384]{1,0:T(8,128)(2,1)S(1)}, u32[]{:S(2)}, u32[]{:S(2)}) %collective-permute-start.38) | collective-permute-done | bytes 258080 | tf_op jit(solution)/shard_map/ppermute | solution.py:579
  182.1 4.3 %project.9 = (f32[336,384]{1,0:T(8,128)}, f32[336,384]{1,0:T(8,128)}) custom-call(s32[4]{0:T(128)} %pad_add_fusion.at_ref.refs_0_, bf16[5376,128]{1,0:T(8,128)(2,1)} %refs_1_.11, bf16[5376,128]{1,0:T(8,128)(2,1)} %refs_2_.9, bf16[256,384]{1,0:T(8,128)(2,1)} %total_partials.1.refs_3_, bf16[256,384]{1,0:T(8,128)(2,1)S(1)} %collective-permute-done.36.refs_4_, ...), custom_call_target="tpu_custom_call" | custom-call | tf_op jit(solution)/shard_map/project/pallas_call | solution.py:536
  186.6 3.3 %collective-permute-start.43 = (bf16[336,384]{1,0:T(8,128)(2,1)S(1)}, bf16[336,384]{1,0:T(8,128)(2,1)S(1)}, u32[]{:S(2)}, u32[]{:S(2)}) collective-permute-start(bf16[336,384]{1,0:T(8,128)(2,1)S(1)} %add_convert_fusion.1), channel_id=1, source_target_pairs={{0,14},{2,0},{4,2},{6,4},{8,6},{10,8},{12,10},{14,12},{1,15},{3,1}... | collective-permute-start | bytes 774152 | tf_op jit(solution)/shard_map/ppermute | solution.py:579
  190.0 3.7 %collective-permute-done.43 = bf16[336,384]{1,0:T(8,128)(2,1)S(1)} collective-permute-done((bf16[336,384]{1,0:T(8,128)(2,1)S(1)}, bf16[336,384]{1,0:T(8,128)(2,1)S(1)}, u32[]{:S(2)}, u32[]{:S(2)}) %collective-permute-start.43) | collective-permute-done | bytes 258080 | tf_op jit(solution)/shard_map/ppermute | solution.py:579
  193.7 3.8 %collective-permute-done.40 = bf16[336,384]{1,0:T(8,128)(2,1)S(1)} collective-permute-done((bf16[336,384]{1,0:T(8,128)(2,1)S(1)}, bf16[336,384]{1,0:T(8,128)(2,1)S(1)}, u32[]{:S(2)}, u32[]{:S(2)}) %collective-permute-start.40) | collective-permute-done | bytes 258080 | tf_op jit(solution)/shard_map/ppermute | solution.py:579
  197.5 0.8 fusion.1
  (118 shorter events, 1.3 us)
Async XLA Ops:
  0.7 8.5 %copy-start.33 = (s32[384]{0:T(512)S(1)}, s32[384]{0:T(512)}, u32[]{:S(2)}) copy-start(s32[384]{0:T(512)} %param.13) | copy-start | bytes 4612
  0.7 8.5 %copy-start.31 = (bf16[384,128]{1,0:T(8,128)(2,1)S(1)}, bf16[384,128]{1,0:T(8,128)(2,1)}, u32[]{:S(2)}) copy-start(bf16[384,128]{1,0:T(8,128)(2,1)} %param.11) | copy-start | bytes 294916
  0.7 8.5 %copy-start.32 = (bf16[384,128]{1,0:T(8,128)(2,1)S(1)}, bf16[384,128]{1,0:T(8,128)(2,1)}, u32[]{:S(2)}) copy-start(bf16[384,128]{1,0:T(8,128)(2,1)} %param.10) | copy-start | bytes 294916
  4.1 22.2 %collective-permute-start.11 = (bf16[4,256,384]{2,1,0:T(8,128)(2,1)}, bf16[4,256,384]{2,1,0:T(8,128)(2,1)S(1)}, u32[]{:S(2)}, u32[]{:S(2)}) collective-permute-start(bf16[4,256,384]{2,1,0:T(8,128)(2,1)} %split_w_out.1), channel_id=1, source_target_pairs={{0,1},{1,0},{2,3},{3,2},{4,5},{5,4},{6,7},{7,6},{8,9},{9,8},{10,11... | collective-permute-start | bytes 2359304 | tf_op jit(solution)/shard_map/ppermute | solution.py:559
  7.2 25.0 %collective-permute-start.13 = (bf16[336,384]{1,0:T(8,128)(2,1)S(1)}, bf16[336,384]{1,0:T(8,128)(2,1)S(1)}, u32[]{:S(2)}, u32[]{:S(2)}) collective-permute-start(bf16[336,384]{1,0:T(8,128)(2,1)S(1)} %bitcast.29), channel_id=1, source_target_pairs={{0,2},{2,4},{4,6},{6,8},{8,10},{10,12},{12,14},{14,0},{1,3},{3,5},... | collective-permute-start | bytes 774152 | tf_op jit(solution)/shard_map/ppermute | solution.py:579
  9.2 56.6 %copy-start.6 = (bf16[400,256]{1,0:T(8,128)(2,1)}, bf16[400,256]{1,0:T(8,128)(2,1)S(1)}, u32[]{:S(2)}) copy-start(bf16[400,256]{1,0:T(8,128)(2,1)S(1)} %fusion.2.refs_3_.refs_6_) | copy-start | bytes 614404
  9.2 24.9 %collective-permute-start.3 = (bf16[400,256]{1,0:T(8,128)(2,1)S(1)}, bf16[400,256]{1,0:T(8,128)(2,1)S(1)}, u32[]{:S(2)}, u32[]{:S(2)}) collective-permute-start(bf16[400,256]{1,0:T(8,128)(2,1)S(1)} %fusion.2.refs_3_.refs_6_), channel_id=1, source_target_pairs={{0,64},{16,80},{32,96},{48,112},{64,128},{80,144},{96,160},{112,17... | collective-permute-start | bytes 614408 | tf_op jit(solution)/shard_map/ppermute | solution.py:571
  26.3 32.6 %copy-start.16 = (bf16[4,256,384]{2,1,0:T(8,128)(2,1)}, bf16[4,256,384]{2,1,0:T(8,128)(2,1)S(1)}, u32[]{:S(2)}) copy-start(bf16[4,256,384]{2,1,0:T(8,128)(2,1)S(1)} %collective-permute-done.11.refs_2_) | copy-start | bytes 2359300
  26.4 32.6 %collective-permute-start.12 = (bf16[4,256,384]{2,1,0:T(8,128)(2,1)S(1)}, bf16[4,256,384]{2,1,0:T(8,128)(2,1)S(1)}, u32[]{:S(2)}, u32[]{:S(2)}) collective-permute-start(bf16[4,256,384]{2,1,0:T(8,128)(2,1)S(1)} %collective-permute-done.11.refs_2_), channel_id=1, source_target_pairs={{0,16},{16,0},{1,17},{17,1},{2,18},{18,2},{3,19},{19,3},{4,20},{20... | collective-permute-start | bytes 2359304 | tf_op jit(solution)/shard_map/ppermute | solution.py:559
  26.4 12.0 %collective-permute-start.14 = (bf16[336,384]{1,0:T(8,128)(2,1)S(1)}, bf16[336,384]{1,0:T(8,128)(2,1)S(1)}, u32[]{:S(2)}, u32[]{:S(2)}) collective-permute-start(bf16[336,384]{1,0:T(8,128)(2,1)S(1)} %bitcast.30), channel_id=1, source_target_pairs={{0,14},{2,0},{4,2},{6,4},{8,6},{10,8},{12,10},{14,12},{1,15},{3,1}... | collective-permute-start | bytes 774152 | tf_op jit(solution)/shard_map/ppermute | solution.py:579
  32.2 12.3 %copy-start.23 = (bf16[336,384]{1,0:T(8,128)(2,1)}, bf16[336,384]{1,0:T(8,128)(2,1)S(1)}, u32[]{:S(2)}) copy-start(bf16[336,384]{1,0:T(8,128)(2,1)S(1)} %collective-permute-done.13.refs_5_) | copy-start | bytes 774148
  32.2 9.8 %collective-permute-start.15 = (bf16[336,384]{1,0:T(8,128)(2,1)S(1)}, bf16[336,384]{1,0:T(8,128)(2,1)S(1)}, u32[]{:S(2)}, u32[]{:S(2)}) collective-permute-start(bf16[336,384]{1,0:T(8,128)(2,1)S(1)} %collective-permute-done.13.refs_5_), channel_id=1, source_target_pairs={{0,2},{2,4},{4,6},{6,8},{8,10},{10,12},{12,14},{14,0},{1,3},{3,5},... | collective-permute-start | bytes 774152 | tf_op jit(solution)/shard_map/ppermute | solution.py:579
  32.2 9.8 %collective-permute-start = (bf16[400,256]{1,0:T(8,128)(2,1)S(1)}, bf16[400,256]{1,0:T(8,128)(2,1)S(1)}, u32[]{:S(2)}, u32[]{:S(2)}) collective-permute-start(bf16[400,256]{1,0:T(8,128)(2,1)S(1)} %fusion.2.refs_3_.refs_6_), channel_id=1, source_target_pairs={{0,32},{16,48},{32,64},{48,80},{64,96},{80,112},{96,128},{112,144}... | collective-permute-start | bytes 614408 | tf_op jit(solution)/shard_map/ppermute | solution.py:571
  34.2 31.6 %copy-start.7 = (bf16[400,256]{1,0:T(8,128)(2,1)}, bf16[400,256]{1,0:T(8,128)(2,1)S(1)}, u32[]{:S(2)}) copy-start(bf16[400,256]{1,0:T(8,128)(2,1)S(1)} %collective-permute-done.3.refs_7_.refs_8_) | copy-start | bytes 614404
  34.2 10.4 %collective-permute-start.1 = (bf16[400,256]{1,0:T(8,128)(2,1)S(1)}, bf16[400,256]{1,0:T(8,128)(2,1)S(1)}, u32[]{:S(2)}, u32[]{:S(2)}) collective-permute-start(bf16[400,256]{1,0:T(8,128)(2,1)S(1)} %fusion.2.refs_3_.refs_6_), channel_id=1, source_target_pairs={{0,16},{16,0},{1,17},{17,1},{2,18},{18,2},{3,19},{19,3},{4,20},{20... | collective-permute-start | bytes 614408 | tf_op jit(solution)/shard_map/ppermute | solution.py:559
  38.4 15.0 %copy-start.24 = (bf16[336,384]{1,0:T(8,128)(2,1)}, bf16[336,384]{1,0:T(8,128)(2,1)S(1)}, u32[]{:S(2)}) copy-start(bf16[336,384]{1,0:T(8,128)(2,1)S(1)} %collective-permute-done.14.refs_6_) | copy-start | bytes 774148
  38.4 9.0 %collective-permute-start.16 = (bf16[336,384]{1,0:T(8,128)(2,1)S(1)}, bf16[336,384]{1,0:T(8,128)(2,1)S(1)}, u32[]{:S(2)}, u32[]{:S(2)}) collective-permute-start(bf16[336,384]{1,0:T(8,128)(2,1)S(1)} %collective-permute-done.14.refs_6_), channel_id=1, source_target_pairs={{0,14},{2,0},{4,2},{6,4},{8,6},{10,8},{12,10},{14,12},{1,15},{3,1}... | collective-permute-start | bytes 774152 | tf_op jit(solution)/shard_map/ppermute | solution.py:579
  42.1 10.8 %copy-start.25 = (bf16[336,384]{1,0:T(8,128)(2,1)}, bf16[336,384]{1,0:T(8,128)(2,1)S(1)}, u32[]{:S(2)}) copy-start(bf16[336,384]{1,0:T(8,128)(2,1)S(1)} %collective-permute-done.15.refs_7_) | copy-start | bytes 774148
  42.1 9.0 %collective-permute-start.17 = (bf16[336,384]{1,0:T(8,128)(2,1)S(1)}, bf16[336,384]{1,0:T(8,128)(2,1)S(1)}, u32[]{:S(2)}, u32[]{:S(2)}) collective-permute-start(bf16[336,384]{1,0:T(8,128)(2,1)S(1)} %collective-permute-done.15.refs_7_), channel_id=1, source_target_pairs={{0,2},{2,4},{4,6},{6,8},{8,10},{10,12},{12,14},{14,0},{1,3},{3,5},... | collective-permute-start | bytes 774152 | tf_op jit(solution)/shard_map/ppermute | solution.py:579
  42.1 23.7 %copy-start.8 = (bf16[400,256]{1,0:T(8,128)(2,1)}, bf16[400,256]{1,0:T(8,128)(2,1)S(1)}, u32[]{:S(2)}) copy-start(bf16[400,256]{1,0:T(8,128)(2,1)S(1)} %collective-permute-done.refs_4_.refs_7_) | copy-start | bytes 614404
  42.1 9.5 %collective-permute-start.5 = (bf16[400,256]{1,0:T(8,128)(2,1)S(1)}, bf16[400,256]{1,0:T(8,128)(2,1)S(1)}, u32[]{:S(2)}, u32[]{:S(2)}) collective-permute-start(bf16[400,256]{1,0:T(8,128)(2,1)S(1)} %fusion.2.refs_3_.refs_6_), channel_id=1, source_target_pairs={{0,96},{16,112},{32,128},{48,144},{64,160},{80,176},{96,192},{112,... | collective-permute-start | bytes 614408 | tf_op jit(solution)/shard_map/ppermute | solution.py:571
  44.6 21.3 %copy-start.9 = (bf16[400,256]{1,0:T(8,128)(2,1)}, bf16[400,256]{1,0:T(8,128)(2,1)S(1)}, u32[]{:S(2)}) copy-start(bf16[400,256]{1,0:T(8,128)(2,1)S(1)} %collective-permute-done.1.refs_5_.refs_11_) | copy-start | bytes 614404
  44.6 8.3 %collective-permute-start.6 = (bf16[400,256]{1,0:T(8,128)(2,1)S(1)}, bf16[400,256]{1,0:T(8,128)(2,1)S(1)}, u32[]{:S(2)}, u32[]{:S(2)}) collective-permute-start(bf16[400,256]{1,0:T(8,128)(2,1)S(1)} %fusion.2.refs_3_.refs_6_), channel_id=1, source_target_pairs={{0,128},{16,144},{32,160},{48,176},{64,192},{80,208},{96,224},{112... | collective-permute-start | bytes 614408 | tf_op jit(solution)/shard_map/ppermute | solution.py:571
  47.3 11.6 %copy-start.26 = (bf16[336,384]{1,0:T(8,128)(2,1)}, bf16[336,384]{1,0:T(8,128)(2,1)S(1)}, u32[]{:S(2)}) copy-start(bf16[336,384]{1,0:T(8,128)(2,1)S(1)} %collective-permute-done.16.refs_8_) | copy-start | bytes 774148
  47.3 8.1 %collective-permute-start.18 = (bf16[336,384]{1,0:T(8,128)(2,1)S(1)}, bf16[336,384]{1,0:T(8,128)(2,1)S(1)}, u32[]{:S(2)}, u32[]{:S(2)}) collective-permute-start(bf16[336,384]{1,0:T(8,128)(2,1)S(1)} %collective-permute-done.16.refs_8_), channel_id=1, source_target_pairs={{0,14},{2,0},{4,2},{6,4},{8,6},{10,8},{12,10},{14,12},{1,15},{3,1}... | collective-permute-start | bytes 774152 | tf_op jit(solution)/shard_map/ppermute | solution.py:579
  51.0 7.9 %copy-start.27 = (bf16[336,384]{1,0:T(8,128)(2,1)}, bf16[336,384]{1,0:T(8,128)(2,1)S(1)}, u32[]{:S(2)}) copy-start(bf16[336,384]{1,0:T(8,128)(2,1)S(1)} %collective-permute-done.17.refs_9_) | copy-start | bytes 774148
  51.0 7.8 %collective-permute-start.19 = (bf16[336,384]{1,0:T(8,128)(2,1)S(1)}, bf16[336,384]{1,0:T(8,128)(2,1)S(1)}, u32[]{:S(2)}, u32[]{:S(2)}) collective-permute-start(bf16[336,384]{1,0:T(8,128)(2,1)S(1)} %collective-permute-done.17.refs_9_), channel_id=1, source_target_pairs={{0,2},{2,4},{4,6},{6,8},{8,10},{10,12},{12,14},{14,0},{1,3},{3,5},... | collective-permute-start | bytes 774152 | tf_op jit(solution)/shard_map/ppermute | solution.py:579
  51.5 14.3 %copy-start.10 = (bf16[400,256]{1,0:T(8,128)(2,1)}, bf16[400,256]{1,0:T(8,128)(2,1)S(1)}, u32[]{:S(2)}) copy-start(bf16[400,256]{1,0:T(8,128)(2,1)S(1)} %collective-permute-done.5.refs_8_.refs_9_) | copy-start | bytes 614404
  51.5 1.4 collective-permute-start.9
  52.9 13.0 %copy-start.11 = (bf16[400,256]{1,0:T(8,128)(2,1)}, bf16[400,256]{1,0:T(8,128)(2,1)S(1)}, u32[]{:S(2)}) copy-start(bf16[400,256]{1,0:T(8,128)(2,1)S(1)} %collective-permute-done.6.refs_9_.refs_10_) | copy-start | bytes 614404
  52.9 13.0 %collective-permute-start.4 = (bf16[400,256]{1,0:T(8,128)(2,1)S(1)}, bf16[400,256]{1,0:T(8,128)(2,1)S(1)}, u32[]{:S(2)}, u32[]{:S(2)}) collective-permute-start(bf16[400,256]{1,0:T(8,128)(2,1)S(1)} %collective-permute-done.3.refs_7_.refs_8_), channel_id=1, source_target_pairs={{0,16},{16,0},{1,17},{17,1},{2,18},{18,2},{3,19},{19,3},{4,20},{20... | collective-permute-start | bytes 614408 | tf_op jit(solution)/shard_map/ppermute | solution.py:559
  52.9 17.8 %collective-permute-start.2 = (bf16[400,256]{1,0:T(8,128)(2,1)S(1)}, bf16[400,256]{1,0:T(8,128)(2,1)S(1)}, u32[]{:S(2)}, u32[]{:S(2)}) collective-permute-start(bf16[400,256]{1,0:T(8,128)(2,1)S(1)} %collective-permute-done.refs_4_.refs_7_), channel_id=1, source_target_pairs={{0,16},{16,0},{1,17},{17,1},{2,18},{18,2},{3,19},{19,3},{4,20},{20... | collective-permute-start | bytes 614408 | tf_op jit(solution)/shard_map/ppermute | solution.py:559
  55.5 22.2 %collective-permute-start.7 = (bf16[400,256]{1,0:T(8,128)(2,1)S(1)}, bf16[400,256]{1,0:T(8,128)(2,1)S(1)}, u32[]{:S(2)}, u32[]{:S(2)}) collective-permute-start(bf16[400,256]{1,0:T(8,128)(2,1)S(1)} %collective-permute-done.5.refs_8_.refs_9_), channel_id=1, source_target_pairs={{0,16},{16,0},{1,17},{17,1},{2,18},{18,2},{3,19},{19,3},{4,20},{20... | collective-permute-start | bytes 614408 | tf_op jit(solution)/shard_map/ppermute | solution.py:559
  58.9 18.8 %collective-permute-start.8 = (bf16[400,256]{1,0:T(8,128)(2,1)S(1)}, bf16[400,256]{1,0:T(8,128)(2,1)S(1)}, u32[]{:S(2)}, u32[]{:S(2)}) collective-permute-start(bf16[400,256]{1,0:T(8,128)(2,1)S(1)} %collective-permute-done.6.refs_9_.refs_10_), channel_id=1, source_target_pairs={{0,16},{16,0},{1,17},{17,1},{2,18},{18,2},{3,19},{19,3},{4,20},{20... | collective-permute-start | bytes 614408 | tf_op jit(solution)/shard_map/ppermute | solution.py:559
  59.6 18.2 %collective-permute-start.10 = (bf16[400,256]{1,0:T(8,128)(2,1)}, bf16[400,256]{1,0:T(8,128)(2,1)S(1)}, u32[]{:S(2)}, u32[]{:S(2)}) collective-permute-start(bf16[400,256]{1,0:T(8,128)(2,1)} %collective-permute-done.9), channel_id=1, source_target_pairs={{0,16},{16,0},{1,17},{17,1},{2,18},{18,2},{3,19},{19,3},{4,20},{20... | collective-permute-start | bytes 614408 | tf_op jit(solution)/shard_map/ppermute | solution.py:559
  65.9 18.5 %collective-permute-start.20 = (bf16[256,384]{1,0:T(8,128)(2,1)S(1)}, bf16[256,384]{1,0:T(8,128)(2,1)S(1)}, u32[]{:S(2)}, u32[]{:S(2)}) collective-permute-start(bf16[256,384]{1,0:T(8,128)(2,1)S(1)} %get-tuple-element.49), channel_id=1, source_target_pairs={{0,1},{1,0},{2,3},{3,2},{4,5},{5,4},{6,7},{7,6},{8,9},{9,8},{10,11... | collective-permute-start | bytes 589832 | tf_op jit(solution)/shard_map/ppermute | solution.py:559
  96.7 22.4 %collective-permute-start.21 = (bf16[5,384,256]{2,1,0:T(8,128)(2,1)}, bf16[5,384,256]{2,1,0:T(8,128)(2,1)S(1)}, u32[]{:S(2)}, u32[]{:S(2)}) collective-permute-start(bf16[5,384,256]{2,1,0:T(8,128)(2,1)} %get-tuple-element.53), channel_id=1, source_target_pairs={{0,16},{16,0},{1,17},{17,1},{2,18},{18,2},{3,19},{19,3},{4,20},{20... | collective-permute-start | bytes 2949128 | tf_op jit(solution)/shard_map/ppermute | solution.py:559
  99.9 45.9 %copy-start.30 = (bf16[256,384]{1,0:T(8,128)(2,1)S(1)}, bf16[256,384]{1,0:T(8,128)(2,1)}, u32[]{:S(2)}) copy-start(bf16[256,384]{1,0:T(8,128)(2,1)} %get-tuple-element.60.refs_2_) | copy-start | bytes 589828
  100.0 12.5 %collective-permute-start.28 = (bf16[336,512]{1,0:T(8,128)(2,1)S(1)}, bf16[336,512]{1,0:T(8,128)(2,1)S(1)}, u32[]{:S(2)}, u32[]{:S(2)}) collective-permute-start(bf16[336,512]{1,0:T(8,128)(2,1)S(1)} %pad_maximum_fusion), channel_id=1, source_target_pairs={{0,1},{1,0},{2,3},{3,2},{4,5},{5,4},{6,7},{7,6},{8,9},{9,8},{10,11... | collective-permute-start | bytes 1032200 | tf_op jit(solution)/shard_map/ppermute | solution.py:559
  100.6 18.4 %collective-permute-start.29 = (bf16[336,512]{1,0:T(8,128)(2,1)S(1)}, bf16[336,512]{1,0:T(8,128)(2,1)}, u32[]{:S(2)}, u32[]{:S(2)}) collective-permute-start(bf16[336,512]{1,0:T(8,128)(2,1)S(1)} %pad_maximum_fusion.1), channel_id=1, source_target_pairs={{0,1},{1,0},{2,3},{3,2},{4,5},{5,4},{6,7},{7,6},{8,9},{9,8},{10,11... | collective-permute-start | bytes 1032200 | tf_op jit(solution)/shard_map/ppermute | solution.py:559
  112.5 37.1 %copy-start = (bf16[336,512]{1,0:T(8,128)(2,1)}, bf16[336,512]{1,0:T(8,128)(2,1)S(1)}, u32[]{:S(2)}) copy-start(bf16[336,512]{1,0:T(8,128)(2,1)S(1)} %collective-permute-done.28.refs_5_.refs_2_.refs_6_) | copy-start | bytes 1032196
  112.5 12.4 %collective-permute-start.30 = (bf16[336,512]{1,0:T(8,128)(2,1)S(1)}, bf16[336,512]{1,0:T(8,128)(2,1)}, u32[]{:S(2)}, u32[]{:S(2)}) collective-permute-start(bf16[336,512]{1,0:T(8,128)(2,1)S(1)} %collective-permute-done.28.refs_5_.refs_2_.refs_6_), channel_id=1, source_target_pairs={{0,32},{32,0},{64,96},{96,64},{1,33},{33,1},{65,97},{97,65},{2,34}... | collective-permute-start | bytes 1032200 | tf_op jit(solution)/shard_map/ppermute | solution.py:563
  119.0 10.5 %collective-permute-start.31 = (bf16[336,512]{1,0:T(8,128)(2,1)}, bf16[336,512]{1,0:T(8,128)(2,1)}, u32[]{:S(2)}, u32[]{:S(2)}) collective-permute-start(bf16[336,512]{1,0:T(8,128)(2,1)} %collective-permute-done.29.refs_6_.refs_3_.refs_7_), channel_id=1, source_target_pairs={{0,32},{32,0},{64,96},{96,64},{1,33},{33,1},{65,97},{97,65},{2,34}... | collective-permute-start | bytes 1032200 | tf_op jit(solution)/shard_map/ppermute | solution.py:563
  121.0 8.5 %collective-permute-start.22 = (bf16[384,256]{1,0:T(8,128)(2,1)S(1)}, bf16[384,256]{1,0:T(8,128)(2,1)S(1)}, u32[]{:S(2)}, u32[]{:S(2)}) collective-permute-start(bf16[384,256]{1,0:T(8,128)(2,1)S(1)} %get-tuple-element.55), channel_id=1, source_target_pairs={{176,16},{208,48},{240,80},{177,17},{209,49},{241,81},{178,18},{21... | collective-permute-start | bytes 589832 | tf_op jit(solution)/shard_map/ppermute | solution.py:575
  121.7 12.2 %collective-permute-start.23 = (bf16[384,256]{1,0:T(8,128)(2,1)S(1)}, bf16[384,256]{1,0:T(8,128)(2,1)S(1)}, u32[]{:S(2)}, u32[]{:S(2)}) collective-permute-start(bf16[384,256]{1,0:T(8,128)(2,1)S(1)} %get-tuple-element.56), channel_id=1, source_target_pairs={{128,0},{144,16},{160,32},{176,48},{192,64},{208,80},{224,96},{240... | collective-permute-start | bytes 589832 | tf_op jit(solution)/shard_map/ppermute | solution.py:575
  123.0 12.7 %collective-permute-start.24 = (bf16[384,256]{1,0:T(8,128)(2,1)S(1)}, bf16[384,256]{1,0:T(8,128)(2,1)S(1)}, u32[]{:S(2)}, u32[]{:S(2)}) collective-permute-start(bf16[384,256]{1,0:T(8,128)(2,1)S(1)} %get-tuple-element.57), channel_id=1, source_target_pairs={{96,0},{112,16},{128,32},{144,48},{160,64},{176,80},{192,96},{208,... | collective-permute-start | bytes 589832 | tf_op jit(solution)/shard_map/ppermute | solution.py:575
  124.9 19.1 %collective-permute-start.25 = (bf16[384,256]{1,0:T(8,128)(2,1)S(1)}, bf16[384,256]{1,0:T(8,128)(2,1)S(1)}, u32[]{:S(2)}, u32[]{:S(2)}) collective-permute-start(bf16[384,256]{1,0:T(8,128)(2,1)S(1)} %get-tuple-element.58), channel_id=1, source_target_pairs={{64,0},{80,16},{96,32},{112,48},{128,64},{144,80},{160,96},{176,11... | collective-permute-start | bytes 589832 | tf_op jit(solution)/shard_map/ppermute | solution.py:575
  129.5 20.0 %collective-permute-start.32 = (bf16[336,512]{1,0:T(8,128)(2,1)S(1)}, bf16[336,512]{1,0:T(8,128)(2,1)S(1)}, u32[]{:S(2)}, u32[]{:S(2)}) collective-permute-start(bf16[336,512]{1,0:T(8,128)(2,1)S(1)} %collective-permute-done.28.refs_5_.refs_2_.refs_6_), channel_id=1, source_target_pairs={{0,16},{16,0},{1,17},{17,1},{2,18},{18,2},{3,19},{19,3},{4,20},{20... | collective-permute-start | bytes 1032200 | tf_op jit(solution)/shard_map/ppermute | solution.py:559
  129.5 16.3 %collective-permute-start.26 = (bf16[384,256]{1,0:T(8,128)(2,1)S(1)}, bf16[384,256]{1,0:T(8,128)(2,1)S(1)}, u32[]{:S(2)}, u32[]{:S(2)}) collective-permute-start(bf16[384,256]{1,0:T(8,128)(2,1)S(1)} %get-tuple-element.59), channel_id=1, source_target_pairs={{32,0},{48,16},{64,32},{80,48},{96,64},{112,80},{128,96},{144,112}... | collective-permute-start | bytes 589832 | tf_op jit(solution)/shard_map/ppermute | solution.py:575
  133.9 22.5 %collective-permute-start.33 = (bf16[336,512]{1,0:T(8,128)(2,1)}, bf16[336,512]{1,0:T(8,128)(2,1)S(1)}, u32[]{:S(2)}, u32[]{:S(2)}) collective-permute-start(bf16[336,512]{1,0:T(8,128)(2,1)} %collective-permute-done.29.refs_6_.refs_3_.refs_7_), channel_id=1, source_target_pairs={{0,16},{16,0},{1,17},{17,1},{2,18},{18,2},{3,19},{19,3},{4,20},{20... | collective-permute-start | bytes 1032200 | tf_op jit(solution)/shard_map/ppermute | solution.py:559
  135.7 20.8 %collective-permute-start.34 = (bf16[336,512]{1,0:T(8,128)(2,1)}, bf16[336,512]{1,0:T(8,128)(2,1)S(1)}, u32[]{:S(2)}, u32[]{:S(2)}) collective-permute-start(bf16[336,512]{1,0:T(8,128)(2,1)} %collective-permute-done.30.refs_7_.refs_4_.refs_8_), channel_id=1, source_target_pairs={{0,16},{16,0},{1,17},{17,1},{2,18},{18,2},{3,19},{19,3},{4,20},{20... | collective-permute-start | bytes 1032200 | tf_op jit(solution)/shard_map/ppermute | solution.py:559
  144.0 12.5 %collective-permute-start.35 = (bf16[336,512]{1,0:T(8,128)(2,1)}, bf16[336,512]{1,0:T(8,128)(2,1)S(1)}, u32[]{:S(2)}, u32[]{:S(2)}) collective-permute-start(bf16[336,512]{1,0:T(8,128)(2,1)} %collective-permute-done.31.refs_8_.refs_5_.refs_9_), channel_id=1, source_target_pairs={{0,16},{16,0},{1,17},{17,1},{2,18},{18,2},{3,19},{19,3},{4,20},{20... | collective-permute-start | bytes 1032200 | tf_op jit(solution)/shard_map/ppermute | solution.py:559
  145.8 10.7 %collective-permute-start.36 = (bf16[256,384]{1,0:T(8,128)(2,1)S(1)}, bf16[256,384]{1,0:T(8,128)(2,1)S(1)}, u32[]{:S(2)}, u32[]{:S(2)}) collective-permute-start(bf16[256,384]{1,0:T(8,128)(2,1)S(1)} %copy-done.30), channel_id=1, source_target_pairs={{0,1},{1,0},{2,3},{3,2},{4,5},{5,4},{6,7},{7,6},{8,9},{9,8},{10,11... | collective-permute-start | bytes 589832 | tf_op jit(solution)/shard_map/ppermute | solution.py:559
  149.5 6.9 %copy-start.1 = (bf16[336,512]{1,0:T(8,128)(2,1)}, bf16[336,512]{1,0:T(8,128)(2,1)S(1)}, u32[]{:S(2)}) copy-start(bf16[336,512]{1,0:T(8,128)(2,1)S(1)} %collective-permute-done.32.refs_9_.refs_6_.refs_10_) | copy-start | bytes 1032196
  149.5 11.7 %collective-permute-start.27 = (bf16[256,384]{1,0:T(8,128)(2,1)}, bf16[256,384]{1,0:T(8,128)(2,1)S(1)}, u32[]{:S(2)}, u32[]{:S(2)}) collective-permute-start(bf16[256,384]{1,0:T(8,128)(2,1)} %total_partials.1.refs_3_), channel_id=1, source_target_pairs={{0,1},{1,0},{2,3},{3,2},{4,5},{5,4},{6,7},{7,6},{8,9},{9,8},{10,11... | collective-permute-start | bytes 589832 | tf_op jit(solution)/shard_map/ppermute | solution.py:559
  164.5 8.6 %collective-permute-start.37 = (bf16[336,384]{1,0:T(8,128)(2,1)S(1)}, bf16[336,384]{1,0:T(8,128)(2,1)S(1)}, u32[]{:S(2)}, u32[]{:S(2)}) collective-permute-start(bf16[336,384]{1,0:T(8,128)(2,1)S(1)} %get-tuple-element.65), channel_id=1, source_target_pairs={{0,2},{2,4},{4,6},{6,8},{8,10},{10,12},{12,14},{14,0},{1,3},{3,5},... | collective-permute-start | bytes 774152 | tf_op jit(solution)/shard_map/ppermute | solution.py:579
  164.6 9.8 %collective-permute-start.41 = (bf16[336,384]{1,0:T(8,128)(2,1)S(1)}, bf16[336,384]{1,0:T(8,128)(2,1)S(1)}, u32[]{:S(2)}, u32[]{:S(2)}) collective-permute-start(bf16[336,384]{1,0:T(8,128)(2,1)S(1)} %get-tuple-element.75), channel_id=1, source_target_pairs={{0,14},{2,0},{4,2},{6,4},{8,6},{10,8},{12,10},{14,12},{1,15},{3,1}... | collective-permute-start | bytes 774152 | tf_op jit(solution)/shard_map/ppermute | solution.py:579
  173.1 8.8 %copy-start.20 = (f32[336,384]{1,0:T(8,128)S(1)}, f32[336,384]{1,0:T(8,128)}, u32[]{:S(2)}) copy-start(f32[336,384]{1,0:T(8,128)} %get-tuple-element.71) | copy-start | bytes 1548292
  174.3 7.6 %collective-permute-start.38 = (bf16[336,384]{1,0:T(8,128)(2,1)S(1)}, bf16[336,384]{1,0:T(8,128)(2,1)S(1)}, u32[]{:S(2)}, u32[]{:S(2)}) collective-permute-start(bf16[336,384]{1,0:T(8,128)(2,1)S(1)} %add_convert_fusion.5), channel_id=1, source_target_pairs={{0,2},{2,4},{4,6},{6,8},{8,10},{10,12},{12,14},{14,0},{1,3},{3,5},... | collective-permute-start | bytes 774152 | tf_op jit(solution)/shard_map/ppermute | solution.py:579
  174.5 12.0 %collective-permute-start.42 = (bf16[336,384]{1,0:T(8,128)(2,1)S(1)}, bf16[336,384]{1,0:T(8,128)(2,1)S(1)}, u32[]{:S(2)}, u32[]{:S(2)}) collective-permute-start(bf16[336,384]{1,0:T(8,128)(2,1)S(1)} %add_convert_fusion.2), channel_id=1, source_target_pairs={{0,14},{2,0},{4,2},{6,4},{8,6},{10,8},{12,10},{14,12},{1,15},{3,1}... | collective-permute-start | bytes 774152 | tf_op jit(solution)/shard_map/ppermute | solution.py:579
  182.0 7.8 %collective-permute-start.39 = (bf16[336,384]{1,0:T(8,128)(2,1)S(1)}, bf16[336,384]{1,0:T(8,128)(2,1)S(1)}, u32[]{:S(2)}, u32[]{:S(2)}) collective-permute-start(bf16[336,384]{1,0:T(8,128)(2,1)S(1)} %add_convert_fusion.4), channel_id=1, source_target_pairs={{0,2},{2,4},{4,6},{6,8},{8,10},{10,12},{12,14},{14,0},{1,3},{3,5},... | collective-permute-start | bytes 774152 | tf_op jit(solution)/shard_map/ppermute | solution.py:579
  186.5 11.1 %copy-start.17 = (f32[336,384]{1,0:T(8,128)S(1)}, f32[336,384]{1,0:T(8,128)}, u32[]{:S(2)}) copy-start(f32[336,384]{1,0:T(8,128)} %get-tuple-element.78) | copy-start | bytes 1548292
  186.6 7.1 %collective-permute-start.43 = (bf16[336,384]{1,0:T(8,128)(2,1)S(1)}, bf16[336,384]{1,0:T(8,128)(2,1)S(1)}, u32[]{:S(2)}, u32[]{:S(2)}) collective-permute-start(bf16[336,384]{1,0:T(8,128)(2,1)S(1)} %add_convert_fusion.1), channel_id=1, source_target_pairs={{0,14},{2,0},{4,2},{6,4},{8,6},{10,8},{12,10},{14,12},{1,15},{3,1}... | collective-permute-start | bytes 774152 | tf_op jit(solution)/shard_map/ppermute | solution.py:579
  189.9 7.6 %collective-permute-start.40 = (bf16[336,384]{1,0:T(8,128)(2,1)S(1)}, bf16[336,384]{1,0:T(8,128)(2,1)S(1)}, u32[]{:S(2)}, u32[]{:S(2)}) collective-permute-start(bf16[336,384]{1,0:T(8,128)(2,1)S(1)} %add_convert_fusion.3), channel_id=1, source_target_pairs={{0,2},{2,4},{4,6},{6,8},{8,10},{10,12},{12,14},{14,0},{1,3},{3,5},... | collective-permute-start | bytes 774152 | tf_op jit(solution)/shard_map/ppermute | solution.py:579
  (14 other events, 30.3 us)

commit v8 on v7

--- a/solution.py
+++ b/solution.py
@@ -551,6 +551,21 @@
     )(at, *weights, *grads, *far_rows, *sums)
 
 
+def add_kernel(ahead_ref, up_ref, behind_ref, down_ref, ahead_out, behind_out):
+    ahead_out[...] = (ahead_ref[...].astype(F32) + up_ref[...]).astype(BF16)
+    behind_out[...] = (behind_ref[...].astype(F32) + down_ref[...]).astype(BF16)
+
+
+def add_both(ahead, up, behind, down):
+    return pl.pallas_call(
+        add_kernel,
+        name="add_both",
+        out_shape=(pltpu.VMEM((FEATS, ROWS), BF16),) * 2,
+        in_specs=[VMEM] * 4,
+        out_specs=(VMEM, VMEM),
+    )(arrive(ahead), arrive(up), arrive(behind), arrive(down))
+
+
 def arrive(x):
     return pltpu.with_memory_space_constraint(x, pltpu.VMEM)
 
@@ -651,9 +666,14 @@
     ahead = round_z(ahead, 1)
     behind = round_z(behind, -1)
     for k in (2, 3):
-        add_ahead, add_behind = rest[2 * k - 4], rest[2 * k - 3]
-        ahead = round_z((ahead.astype(F32) + add_ahead).astype(BF16), 1)
-        behind = round_z((behind.astype(F32) + add_behind).astype(BF16), -1)
+        up, down = rest[2 * k - 4], rest[2 * k - 3]
+        if k == 2:
+            ahead = (ahead.astype(F32) + up).astype(BF16)
+            behind = (behind.astype(F32) + down).astype(BF16)
+        else:
+            ahead, behind = add_both(ahead, up, behind, down)
+        ahead = round_z(ahead, 1)
+        behind = round_z(behind, -1)
     ahead = round_z((ahead.astype(F32) + rest[4]).astype(BF16), 1)
     result = (ahead.astype(F32) + behind.astype(F32) + rest[5]).astype(BF16)
     return result.T

time: 199 us -> 202 us (1.015)
  waiting for transfers between devices: 66.5 us -> 69.8 us
  starting transfers between devices: 62.7 us -> 60.4 us
    ppermute x14, waiting for transfers between devices: 22.5 us -> 25.8 us  [round_z(): return lax.ppermute(x, 'z', [(i, (i + step) % RING) for i in range(RING)])]
    ppermute x14, starting transfers between devices: 25.3 us -> 22.9 us  [round_z(): return lax.ppermute(x, 'z', [(i, (i + step) % RING) for i in range(RING)])]
  transfers between devices with their start and end apart: 44 -> 44, of which waited for: 15 -> 16; matrix products, arithmetic and copies ran while one was open for 2% -> 3% of each run, Pallas kernels for 20% -> 20%
where the time goes in v8:
time: 202 us; the launch traced here: 201 us
  waiting for transfers between devices  69.8 us (35%)
  starting transfers between devices  60.4 us (30%)
  Pallas kernels  59.7 us (30%)
  local copies, waits for them, and re-layouts  5.72 us (3%)
  other arithmetic  4.9 us (2%)
    ppermute x18, waiting for transfers between devices, swapped(): return lax.ppermute(x, axis, [(0, 1), (1, 0)])  29.3 us
    ppermute x14, waiting for transfers between devices, round_z(): return lax.ppermute(x, 'z', [(i, (i + step) % RING) for i in range(RING)])  25.8 us
    ppermute x14, starting transfers between devices, round_z(): return lax.ppermute(x, 'z', [(i, (i + step) % RING) for i in range(RING)])  22.9 us
    pallas_call x5, Pallas kernels, project(): pl.pallas_call(lambda *refs: project_kernel(deltas, own_lanes, far, len(g...  21.6 us
    ppermute x18, starting transfers between devices, swapped(): return lax.ppermute(x, axis, [(0, 1), (1, 0)])  17.1 us
    pallas_call x1, Pallas kernels, attention_grads(): pl.pallas_call(grads_kernel, name='attention_grads', out_shape=(jax.Shape...  12.3 us
    pallas_call x2, Pallas kernels, attention_stats(): pl.pallas_call(lambda *refs: stats_kernel(low, high, *refs), name='stats_...  12.1 us
    ppermute x5, waiting for transfers between devices, chips_back(): return arrive(lax.ppermute(x, AA, [(j, i) for i, j in chip_pairs(d)]))  11.5 us
  transfers between devices with their start and end apart: 44, of which 16 were waited for; matrix products, arithmetic and copies ran while one was open for 3% of the time, Pallas kernels for 20%

profile of v8, /device:TPU:24, one launch (start us, length us, event | category | flops | bytes accessed | tf_op | source)
XLA Modules:
  0.0 201.1 jit_solution(380925814431750863)
XLA Ops:
  0.0 0.6 pad_add_fusion.at_ref.refs_0_
  0.7 3.5 %split_w_out.1 = bf16[4,256,384]{2,1,0:T(8,128)(2,1)} custom-call(s32[4]{0:T(128)} %pad_add_fusion.at_ref.refs_0_, bf16[256,5376]{1,0:T(8,128)(2,1)} %refs_1_.6), custom_call_target="tpu_custom_call" | custom-call | tf_op jit(solution)/shard_map/split_w_out/pallas_call | solution.py:348
  4.1 3.1 %collective-permute-start.11 = (bf16[4,256,384]{2,1,0:T(8,128)(2,1)}, bf16[4,256,384]{2,1,0:T(8,128)(2,1)S(1)}, u32[]{:S(2)}, u32[]{:S(2)}) collective-permute-start(bf16[4,256,384]{2,1,0:T(8,128)(2,1)} %split_w_out.1), channel_id=1, source_target_pairs={{0,1},{1,0},{2,3},{3,2},{4,5},{5,4},{6,7},{7,6},{8,9},{9,8},{10,11... | collective-permute-start | bytes 2359304 | tf_op jit(solution)/shard_map/ppermute | solution.py:574
  7.2 1.9 collective-permute-start.13
  9.2 3.2 %collective-permute-start.3 = (bf16[400,256]{1,0:T(8,128)(2,1)S(1)}, bf16[400,256]{1,0:T(8,128)(2,1)S(1)}, u32[]{:S(2)}, u32[]{:S(2)}) collective-permute-start(bf16[400,256]{1,0:T(8,128)(2,1)S(1)} %fusion.2.refs_3_.refs_6_), channel_id=1, source_target_pairs={{0,64},{16,80},{32,96},{48,112},{64,128},{80,144},{96,160},{112,17... | collective-permute-start | bytes 614408 | tf_op jit(solution)/shard_map/ppermute | solution.py:586
  12.4 13.9 %collective-permute-done.11.refs_2_ = bf16[4,256,384]{2,1,0:T(8,128)(2,1)S(1)} collective-permute-done((bf16[4,256,384]{2,1,0:T(8,128)(2,1)}, bf16[4,256,384]{2,1,0:T(8,128)(2,1)S(1)}, u32[]{:S(2)}, u32[]{:S(2)}) %collective-permute-start.11) | collective-permute-done | bytes 786464 | tf_op jit(solution)/shard_map/ppermute | solution.py:574
  26.4 5.9 %collective-permute-start.14 = (bf16[336,384]{1,0:T(8,128)(2,1)S(1)}, bf16[336,384]{1,0:T(8,128)(2,1)S(1)}, u32[]{:S(2)}, u32[]{:S(2)}) collective-permute-start(bf16[336,384]{1,0:T(8,128)(2,1)S(1)} %bitcast.30), channel_id=1, source_target_pairs={{0,14},{2,0},{4,2},{6,4},{8,6},{10,8},{12,10},{14,12},{1,15},{3,1}... | collective-permute-start | bytes 774152 | tf_op jit(solution)/shard_map/ppermute | solution.py:594
  32.2 1.9 collective-permute-start
  34.5 3.9 %collective-permute-done.14.refs_6_ = bf16[336,384]{1,0:T(8,128)(2,1)S(1)} collective-permute-done((bf16[336,384]{1,0:T(8,128)(2,1)S(1)}, bf16[336,384]{1,0:T(8,128)(2,1)S(1)}, u32[]{:S(2)}, u32[]{:S(2)}) %collective-permute-start.14) | collective-permute-done | bytes 258080 | tf_op jit(solution)/shard_map/ppermute | solution.py:594
  38.4 3.7 %collective-permute-start.16 = (bf16[336,384]{1,0:T(8,128)(2,1)S(1)}, bf16[336,384]{1,0:T(8,128)(2,1)S(1)}, u32[]{:S(2)}, u32[]{:S(2)}) collective-permute-start(bf16[336,384]{1,0:T(8,128)(2,1)S(1)} %collective-permute-done.14.refs_6_), channel_id=1, source_target_pairs={{0,14},{2,0},{4,2},{6,4},{8,6},{10,8},{12,10},{14,12},{1,15},{3,1}... | collective-permute-start | bytes 774152 | tf_op jit(solution)/shard_map/ppermute | solution.py:594
  42.1 2.4 %collective-permute-start.5 = (bf16[400,256]{1,0:T(8,128)(2,1)S(1)}, bf16[400,256]{1,0:T(8,128)(2,1)S(1)}, u32[]{:S(2)}, u32[]{:S(2)}) collective-permute-start(bf16[400,256]{1,0:T(8,128)(2,1)S(1)} %fusion.2.refs_3_.refs_6_), channel_id=1, source_target_pairs={{0,96},{16,112},{32,128},{48,144},{64,160},{80,176},{96,192},{112,... | collective-permute-start | bytes 614408 | tf_op jit(solution)/shard_map/ppermute | solution.py:586
  44.6 1.3 collective-permute-start.6
  45.9 1.5 collective-permute-done.16.refs_8_
  47.3 3.7 %collective-permute-start.18 = (bf16[336,384]{1,0:T(8,128)(2,1)S(1)}, bf16[336,384]{1,0:T(8,128)(2,1)S(1)}, u32[]{:S(2)}, u32[]{:S(2)}) collective-permute-start(bf16[336,384]{1,0:T(8,128)(2,1)S(1)} %collective-permute-done.16.refs_8_), channel_id=1, source_target_pairs={{0,14},{2,0},{4,2},{6,4},{8,6},{10,8},{12,10},{14,12},{1,15},{3,1}... | collective-permute-start | bytes 774152 | tf_op jit(solution)/shard_map/ppermute | solution.py:594
  51.5 1.3 collective-permute-start.9
  53.4 2.1 %collective-permute-done.18.refs_10_ = bf16[336,384]{1,0:T(8,128)(2,1)S(1)} collective-permute-done((bf16[336,384]{1,0:T(8,128)(2,1)S(1)}, bf16[336,384]{1,0:T(8,128)(2,1)S(1)}, u32[]{:S(2)}, u32[]{:S(2)}) %collective-permute-start.18) | collective-permute-done | bytes 258080 | tf_op jit(solution)/shard_map/ppermute | solution.py:594
  55.5 3.4 %collective-permute-done.19.refs_11_ = bf16[336,384]{1,0:T(8,128)(2,1)S(1)} collective-permute-done((bf16[336,384]{1,0:T(8,128)(2,1)S(1)}, bf16[336,384]{1,0:T(8,128)(2,1)S(1)}, u32[]{:S(2)}, u32[]{:S(2)}) %collective-permute-start.19) | collective-permute-done | bytes 258080 | tf_op jit(solution)/shard_map/ppermute | solution.py:594
  58.9 0.6 copy-done.26
  59.6 6.2 %dout_parts.1 = (f32[256,384]{1,0:T(8,128)}, bf16[256,384]{1,0:T(8,128)(2,1)S(1)}) custom-call(s32[4]{0:T(128)} %pad_add_fusion.at_ref.refs_0_, bf16[256,5376]{1,0:T(8,128)(2,1)} %refs_1_.6, bf16[4,256,384]{2,1,0:T(8,128)(2,1)} %copy-done.17, bf16[4,256,384]{2,1,0:T(8,128)(2,1)S(1)} %collective-permute-done.12.refs_3_, bf16[336,384]{1,0:T(8,128)(2,1)} %bitcast.28, ...), custom_call_target="tpu_custom_call" | custom-call | tf_op jit(solution)/shard_map/dout_parts/pallas_call | solution.py:408
  65.8 3.3 %collective-permute-start.20 = (bf16[256,384]{1,0:T(8,128)(2,1)S(1)}, bf16[256,384]{1,0:T(8,128)(2,1)S(1)}, u32[]{:S(2)}, u32[]{:S(2)}) collective-permute-start(bf16[256,384]{1,0:T(8,128)(2,1)S(1)} %get-tuple-element.51), channel_id=1, source_target_pairs={{0,1},{1,0},{2,3},{3,2},{4,5},{5,4},{6,7},{7,6},{8,9},{9,8},{10,11... | collective-permute-start | bytes 589832 | tf_op jit(solution)/shard_map/ppermute | solution.py:574
  69.1 0.6 broadcast_in_dim.8.refs_1_
  69.7 1.0 dynamic-slice_bitcast_fusion
  70.8 0.7 copy-done.13
  71.4 6.3 %stats_near.1 = (f32[1,768]{1,0:T(1,128)}, f32[1,768]{1,0:T(1,128)}, f32[128,768]{1,0:T(8,128)}, s32[1,384]{1,0:T(1,128)}) custom-call(s32[1]{0:T(128)} %bitcast.4.refs_0_.own_ref, s32[1,384]{1,0:T(1,128)} %broadcast_in_dim.8.refs_1_, bf16[384,256]{1,0:T(8,128)(2,1)} %refs_1_.7, bf16[400,256]{1,0:T(8,128)(2,1)} %copy-done.7, bf16[400,256]{1,0:T(8,128)(2,1)} %copy-done.9, ...), custom_call_target="tpu_custom_call" | custom-call | tf_op jit(solution)/shard_map/stats_near/pallas_call | solution.py:284
  77.8 0.6 copy-done.14
  78.6 5.8 %stats_far.1 = (f32[1,768]{1,0:T(1,128)}, f32[128,768]{1,0:T(8,128)}, s32[1,384]{1,0:T(1,128)}, s32[1]{0:T(128)}) custom-call(s32[1]{0:T(128)} %bitcast.4.refs_0_.own_ref, s32[1,384]{1,0:T(1,128)} %broadcast_in_dim.8.refs_1_, bf16[384,256]{1,0:T(8,128)(2,1)} %refs_1_.7, f32[1,768]{1,0:T(1,128)} %get-tuple-element.44.refs_3_, ...), custom_call_target="tpu_custom_call" | custom-call | tf_op jit(solution)/shard_map/stats_far/pallas_call | solution.py:284
  84.4 12.3 %attention_grads.1 = (bf16[256,384]{1,0:T(8,128)(2,1)}, bf16[5,384,256]{2,1,0:T(8,128)(2,1)}, bf16[5,384,256]{2,1,0:T(8,128)(2,1)}) custom-call(s32[1]{0:T(128)} %bitcast.4.refs_0_.own_ref, s32[1]{0:T(128)} %get-tuple-element.48.low_ref, s32[1,384]{1,0:T(1,128)} %get-tuple-element.49.refs_0_, bf16[384,256]{1,0:T(8,128)(2,1)} %refs_1_.7, ...), custom_call_target="tpu_custom_call" | custom-call | tf_op jit(solution)/shard_map/attention_grads/pallas_call | solution.py:298
  96.8 2.2 %collective-permute-start.21 = (bf16[5,384,256]{2,1,0:T(8,128)(2,1)}, bf16[5,384,256]{2,1,0:T(8,128)(2,1)S(1)}, u32[]{:S(2)}, u32[]{:S(2)}) collective-permute-start(bf16[5,384,256]{2,1,0:T(8,128)(2,1)} %get-tuple-element.55), channel_id=1, source_target_pairs={{0,16},{16,0},{1,17},{17,1},{2,18},{18,2},{3,19},{19,3},{4,20},{20... | collective-permute-start | bytes 2949128 | tf_op jit(solution)/shard_map/ppermute | solution.py:574
  99.0 1.0 dynamic-slice_bitcast_fusion.2
  100.0 0.6 collective-permute-start.28
  100.7 3.1 %collective-permute-start.29 = (bf16[336,512]{1,0:T(8,128)(2,1)S(1)}, bf16[336,512]{1,0:T(8,128)(2,1)}, u32[]{:S(2)}, u32[]{:S(2)}) collective-permute-start(bf16[336,512]{1,0:T(8,128)(2,1)S(1)} %pad_maximum_fusion.1), channel_id=1, source_target_pairs={{0,1},{1,0},{2,3},{3,2},{4,5},{5,4},{6,7},{7,6},{8,9},{9,8},{10,11... | collective-permute-start | bytes 1032200 | tf_op jit(solution)/shard_map/ppermute | solution.py:574
  103.8 8.8 %collective-permute-done.28.refs_5_.refs_2_.refs_6_ = bf16[336,512]{1,0:T(8,128)(2,1)S(1)} collective-permute-done((bf16[336,512]{1,0:T(8,128)(2,1)S(1)}, bf16[336,512]{1,0:T(8,128)(2,1)S(1)}, u32[]{:S(2)}, u32[]{:S(2)}) %collective-permute-start.28) | collective-permute-done | bytes 344096 | tf_op jit(solution)/shard_map/ppermute | solution.py:574
  112.6 6.5 %collective-permute-done.29.refs_6_.refs_3_.refs_7_ = bf16[336,512]{1,0:T(8,128)(2,1)} collective-permute-done((bf16[336,512]{1,0:T(8,128)(2,1)S(1)}, bf16[336,512]{1,0:T(8,128)(2,1)}, u32[]{:S(2)}, u32[]{:S(2)}) %collective-permute-start.29) | collective-permute-done | bytes 344096 | tf_op jit(solution)/shard_map/ppermute | solution.py:574
  119.1 2.0 join_partials.1
  121.1 0.7 collective-permute-start.22
  121.8 1.3 collective-permute-start.23
  123.1 1.9 collective-permute-start.24
  125.0 1.9 collective-permute-start.25
  127.0 2.7 %collective-permute-done.31.refs_8_.refs_5_.refs_9_ = bf16[336,512]{1,0:T(8,128)(2,1)} collective-permute-done((bf16[336,512]{1,0:T(8,128)(2,1)}, bf16[336,512]{1,0:T(8,128)(2,1)}, u32[]{:S(2)}, u32[]{:S(2)}) %collective-permute-start.31) | collective-permute-done | bytes 344096 | tf_op jit(solution)/shard_map/ppermute | solution.py:578
  129.6 4.4 %collective-permute-start.26 = (bf16[384,256]{1,0:T(8,128)(2,1)S(1)}, bf16[384,256]{1,0:T(8,128)(2,1)S(1)}, u32[]{:S(2)}, u32[]{:S(2)}) collective-permute-start(bf16[384,256]{1,0:T(8,128)(2,1)S(1)} %get-tuple-element.61), channel_id=1, source_target_pairs={{32,0},{48,16},{64,32},{80,48},{96,64},{112,80},{128,96},{144,112}... | collective-permute-start | bytes 589832 | tf_op jit(solution)/shard_map/ppermute | solution.py:590
  134.3 1.4 collective-permute-done.24.refs_2_
  135.8 8.3 %collective-permute-done.25.refs_3_ = bf16[384,256]{1,0:T(8,128)(2,1)S(1)} collective-permute-done((bf16[384,256]{1,0:T(8,128)(2,1)S(1)}, bf16[384,256]{1,0:T(8,128)(2,1)S(1)}, u32[]{:S(2)}, u32[]{:S(2)}) %collective-permute-start.25) | collective-permute-done | bytes 196640 | tf_op jit(solution)/shard_map/ppermute | solution.py:590
  144.1 1.8 collective-permute-done.26.refs_4_
  145.9 1.9 collective-permute-start.36
  147.7 1.9 total_partials.1.refs_3_
  149.6 1.8 collective-permute-start.27
  151.4 5.2 %project.5 = (f32[336,384]{1,0:T(8,128)}, f32[336,384]{1,0:T(8,128)}, f32[336,384]{1,0:T(8,128)}, f32[336,384]{1,0:T(8,128)}, f32[336,384]{1,0:T(8,128)}, /*inde...) custom-call(s32[4]{0:T(128)} %pad_add_fusion.at_ref.refs_0_, bf16[5376,256]{1,0:T(8,128)(2,1)} %refs_1_.8, ...), custom_call_target="tpu_custom_call" | custom-call | tf_op jit(solution)/shard_map/project/pallas_call | solution.py:536
  156.6 0.7 copy-done.4
  157.5 3.7 %project.6 = (f32[336,384]{1,0:T(8,128)}, f32[336,384]{1,0:T(8,128)}) custom-call(s32[4]{0:T(128)} %pad_add_fusion.at_ref.refs_0_, bf16[5376,128]{1,0:T(8,128)(2,1)} %refs_1_.11, bf16[5376,128]{1,0:T(8,128)(2,1)} %refs_2_.9, bf16[256,384]{1,0:T(8,128)(2,1)} %total_partials.1.refs_3_, bf16[256,384]{1,0:T(8,128)(2,1)S(1)} %collective-permute-done.36.refs_4_, ...), custom_call_target="tpu_custom_call" | custom-call | tf_op jit(solution)/shard_map/project/pallas_call | solution.py:536
  161.2 3.3 %project.7 = (bf16[336,384]{1,0:T(8,128)(2,1)S(1)}, bf16[336,384]{1,0:T(8,128)(2,1)S(1)}) custom-call(s32[4]{0:T(128)} %pad_add_fusion.at_ref.refs_0_, bf16[256,384]{1,0:T(8,128)(2,1)S(1)} %collective-permute-done.27.refs_1_.refs_5_, bf16[336,512]{1,0:T(8,128)(2,1)} %copy-done.2, bf16[336,512]{1,0:T(8,128)(2,1)} %collective-permute-done.29.refs_6_.refs_3_.refs_7_, ...), custom_call_target="tpu_custom_call" | custom-call | tf_op jit(solution)/shard_map/project/pallas_call | solution.py:536
  164.5 0.8 collective-permute-start.39
  165.3 1.3 collective-permute-start.37
  166.6 5.3 %project.8 = (f32[336,384]{1,0:T(8,128)}, f32[336,384]{1,0:T(8,128)}, f32[336,384]{1,0:T(8,128)}, f32[336,384]{1,0:T(8,128)}) custom-call(s32[4]{0:T(128)} %pad_add_fusion.at_ref.refs_0_, bf16[5376,128]{1,0:T(8,128)(2,1)} %refs_1_.11, bf16[5376,128]{1,0:T(8,128)(2,1)} %refs_2_.9, bf16[256,384]{1,0:T(8,128)(2,1)} %total_partials.1.refs_3_, ...), custom_call_target="tpu_custom_call" | custom-call | tf_op jit(solution)/shard_map/project/pallas_call | solution.py:536
  171.9 1.2 add_convert_fusion.2
  173.1 2.0 %collective-permute-start.40 = (bf16[336,384]{1,0:T(8,128)(2,1)S(1)}, bf16[336,384]{1,0:T(8,128)(2,1)S(1)}, u32[]{:S(2)}, u32[]{:S(2)}) collective-permute-start(bf16[336,384]{1,0:T(8,128)(2,1)S(1)} %add_convert_fusion.2), channel_id=1, source_target_pairs={{0,14},{2,0},{4,2},{6,4},{8,6},{10,8},{12,10},{14,12},{1,15},{3,1}... | collective-permute-start | bytes 774152 | tf_op jit(solution)/shard_map/ppermute | solution.py:594
  175.1 1.1 add_convert_fusion.3
  176.4 3.1 %collective-permute-done.40.behind_ref = bf16[336,384]{1,0:T(8,128)(2,1)S(1)} collective-permute-done((bf16[336,384]{1,0:T(8,128)(2,1)S(1)}, bf16[336,384]{1,0:T(8,128)(2,1)S(1)}, u32[]{:S(2)}, u32[]{:S(2)}) %collective-permute-start.40) | collective-permute-done | bytes 258080 | tf_op jit(solution)/shard_map/ppermute | solution.py:594
  179.5 4.3 %collective-permute-done.38.ahead_ref = bf16[336,384]{1,0:T(8,128)(2,1)S(1)} collective-permute-done((bf16[336,384]{1,0:T(8,128)(2,1)S(1)}, bf16[336,384]{1,0:T(8,128)(2,1)S(1)}, u32[]{:S(2)}, u32[]{:S(2)}) %collective-permute-start.38) | collective-permute-done | bytes 258080 | tf_op jit(solution)/shard_map/ppermute | solution.py:594
  184.1 4.2 %project.9 = (f32[336,384]{1,0:T(8,128)}, f32[336,384]{1,0:T(8,128)}) custom-call(s32[4]{0:T(128)} %pad_add_fusion.at_ref.refs_0_, bf16[5376,128]{1,0:T(8,128)(2,1)} %refs_1_.11, bf16[5376,128]{1,0:T(8,128)(2,1)} %refs_2_.9, bf16[256,384]{1,0:T(8,128)(2,1)} %total_partials.1.refs_3_, bf16[256,384]{1,0:T(8,128)(2,1)S(1)} %collective-permute-done.36.refs_4_, ...), custom_call_target="tpu_custom_call" | custom-call | tf_op jit(solution)/shard_map/project/pallas_call | solution.py:536
  188.3 3.3 %collective-permute-start.43 = (bf16[336,384]{1,0:T(8,128)(2,1)S(1)}, bf16[336,384]{1,0:T(8,128)(2,1)S(1)}, u32[]{:S(2)}, u32[]{:S(2)}) collective-permute-start(bf16[336,384]{1,0:T(8,128)(2,1)S(1)} %get-tuple-element.81), channel_id=1, source_target_pairs={{0,14},{2,0},{4,2},{6,4},{8,6},{10,8},{12,10},{14,12},{1,15},{3,1}... | collective-permute-start | bytes 774152 | tf_op jit(solution)/shard_map/ppermute | solution.py:594
  191.6 1.1 add_convert_fusion.1
  192.8 2.6 %collective-permute-done.43 = bf16[336,384]{1,0:T(8,128)(2,1)S(1)} collective-permute-done((bf16[336,384]{1,0:T(8,128)(2,1)S(1)}, bf16[336,384]{1,0:T(8,128)(2,1)S(1)}, u32[]{:S(2)}, u32[]{:S(2)}) %collective-permute-start.43) | collective-permute-done | bytes 258080 | tf_op jit(solution)/shard_map/ppermute | solution.py:594
  195.5 4.9 %collective-permute-done.42 = bf16[336,384]{1,0:T(8,128)(2,1)S(1)} collective-permute-done((bf16[336,384]{1,0:T(8,128)(2,1)S(1)}, bf16[336,384]{1,0:T(8,128)(2,1)S(1)}, u32[]{:S(2)}, u32[]{:S(2)}) %collective-permute-start.42) | collective-permute-done | bytes 258080 | tf_op jit(solution)/shard_map/ppermute | solution.py:594
  200.3 0.8 fusion.1
  (111 shorter events, 2.8 us)
Async XLA Ops:
  0.6 8.5 %copy-start.30 = (s32[384]{0:T(512)S(1)}, s32[384]{0:T(512)}, u32[]{:S(2)}) copy-start(s32[384]{0:T(512)} %param.13) | copy-start | bytes 4612
  0.6 8.5 %copy-start.28 = (bf16[384,128]{1,0:T(8,128)(2,1)S(1)}, bf16[384,128]{1,0:T(8,128)(2,1)}, u32[]{:S(2)}) copy-start(bf16[384,128]{1,0:T(8,128)(2,1)} %param.11) | copy-start | bytes 294916
  0.6 8.5 %copy-start.29 = (bf16[384,128]{1,0:T(8,128)(2,1)S(1)}, bf16[384,128]{1,0:T(8,128)(2,1)}, u32[]{:S(2)}) copy-start(bf16[384,128]{1,0:T(8,128)(2,1)} %param.10) | copy-start | bytes 294916
  4.1 22.2 %collective-permute-start.11 = (bf16[4,256,384]{2,1,0:T(8,128)(2,1)}, bf16[4,256,384]{2,1,0:T(8,128)(2,1)S(1)}, u32[]{:S(2)}, u32[]{:S(2)}) collective-permute-start(bf16[4,256,384]{2,1,0:T(8,128)(2,1)} %split_w_out.1), channel_id=1, source_target_pairs={{0,1},{1,0},{2,3},{3,2},{4,5},{5,4},{6,7},{7,6},{8,9},{9,8},{10,11... | collective-permute-start | bytes 2359304 | tf_op jit(solution)/shard_map/ppermute | solution.py:574
  7.2 25.0 %collective-permute-start.13 = (bf16[336,384]{1,0:T(8,128)(2,1)S(1)}, bf16[336,384]{1,0:T(8,128)(2,1)S(1)}, u32[]{:S(2)}, u32[]{:S(2)}) collective-permute-start(bf16[336,384]{1,0:T(8,128)(2,1)S(1)} %bitcast.29), channel_id=1, source_target_pairs={{0,2},{2,4},{4,6},{6,8},{8,10},{10,12},{12,14},{14,0},{1,3},{3,5},... | collective-permute-start | bytes 774152 | tf_op jit(solution)/shard_map/ppermute | solution.py:594
  9.2 56.5 %copy-start.7 = (bf16[400,256]{1,0:T(8,128)(2,1)}, bf16[400,256]{1,0:T(8,128)(2,1)S(1)}, u32[]{:S(2)}) copy-start(bf16[400,256]{1,0:T(8,128)(2,1)S(1)} %fusion.2.refs_3_.refs_6_) | copy-start | bytes 614404
  9.2 24.9 %collective-permute-start.3 = (bf16[400,256]{1,0:T(8,128)(2,1)S(1)}, bf16[400,256]{1,0:T(8,128)(2,1)S(1)}, u32[]{:S(2)}, u32[]{:S(2)}) collective-permute-start(bf16[400,256]{1,0:T(8,128)(2,1)S(1)} %fusion.2.refs_3_.refs_6_), channel_id=1, source_target_pairs={{0,64},{16,80},{32,96},{48,112},{64,128},{80,144},{96,160},{112,17... | collective-permute-start | bytes 614408 | tf_op jit(solution)/shard_map/ppermute | solution.py:586
  26.3 32.6 %copy-start.17 = (bf16[4,256,384]{2,1,0:T(8,128)(2,1)}, bf16[4,256,384]{2,1,0:T(8,128)(2,1)S(1)}, u32[]{:S(2)}) copy-start(bf16[4,256,384]{2,1,0:T(8,128)(2,1)S(1)} %collective-permute-done.11.refs_2_) | copy-start | bytes 2359300
  26.4 32.6 %collective-permute-start.12 = (bf16[4,256,384]{2,1,0:T(8,128)(2,1)S(1)}, bf16[4,256,384]{2,1,0:T(8,128)(2,1)S(1)}, u32[]{:S(2)}, u32[]{:S(2)}) collective-permute-start(bf16[4,256,384]{2,1,0:T(8,128)(2,1)S(1)} %collective-permute-done.11.refs_2_), channel_id=1, source_target_pairs={{0,16},{16,0},{1,17},{17,1},{2,18},{18,2},{3,19},{19,3},{4,20},{20... | collective-permute-start | bytes 2359304 | tf_op jit(solution)/shard_map/ppermute | solution.py:574
  26.4 12.0 %collective-permute-start.14 = (bf16[336,384]{1,0:T(8,128)(2,1)S(1)}, bf16[336,384]{1,0:T(8,128)(2,1)S(1)}, u32[]{:S(2)}, u32[]{:S(2)}) collective-permute-start(bf16[336,384]{1,0:T(8,128)(2,1)S(1)} %bitcast.30), channel_id=1, source_target_pairs={{0,14},{2,0},{4,2},{6,4},{8,6},{10,8},{12,10},{14,12},{1,15},{3,1}... | collective-permute-start | bytes 774152 | tf_op jit(solution)/shard_map/ppermute | solution.py:594
  32.2 12.3 %copy-start.20 = (bf16[336,384]{1,0:T(8,128)(2,1)}, bf16[336,384]{1,0:T(8,128)(2,1)S(1)}, u32[]{:S(2)}) copy-start(bf16[336,384]{1,0:T(8,128)(2,1)S(1)} %collective-permute-done.13.refs_5_) | copy-start | bytes 774148
  32.2 9.8 %collective-permute-start.15 = (bf16[336,384]{1,0:T(8,128)(2,1)S(1)}, bf16[336,384]{1,0:T(8,128)(2,1)S(1)}, u32[]{:S(2)}, u32[]{:S(2)}) collective-permute-start(bf16[336,384]{1,0:T(8,128)(2,1)S(1)} %collective-permute-done.13.refs_5_), channel_id=1, source_target_pairs={{0,2},{2,4},{4,6},{6,8},{8,10},{10,12},{12,14},{14,0},{1,3},{3,5},... | collective-permute-start | bytes 774152 | tf_op jit(solution)/shard_map/ppermute | solution.py:594
  32.2 9.8 %collective-permute-start = (bf16[400,256]{1,0:T(8,128)(2,1)S(1)}, bf16[400,256]{1,0:T(8,128)(2,1)S(1)}, u32[]{:S(2)}, u32[]{:S(2)}) collective-permute-start(bf16[400,256]{1,0:T(8,128)(2,1)S(1)} %fusion.2.refs_3_.refs_6_), channel_id=1, source_target_pairs={{0,32},{16,48},{32,64},{48,80},{64,96},{80,112},{96,128},{112,144}... | collective-permute-start | bytes 614408 | tf_op jit(solution)/shard_map/ppermute | solution.py:586
  34.2 31.6 %copy-start.8 = (bf16[400,256]{1,0:T(8,128)(2,1)}, bf16[400,256]{1,0:T(8,128)(2,1)S(1)}, u32[]{:S(2)}) copy-start(bf16[400,256]{1,0:T(8,128)(2,1)S(1)} %collective-permute-done.3.refs_7_.refs_8_) | copy-start | bytes 614404
  34.2 10.4 %collective-permute-start.1 = (bf16[400,256]{1,0:T(8,128)(2,1)S(1)}, bf16[400,256]{1,0:T(8,128)(2,1)S(1)}, u32[]{:S(2)}, u32[]{:S(2)}) collective-permute-start(bf16[400,256]{1,0:T(8,128)(2,1)S(1)} %fusion.2.refs_3_.refs_6_), channel_id=1, source_target_pairs={{0,16},{16,0},{1,17},{17,1},{2,18},{18,2},{3,19},{19,3},{4,20},{20... | collective-permute-start | bytes 614408 | tf_op jit(solution)/shard_map/ppermute | solution.py:574
  38.4 15.1 %copy-start.21 = (bf16[336,384]{1,0:T(8,128)(2,1)}, bf16[336,384]{1,0:T(8,128)(2,1)S(1)}, u32[]{:S(2)}) copy-start(bf16[336,384]{1,0:T(8,128)(2,1)S(1)} %collective-permute-done.14.refs_6_) | copy-start | bytes 774148
  38.4 9.0 %collective-permute-start.16 = (bf16[336,384]{1,0:T(8,128)(2,1)S(1)}, bf16[336,384]{1,0:T(8,128)(2,1)S(1)}, u32[]{:S(2)}, u32[]{:S(2)}) collective-permute-start(bf16[336,384]{1,0:T(8,128)(2,1)S(1)} %collective-permute-done.14.refs_6_), channel_id=1, source_target_pairs={{0,14},{2,0},{4,2},{6,4},{8,6},{10,8},{12,10},{14,12},{1,15},{3,1}... | collective-permute-start | bytes 774152 | tf_op jit(solution)/shard_map/ppermute | solution.py:594
  42.1 10.8 %copy-start.22 = (bf16[336,384]{1,0:T(8,128)(2,1)}, bf16[336,384]{1,0:T(8,128)(2,1)S(1)}, u32[]{:S(2)}) copy-start(bf16[336,384]{1,0:T(8,128)(2,1)S(1)} %collective-permute-done.15.refs_7_) | copy-start | bytes 774148
  42.1 9.0 %collective-permute-start.17 = (bf16[336,384]{1,0:T(8,128)(2,1)S(1)}, bf16[336,384]{1,0:T(8,128)(2,1)S(1)}, u32[]{:S(2)}, u32[]{:S(2)}) collective-permute-start(bf16[336,384]{1,0:T(8,128)(2,1)S(1)} %collective-permute-done.15.refs_7_), channel_id=1, source_target_pairs={{0,2},{2,4},{4,6},{6,8},{8,10},{10,12},{12,14},{14,0},{1,3},{3,5},... | collective-permute-start | bytes 774152 | tf_op jit(solution)/shard_map/ppermute | solution.py:594
  42.1 23.7 %copy-start.9 = (bf16[400,256]{1,0:T(8,128)(2,1)}, bf16[400,256]{1,0:T(8,128)(2,1)S(1)}, u32[]{:S(2)}) copy-start(bf16[400,256]{1,0:T(8,128)(2,1)S(1)} %collective-permute-done.refs_4_.refs_7_) | copy-start | bytes 614404
  42.1 9.5 %collective-permute-start.5 = (bf16[400,256]{1,0:T(8,128)(2,1)S(1)}, bf16[400,256]{1,0:T(8,128)(2,1)S(1)}, u32[]{:S(2)}, u32[]{:S(2)}) collective-permute-start(bf16[400,256]{1,0:T(8,128)(2,1)S(1)} %fusion.2.refs_3_.refs_6_), channel_id=1, source_target_pairs={{0,96},{16,112},{32,128},{48,144},{64,160},{80,176},{96,192},{112,... | collective-permute-start | bytes 614408 | tf_op jit(solution)/shard_map/ppermute | solution.py:586
  44.6 21.2 %copy-start.10 = (bf16[400,256]{1,0:T(8,128)(2,1)}, bf16[400,256]{1,0:T(8,128)(2,1)S(1)}, u32[]{:S(2)}) copy-start(bf16[400,256]{1,0:T(8,128)(2,1)S(1)} %collective-permute-done.1.refs_5_.refs_11_) | copy-start | bytes 614404
  44.6 8.3 %collective-permute-start.6 = (bf16[400,256]{1,0:T(8,128)(2,1)S(1)}, bf16[400,256]{1,0:T(8,128)(2,1)S(1)}, u32[]{:S(2)}, u32[]{:S(2)}) collective-permute-start(bf16[400,256]{1,0:T(8,128)(2,1)S(1)} %fusion.2.refs_3_.refs_6_), channel_id=1, source_target_pairs={{0,128},{16,144},{32,160},{48,176},{64,192},{80,208},{96,224},{112... | collective-permute-start | bytes 614408 | tf_op jit(solution)/shard_map/ppermute | solution.py:586
  47.3 11.6 %copy-start.23 = (bf16[336,384]{1,0:T(8,128)(2,1)}, bf16[336,384]{1,0:T(8,128)(2,1)S(1)}, u32[]{:S(2)}) copy-start(bf16[336,384]{1,0:T(8,128)(2,1)S(1)} %collective-permute-done.16.refs_8_) | copy-start | bytes 774148
  47.3 8.1 %collective-permute-start.18 = (bf16[336,384]{1,0:T(8,128)(2,1)S(1)}, bf16[336,384]{1,0:T(8,128)(2,1)S(1)}, u32[]{:S(2)}, u32[]{:S(2)}) collective-permute-start(bf16[336,384]{1,0:T(8,128)(2,1)S(1)} %collective-permute-done.16.refs_8_), channel_id=1, source_target_pairs={{0,14},{2,0},{4,2},{6,4},{8,6},{10,8},{12,10},{14,12},{1,15},{3,1}... | collective-permute-start | bytes 774152 | tf_op jit(solution)/shard_map/ppermute | solution.py:594
  51.0 7.9 %copy-start.24 = (bf16[336,384]{1,0:T(8,128)(2,1)}, bf16[336,384]{1,0:T(8,128)(2,1)S(1)}, u32[]{:S(2)}) copy-start(bf16[336,384]{1,0:T(8,128)(2,1)S(1)} %collective-permute-done.17.refs_9_) | copy-start | bytes 774148
  51.0 7.8 %collective-permute-start.19 = (bf16[336,384]{1,0:T(8,128)(2,1)S(1)}, bf16[336,384]{1,0:T(8,128)(2,1)S(1)}, u32[]{:S(2)}, u32[]{:S(2)}) collective-permute-start(bf16[336,384]{1,0:T(8,128)(2,1)S(1)} %collective-permute-done.17.refs_9_), channel_id=1, source_target_pairs={{0,2},{2,4},{4,6},{6,8},{8,10},{10,12},{12,14},{14,0},{1,3},{3,5},... | collective-permute-start | bytes 774152 | tf_op jit(solution)/shard_map/ppermute | solution.py:594
  51.5 14.3 %copy-start.11 = (bf16[400,256]{1,0:T(8,128)(2,1)}, bf16[400,256]{1,0:T(8,128)(2,1)S(1)}, u32[]{:S(2)}) copy-start(bf16[400,256]{1,0:T(8,128)(2,1)S(1)} %collective-permute-done.5.refs_8_.refs_9_) | copy-start | bytes 614404
  51.5 1.4 collective-permute-start.9
  52.9 12.9 %copy-start.12 = (bf16[400,256]{1,0:T(8,128)(2,1)}, bf16[400,256]{1,0:T(8,128)(2,1)S(1)}, u32[]{:S(2)}) copy-start(bf16[400,256]{1,0:T(8,128)(2,1)S(1)} %collective-permute-done.6.refs_9_.refs_10_) | copy-start | bytes 614404
  52.9 12.9 %collective-permute-start.4 = (bf16[400,256]{1,0:T(8,128)(2,1)S(1)}, bf16[400,256]{1,0:T(8,128)(2,1)S(1)}, u32[]{:S(2)}, u32[]{:S(2)}) collective-permute-start(bf16[400,256]{1,0:T(8,128)(2,1)S(1)} %collective-permute-done.3.refs_7_.refs_8_), channel_id=1, source_target_pairs={{0,16},{16,0},{1,17},{17,1},{2,18},{18,2},{3,19},{19,3},{4,20},{20... | collective-permute-start | bytes 614408 | tf_op jit(solution)/shard_map/ppermute | solution.py:574
  52.9 17.8 %collective-permute-start.2 = (bf16[400,256]{1,0:T(8,128)(2,1)S(1)}, bf16[400,256]{1,0:T(8,128)(2,1)S(1)}, u32[]{:S(2)}, u32[]{:S(2)}) collective-permute-start(bf16[400,256]{1,0:T(8,128)(2,1)S(1)} %collective-permute-done.refs_4_.refs_7_), channel_id=1, source_target_pairs={{0,16},{16,0},{1,17},{17,1},{2,18},{18,2},{3,19},{19,3},{4,20},{20... | collective-permute-start | bytes 614408 | tf_op jit(solution)/shard_map/ppermute | solution.py:574
  55.5 22.3 %collective-permute-start.7 = (bf16[400,256]{1,0:T(8,128)(2,1)S(1)}, bf16[400,256]{1,0:T(8,128)(2,1)S(1)}, u32[]{:S(2)}, u32[]{:S(2)}) collective-permute-start(bf16[400,256]{1,0:T(8,128)(2,1)S(1)} %collective-permute-done.5.refs_8_.refs_9_), channel_id=1, source_target_pairs={{0,16},{16,0},{1,17},{17,1},{2,18},{18,2},{3,19},{19,3},{4,20},{20... | collective-permute-start | bytes 614408 | tf_op jit(solution)/shard_map/ppermute | solution.py:574
  58.9 18.9 %collective-permute-start.8 = (bf16[400,256]{1,0:T(8,128)(2,1)S(1)}, bf16[400,256]{1,0:T(8,128)(2,1)S(1)}, u32[]{:S(2)}, u32[]{:S(2)}) collective-permute-start(bf16[400,256]{1,0:T(8,128)(2,1)S(1)} %collective-permute-done.6.refs_9_.refs_10_), channel_id=1, source_target_pairs={{0,16},{16,0},{1,17},{17,1},{2,18},{18,2},{3,19},{19,3},{4,20},{20... | collective-permute-start | bytes 614408 | tf_op jit(solution)/shard_map/ppermute | solution.py:574
  59.6 18.2 %collective-permute-start.10 = (bf16[400,256]{1,0:T(8,128)(2,1)}, bf16[400,256]{1,0:T(8,128)(2,1)S(1)}, u32[]{:S(2)}, u32[]{:S(2)}) collective-permute-start(bf16[400,256]{1,0:T(8,128)(2,1)} %collective-permute-done.9), channel_id=1, source_target_pairs={{0,16},{16,0},{1,17},{17,1},{2,18},{18,2},{3,19},{19,3},{4,20},{20... | collective-permute-start | bytes 614408 | tf_op jit(solution)/shard_map/ppermute | solution.py:574
  65.8 18.6 %collective-permute-start.20 = (bf16[256,384]{1,0:T(8,128)(2,1)S(1)}, bf16[256,384]{1,0:T(8,128)(2,1)S(1)}, u32[]{:S(2)}, u32[]{:S(2)}) collective-permute-start(bf16[256,384]{1,0:T(8,128)(2,1)S(1)} %get-tuple-element.51), channel_id=1, source_target_pairs={{0,1},{1,0},{2,3},{3,2},{4,5},{5,4},{6,7},{7,6},{8,9},{9,8},{10,11... | collective-permute-start | bytes 589832 | tf_op jit(solution)/shard_map/ppermute | solution.py:574
  96.8 22.4 %collective-permute-start.21 = (bf16[5,384,256]{2,1,0:T(8,128)(2,1)}, bf16[5,384,256]{2,1,0:T(8,128)(2,1)S(1)}, u32[]{:S(2)}, u32[]{:S(2)}) collective-permute-start(bf16[5,384,256]{2,1,0:T(8,128)(2,1)} %get-tuple-element.55), channel_id=1, source_target_pairs={{0,16},{16,0},{1,17},{17,1},{2,18},{18,2},{3,19},{19,3},{4,20},{20... | collective-permute-start | bytes 2949128 | tf_op jit(solution)/shard_map/ppermute | solution.py:574
  100.0 45.9 %copy-start.27 = (bf16[256,384]{1,0:T(8,128)(2,1)S(1)}, bf16[256,384]{1,0:T(8,128)(2,1)}, u32[]{:S(2)}) copy-start(bf16[256,384]{1,0:T(8,128)(2,1)} %get-tuple-element.62.refs_2_) | copy-start | bytes 589828
  100.0 12.5 %collective-permute-start.28 = (bf16[336,512]{1,0:T(8,128)(2,1)S(1)}, bf16[336,512]{1,0:T(8,128)(2,1)S(1)}, u32[]{:S(2)}, u32[]{:S(2)}) collective-permute-start(bf16[336,512]{1,0:T(8,128)(2,1)S(1)} %pad_maximum_fusion), channel_id=1, source_target_pairs={{0,1},{1,0},{2,3},{3,2},{4,5},{5,4},{6,7},{7,6},{8,9},{9,8},{10,11... | collective-permute-start | bytes 1032200 | tf_op jit(solution)/shard_map/ppermute | solution.py:574
  100.7 18.4 %collective-permute-start.29 = (bf16[336,512]{1,0:T(8,128)(2,1)S(1)}, bf16[336,512]{1,0:T(8,128)(2,1)}, u32[]{:S(2)}, u32[]{:S(2)}) collective-permute-start(bf16[336,512]{1,0:T(8,128)(2,1)S(1)} %pad_maximum_fusion.1), channel_id=1, source_target_pairs={{0,1},{1,0},{2,3},{3,2},{4,5},{5,4},{6,7},{7,6},{8,9},{9,8},{10,11... | collective-permute-start | bytes 1032200 | tf_op jit(solution)/shard_map/ppermute | solution.py:574
  112.6 37.0 %copy-start.2 = (bf16[336,512]{1,0:T(8,128)(2,1)}, bf16[336,512]{1,0:T(8,128)(2,1)S(1)}, u32[]{:S(2)}) copy-start(bf16[336,512]{1,0:T(8,128)(2,1)S(1)} %collective-permute-done.28.refs_5_.refs_2_.refs_6_) | copy-start | bytes 1032196
  112.6 12.4 %collective-permute-start.30 = (bf16[336,512]{1,0:T(8,128)(2,1)S(1)}, bf16[336,512]{1,0:T(8,128)(2,1)}, u32[]{:S(2)}, u32[]{:S(2)}) collective-permute-start(bf16[336,512]{1,0:T(8,128)(2,1)S(1)} %collective-permute-done.28.refs_5_.refs_2_.refs_6_), channel_id=1, source_target_pairs={{0,32},{32,0},{64,96},{96,64},{1,33},{33,1},{65,97},{97,65},{2,34}... | collective-permute-start | bytes 1032200 | tf_op jit(solution)/shard_map/ppermute | solution.py:578
  119.1 10.5 %collective-permute-start.31 = (bf16[336,512]{1,0:T(8,128)(2,1)}, bf16[336,512]{1,0:T(8,128)(2,1)}, u32[]{:S(2)}, u32[]{:S(2)}) collective-permute-start(bf16[336,512]{1,0:T(8,128)(2,1)} %collective-permute-done.29.refs_6_.refs_3_.refs_7_), channel_id=1, source_target_pairs={{0,32},{32,0},{64,96},{96,64},{1,33},{33,1},{65,97},{97,65},{2,34}... | collective-permute-start | bytes 1032200 | tf_op jit(solution)/shard_map/ppermute | solution.py:578
  121.1 8.5 %collective-permute-start.22 = (bf16[384,256]{1,0:T(8,128)(2,1)S(1)}, bf16[384,256]{1,0:T(8,128)(2,1)S(1)}, u32[]{:S(2)}, u32[]{:S(2)}) collective-permute-start(bf16[384,256]{1,0:T(8,128)(2,1)S(1)} %get-tuple-element.57), channel_id=1, source_target_pairs={{176,16},{208,48},{240,80},{177,17},{209,49},{241,81},{178,18},{21... | collective-permute-start | bytes 589832 | tf_op jit(solution)/shard_map/ppermute | solution.py:590
  121.8 12.2 %collective-permute-start.23 = (bf16[384,256]{1,0:T(8,128)(2,1)S(1)}, bf16[384,256]{1,0:T(8,128)(2,1)S(1)}, u32[]{:S(2)}, u32[]{:S(2)}) collective-permute-start(bf16[384,256]{1,0:T(8,128)(2,1)S(1)} %get-tuple-element.58), channel_id=1, source_target_pairs={{128,0},{144,16},{160,32},{176,48},{192,64},{208,80},{224,96},{240... | collective-permute-start | bytes 589832 | tf_op jit(solution)/shard_map/ppermute | solution.py:590
  123.1 12.7 %collective-permute-start.24 = (bf16[384,256]{1,0:T(8,128)(2,1)S(1)}, bf16[384,256]{1,0:T(8,128)(2,1)S(1)}, u32[]{:S(2)}, u32[]{:S(2)}) collective-permute-start(bf16[384,256]{1,0:T(8,128)(2,1)S(1)} %get-tuple-element.59), channel_id=1, source_target_pairs={{96,0},{112,16},{128,32},{144,48},{160,64},{176,80},{192,96},{208,... | collective-permute-start | bytes 589832 | tf_op jit(solution)/shard_map/ppermute | solution.py:590
  125.0 19.1 %collective-permute-start.25 = (bf16[384,256]{1,0:T(8,128)(2,1)S(1)}, bf16[384,256]{1,0:T(8,128)(2,1)S(1)}, u32[]{:S(2)}, u32[]{:S(2)}) collective-permute-start(bf16[384,256]{1,0:T(8,128)(2,1)S(1)} %get-tuple-element.60), channel_id=1, source_target_pairs={{64,0},{80,16},{96,32},{112,48},{128,64},{144,80},{160,96},{176,11... | collective-permute-start | bytes 589832 | tf_op jit(solution)/shard_map/ppermute | solution.py:590
  129.6 20.0 %collective-permute-start.32 = (bf16[336,512]{1,0:T(8,128)(2,1)S(1)}, bf16[336,512]{1,0:T(8,128)(2,1)S(1)}, u32[]{:S(2)}, u32[]{:S(2)}) collective-permute-start(bf16[336,512]{1,0:T(8,128)(2,1)S(1)} %collective-permute-done.28.refs_5_.refs_2_.refs_6_), channel_id=1, source_target_pairs={{0,16},{16,0},{1,17},{17,1},{2,18},{18,2},{3,19},{19,3},{4,20},{20... | collective-permute-start | bytes 1032200 | tf_op jit(solution)/shard_map/ppermute | solution.py:574
  129.6 16.3 %collective-permute-start.26 = (bf16[384,256]{1,0:T(8,128)(2,1)S(1)}, bf16[384,256]{1,0:T(8,128)(2,1)S(1)}, u32[]{:S(2)}, u32[]{:S(2)}) collective-permute-start(bf16[384,256]{1,0:T(8,128)(2,1)S(1)} %get-tuple-element.61), channel_id=1, source_target_pairs={{32,0},{48,16},{64,32},{80,48},{96,64},{112,80},{128,96},{144,112}... | collective-permute-start | bytes 589832 | tf_op jit(solution)/shard_map/ppermute | solution.py:590
  134.0 22.5 %collective-permute-start.33 = (bf16[336,512]{1,0:T(8,128)(2,1)}, bf16[336,512]{1,0:T(8,128)(2,1)S(1)}, u32[]{:S(2)}, u32[]{:S(2)}) collective-permute-start(bf16[336,512]{1,0:T(8,128)(2,1)} %collective-permute-done.29.refs_6_.refs_3_.refs_7_), channel_id=1, source_target_pairs={{0,16},{16,0},{1,17},{17,1},{2,18},{18,2},{3,19},{19,3},{4,20},{20... | collective-permute-start | bytes 1032200 | tf_op jit(solution)/shard_map/ppermute | solution.py:574
  135.8 20.8 %collective-permute-start.34 = (bf16[336,512]{1,0:T(8,128)(2,1)}, bf16[336,512]{1,0:T(8,128)(2,1)}, u32[]{:S(2)}, u32[]{:S(2)}) collective-permute-start(bf16[336,512]{1,0:T(8,128)(2,1)} %collective-permute-done.30.refs_7_.refs_4_.refs_8_), channel_id=1, source_target_pairs={{0,16},{16,0},{1,17},{17,1},{2,18},{18,2},{3,19},{19,3},{4,20},{20... | collective-permute-start | bytes 1032200 | tf_op jit(solution)/shard_map/ppermute | solution.py:574
  144.1 12.5 %collective-permute-start.35 = (bf16[336,512]{1,0:T(8,128)(2,1)}, bf16[336,512]{1,0:T(8,128)(2,1)S(1)}, u32[]{:S(2)}, u32[]{:S(2)}) collective-permute-start(bf16[336,512]{1,0:T(8,128)(2,1)} %collective-permute-done.31.refs_8_.refs_5_.refs_9_), channel_id=1, source_target_pairs={{0,16},{16,0},{1,17},{17,1},{2,18},{18,2},{3,19},{19,3},{4,20},{20... | collective-permute-start | bytes 1032200 | tf_op jit(solution)/shard_map/ppermute | solution.py:574
  145.9 10.7 %collective-permute-start.36 = (bf16[256,384]{1,0:T(8,128)(2,1)S(1)}, bf16[256,384]{1,0:T(8,128)(2,1)S(1)}, u32[]{:S(2)}, u32[]{:S(2)}) collective-permute-start(bf16[256,384]{1,0:T(8,128)(2,1)S(1)} %copy-done.27), channel_id=1, source_target_pairs={{0,1},{1,0},{2,3},{3,2},{4,5},{5,4},{6,7},{7,6},{8,9},{9,8},{10,11... | collective-permute-start | bytes 589832 | tf_op jit(solution)/shard_map/ppermute | solution.py:574
  149.6 11.6 %collective-permute-start.27 = (bf16[256,384]{1,0:T(8,128)(2,1)}, bf16[256,384]{1,0:T(8,128)(2,1)S(1)}, u32[]{:S(2)}, u32[]{:S(2)}) collective-permute-start(bf16[256,384]{1,0:T(8,128)(2,1)} %total_partials.1.refs_3_), channel_id=1, source_target_pairs={{0,1},{1,0},{2,3},{3,2},{4,5},{5,4},{6,7},{7,6},{8,9},{9,8},{10,11... | collective-permute-start | bytes 589832 | tf_op jit(solution)/shard_map/ppermute | solution.py:574
  164.5 7.4 %collective-permute-start.39 = (bf16[336,384]{1,0:T(8,128)(2,1)S(1)}, bf16[336,384]{1,0:T(8,128)(2,1)S(1)}, u32[]{:S(2)}, u32[]{:S(2)}) collective-permute-start(bf16[336,384]{1,0:T(8,128)(2,1)S(1)} %get-tuple-element.74), channel_id=1, source_target_pairs={{0,14},{2,0},{4,2},{6,4},{8,6},{10,8},{12,10},{14,12},{1,15},{3,1}... | collective-permute-start | bytes 774152 | tf_op jit(solution)/shard_map/ppermute | solution.py:594
  165.3 9.8 %collective-permute-start.37 = (bf16[336,384]{1,0:T(8,128)(2,1)S(1)}, bf16[336,384]{1,0:T(8,128)(2,1)S(1)}, u32[]{:S(2)}, u32[]{:S(2)}) collective-permute-start(bf16[336,384]{1,0:T(8,128)(2,1)S(1)} %get-tuple-element.67), channel_id=1, source_target_pairs={{0,2},{2,4},{4,6},{6,8},{8,10},{10,12},{12,14},{14,0},{1,3},{3,5},... | collective-permute-start | bytes 774152 | tf_op jit(solution)/shard_map/ppermute | solution.py:594
  171.9 12.0 %copy-start = (f32[336,384]{1,0:T(8,128)S(1)}, f32[336,384]{1,0:T(8,128)}, u32[]{:S(2)}) copy-start(f32[336,384]{1,0:T(8,128)} %get-tuple-element.73.up_ref) | copy-start | bytes 1548292
  171.9 12.0 %copy-start.1 = (f32[336,384]{1,0:T(8,128)S(1)}, f32[336,384]{1,0:T(8,128)}, u32[]{:S(2)}) copy-start(f32[336,384]{1,0:T(8,128)} %get-tuple-element.76.down_ref) | copy-start | bytes 1548292
  173.1 6.4 %collective-permute-start.40 = (bf16[336,384]{1,0:T(8,128)(2,1)S(1)}, bf16[336,384]{1,0:T(8,128)(2,1)S(1)}, u32[]{:S(2)}, u32[]{:S(2)}) collective-permute-start(bf16[336,384]{1,0:T(8,128)(2,1)S(1)} %add_convert_fusion.2), channel_id=1, source_target_pairs={{0,14},{2,0},{4,2},{6,4},{8,6},{10,8},{12,10},{14,12},{1,15},{3,1}... | collective-permute-start | bytes 774152 | tf_op jit(solution)/shard_map/ppermute | solution.py:594
  176.3 7.6 %collective-permute-start.38 = (bf16[336,384]{1,0:T(8,128)(2,1)S(1)}, bf16[336,384]{1,0:T(8,128)(2,1)S(1)}, u32[]{:S(2)}, u32[]{:S(2)}) collective-permute-start(bf16[336,384]{1,0:T(8,128)(2,1)S(1)} %add_convert_fusion.3), channel_id=1, source_target_pairs={{0,2},{2,4},{4,6},{6,8},{8,10},{10,12},{12,14},{14,0},{1,3},{3,5},... | collective-permute-start | bytes 774152 | tf_op jit(solution)/shard_map/ppermute | solution.py:594
  184.0 7.6 %collective-permute-start.41 = (bf16[336,384]{1,0:T(8,128)(2,1)S(1)}, bf16[336,384]{1,0:T(8,128)(2,1)S(1)}, u32[]{:S(2)}, u32[]{:S(2)}) collective-permute-start(bf16[336,384]{1,0:T(8,128)(2,1)S(1)} %get-tuple-element.77), channel_id=1, source_target_pairs={{0,2},{2,4},{4,6},{6,8},{8,10},{10,12},{12,14},{14,0},{1,3},{3,5},... | collective-permute-start | bytes 774152 | tf_op jit(solution)/shard_map/ppermute | solution.py:594
  188.3 12.0 %copy-start.18 = (f32[336,384]{1,0:T(8,128)S(1)}, f32[336,384]{1,0:T(8,128)}, u32[]{:S(2)}) copy-start(f32[336,384]{1,0:T(8,128)} %get-tuple-element.82) | copy-start | bytes 1548292
  188.3 7.1 %collective-permute-start.43 = (bf16[336,384]{1,0:T(8,128)(2,1)S(1)}, bf16[336,384]{1,0:T(8,128)(2,1)S(1)}, u32[]{:S(2)}, u32[]{:S(2)}) collective-permute-start(bf16[336,384]{1,0:T(8,128)(2,1)S(1)} %get-tuple-element.81), channel_id=1, source_target_pairs={{0,14},{2,0},{4,2},{6,4},{8,6},{10,8},{12,10},{14,12},{1,15},{3,1}... | collective-permute-start | bytes 774152 | tf_op jit(solution)/shard_map/ppermute | solution.py:594
  192.7 7.6 %collective-permute-start.42 = (bf16[336,384]{1,0:T(8,128)(2,1)S(1)}, bf16[336,384]{1,0:T(8,128)(2,1)S(1)}, u32[]{:S(2)}, u32[]{:S(2)}) collective-permute-start(bf16[336,384]{1,0:T(8,128)(2,1)S(1)} %add_convert_fusion.1), channel_id=1, source_target_pairs={{0,2},{2,4},{4,6},{6,8},{8,10},{10,12},{12,14},{14,0},{1,3},{3,5},... | collective-permute-start | bytes 774152 | tf_op jit(solution)/shard_map/ppermute | solution.py:594
  (11 other events, 27.2 us)
